TPU v7x, 256 devices: a whole 4x4x8 slice. The times are simulated.
256 devices in a mesh: row: 8 (over y, core), col: 32 (over z, x).
Axes of the slice: x: 4, y: 4, z: 8, core: 2. Of those that a mesh axis runs over, the one named last changes fastest.
Arguments:
- left_values: bfloat16 [16384, 4096], P('col', 'row'), may hold values from 0.1 to 18, as said below
- left_pattern: int32 [128, 32], replicated, may hold values from 0 to 1, as said below
- right_values: bfloat16 [4096, 8192], P('col', 'row'), may hold values from 0.099609375 to 1
- right_pattern: int32 [32, 64], replicated, may hold values from 0 to 1, as said below
Outputs:
- flow: float32 [16384, 8192], P('col', 'row')
Inputs may be any that keep to these rules, and one draw needn't show every extreme that they name: left_pattern[i, i % 32] is 1 for every block row i; in every block row, each aligned group of 4 block columns holds at most 2 ones, and some group holds exactly 2. right_pattern[j % 32, j] is 1 for every block column j; in every block row, each aligned group of 8 block columns holds at most 4 ones, and some group holds exactly 4. `left_values`: positive entries.
All inputs are finite; a program needn't handle non-finite values.
Results may differ from a plain program's by a relative error of at most 0.0003.
Values may be sent and summed in bfloat16 or wider, within the bound.
No kernel may reach another device: no remote copies, remote signals or barrier semaphores. Data moves between devices by JAX's collectives and lax.ppermute only.
A program may use at most 64 MiB of HBM per device.

v0:
```python
import jax
import jax.numpy as jnp
from jax import lax
from jax.sharding import Mesh
from jax.sharding import PartitionSpec as P

BLOCK = 128
COL = ("col_0", "col_1")


def copy_for_each(shard, axis):
    size = lax.axis_size(axis)
    return lax.all_to_all(
        jnp.broadcast_to(shard[None], (size, *shard.shape)), axis, 0, 0, tiled=True
    )


def joined_along(pieces, dim):
    lengths = list(pieces.shape[1:])
    lengths[dim] *= pieces.shape[0]
    return jnp.moveaxis(pieces, 0, dim).reshape(lengths)


def gathered_copies(shard, axis, dim):
    pieces = copy_for_each(shard, axis)
    return joined_along(pieces, dim)


def gathered_by_axis(shard, axes, dim):
    for axis in reversed(axes):
        shard = lax.all_gather(shard, axis, axis=dim, tiled=True)
    return shard


def over_copies(shard, axis):
    return copy_for_each(shard, axis).sum(axis=0)


def expand(values, pattern):
    block_rows, block_cols = pattern.shape
    height, width = values.shape
    shaped = values.reshape(block_rows, height // block_rows, block_cols, width // block_cols)
    masked = shaped * pattern.astype(values.dtype)[:, None, :, None]
    return masked.reshape(height, width)


def shards(left_values, left_pattern, right_values, right_pattern):
    col_index = lax.axis_index(COL)
    row_index = lax.axis_index("row")
    row_count = lax.axis_size("row")
    rows_local, inner_local = left_values.shape
    left_blocks = rows_local // BLOCK
    inner_left_blocks = inner_local // BLOCK
    left_mask = lax.dynamic_slice(
        left_pattern,
        (col_index * left_blocks, row_index * inner_left_blocks),
        (left_blocks, inner_left_blocks),
    )
    masked_left = expand(left_values, left_mask)
    left_slots = max(1, inner_left_blocks // 2)
    my_rows = lax.dynamic_slice_in_dim(left_pattern, col_index * left_blocks, left_blocks, 0)
    grouped_rows = my_rows.reshape(left_blocks, row_count, inner_left_blocks)
    left_order = jnp.argsort(1 - grouped_rows, axis=2, stable=True)[:, :, :left_slots]
    left_selector = (
        left_order[:, :, :, None] == jnp.arange(inner_left_blocks)[None, None, None, :]
    ).astype(jnp.bfloat16)
    own_left = lax.dynamic_index_in_dim(left_selector, row_index, 1, keepdims=False)
    shaped_left = masked_left.reshape(left_blocks, BLOCK, inner_left_blocks, BLOCK)
    packed_left = jnp.einsum(
        "idkn,isk->idsn", shaped_left, own_left, preferred_element_type=jnp.bfloat16
    )
    gathered_left = gathered_copies(packed_left, "row", 2)
    gathered_left = gathered_left.reshape(left_blocks, BLOCK, row_count, left_slots, BLOCK)
    unpacked_left = jnp.einsum(
        "idrsn,irsk->idrkn", gathered_left, left_selector, preferred_element_type=jnp.bfloat16
    )
    whole_left = unpacked_left.reshape(rows_local, row_count * inner_local)
    inner_rows, cols_local = right_values.shape
    right_blocks = inner_rows // BLOCK
    col_blocks = cols_local // BLOCK
    right_mask = lax.dynamic_slice(
        right_pattern,
        (col_index * right_blocks, row_index * col_blocks),
        (right_blocks, col_blocks),
    )
    masked_right = expand(right_values, right_mask)
    slot_total = col_blocks // 2
    group_mask = lax.dynamic_slice_in_dim(right_pattern, row_index * col_blocks, col_blocks, 1)
    slot_order = jnp.argsort(1 - group_mask, axis=1, stable=True)[:, :slot_total]
    selector = (slot_order[:, :, None] == jnp.arange(col_blocks)[None, None, :]).astype(
        jnp.bfloat16
    )
    own_selector = lax.dynamic_slice_in_dim(selector, col_index * right_blocks, right_blocks, 0)
    shaped_right = masked_right.reshape(right_blocks, BLOCK, col_blocks, BLOCK)
    packed = jnp.einsum(
        "kdjn,ksj->kdsn", shaped_right, own_selector, preferred_element_type=jnp.bfloat16
    )
    packed = packed.reshape(right_blocks * BLOCK, slot_total, BLOCK)
    incoming = gathered_by_axis(packed, COL, 0)
    piece_blocks = incoming.shape[0] // BLOCK
    shaped_piece = incoming.reshape(piece_blocks, BLOCK, slot_total, BLOCK)
    unpacked = jnp.einsum(
        "kdsn,ksj->kdjn", shaped_piece, selector, preferred_element_type=jnp.bfloat16
    )
    unpacked = unpacked.reshape(piece_blocks * BLOCK, cols_local)
    product = jnp.dot(whole_left, unpacked, preferred_element_type=jnp.float32)
    inflated = product * product
    totals = over_copies(jnp.sum(inflated, axis=0), COL)
    column_mean = totals / (rows_local * lax.axis_size(COL))
    return inflated / column_mean[None, :]


def solution(mesh):
    finer = Mesh(mesh.devices.reshape(mesh.shape["row"], 8, 4), ("row", "col_0", "col_1"))
    return jax.shard_map(
        shards,
        mesh=finer,
        in_specs=(P(COL, "row"), P(), P(COL, "row"), P()),
        out_specs=P(COL, "row"),
        check_vma=False,
    )
```

profile of v0, /device:TPU:24, one launch (start us, length us, event | category | flops | bytes accessed | tf_op | source)
XLA Modules:
  0.0 118.0 jit_solution(6438968827592128584)
XLA Ops:
  6.5 0.0 all-gather.4.cloned.1.call-start
  6.5 0.8 constant_dynamic-slice_fusion
  7.3 0.8 convert_bitcast_fusion
  8.1 0.1 broadcast_bitcast_fusion
  8.2 0.1 copy.71
  8.2 0.7 sort.35
  8.9 0.1 copy.59
  9.0 0.1 iota_compare_fusion
  9.1 1.0 multiply_bitcast_fusion
  10.1 0.2 convolution_bitcast_fusion.2
  10.3 13.9 %all-gather = bf16[1,512,4,128]{3,2,0,1:T(4,128)(2,1)} all-gather(bf16[1,128,4,128]{3,2,0,1:T(4,128)(2,1)S(1)} %convolution_bitcast_fusion.2), channel_id=2, replica_groups=mesh['row'=8,'col_0'=8,'col_1'=4] {'col_1'}, dimensions={1}, use_global_device_ids=true | all-gather | bytes 655360 | tf_op jit(solution)/shard_map/all_gather | solution.py:31
  24.2 0.0 all-gather.4.cloned.1.call-update
  24.2 0.8 dynamic-slice_convert_fusion
  25.0 0.1 copy.53
  25.1 0.8 dynamic-slice_subtract_fusion
  25.9 0.1 copy.51
  26.0 1.3 %sort.34 = (s32[4,8,4]{1,2,0:T(4,128)}, s32[4,8,4]{1,2,0:T(4,128)S(1)}) sort(s32[4,8,4]{1,2,0:T(4,128)S(1)} %copy.51, s32[4,8,4]{1,2,0:T(4,128)S(1)} %iota.22), dimensions={2}, to_apply=%region_0.0 | sort | flops 896 | bytes 2048 | tf_op jit(solution)/shard_map/jit(argsort)/sort | solution.py:63
  27.3 0.1 copy.52
  27.4 1.2 reshape.46
  28.6 0.1 fusion.12
  28.7 0.5 convolution_bitcast_fusion.1
  29.2 1.9 %broadcast_in_dim.4 = bf16[8,4,128,2,128]{4,3,2,1,0:T(2,128)(2,1)S(1)} broadcast(bf16[4,128,2,128]{3,2,1,0:T(2,128)(2,1)S(1)} %convolution_bitcast_fusion.1), dimensions={1,2,3,4} | broadcast | bytes 2359296 | tf_op jit(solution)/shard_map/broadcast_in_dim | solution.py:14
  31.1 30.0 %all_to_all.11 = bf16[8,4,128,2,128]{4,3,2,1,0:T(2,128)(2,1)S(1)} all-to-all(bf16[8,4,128,2,128]{4,3,2,1,0:T(2,128)(2,1)S(1)} %broadcast_in_dim.4), channel_id=1, replica_groups=mesh['row'=8,'col_0'=8,'col_1'=4] {'row'}, dimensions={0} | all-to-all | bytes 4194304 | tf_op jit(solution)/shard_map/all_to_all | solution.py:13
  61.0 3.5 %convolution_bitcast_fusion = bf16[4,128,8,4,128]{4,3,1,2,0:T(4,128)(2,1)S(1)} fusion(bf16[8,4,128,2,128]{4,3,2,1,0:T(2,128)(2,1)S(1)} %all_to_all.11, pred[4,8,2,4,1]{3,0,2,1,4:T(4,128)(4,1)S(1)} %get-tuple-element.9), kind=kOutput, calls=%fused_computation.3 | convolution fusion | flops 8388608 | bytes 6291712 | tf_op jit(solution)/shard_map/idrsn,irsk->idrkn/dot_general | solution.py:74
  64.5 3.6 %copy.57 = bf16[4,128,8,4,128]{4,3,2,1,0:T(4,128)(2,1)} copy(bf16[4,128,8,4,128]{4,3,1,2,0:T(4,128)(2,1)S(1)} %convolution_bitcast_fusion) | data formatting | bytes 8388608 | tf_op jit(solution)/shard_map/idrsn,irsk->idrkn/transpose | solution.py:74
  68.1 7.8 %reshape.47 = bf16[512,4096]{1,0:T(8,128)(2,1)} reshape(bf16[4,128,8,4,128]{4,3,2,1,0:T(4,128)(2,1)} %copy.57) | data formatting | bytes 8388608 | tf_op jit(solution)/shard_map/reshape | solution.py:77
  75.9 6.1 %all-gather.4.cloned.1.call-done = bf16[1,4096,4,128]{3,2,0,1:T(4,128)(2,1)} async-done(((bf16[1,512,4,128]{3,2,0,1:T(4,128)(2,1)}), bf16[1,4096,4,128]{3,2,0,1:T(4,128)(2,1)}) %all-gather.4.cloned.1.call-update) | async-done | bytes 4194320 | tf_op jit(solution)/shard_map/all_gather | solution.py:31
  82.0 0.0 copy-start
  82.0 5.5 %fusion.5 = bf16[32,8,128,128]{3,1,2,0:T(8,128)(2,1)S(1)} fusion(bf16[32,128,4,128]{3,2,1,0:T(4,128)(2,1)} %bitcast.49, s32[32,4]{1,0:T(8,128)S(1)} %copy.59), kind=kOutput, calls=%fused_computation.13 | convolution fusion | flops 33555456 | bytes 12583424 | tf_op jit(solution)/shard_map/kdsn,ksj->kdjn/dot_general | solution.py:102
  87.5 0.0 copy-done
  87.5 4.5 %multiply_reduce_fusion = (f32[1024]{0:T(1024)S(1)}, f32[512,1024]{1,0:T(8,128)S(1)}) fusion(bf16[512,4096]{1,0:T(8,128)(2,1)S(1)} %copy-done, bf16[512,8,8,128]{3,2,1,0:T(8,128)(2,1)S(1)} %bitcast.48), kind=kOutput, calls=%fused_computation.6 | convolution fusion | flops 4296014848 | bytes 14684160 | tf_op jit(solution)/shard_map/dot_general | solution.py:106
  92.0 0.1 broadcast_in_dim.5
  92.1 17.4 %all_to_all.12 = f32[32,1,1024]{2,1,0:T(1,128)S(1)} all-to-all(f32[32,1,1024]{2,1,0:T(1,128)S(1)} %broadcast_in_dim.5), channel_id=1, replica_groups=mesh['row'=8,'col_0'=8,'col_1'=4] {'col_0','col_1'}, dimensions={0} | all-to-all | bytes 262144 | tf_op jit(solution)/shard_map/all_to_all | solution.py:13
  109.5 0.1 reduce_sum.19
  109.6 1.6 %multiply_divide_fusion = f32[512,1024]{1,0:T(8,128)} fusion(f32[512,1024]{1,0:T(8,128)S(1)} %get-tuple-element.12, f32[1024]{0:T(1024)S(1)} %broadcast_multiply_fusion), kind=kLoop, calls=%fused_computation.5 | loop fusion | flops 1048576 | bytes 4198400 | tf_op jit(solution)/shard_map/div | solution.py:110
  (8 shorter events, 0.1 us)
Async XLA Ops:
  6.5 75.5 %all-gather.4.cloned.1.call-start = ((), (), s32[]{:S(2)}) async-start(), calls=%async_computation.2 | async-start | bytes 4718592 | tf_op jit(solution)/shard_map/all_gather | solution.py:31
  82.0 5.5 %copy-start = (bf16[512,4096]{1,0:T(8,128)(2,1)S(1)}, bf16[512,4096]{1,0:T(8,128)(2,1)}, u32[]{:S(2)}) copy-start(bf16[512,4096]{1,0:T(8,128)(2,1)} %reshape.47) | copy-start | bytes 12582916
Sparse Core Ops, SparseCore 0:
  24.4 57.5 all-gather.3
where the time goes:
time: 119 us; the launch traced here: 118 us
  blocking collectives  61.2 us (51%)
  local copies, waits for them, and re-layouts  15.9 us (13%)
  matrix products  14.2 us (12%)
  between operations  13.5 us (11%)
  other arithmetic  7.13 us (6%)
  waiting for transfers between devices  6.08 us (5%)
    all_to_all x2, blocking collectives, copy_for_each(): lax.all_to_all(jnp.broadcast_to(shard[None], (size, *shard.shape)), axis,...  47.3 us
    all_gather x1, blocking collectives, gathered_by_axis(): shard = lax.all_gather(shard, axis, axis=dim, tiled=True)  13.9 us
    reshape x1, local copies, waits for them, and re-layouts, shards(): whole_left = unpacked_left.reshape(rows_local, row_count * inner_local)  7.82 us
    all_gather x1, waiting for transfers between devices, gathered_by_axis(): shard = lax.all_gather(shard, axis, axis=dim, tiled=True)  6.06 us
    dot_general x1, matrix products, shards(): jnp.einsum('kdsn,ksj->kdjn', shaped_piece, selector, preferred_element_ty...  5.49 us
    dot_general x1, matrix products, shards(): product = jnp.dot(whole_left, unpacked, preferred_element_type=jnp.float32)  4.5 us
    transpose x1, local copies, waits for them, and re-layouts, shards(): jnp.einsum('idrsn,irsk->idrkn', gathered_left, left_selector, preferred_e...  3.6 us
    dot_general x1, matrix products, shards(): jnp.einsum('idrsn,irsk->idrkn', gathered_left, left_selector, preferred_e...  3.48 us
  transfers between devices with their start and end apart: 1, of which 1 were waited for; matrix products, arithmetic and copies ran while one was open for 18% of the time, Pallas kernels for 0%

commit v1 on v0

v1 whole, which is shorter than its diff:
```python
import functools

import jax
import jax.numpy as jnp
from jax import lax
from jax.experimental import pallas as pl
from jax.experimental.pallas import tpu as pltpu
from jax.sharding import Mesh
from jax.sharding import PartitionSpec as P

BLOCK = 128
SLOTS = 4
LEFT_SLOTS = 2
X_SHIFTS = (0, 3, 1, 2)
VMEM_LIMIT = 40 * 1024 * 1024


def lanes(start, blocks=1):
    return pl.ds(pl.multiple_of(start * BLOCK, BLOCK), blocks * BLOCK)


def pack_kernel(right_pattern, left_pattern, right, left, right_out, left_out):
    row = lax.axis_index("row")
    col = lax.axis_index("z") * lax.axis_size("x") + lax.axis_index("x")
    col_blocks = right.shape[1] // BLOCK
    right_out[...] = jnp.zeros_like(right_out)
    slot = jnp.int32(0)
    for j in range(col_blocks):
        present = right_pattern[col, row * col_blocks + j]

        @pl.when(present != 0)
        def _(j=j, slot=slot):
            right_out[:, lanes(slot)] = right[:, j * BLOCK : (j + 1) * BLOCK]

        slot = slot + present
    left_out[...] = jnp.zeros_like(left_out)
    block_rows, inner_blocks = left.shape[0] // BLOCK, left.shape[1] // BLOCK
    for i in range(block_rows):
        rows = slice(i * BLOCK, (i + 1) * BLOCK)
        slot = jnp.int32(0)
        for k in range(inner_blocks):
            present = left_pattern[row * inner_blocks + k, col * block_rows + i]

            @pl.when(present != 0)
            def _(k=k, slot=slot, rows=rows):
                left_out[rows, lanes(slot)] = left[rows, k * BLOCK : (k + 1) * BLOCK]

            slot = slot + present


def pack(right_pattern, left_pattern, right, left):
    return pl.pallas_call(
        pack_kernel,
        out_shape=(
            jax.ShapeDtypeStruct((right.shape[0], SLOTS * BLOCK), right.dtype),
            jax.ShapeDtypeStruct((left.shape[0], LEFT_SLOTS * BLOCK), left.dtype),
        ),
        in_specs=[pl.BlockSpec(memory_space=pltpu.SMEM)] * 2
        + [pl.BlockSpec(memory_space=pltpu.VMEM)] * 2,
        out_specs=[pl.BlockSpec(memory_space=pltpu.VMEM)] * 2,
        compiler_params=pltpu.CompilerParams(vmem_limit_bytes=8 * 1024 * 1024),
        name="pack",
    )(right_pattern, left_pattern, right, left)


def product_kernel(shifts, first, last, right_pattern, left_pattern, *refs):
    refs = list(refs)
    left = refs.pop(0)
    pieces = [refs.pop(0) for _ in range(2 * len(shifts))]
    total = None if first else refs.pop(0)
    out = refs.pop(0)
    sums = refs.pop(0) if last else None
    packed_left, dense_left, dense_right, sem = refs
    row, z, x = lax.axis_index("row"), lax.axis_index("z"), lax.axis_index("x")
    z_size, x_size = lax.axis_size("z"), lax.axis_size("x")
    block_rows = dense_left.shape[0] // BLOCK
    col_blocks = dense_right.shape[1] // BLOCK
    col = z * x_size + x
    groups = [lax.rem(z + shift + z_size, z_size) for shift in shifts]
    copies = [
        pltpu.make_async_copy(left.at[group], packed_left.at[n], sem.at[n])
        for n, group in enumerate(groups)
    ]
    for copy in copies:
        copy.start()
    zero = jnp.zeros((BLOCK, BLOCK), dense_right.dtype)
    for n, group in enumerate(groups):
        for m, x_shift in enumerate(X_SHIFTS):
            k = group * x_size + lax.rem(x + x_shift, x_size)
            piece = pieces[2 * n + m // 2]
            piece_rows = slice((m % 2) * BLOCK, (m % 2 + 1) * BLOCK)
            rows = slice((n * x_size + m) * BLOCK, (n * x_size + m + 1) * BLOCK)
            slot = jnp.int32(0)
            for j in range(col_blocks):
                present = right_pattern[k, row * col_blocks + j]

                @pl.when(present != 0)
                def _(j=j, slot=slot, rows=rows, piece=piece, piece_rows=piece_rows):
                    dense_right[rows, j * BLOCK : (j + 1) * BLOCK] = piece[piece_rows, lanes(slot)]

                @pl.when(present == 0)
                def _(j=j, rows=rows):
                    dense_right[rows, j * BLOCK : (j + 1) * BLOCK] = zero

                slot = slot + present
    for copy in copies:
        copy.wait()
    for n, group in enumerate(groups):
        for i in range(block_rows):
            rows = slice(i * BLOCK, (i + 1) * BLOCK)
            for m, x_shift in enumerate(X_SHIFTS):
                inside = lax.rem(x + x_shift, x_size)
                k = group * x_size + inside
                present = left_pattern[k, col * block_rows + i]
                before = jnp.int32(0)
                for other in range(x_size):
                    there = left_pattern[group * x_size + other, col * block_rows + i]
                    before = before + jnp.where(other < inside, there, 0)
                columns = slice((n * x_size + m) * BLOCK, (n * x_size + m + 1) * BLOCK)

                @pl.when(present != 0)
                def _(n=n, rows=rows, columns=columns, before=before):
                    dense_left[rows, columns] = packed_left[n, rows, lanes(before)]

                @pl.when(present == 0)
                def _(rows=rows, columns=columns):
                    dense_left[rows, columns] = zero

    width = 256

    @pl.loop(0, out.shape[1] // width)
    def _(t):
        columns = pl.ds(pl.multiple_of(t * width, width), width)
        value = jnp.dot(
            dense_left[...], dense_right[:, columns], preferred_element_type=jnp.float32
        )
        if not first:
            value = value + total[:, columns]
        if last:
            value = value * value
            sums[:, columns] = jnp.sum(value, axis=0, keepdims=True)
        out[:, columns] = value


def product(shifts, right_pattern, left_pattern, left, pieces, total, last):
    rows, cols = left.shape[1], right_pattern.shape[1] // 8 * BLOCK
    inner = len(shifts) * 4 * BLOCK
    out_shape = [jax.ShapeDtypeStruct((rows, cols), jnp.float32)]
    if last:
        out_shape.append(jax.ShapeDtypeStruct((1, cols), jnp.float32))
    vmem = pl.BlockSpec(memory_space=pltpu.VMEM)
    operands = [right_pattern, left_pattern, left, *pieces]
    aliases = {}
    if total is not None:
        aliases = {len(operands): 0}
        operands.append(total)
    return pl.pallas_call(
        functools.partial(product_kernel, shifts, total is None, last),
        out_shape=out_shape,
        in_specs=[pl.BlockSpec(memory_space=pltpu.SMEM)] * 2
        + [pl.BlockSpec(memory_space=pl.ANY)]
        + [vmem] * (len(operands) - 3),
        out_specs=[vmem] * len(out_shape),
        scratch_shapes=[
            pltpu.VMEM((len(shifts), rows, LEFT_SLOTS * BLOCK), jnp.bfloat16),
            pltpu.VMEM((rows, inner), jnp.bfloat16),
            pltpu.VMEM((inner, cols), jnp.bfloat16),
            pltpu.SemaphoreType.DMA((len(shifts),)),
        ],
        input_output_aliases=aliases,
        compiler_params=pltpu.CompilerParams(vmem_limit_bytes=VMEM_LIMIT),
        cost_estimate=pl.CostEstimate(
            flops=2 * rows * inner * cols, bytes_accessed=4 * 1024 * 1024, transcendentals=0
        ),
        name="product_" + "_".join(str(s % 8) for s in shifts),
    )(*operands)


def moved(value, axis, step):
    size = lax.axis_size(axis)
    return lax.ppermute(value, axis, [(i, (i + step) % size) for i in range(size)])


def shards(left_values, left_pattern, right_values, right_pattern):
    left_pattern = left_pattern.T
    packed_right, packed_left = pack(right_pattern, left_pattern, right_values, left_values)
    left = lax.all_gather(packed_left, "row", axis=0, tiled=False)
    near = [packed_right] + [moved(packed_right, "x", -shift) for shift in X_SHIFTS[1:]]
    own = [jnp.concatenate(near[:2], 0), jnp.concatenate(near[2:], 0)]
    up, down = own, own
    blocks = {0: own}
    for step in range(1, 5):
        up = [moved(piece, "z", 1) for piece in up]
        blocks[-step] = up
        if step < 4:
            down = [moved(piece, "z", -1) for piece in down]
            blocks[step] = down
    total = None
    for shifts in ((0, -1, 1), (-2, 2), (-3, 3), (-4,)):
        pieces = [piece for shift in shifts for piece in blocks[shift]]
        last = shifts == (-4,)
        results = product(shifts, right_pattern, left_pattern, left, pieces, total, last)
        total = results[0]
    sums = results[1]
    count = lax.axis_size("z") * lax.axis_size("x")
    spread = lax.all_to_all(
        jnp.broadcast_to(sums, (count, sums.shape[1])), ("z", "x"), 0, 0, tiled=True
    )
    column_mean = jnp.sum(spread, axis=0) / (total.shape[0] * count)
    return total / column_mean[None, :]


def solution(mesh):
    finer = Mesh(mesh.devices.reshape(mesh.shape["row"], 8, 4), ("row", "z", "x"))
    return jax.shard_map(
        shards,
        mesh=finer,
        in_specs=(P(("z", "x"), "row"), P(), P(("z", "x"), "row"), P()),
        out_specs=P(("z", "x"), "row"),
        check_vma=False,
    )
```

time: 119 us -> 118 us (level)
  blocking collectives: 61.2 us -> 18.4 us
  starting transfers between devices: 0.01 us -> 25.7 us
  Pallas kernels: 0 us -> 21 us
  waiting for transfers between devices: 6.08 us -> 22.3 us
  matrix products: 14.2 us -> 0 us
  other arithmetic: 7.13 us -> 1.68 us
  local copies, waits for them, and re-layouts: 15.9 us -> 14.4 us
    all_to_all x2 -> x1, blocking collectives: 47.3 us -> 18.4 us  [shards(): lax.all_to_all(jnp.broadcast_to(sums, (count, sums.shape[1])), ('z', 'x')...]
    ppermute x0 -> x17, starting transfers between devices: none -> 25.7 us  [moved(): lax.ppermute(value, axis, [(i, (i + step) % size) for i in range(size)])]
    ppermute x0 -> x17, waiting for transfers between devices: none -> 22.3 us  [moved(): lax.ppermute(value, axis, [(i, (i + step) % size) for i in range(size)])]
    pallas_call x0 -> x5, Pallas kernels: none -> 21 us  [the longest x4 18.9 us: product(): pl.pallas_call(functools.partial(product_kernel, shifts, total is None, l...]
    dot_general x5 -> x0, matrix products: 14.2 us -> none  [the longest x1 5.49 us: shards(): jnp.einsum('kdsn,ksj->kdjn', shaped_piece, selector, preferred_element_ty...]
    unnamed x4 -> x40, local copies, waits for them, and re-layouts: 0.11 us -> 14.3 us
    all_gather x1 -> x0, blocking collectives: 13.9 us -> none  [gathered_by_axis(): shard = lax.all_gather(shard, axis, axis=dim, tiled=True)]
    reshape x2 -> x0, local copies, waits for them, and re-layouts: 8.98 us -> none  [the longest x1 7.82 us: shards(): whole_left = unpacked_left.reshape(rows_local, row_count * inner_local)]
  transfers between devices with their start and end apart: 1 -> 18, of which waited for: 1 -> 6; matrix products, arithmetic and copies ran while one was open for 18% -> 0% of each run, Pallas kernels for 0% -> 13%
where the time goes in v1:
time: 118 us; the launch traced here: 117 us
  starting transfers between devices  25.7 us (22%)
  waiting for transfers between devices  22.3 us (19%)
  Pallas kernels  21 us (18%)
  blocking collectives  18.4 us (16%)
  local copies, waits for them, and re-layouts  14.4 us (12%)
  between operations  13.5 us (11%)
  other arithmetic  1.68 us (1%)
    ppermute x17, starting transfers between devices, moved(): lax.ppermute(value, axis, [(i, (i + step) % size) for i in range(size)])  25.7 us
    ppermute x17, waiting for transfers between devices, moved(): lax.ppermute(value, axis, [(i, (i + step) % size) for i in range(size)])  22.3 us
    pallas_call x4, Pallas kernels, product(): pl.pallas_call(functools.partial(product_kernel, shifts, total is None, l...  18.9 us
    all_to_all x1, blocking collectives, shards(): lax.all_to_all(jnp.broadcast_to(sums, (count, sums.shape[1])), ('z', 'x')...  18.4 us
    unnamed x40, local copies, waits for them, and re-layouts  14.3 us
  transfers between devices with their start and end apart: 18, of which 6 were waited for; matrix products, arithmetic and copies ran while one was open for 0% of the time, Pallas kernels for 13%

profile of v1, /device:TPU:24, one launch (start us, length us, event | category | flops | bytes accessed | tf_op | source)
XLA Modules:
  0.0 117.0 jit_solution(2298361999771935591)
XLA Ops:
  6.5 0.0 all-gather.3.cloned.1.call-start
  6.5 1.0 copy-done.1
  7.6 0.7 copy-done.2
  8.3 0.7 copy-done.4
  9.0 0.9 copy-done.6
  10.0 2.1 %pack.1 = (bf16[128,512]{1,0:T(8,128)(2,1)S(1)}, bf16[512,256]{1,0:T(8,128)(2,1)}) custom-call(s32[32,64]{1,0:T(8,128)S(1)} %copy-done.2, s32[32,128]{1,0:T(8,128)S(1)} %bitcast.7, bf16[128,1024]{1,0:T(8,128)(2,1)S(1)} %copy-done.6, bf16[512,512]{1,0:T(8,128)(2,1)S(1)} %copy-done.1), custom_call_target="tpu_custom_call" | custom-call | tf_op jit(solution)/shard_map/pack/pallas_call | solution.py:52
  12.0 0.0 all-gather.3.cloned.1.call-update
  12.1 2.8 %collective-permute-start.5 = (bf16[128,512]{1,0:T(8,128)(2,1)S(1)}, bf16[128,512]{1,0:T(8,128)(2,1)S(1)}, u32[]{:S(2)}, u32[]{:S(2)}) collective-permute-start(bf16[128,512]{1,0:T(8,128)(2,1)S(1)} %get-tuple-element.10), channel_id=1, source_target_pairs={{0,3},{1,0},{2,1},{3,2},{4,7},{5,4},{6,5},{7,6},{8,11},{9,8},{10,9... | collective-permute-start | bytes 393224 | tf_op jit(solution)/shard_map/ppermute | solution.py:181
  14.9 0.8 collective-permute-start.6
  15.7 0.9 collective-permute-start
  16.6 3.9 %collective-permute-done.5 = bf16[128,512]{1,0:T(8,128)(2,1)S(1)} collective-permute-done((bf16[128,512]{1,0:T(8,128)(2,1)S(1)}, bf16[128,512]{1,0:T(8,128)(2,1)S(1)}, u32[]{:S(2)}, u32[]{:S(2)}) %collective-permute-start.5) | collective-permute-done | bytes 131104 | tf_op jit(solution)/shard_map/ppermute | solution.py:181
  20.5 2.3 %collective-permute-done.6 = bf16[128,512]{1,0:T(8,128)(2,1)S(1)} collective-permute-done((bf16[128,512]{1,0:T(8,128)(2,1)S(1)}, bf16[128,512]{1,0:T(8,128)(2,1)S(1)}, u32[]{:S(2)}, u32[]{:S(2)}) %collective-permute-start.6) | collective-permute-done | bytes 131104 | tf_op jit(solution)/shard_map/ppermute | solution.py:181
  22.8 0.0 copy-start.9
  22.8 2.0 %collective-permute-start.7 = (bf16[256,512]{1,0:T(8,128)(2,1)S(1)}, bf16[256,512]{1,0:T(8,128)(2,1)S(1)}, u32[]{:S(2)}, u32[]{:S(2)}) collective-permute-start(bf16[256,512]{1,0:T(8,128)(2,1)S(1)} %constant_dynamic-update-slice_fusion.2.refs_2_), channel_id=1, source_target_pairs={{0,4},{4,8},{8,12},{12,16},{16,20},{20,24},{24,28},{28,0},{1,5},{5... | collective-permute-start | bytes 786440 | tf_op jit(solution)/shard_map/ppermute | solution.py:181
  24.8 0.0 collective-permute-done
  24.8 2.0 %collective-permute-start.1 = (bf16[256,512]{1,0:T(8,128)(2,1)S(1)}, bf16[256,512]{1,0:T(8,128)(2,1)S(1)}, u32[]{:S(2)}, u32[]{:S(2)}) collective-permute-start(bf16[256,512]{1,0:T(8,128)(2,1)S(1)} %constant_dynamic-update-slice_fusion.refs_1_), channel_id=1, source_target_pairs={{0,4},{4,8},{8,12},{12,16},{16,20},{20,24},{24,28},{28,0},{1,5},{5... | collective-permute-start | bytes 786440 | tf_op jit(solution)/shard_map/ppermute | solution.py:181
  26.8 3.4 %collective-permute-start.14 = (bf16[256,512]{1,0:T(8,128)(2,1)S(1)}, bf16[256,512]{1,0:T(8,128)(2,1)S(1)}, u32[]{:S(2)}, u32[]{:S(2)}) collective-permute-start(bf16[256,512]{1,0:T(8,128)(2,1)S(1)} %constant_dynamic-update-slice_fusion.2.refs_2_), channel_id=1, source_target_pairs={{0,28},{4,0},{8,4},{12,8},{16,12},{20,16},{24,20},{28,24},{1,29},{... | collective-permute-start | bytes 786440 | tf_op jit(solution)/shard_map/ppermute | solution.py:181
  30.2 1.9 %collective-permute-start.11 = (bf16[256,512]{1,0:T(8,128)(2,1)S(1)}, bf16[256,512]{1,0:T(8,128)(2,1)S(1)}, u32[]{:S(2)}, u32[]{:S(2)}) collective-permute-start(bf16[256,512]{1,0:T(8,128)(2,1)S(1)} %constant_dynamic-update-slice_fusion.refs_1_), channel_id=1, source_target_pairs={{0,28},{4,0},{8,4},{12,8},{16,12},{20,16},{24,20},{28,24},{1,29},{... | collective-permute-start | bytes 786440 | tf_op jit(solution)/shard_map/ppermute | solution.py:181
  32.1 0.7 copy-done.7
  32.8 2.6 %collective-permute-done.7.refs_4_ = bf16[256,512]{1,0:T(8,128)(2,1)S(1)} collective-permute-done((bf16[256,512]{1,0:T(8,128)(2,1)S(1)}, bf16[256,512]{1,0:T(8,128)(2,1)S(1)}, u32[]{:S(2)}, u32[]{:S(2)}) %collective-permute-start.7) | collective-permute-done | bytes 262176 | tf_op jit(solution)/shard_map/ppermute | solution.py:181
  35.4 0.0 collective-permute-start.8
  35.4 0.7 copy-done.11
  36.1 4.9 %collective-permute-done.1.refs_3_ = bf16[256,512]{1,0:T(8,128)(2,1)S(1)} collective-permute-done((bf16[256,512]{1,0:T(8,128)(2,1)S(1)}, bf16[256,512]{1,0:T(8,128)(2,1)S(1)}, u32[]{:S(2)}, u32[]{:S(2)}) %collective-permute-start.1) | collective-permute-done | bytes 262176 | tf_op jit(solution)/shard_map/ppermute | solution.py:181
  41.0 0.0 collective-permute-start.2
  41.1 0.7 copy-done.13
  41.8 0.0 collective-permute-done.14.refs_6_
  41.8 3.2 %collective-permute-start.15 = (bf16[256,512]{1,0:T(8,128)(2,1)S(1)}, bf16[256,512]{1,0:T(8,128)(2,1)S(1)}, u32[]{:S(2)}, u32[]{:S(2)}) collective-permute-start(bf16[256,512]{1,0:T(8,128)(2,1)S(1)} %collective-permute-done.14.refs_6_), channel_id=1, source_target_pairs={{0,28},{4,0},{8,4},{12,8},{16,12},{20,16},{24,20},{28,24},{1,29},{... | collective-permute-start | bytes 786440 | tf_op jit(solution)/shard_map/ppermute | solution.py:181
  45.0 0.7 copy-done.15
  45.7 0.0 collective-permute-done.11.refs_5_
  45.7 1.0 collective-permute-start.12
  46.7 0.7 copy-done.17
  47.4 0.0 collective-permute-done.8.refs_2_
  47.4 1.0 collective-permute-start.9
  48.5 3.1 %collective-permute-done.2.refs_1_ = bf16[256,512]{1,0:T(8,128)(2,1)S(1)} collective-permute-done((bf16[256,512]{1,0:T(8,128)(2,1)S(1)}, bf16[256,512]{1,0:T(8,128)(2,1)S(1)}, u32[]{:S(2)}, u32[]{:S(2)}) %collective-permute-start.2) | collective-permute-done | bytes 262176 | tf_op jit(solution)/shard_map/ppermute | solution.py:181
  51.5 0.0 collective-permute-start.3
  51.5 0.0 collective-permute-done.15.refs_4_
  51.5 3.2 %collective-permute-start.16 = (bf16[256,512]{1,0:T(8,128)(2,1)S(1)}, bf16[256,512]{1,0:T(8,128)(2,1)}, u32[]{:S(2)}, u32[]{:S(2)}) collective-permute-start(bf16[256,512]{1,0:T(8,128)(2,1)S(1)} %collective-permute-done.15.refs_4_), channel_id=1, source_target_pairs={{0,28},{4,0},{8,4},{12,8},{16,12},{20,16},{24,20},{28,24},{1,29},{... | collective-permute-start | bytes 786440 | tf_op jit(solution)/shard_map/ppermute | solution.py:181
  54.8 0.0 collective-permute-done.12.refs_3_
  54.8 3.3 %collective-permute-start.13 = (bf16[256,512]{1,0:T(8,128)(2,1)S(1)}, bf16[256,512]{1,0:T(8,128)(2,1)}, u32[]{:S(2)}, u32[]{:S(2)}) collective-permute-start(bf16[256,512]{1,0:T(8,128)(2,1)S(1)} %collective-permute-done.12.refs_3_), channel_id=1, source_target_pairs={{0,28},{4,0},{8,4},{12,8},{16,12},{20,16},{24,20},{28,24},{1,29},{... | collective-permute-start | bytes 786440 | tf_op jit(solution)/shard_map/ppermute | solution.py:181
  58.1 0.0 collective-permute-done.9.refs_2_
  58.1 0.0 collective-permute-start.10
  58.1 5.5 %collective-permute-done.3.refs_1_ = bf16[256,512]{1,0:T(8,128)(2,1)} collective-permute-done((bf16[256,512]{1,0:T(8,128)(2,1)S(1)}, bf16[256,512]{1,0:T(8,128)(2,1)}, u32[]{:S(2)}, u32[]{:S(2)}) %collective-permute-start.3) | collective-permute-done | bytes 262176 | tf_op jit(solution)/shard_map/ppermute | solution.py:181
  63.6 0.0 collective-permute-start.4
  63.6 0.0 copy-done.9
  63.6 0.0 copy-done.3
  63.7 1.6 %copy-done = bf16[4096,256]{1,0:T(8,128)(2,1)S(1)} copy-done((bf16[4096,256]{1,0:T(8,128)(2,1)S(1)}, bf16[4096,256]{1,0:T(8,128)(2,1)}, u32[]{:S(2)}) %copy-start) | copy-done | bytes 2097176
  65.2 0.9 copy-done.8
  66.2 0.9 copy-done.10
  67.1 0.9 copy-done.12
  68.1 0.9 copy-done.14
  69.0 0.9 copy-done.16
  70.0 0.9 copy-done.18
  70.9 6.2 %product_0_7_1.1.refs_5_ = f32[512,1024]{1,0:T(8,128)S(1)} custom-call(s32[32,64]{1,0:T(8,128)S(1)} %copy-done.3, s32[32,128]{1,0:T(8,128)S(1)} %bitcast.8, bf16[8,512,256]{2,1,0:T(8,128)(2,1)S(1)} %bitcast.3, bf16[256,512]{1,0:T(8,128)(2,1)S(1)} %copy-done.8, bf16[256,512]{1,0:T(8,128)(2,1)S(1)} %copy-done.10, bf16[256,512]{1,0:T(8,128)(2,1)S(1)} %copy-done.14, ...), custom_call_target="tpu_custom_call" | custom-call | flops 1610612736 | bytes 4194304 | tf_op jit(solution)/shard_map/product_0_7_1/pallas_call | solution.py:157
  77.2 4.7 %product_6_2.1.refs_5_ = f32[512,1024]{1,0:T(8,128)S(1)} custom-call(s32[32,64]{1,0:T(8,128)S(1)} %copy-done.3, s32[32,128]{1,0:T(8,128)S(1)} %bitcast.9, bf16[8,512,256]{2,1,0:T(8,128)(2,1)S(1)} %bitcast.4, bf16[256,512]{1,0:T(8,128)(2,1)S(1)} %collective-permute-done.2.refs_1_, ...), custom_call_target="tpu_custom_call", output_to_operand_aliasing={{}: (7, {})} | custom-call | flops 1073741824 | bytes 4194304 | tf_op jit(solution)/shard_map/product_6_2/pallas_call | solution.py:157
  81.9 0.0 collective-permute-done.16.refs_4_
  81.9 0.0 collective-permute-done.13.refs_3_
  81.9 4.7 %product_5_3.1.refs_3_ = f32[512,1024]{1,0:T(8,128)S(1)} custom-call(s32[32,64]{1,0:T(8,128)S(1)} %copy-done.3, s32[32,128]{1,0:T(8,128)S(1)} %bitcast.10, bf16[8,512,256]{2,1,0:T(8,128)(2,1)S(1)} %bitcast.5, bf16[256,512]{1,0:T(8,128)(2,1)} %collective-permute-done.3.refs_1_, ...), custom_call_target="tpu_custom_call", output_to_operand_aliasing={{}: (7, {})} | custom-call | flops 1073741824 | bytes 4194304 | tf_op jit(solution)/shard_map/product_5_3/pallas_call | solution.py:157
  86.6 0.0 collective-permute-done.10.refs_2_
  86.7 0.0 collective-permute-done.4.refs_1_
  86.7 3.3 %product_4.1 = (f32[512,1024]{1,0:T(8,128)S(1)}, f32[1,1024]{1,0:T(1,128)S(1)}) custom-call(s32[32,64]{1,0:T(8,128)S(1)} %copy-done.3, s32[32,128]{1,0:T(8,128)S(1)} %bitcast.11, bf16[8,512,256]{2,1,0:T(8,128)(2,1)S(1)} %bitcast.6, bf16[256,512]{1,0:T(8,128)(2,1)} %collective-permute-done.4.refs_1_, ...), custom_call_target="tpu_custom_call", output_to_operand_aliasing={{0}: (5, {})} | custom-call | flops 536870912 | bytes 4194304 | tf_op jit(solution)/shard_map/product_4/pallas_call | solution.py:157
  89.9 0.1 broadcast_in_dim.2
  90.0 18.4 %all_to_all.6 = f32[32,1,1024]{2,1,0:T(1,128)S(1)} all-to-all(f32[32,1,1024]{2,1,0:T(1,128)S(1)} %broadcast_in_dim.2), channel_id=1, replica_groups=mesh['row'=8,'z'=8,'x'=4] {'z','x'}, dimensions={0} | all-to-all | bytes 262144 | tf_op jit(solution)/shard_map/all_to_all | solution.py:206
  108.5 0.1 reduce_sum.9
  108.6 1.6 %broadcast_divide_fusion = f32[512,1024]{1,0:T(8,128)} fusion(f32[512,1024]{1,0:T(8,128)S(1)} %get-tuple-element.11, f32[1024]{0:T(1024)S(1)} %broadcast_multiply_fusion), kind=kLoop, calls=%fused_computation | loop fusion | flops 524288 | bytes 4198400 | tf_op jit(solution)/shard_map/div | solution.py:210
  (25 shorter events, 0.1 us)
Async XLA Ops:
  6.5 57.1 %all-gather.3.cloned.1.call-start = ((), (), s32[]{:S(2)}) async-start(), calls=%async_computation.1 | async-start | bytes 2359296 | tf_op jit(solution)/shard_map/all_gather | solution.py:187
  6.5 1.0 copy-start.1
  7.6 0.7 copy-start.2
  8.3 0.7 copy-start.4
  9.0 0.9 copy-start.6
  10.0 53.7 %copy-start.3 = (s32[32,64]{1,0:T(8,128)S(1)}, s32[32,64]{1,0:T(8,128)}, u32[]{:S(2)}) copy-start(s32[32,64]{1,0:T(8,128)} %right_pattern.9) | copy-start | bytes 24580
  10.0 53.7 %copy-start.5 = (s32[128,32]{0,1:T(8,128)S(1)}, s32[128,32]{0,1:T(8,128)}, u32[]{:S(2)}) copy-start(s32[128,32]{0,1:T(8,128)} %param.5) | copy-start | bytes 49156
  12.1 8.4 %collective-permute-start.5 = (bf16[128,512]{1,0:T(8,128)(2,1)S(1)}, bf16[128,512]{1,0:T(8,128)(2,1)S(1)}, u32[]{:S(2)}, u32[]{:S(2)}) collective-permute-start(bf16[128,512]{1,0:T(8,128)(2,1)S(1)} %get-tuple-element.10), channel_id=1, source_target_pairs={{0,3},{1,0},{2,1},{3,2},{4,7},{5,4},{6,5},{7,6},{8,11},{9,8},{10,9... | collective-permute-start | bytes 393224 | tf_op jit(solution)/shard_map/ppermute | solution.py:181
  14.9 7.9 %collective-permute-start.6 = (bf16[128,512]{1,0:T(8,128)(2,1)S(1)}, bf16[128,512]{1,0:T(8,128)(2,1)S(1)}, u32[]{:S(2)}, u32[]{:S(2)}) collective-permute-start(bf16[128,512]{1,0:T(8,128)(2,1)S(1)} %get-tuple-element.10), channel_id=1, source_target_pairs={{0,2},{1,3},{2,0},{3,1},{4,6},{5,7},{6,4},{7,5},{8,10},{9,11},{10,... | collective-permute-start | bytes 393224 | tf_op jit(solution)/shard_map/ppermute | solution.py:181
  15.7 9.1 %collective-permute-start = (bf16[128,512]{1,0:T(8,128)(2,1)S(1)}, bf16[128,512]{1,0:T(8,128)(2,1)S(1)}, u32[]{:S(2)}, u32[]{:S(2)}) collective-permute-start(bf16[128,512]{1,0:T(8,128)(2,1)S(1)} %get-tuple-element.10), channel_id=1, source_target_pairs={{0,1},{1,2},{2,3},{3,0},{4,5},{5,6},{6,7},{7,4},{8,9},{9,10},{10,1... | collective-permute-start | bytes 393224 | tf_op jit(solution)/shard_map/ppermute | solution.py:181
  22.8 40.9 %copy-start.9 = (bf16[256,512]{1,0:T(8,128)(2,1)}, bf16[256,512]{1,0:T(8,128)(2,1)S(1)}, u32[]{:S(2)}) copy-start(bf16[256,512]{1,0:T(8,128)(2,1)S(1)} %constant_dynamic-update-slice_fusion.2.refs_2_) | copy-start | bytes 786436
  22.8 12.6 %collective-permute-start.7 = (bf16[256,512]{1,0:T(8,128)(2,1)S(1)}, bf16[256,512]{1,0:T(8,128)(2,1)S(1)}, u32[]{:S(2)}, u32[]{:S(2)}) collective-permute-start(bf16[256,512]{1,0:T(8,128)(2,1)S(1)} %constant_dynamic-update-slice_fusion.2.refs_2_), channel_id=1, source_target_pairs={{0,4},{4,8},{8,12},{12,16},{16,20},{20,24},{24,28},{28,0},{1,5},{5... | collective-permute-start | bytes 786440 | tf_op jit(solution)/shard_map/ppermute | solution.py:181
  24.8 16.2 %collective-permute-start.1 = (bf16[256,512]{1,0:T(8,128)(2,1)S(1)}, bf16[256,512]{1,0:T(8,128)(2,1)S(1)}, u32[]{:S(2)}, u32[]{:S(2)}) collective-permute-start(bf16[256,512]{1,0:T(8,128)(2,1)S(1)} %constant_dynamic-update-slice_fusion.refs_1_), channel_id=1, source_target_pairs={{0,4},{4,8},{8,12},{12,16},{16,20},{20,24},{24,28},{28,0},{1,5},{5... | collective-permute-start | bytes 786440 | tf_op jit(solution)/shard_map/ppermute | solution.py:181
  26.8 15.0 %collective-permute-start.14 = (bf16[256,512]{1,0:T(8,128)(2,1)S(1)}, bf16[256,512]{1,0:T(8,128)(2,1)S(1)}, u32[]{:S(2)}, u32[]{:S(2)}) collective-permute-start(bf16[256,512]{1,0:T(8,128)(2,1)S(1)} %constant_dynamic-update-slice_fusion.2.refs_2_), channel_id=1, source_target_pairs={{0,28},{4,0},{8,4},{12,8},{16,12},{20,16},{24,20},{28,24},{1,29},{... | collective-permute-start | bytes 786440 | tf_op jit(solution)/shard_map/ppermute | solution.py:181
  30.2 15.5 %collective-permute-start.11 = (bf16[256,512]{1,0:T(8,128)(2,1)S(1)}, bf16[256,512]{1,0:T(8,128)(2,1)S(1)}, u32[]{:S(2)}, u32[]{:S(2)}) collective-permute-start(bf16[256,512]{1,0:T(8,128)(2,1)S(1)} %constant_dynamic-update-slice_fusion.refs_1_), channel_id=1, source_target_pairs={{0,28},{4,0},{8,4},{12,8},{16,12},{20,16},{24,20},{28,24},{1,29},{... | collective-permute-start | bytes 786440 | tf_op jit(solution)/shard_map/ppermute | solution.py:181
  32.1 0.7 copy-start.7
  35.4 12.0 %collective-permute-start.8 = (bf16[256,512]{1,0:T(8,128)(2,1)S(1)}, bf16[256,512]{1,0:T(8,128)(2,1)S(1)}, u32[]{:S(2)}, u32[]{:S(2)}) collective-permute-start(bf16[256,512]{1,0:T(8,128)(2,1)S(1)} %collective-permute-done.7.refs_4_), channel_id=1, source_target_pairs={{0,4},{4,8},{8,12},{12,16},{16,20},{20,24},{24,28},{28,0},{1,5},{5... | collective-permute-start | bytes 786440 | tf_op jit(solution)/shard_map/ppermute | solution.py:181
  35.4 0.7 copy-start.11
  41.0 10.5 %collective-permute-start.2 = (bf16[256,512]{1,0:T(8,128)(2,1)S(1)}, bf16[256,512]{1,0:T(8,128)(2,1)S(1)}, u32[]{:S(2)}, u32[]{:S(2)}) collective-permute-start(bf16[256,512]{1,0:T(8,128)(2,1)S(1)} %collective-permute-done.1.refs_3_), channel_id=1, source_target_pairs={{0,4},{4,8},{8,12},{12,16},{16,20},{20,24},{24,28},{28,0},{1,5},{5... | collective-permute-start | bytes 786440 | tf_op jit(solution)/shard_map/ppermute | solution.py:181
  41.0 0.7 copy-start.13
  41.8 9.8 %collective-permute-start.15 = (bf16[256,512]{1,0:T(8,128)(2,1)S(1)}, bf16[256,512]{1,0:T(8,128)(2,1)S(1)}, u32[]{:S(2)}, u32[]{:S(2)}) collective-permute-start(bf16[256,512]{1,0:T(8,128)(2,1)S(1)} %collective-permute-done.14.refs_6_), channel_id=1, source_target_pairs={{0,28},{4,0},{8,4},{12,8},{16,12},{20,16},{24,20},{28,24},{1,29},{... | collective-permute-start | bytes 786440 | tf_op jit(solution)/shard_map/ppermute | solution.py:181
  45.0 0.7 copy-start.15
  45.7 9.1 %collective-permute-start.12 = (bf16[256,512]{1,0:T(8,128)(2,1)S(1)}, bf16[256,512]{1,0:T(8,128)(2,1)S(1)}, u32[]{:S(2)}, u32[]{:S(2)}) collective-permute-start(bf16[256,512]{1,0:T(8,128)(2,1)S(1)} %collective-permute-done.11.refs_5_), channel_id=1, source_target_pairs={{0,28},{4,0},{8,4},{12,8},{16,12},{20,16},{24,20},{28,24},{1,29},{... | collective-permute-start | bytes 786440 | tf_op jit(solution)/shard_map/ppermute | solution.py:181
  46.7 0.7 copy-start.17
  47.4 10.6 %collective-permute-start.9 = (bf16[256,512]{1,0:T(8,128)(2,1)S(1)}, bf16[256,512]{1,0:T(8,128)(2,1)S(1)}, u32[]{:S(2)}, u32[]{:S(2)}) collective-permute-start(bf16[256,512]{1,0:T(8,128)(2,1)S(1)} %collective-permute-done.8.refs_2_), channel_id=1, source_target_pairs={{0,4},{4,8},{8,12},{12,16},{16,20},{20,24},{24,28},{28,0},{1,5},{5... | collective-permute-start | bytes 786440 | tf_op jit(solution)/shard_map/ppermute | solution.py:181
  51.5 12.1 %collective-permute-start.3 = (bf16[256,512]{1,0:T(8,128)(2,1)S(1)}, bf16[256,512]{1,0:T(8,128)(2,1)}, u32[]{:S(2)}, u32[]{:S(2)}) collective-permute-start(bf16[256,512]{1,0:T(8,128)(2,1)S(1)} %collective-permute-done.2.refs_1_), channel_id=1, source_target_pairs={{0,4},{4,8},{8,12},{12,16},{16,20},{20,24},{24,28},{28,0},{1,5},{5... | collective-permute-start | bytes 786440 | tf_op jit(solution)/shard_map/ppermute | solution.py:181
  51.5 30.3 %collective-permute-start.16 = (bf16[256,512]{1,0:T(8,128)(2,1)S(1)}, bf16[256,512]{1,0:T(8,128)(2,1)}, u32[]{:S(2)}, u32[]{:S(2)}) collective-permute-start(bf16[256,512]{1,0:T(8,128)(2,1)S(1)} %collective-permute-done.15.refs_4_), channel_id=1, source_target_pairs={{0,28},{4,0},{8,4},{12,8},{16,12},{20,16},{24,20},{28,24},{1,29},{... | collective-permute-start | bytes 786440 | tf_op jit(solution)/shard_map/ppermute | solution.py:181
  54.8 27.1 %collective-permute-start.13 = (bf16[256,512]{1,0:T(8,128)(2,1)S(1)}, bf16[256,512]{1,0:T(8,128)(2,1)}, u32[]{:S(2)}, u32[]{:S(2)}) collective-permute-start(bf16[256,512]{1,0:T(8,128)(2,1)S(1)} %collective-permute-done.12.refs_3_), channel_id=1, source_target_pairs={{0,28},{4,0},{8,4},{12,8},{16,12},{20,16},{24,20},{28,24},{1,29},{... | collective-permute-start | bytes 786440 | tf_op jit(solution)/shard_map/ppermute | solution.py:181
  58.1 28.6 %collective-permute-start.10 = (bf16[256,512]{1,0:T(8,128)(2,1)S(1)}, bf16[256,512]{1,0:T(8,128)(2,1)}, u32[]{:S(2)}, u32[]{:S(2)}) collective-permute-start(bf16[256,512]{1,0:T(8,128)(2,1)S(1)} %collective-permute-done.9.refs_2_), channel_id=1, source_target_pairs={{0,4},{4,8},{8,12},{12,16},{16,20},{20,24},{24,28},{28,0},{1,5},{5... | collective-permute-start | bytes 786440 | tf_op jit(solution)/shard_map/ppermute | solution.py:181
  63.6 23.0 %collective-permute-start.4 = (bf16[256,512]{1,0:T(8,128)(2,1)}, bf16[256,512]{1,0:T(8,128)(2,1)}, u32[]{:S(2)}, u32[]{:S(2)}) collective-permute-start(bf16[256,512]{1,0:T(8,128)(2,1)} %collective-permute-done.3.refs_1_), channel_id=1, source_target_pairs={{0,4},{4,8},{8,12},{12,16},{16,20},{20,24},{24,28},{28,0},{1,5},{5... | collective-permute-start | bytes 786440 | tf_op jit(solution)/shard_map/ppermute | solution.py:181
  63.7 1.6 %copy-start = (bf16[4096,256]{1,0:T(8,128)(2,1)S(1)}, bf16[4096,256]{1,0:T(8,128)(2,1)}, u32[]{:S(2)}) copy-start(bf16[4096,256]{1,0:T(8,128)(2,1)} %all-gather.3.cloned.1.call-done) | copy-start | bytes 6291460
  65.2 0.9 copy-start.8
  66.2 0.9 copy-start.10
  67.1 0.9 copy-start.12
  68.1 0.9 copy-start.14
  69.0 0.9 copy-start.16
  70.0 0.9 copy-start.18
Sparse Core Ops, SparseCore 0:
  12.2 29.0 all-gather.2

commit v2 on v1

v2 whole, which is shorter than its diff:
```python
import functools

import jax
import jax.numpy as jnp
from jax import lax
from jax.experimental import pallas as pl
from jax.experimental.pallas import tpu as pltpu
from jax.sharding import Mesh
from jax.sharding import PartitionSpec as P

BLOCK = 128
SLOTS = 4
LEFT_SLOTS = 2
X_SHIFTS = (0, 3, 1, 2)
VMEM_LIMIT = 20 * 1024 * 1024


def lanes(start, blocks=1):
    return pl.ds(pl.multiple_of(start * BLOCK, BLOCK), blocks * BLOCK)


def pack_kernel(right_pattern, left_pattern, right, left, right_out, left_out, sem):
    row = lax.axis_index("row")
    col = lax.axis_index("z") * lax.axis_size("x") + lax.axis_index("x")
    col_blocks = right.shape[1] // BLOCK
    copies = []
    slot = jnp.int32(0)
    for j in range(col_blocks):
        present = right_pattern[col, row * col_blocks + j]
        copies.append((
            present,
            pltpu.make_async_copy(
                right.at[:, j * BLOCK : (j + 1) * BLOCK],
                right_out.at[:, lanes(jnp.minimum(slot, SLOTS - 1))],
                sem.at[len(copies)],
            ),
        ))
        slot = slot + present
    block_rows, inner_blocks = left.shape[0] // BLOCK, left.shape[1] // BLOCK
    for i in range(block_rows):
        rows = slice(i * BLOCK, (i + 1) * BLOCK)
        slot = jnp.int32(0)
        for k in range(inner_blocks):
            present = left_pattern[row * inner_blocks + k, col * block_rows + i]
            copies.append((
                present,
                pltpu.make_async_copy(
                    left.at[rows, k * BLOCK : (k + 1) * BLOCK],
                    left_out.at[rows, lanes(jnp.minimum(slot, LEFT_SLOTS - 1))],
                    sem.at[len(copies)],
                ),
            ))
            slot = slot + present
    for present, copy in copies:
        pl.when(present != 0)(copy.start)
    for present, copy in copies:
        pl.when(present != 0)(copy.wait)


def pack(right_pattern, left_pattern, right, left):
    count = right.shape[1] // BLOCK + left.shape[0] // BLOCK * (left.shape[1] // BLOCK)
    return pl.pallas_call(
        pack_kernel,
        out_shape=(
            jax.ShapeDtypeStruct((right.shape[0], SLOTS * BLOCK), right.dtype),
            jax.ShapeDtypeStruct((left.shape[0], LEFT_SLOTS * BLOCK), left.dtype),
        ),
        in_specs=[pl.BlockSpec(memory_space=pltpu.SMEM)] * 2
        + [pl.BlockSpec(memory_space=pl.ANY)] * 2,
        out_specs=[pl.BlockSpec(memory_space=pl.ANY)] * 2,
        scratch_shapes=[pltpu.SemaphoreType.DMA((count,))],
        name="pack",
    )(right_pattern, left_pattern, right, left)


def product_kernel(shifts, first, last, right_pattern, left_pattern, *refs):
    refs = list(refs)
    left = refs.pop(0)
    pieces = [refs.pop(0) for _ in range(2 * len(shifts))]
    total = None if first else refs.pop(0)
    out = refs.pop(0)
    sums = refs.pop(0) if last else None
    packed_left, packed_right, dense_left, dense_right, sem = refs
    row, z, x = lax.axis_index("row"), lax.axis_index("z"), lax.axis_index("x")
    z_size, x_size = lax.axis_size("z"), lax.axis_size("x")
    block_rows = dense_left.shape[0] // BLOCK
    col_blocks = dense_right.shape[1] // BLOCK
    col = z * x_size + x
    groups = [lax.rem(z + shift + z_size, z_size) for shift in shifts]
    half = pieces[0].shape[0]
    copies = []
    for n, group in enumerate(groups):
        copies.append(pltpu.make_async_copy(left.at[group], packed_left.at[n], sem.at[len(copies)]))
        for h in range(2):
            copies.append(
                pltpu.make_async_copy(
                    pieces[2 * n + h],
                    packed_right.at[pl.ds((2 * n + h) * half, half)],
                    sem.at[len(copies)],
                )
            )
    for copy in copies:
        copy.start()
    left_plan, right_plan = [], []
    for n, group in enumerate(groups):
        for m, x_shift in enumerate(X_SHIFTS):
            inside = lax.rem(x + x_shift, x_size)
            k = group * x_size + inside
            at = slice((n * x_size + m) * BLOCK, (n * x_size + m + 1) * BLOCK)
            slot = jnp.int32(0)
            for j in range(col_blocks):
                present = right_pattern[k, row * col_blocks + j]
                right_plan.append((at, j, present, jnp.minimum(slot, SLOTS - 1)))
                slot = slot + present
            for i in range(block_rows):
                present = left_pattern[k, col * block_rows + i]
                before = jnp.int32(0)
                for other in range(x_size):
                    there = left_pattern[group * x_size + other, col * block_rows + i]
                    before = before + jnp.where(other < inside, there, 0)
                left_plan.append((n, i, at, present, jnp.minimum(before, LEFT_SLOTS - 1)))
    for copy in copies:
        copy.wait()
    zero = jnp.zeros((BLOCK, BLOCK), dense_right.dtype)
    for at, j, present, slot in right_plan:
        value = packed_right[at, lanes(slot)]
        dense_right[at, j * BLOCK : (j + 1) * BLOCK] = jnp.where(present != 0, value, zero)
    for n, i, at, present, slot in left_plan:
        rows = slice(i * BLOCK, (i + 1) * BLOCK)
        value = packed_left[n, rows, lanes(slot)]
        dense_left[rows, at] = jnp.where(present != 0, value, zero)

    width = 256

    @pl.loop(0, out.shape[1] // width)
    def _(t):
        columns = pl.ds(pl.multiple_of(t * width, width), width)
        value = jnp.dot(
            dense_left[...], dense_right[:, columns], preferred_element_type=jnp.float32
        )
        if not first:
            value = value + total[:, columns]
        if last:
            value = value * value
            sums[:, columns] = jnp.sum(value, axis=0, keepdims=True)
        out[:, columns] = value


def product(shifts, right_pattern, left_pattern, left, pieces, total, last):
    rows, cols = left.shape[1], right_pattern.shape[1] // 8 * BLOCK
    inner = len(shifts) * 4 * BLOCK
    out_shape = [jax.ShapeDtypeStruct((rows, cols), jnp.float32)]
    if last:
        out_shape.append(jax.ShapeDtypeStruct((1, cols), jnp.float32))
    vmem = pl.BlockSpec(memory_space=pltpu.VMEM)
    left = pltpu.with_memory_space_constraint(left, pltpu.HBM)
    if not last:
        pieces = [pltpu.with_memory_space_constraint(piece, pltpu.HBM) for piece in pieces]
    operands = [right_pattern, left_pattern, left, *pieces]
    in_specs = [pl.BlockSpec(memory_space=pltpu.SMEM)] * 2
    in_specs += [pl.BlockSpec(memory_space=pl.ANY)] * (len(operands) - 2)
    aliases = {}
    if total is not None:
        aliases = {len(operands): 0}
        operands.append(total)
        in_specs.append(vmem)
    return pl.pallas_call(
        functools.partial(product_kernel, shifts, total is None, last),
        out_shape=out_shape,
        in_specs=in_specs,
        out_specs=[vmem] * len(out_shape),
        scratch_shapes=[
            pltpu.VMEM((len(shifts), rows, LEFT_SLOTS * BLOCK), jnp.bfloat16),
            pltpu.VMEM((inner, SLOTS * BLOCK), jnp.bfloat16),
            pltpu.VMEM((rows, inner), jnp.bfloat16),
            pltpu.VMEM((inner, cols), jnp.bfloat16),
            pltpu.SemaphoreType.DMA((3 * len(shifts),)),
        ],
        input_output_aliases=aliases,
        compiler_params=pltpu.CompilerParams(vmem_limit_bytes=VMEM_LIMIT),
        cost_estimate=pl.CostEstimate(
            flops=2 * rows * inner * cols, bytes_accessed=4 * 1024 * 1024, transcendentals=0
        ),
        name="product_" + "_".join(str(s % 8) for s in shifts),
    )(*operands)


def moved(value, axis, step):
    size = lax.axis_size(axis)
    return lax.ppermute(value, axis, [(i, (i + step) % size) for i in range(size)])


def shards(left_values, left_pattern, right_values, right_pattern):
    left_pattern = left_pattern.T
    packed_right, packed_left = pack(right_pattern, left_pattern, right_values, left_values)
    left = lax.all_gather(packed_left, "row", axis=0, tiled=False)
    near = [packed_right] + [moved(packed_right, "x", -shift) for shift in X_SHIFTS[1:]]
    own = [jnp.concatenate(near[:2], 0), jnp.concatenate(near[2:], 0)]
    up, down = own, own
    blocks = {0: own}
    for step in range(1, 4):
        up = [moved(piece, "z", 1) for piece in up]
        down = [moved(piece, "z", -1) for piece in down]
        if step == 3:
            left, up, down = lax.optimization_barrier((left, up, down))
        blocks[-step], blocks[step] = up, down
    blocks[4] = [moved(up[0], "z", 1), moved(down[1], "z", -1)]
    total = None
    for shifts in ((0, -1, 1, -2, 2), (-3, 3), (4,)):
        pieces = [piece for shift in shifts for piece in blocks[shift]]
        last = shifts == (4,)
        results = product(shifts, right_pattern, left_pattern, left, pieces, total, last)
        total = results[0]
    sums = results[1]
    count = lax.axis_size("z") * lax.axis_size("x")
    spread = lax.all_to_all(
        jnp.broadcast_to(sums, (count, sums.shape[1])), ("z", "x"), 0, 0, tiled=True
    )
    column_mean = jnp.sum(spread, axis=0) / (total.shape[0] * count)
    return total / column_mean[None, :]


def solution(mesh):
    finer = Mesh(mesh.devices.reshape(mesh.shape["row"], 8, 4), ("row", "z", "x"))
    return jax.shard_map(
        shards,
        mesh=finer,
        in_specs=(P(("z", "x"), "row"), P(), P(("z", "x"), "row"), P()),
        out_specs=P(("z", "x"), "row"),
        check_vma=False,
    )
```

time: 118 us -> 117 us (level)
  local copies, waits for them, and re-layouts: 14.4 us -> 1.14 us
  Pallas kernels: 21 us -> 30.3 us
  starting transfers between devices: 25.7 us -> 34.9 us
  waiting for transfers between devices: 22.3 us -> 18.3 us
  blocking collectives: 18.4 us -> 14.9 us
    unnamed x40 -> x34, local copies, waits for them, and re-layouts: 14.3 us -> 1.05 us
    pallas_call x1, Pallas kernels: 2.07 us -> 11.7 us  [pack(): pl.pallas_call(pack_kernel, out_shape=(jax.ShapeDtypeStruct((right.shape[...]
    ppermute x17, starting transfers between devices: 25.7 us -> 34.8 us  [moved(): lax.ppermute(value, axis, [(i, (i + step) % size) for i in range(size)])]
    ppermute x17, waiting for transfers between devices: 22.3 us -> 18.3 us  [moved(): lax.ppermute(value, axis, [(i, (i + step) % size) for i in range(size)])]
    all_to_all x1, blocking collectives: 18.4 us -> 14.9 us  [shards(): lax.all_to_all(jnp.broadcast_to(sums, (count, sums.shape[1])), ('z', 'x')...]
    pallas_call x4 -> x3, Pallas kernels: 18.9 us -> 18.6 us  [product(): pl.pallas_call(functools.partial(product_kernel, shifts, total is None, l...]
  transfers between devices with their start and end apart: 18 -> 18, of which waited for: 6 -> 8; matrix products, arithmetic and copies ran while one was open for 0% -> 1% of each run, Pallas kernels for 13% -> 13%
where the time goes in v2:
time: 117 us; the launch traced here: 115 us
  starting transfers between devices  34.9 us (30%)
  Pallas kernels  30.3 us (26%)
  waiting for transfers between devices  18.3 us (16%)
  blocking collectives  14.9 us (13%)
  between operations  13.6 us (12%)
  other arithmetic  1.68 us (1%)
    ppermute x17, starting transfers between devices, moved(): lax.ppermute(value, axis, [(i, (i + step) % size) for i in range(size)])  34.8 us
    pallas_call x3, Pallas kernels, product(): pl.pallas_call(functools.partial(product_kernel, shifts, total is None, l...  18.6 us
    ppermute x17, waiting for transfers between devices, moved(): lax.ppermute(value, axis, [(i, (i + step) % size) for i in range(size)])  18.3 us
    all_to_all x1, blocking collectives, shards(): lax.all_to_all(jnp.broadcast_to(sums, (count, sums.shape[1])), ('z', 'x')...  14.9 us
    pallas_call x1, Pallas kernels, pack(): pl.pallas_call(pack_kernel, out_shape=(jax.ShapeDtypeStruct((right.shape[...  11.7 us
  transfers between devices with their start and end apart: 18, of which 8 were waited for; matrix products, arithmetic and copies ran while one was open for 1% of the time, Pallas kernels for 13%

profile of v2, /device:TPU:24, one launch (start us, length us, event | category | flops | bytes accessed | tf_op | source)
XLA Modules:
  0.0 114.8 jit_solution(5563199622492175020)
XLA Ops:
  6.5 0.0 all-gather.3.cloned.1.call-start
  6.5 11.7 %pack.1 = (bf16[128,512]{1,0:T(8,128)(2,1)}, bf16[512,256]{1,0:T(8,128)(2,1)}) custom-call(s32[32,64]{1,0:T(8,128)} %right_pattern.7, s32[32,128]{1,0:T(8,128)} %bitcast.3, bf16[128,1024]{1,0:T(8,128)(2,1)} %right.1, bf16[512,512]{1,0:T(8,128)(2,1)} %left.1), custom_call_target="tpu_custom_call" | custom-call | tf_op jit(solution)/shard_map/pack/pallas_call | solution.py:62
  18.2 0.0 all-gather.3.cloned.1.call-update
  18.2 0.1 collective-permute-start
  18.3 5.2 %collective-permute-start.5 = (bf16[128,512]{1,0:T(8,128)(2,1)}, bf16[128,512]{1,0:T(8,128)(2,1)S(1)}, u32[]{:S(2)}, u32[]{:S(2)}) collective-permute-start(bf16[128,512]{1,0:T(8,128)(2,1)} %get-tuple-element.15), channel_id=1, source_target_pairs={{0,2},{1,3},{2,0},{3,1},{4,6},{5,7},{6,4},{7,5},{8,10},{9,11},{10,... | collective-permute-start | bytes 393224 | tf_op jit(solution)/shard_map/ppermute | solution.py:190
  23.5 0.0 collective-permute-start.4
  23.5 1.0 constant_dynamic-update-slice_fusion.1
  24.5 1.8 %collective-permute-done = bf16[128,512]{1,0:T(8,128)(2,1)S(1)} collective-permute-done((bf16[128,512]{1,0:T(8,128)(2,1)}, bf16[128,512]{1,0:T(8,128)(2,1)S(1)}, u32[]{:S(2)}, u32[]{:S(2)}) %collective-permute-start) | collective-permute-done | bytes 131104 | tf_op jit(solution)/shard_map/ppermute | solution.py:190
  26.3 0.0 copy-start.7
  26.3 8.1 %collective-permute-start.9 = (bf16[256,512]{1,0:T(8,128)(2,1)S(1)}, bf16[256,512]{1,0:T(8,128)(2,1)S(1)}, u32[]{:S(2)}, u32[]{:S(2)}) collective-permute-start(bf16[256,512]{1,0:T(8,128)(2,1)S(1)} %constant_dynamic-update-slice_fusion.refs_1_), channel_id=1, source_target_pairs={{0,28},{4,0},{8,4},{12,8},{16,12},{20,16},{24,20},{28,24},{1,29},{... | collective-permute-start | bytes 786440 | tf_op jit(solution)/shard_map/ppermute | solution.py:190
  34.5 0.0 collective-permute-start.1
  34.5 0.0 collective-permute-done.4
  34.5 0.0 collective-permute-done.5
  34.5 0.0 copy-start.6
  34.5 3.3 %collective-permute-start.12 = (bf16[256,512]{1,0:T(8,128)(2,1)S(1)}, bf16[256,512]{1,0:T(8,128)(2,1)S(1)}, u32[]{:S(2)}, u32[]{:S(2)}) collective-permute-start(bf16[256,512]{1,0:T(8,128)(2,1)S(1)} %constant_dynamic-update-slice_fusion.2.refs_2_), channel_id=1, source_target_pairs={{0,28},{4,0},{8,4},{12,8},{16,12},{20,16},{24,20},{28,24},{1,29},{... | collective-permute-start | bytes 786440 | tf_op jit(solution)/shard_map/ppermute | solution.py:190
  37.8 0.0 collective-permute-start.6
  37.8 3.3 %collective-permute-done.9.refs_5_ = bf16[256,512]{1,0:T(8,128)(2,1)S(1)} collective-permute-done((bf16[256,512]{1,0:T(8,128)(2,1)S(1)}, bf16[256,512]{1,0:T(8,128)(2,1)S(1)}, u32[]{:S(2)}, u32[]{:S(2)}) %collective-permute-start.9) | collective-permute-done | bytes 262176 | tf_op jit(solution)/shard_map/ppermute | solution.py:190
  41.1 3.7 %collective-permute-start.10 = (bf16[256,512]{1,0:T(8,128)(2,1)S(1)}, bf16[256,512]{1,0:T(8,128)(2,1)S(1)}, u32[]{:S(2)}, u32[]{:S(2)}) collective-permute-start(bf16[256,512]{1,0:T(8,128)(2,1)S(1)} %collective-permute-done.9.refs_5_), channel_id=1, source_target_pairs={{0,28},{4,0},{8,4},{12,8},{16,12},{20,16},{24,20},{28,24},{1,29},{... | collective-permute-start | bytes 786440 | tf_op jit(solution)/shard_map/ppermute | solution.py:190
  44.8 0.0 collective-permute-done.1.refs_3_
  44.8 0.0 collective-permute-start.2
  44.8 1.9 %collective-permute-done.12.refs_6_ = bf16[256,512]{1,0:T(8,128)(2,1)S(1)} collective-permute-done((bf16[256,512]{1,0:T(8,128)(2,1)S(1)}, bf16[256,512]{1,0:T(8,128)(2,1)S(1)}, u32[]{:S(2)}, u32[]{:S(2)}) %collective-permute-start.12) | collective-permute-done | bytes 262176 | tf_op jit(solution)/shard_map/ppermute | solution.py:190
  46.7 3.7 %collective-permute-start.13 = (bf16[256,512]{1,0:T(8,128)(2,1)S(1)}, bf16[256,512]{1,0:T(8,128)(2,1)S(1)}, u32[]{:S(2)}, u32[]{:S(2)}) collective-permute-start(bf16[256,512]{1,0:T(8,128)(2,1)S(1)} %collective-permute-done.12.refs_6_), channel_id=1, source_target_pairs={{0,28},{4,0},{8,4},{12,8},{16,12},{20,16},{24,20},{28,24},{1,29},{... | collective-permute-start | bytes 786440 | tf_op jit(solution)/shard_map/ppermute | solution.py:190
  50.4 0.0 collective-permute-done.6.refs_4_
  50.5 0.0 collective-permute-start.7
  50.5 0.0 copy-done.7
  50.5 1.9 %collective-permute-done.10.refs_9_ = bf16[256,512]{1,0:T(8,128)(2,1)S(1)} collective-permute-done((bf16[256,512]{1,0:T(8,128)(2,1)S(1)}, bf16[256,512]{1,0:T(8,128)(2,1)S(1)}, u32[]{:S(2)}, u32[]{:S(2)}) %collective-permute-start.10) | collective-permute-done | bytes 262176 | tf_op jit(solution)/shard_map/ppermute | solution.py:190
  52.4 3.7 %collective-permute-start.11 = (bf16[256,512]{1,0:T(8,128)(2,1)S(1)}, bf16[256,512]{1,0:T(8,128)(2,1)S(1)}, u32[]{:S(2)}, u32[]{:S(2)}) collective-permute-start(bf16[256,512]{1,0:T(8,128)(2,1)S(1)} %collective-permute-done.10.refs_9_), channel_id=1, source_target_pairs={{0,28},{4,0},{8,4},{12,8},{16,12},{20,16},{24,20},{28,24},{1,29},{... | collective-permute-start | bytes 786440 | tf_op jit(solution)/shard_map/ppermute | solution.py:190
  56.0 0.0 copy-done.8
  56.0 0.0 collective-permute-done.2.refs_7_
  56.1 0.0 collective-permute-start.3
  56.1 0.0 copy-done.9
  56.1 1.8 %collective-permute-done.13.refs_10_ = bf16[256,512]{1,0:T(8,128)(2,1)S(1)} collective-permute-done((bf16[256,512]{1,0:T(8,128)(2,1)S(1)}, bf16[256,512]{1,0:T(8,128)(2,1)S(1)}, u32[]{:S(2)}, u32[]{:S(2)}) %collective-permute-start.13) | collective-permute-done | bytes 262176 | tf_op jit(solution)/shard_map/ppermute | solution.py:190
  58.0 3.7 %collective-permute-start.14 = (bf16[256,512]{1,0:T(8,128)(2,1)S(1)}, bf16[256,512]{1,0:T(8,128)(2,1)S(1)}, u32[]{:S(2)}, u32[]{:S(2)}) collective-permute-start(bf16[256,512]{1,0:T(8,128)(2,1)S(1)} %collective-permute-done.13.refs_10_), channel_id=1, source_target_pairs={{0,28},{4,0},{8,4},{12,8},{16,12},{20,16},{24,20},{28,24},{1,29},{... | collective-permute-start | bytes 786440 | tf_op jit(solution)/shard_map/ppermute | solution.py:190
  61.7 0.0 copy-done.10
  61.7 0.0 collective-permute-done.7.refs_8_
  61.7 0.0 collective-permute-start.8
  61.8 1.2 %collective-permute-done.11.refs_3_ = bf16[256,512]{1,0:T(8,128)(2,1)S(1)} collective-permute-done((bf16[256,512]{1,0:T(8,128)(2,1)S(1)}, bf16[256,512]{1,0:T(8,128)(2,1)S(1)}, u32[]{:S(2)}, u32[]{:S(2)}) %collective-permute-start.11) | collective-permute-done | bytes 262176 | tf_op jit(solution)/shard_map/ppermute | solution.py:190
  62.9 3.4 %collective-permute-done.3.refs_1_ = bf16[256,512]{1,0:T(8,128)(2,1)S(1)} collective-permute-done((bf16[256,512]{1,0:T(8,128)(2,1)S(1)}, bf16[256,512]{1,0:T(8,128)(2,1)S(1)}, u32[]{:S(2)}, u32[]{:S(2)}) %collective-permute-start.3) | collective-permute-done | bytes 262176 | tf_op jit(solution)/shard_map/ppermute | solution.py:190
  66.3 0.0 collective-permute-done.14.refs_4_
  66.3 0.0 copy-done.11
  66.3 0.0 copy-done.12
  66.4 0.0 copy-done.13
  66.4 0.0 copy-done.14
  66.4 0.0 copy-done.15
  66.4 0.0 copy-start.4
  66.4 2.9 %collective-permute-done.8.refs_2_ = bf16[256,512]{1,0:T(8,128)(2,1)S(1)} collective-permute-done((bf16[256,512]{1,0:T(8,128)(2,1)S(1)}, bf16[256,512]{1,0:T(8,128)(2,1)S(1)}, u32[]{:S(2)}, u32[]{:S(2)}) %collective-permute-start.8) | collective-permute-done | bytes 262176 | tf_op jit(solution)/shard_map/ppermute | solution.py:190
  69.3 0.0 collective-permute-start.15
  69.3 3.2 %collective-permute-start.16 = (bf16[256,512]{1,0:T(8,128)(2,1)S(1)}, bf16[256,512]{1,0:T(8,128)(2,1)S(1)}, u32[]{:S(2)}, u32[]{:S(2)}) collective-permute-start(bf16[256,512]{1,0:T(8,128)(2,1)S(1)} %collective-permute-done.14.refs_4_), channel_id=1, source_target_pairs={{0,28},{4,0},{8,4},{12,8},{16,12},{20,16},{24,20},{28,24},{1,29},{... | collective-permute-start | bytes 786440 | tf_op jit(solution)/shard_map/ppermute | solution.py:190
  72.6 0.0 copy-done.6
  72.6 0.0 copy-done
  72.6 0.0 copy-done.1
  72.6 9.3 %product_0_7_1_6_2.1.refs_5_ = f32[512,1024]{1,0:T(8,128)S(1)} custom-call(s32[32,64]{1,0:T(8,128)S(1)} %copy-done, s32[32,128]{1,0:T(8,128)S(1)} %bitcast.4, bf16[8,512,256]{2,1,0:T(8,128)(2,1)} %bitcast.8, bf16[256,512]{1,0:T(8,128)(2,1)} %copy-done.7, bf16[256,512]{1,0:T(8,128)(2,1)} %copy-done.6, bf16[256,512]{1,0:T(8,128)(2,1)} %copy-done.9, ...), custom_call_target="tpu_custom_call" | custom-call | flops 2684354560 | bytes 4194304 | tf_op jit(solution)/shard_map/product_0_7_1_6_2/pallas_call | solution.py:167
  81.9 0.0 copy-done.2
  81.9 0.0 copy-done.3
  81.9 0.0 copy-done.4
  81.9 0.0 copy-done.5
  81.9 5.5 %product_5_3.1.refs_3_ = f32[512,1024]{1,0:T(8,128)S(1)} custom-call(s32[32,64]{1,0:T(8,128)S(1)} %copy-done, s32[32,128]{1,0:T(8,128)S(1)} %bitcast.5, bf16[8,512,256]{2,1,0:T(8,128)(2,1)} %bitcast.9, bf16[256,512]{1,0:T(8,128)(2,1)} %copy-done.3, bf16[256,512]{1,0:T(8,128)(2,1)} %copy-done.5, ...), custom_call_target="tpu_custom_call", output_to_operand_aliasing={{}: (7, {})} | custom-call | flops 1073741824 | bytes 4194304 | tf_op jit(solution)/shard_map/product_5_3/pallas_call | solution.py:167
  87.4 0.0 collective-permute-done.15.refs_1_
  87.5 0.0 collective-permute-done.16.refs_2_
  87.5 3.8 %product_4.1 = (f32[512,1024]{1,0:T(8,128)S(1)}, f32[1,1024]{1,0:T(1,128)S(1)}) custom-call(s32[32,64]{1,0:T(8,128)S(1)} %copy-done, s32[32,128]{1,0:T(8,128)S(1)} %bitcast.6, bf16[8,512,256]{2,1,0:T(8,128)(2,1)} %bitcast.10, bf16[256,512]{1,0:T(8,128)(2,1)S(1)} %collective-permute-done.15.refs_1_, ...), custom_call_target="tpu_custom_call", output_to_operand_aliasing={{0}: (5, {})} | custom-call | flops 536870912 | bytes 4194304 | tf_op jit(solution)/shard_map/product_4/pallas_call | solution.py:167
  91.3 0.1 broadcast_in_dim.2
  91.4 14.9 %all_to_all.6 = f32[32,1,1024]{2,1,0:T(1,128)S(1)} all-to-all(f32[32,1,1024]{2,1,0:T(1,128)S(1)} %broadcast_in_dim.2), channel_id=1, replica_groups=mesh['row'=8,'z'=8,'x'=4] {'z','x'}, dimensions={0} | all-to-all | bytes 262144 | tf_op jit(solution)/shard_map/all_to_all | solution.py:216
  106.3 0.1 reduce_sum.9
  106.4 1.6 %broadcast_divide_fusion = f32[512,1024]{1,0:T(8,128)} fusion(f32[512,1024]{1,0:T(8,128)S(1)} %get-tuple-element.21, f32[1024]{0:T(1024)S(1)} %broadcast_multiply_fusion), kind=kLoop, calls=%fused_computation | loop fusion | flops 524288 | bytes 4198400 | tf_op jit(solution)/shard_map/div | solution.py:220
  (18 shorter events, 0.1 us)
Async XLA Ops:
  6.5 66.0 %copy-start = (s32[32,64]{1,0:T(8,128)S(1)}, s32[32,64]{1,0:T(8,128)}, u32[]{:S(2)}) copy-start(s32[32,64]{1,0:T(8,128)} %right_pattern.7) | copy-start | bytes 24580
  6.5 66.0 %copy-start.1 = (s32[128,32]{0,1:T(8,128)S(1)}, s32[128,32]{0,1:T(8,128)}, u32[]{:S(2)}) copy-start(s32[128,32]{0,1:T(8,128)} %param.5) | copy-start | bytes 49156
  6.5 62.8 %all-gather.3.cloned.1.call-start = ((), (), s32[]{:S(2)}) async-start(), calls=%async_computation.1 | async-start | bytes 2359296 | tf_op jit(solution)/shard_map/all_gather | solution.py:196
  18.2 8.1 %collective-permute-start = (bf16[128,512]{1,0:T(8,128)(2,1)}, bf16[128,512]{1,0:T(8,128)(2,1)S(1)}, u32[]{:S(2)}, u32[]{:S(2)}) collective-permute-start(bf16[128,512]{1,0:T(8,128)(2,1)} %get-tuple-element.15), channel_id=1, source_target_pairs={{0,1},{1,2},{2,3},{3,0},{4,5},{5,6},{6,7},{7,4},{8,9},{9,10},{10,1... | collective-permute-start | bytes 393224 | tf_op jit(solution)/shard_map/ppermute | solution.py:190
  18.3 16.2 %collective-permute-start.5 = (bf16[128,512]{1,0:T(8,128)(2,1)}, bf16[128,512]{1,0:T(8,128)(2,1)S(1)}, u32[]{:S(2)}, u32[]{:S(2)}) collective-permute-start(bf16[128,512]{1,0:T(8,128)(2,1)} %get-tuple-element.15), channel_id=1, source_target_pairs={{0,2},{1,3},{2,0},{3,1},{4,6},{5,7},{6,4},{7,5},{8,10},{9,11},{10,... | collective-permute-start | bytes 393224 | tf_op jit(solution)/shard_map/ppermute | solution.py:190
  23.5 10.9 %collective-permute-start.4 = (bf16[128,512]{1,0:T(8,128)(2,1)}, bf16[128,512]{1,0:T(8,128)(2,1)S(1)}, u32[]{:S(2)}, u32[]{:S(2)}) collective-permute-start(bf16[128,512]{1,0:T(8,128)(2,1)} %get-tuple-element.15), channel_id=1, source_target_pairs={{0,3},{1,0},{2,1},{3,2},{4,7},{5,4},{6,5},{7,6},{8,11},{9,8},{10,9... | collective-permute-start | bytes 393224 | tf_op jit(solution)/shard_map/ppermute | solution.py:190
  26.3 24.2 %copy-start.7 = (bf16[256,512]{1,0:T(8,128)(2,1)}, bf16[256,512]{1,0:T(8,128)(2,1)S(1)}, u32[]{:S(2)}) copy-start(bf16[256,512]{1,0:T(8,128)(2,1)S(1)} %constant_dynamic-update-slice_fusion.refs_1_) | copy-start | bytes 786436
  26.3 14.8 %collective-permute-start.9 = (bf16[256,512]{1,0:T(8,128)(2,1)S(1)}, bf16[256,512]{1,0:T(8,128)(2,1)S(1)}, u32[]{:S(2)}, u32[]{:S(2)}) collective-permute-start(bf16[256,512]{1,0:T(8,128)(2,1)S(1)} %constant_dynamic-update-slice_fusion.refs_1_), channel_id=1, source_target_pairs={{0,28},{4,0},{8,4},{12,8},{16,12},{20,16},{24,20},{28,24},{1,29},{... | collective-permute-start | bytes 786440 | tf_op jit(solution)/shard_map/ppermute | solution.py:190
  34.5 10.4 %collective-permute-start.1 = (bf16[256,512]{1,0:T(8,128)(2,1)S(1)}, bf16[256,512]{1,0:T(8,128)(2,1)S(1)}, u32[]{:S(2)}, u32[]{:S(2)}) collective-permute-start(bf16[256,512]{1,0:T(8,128)(2,1)S(1)} %constant_dynamic-update-slice_fusion.refs_1_), channel_id=1, source_target_pairs={{0,4},{4,8},{8,12},{12,16},{16,20},{20,24},{24,28},{28,0},{1,5},{5... | collective-permute-start | bytes 786440 | tf_op jit(solution)/shard_map/ppermute | solution.py:190
  34.5 38.1 %copy-start.6 = (bf16[256,512]{1,0:T(8,128)(2,1)}, bf16[256,512]{1,0:T(8,128)(2,1)S(1)}, u32[]{:S(2)}) copy-start(bf16[256,512]{1,0:T(8,128)(2,1)S(1)} %constant_dynamic-update-slice_fusion.2.refs_2_) | copy-start | bytes 786436
  34.5 12.2 %collective-permute-start.12 = (bf16[256,512]{1,0:T(8,128)(2,1)S(1)}, bf16[256,512]{1,0:T(8,128)(2,1)S(1)}, u32[]{:S(2)}, u32[]{:S(2)}) collective-permute-start(bf16[256,512]{1,0:T(8,128)(2,1)S(1)} %constant_dynamic-update-slice_fusion.2.refs_2_), channel_id=1, source_target_pairs={{0,28},{4,0},{8,4},{12,8},{16,12},{20,16},{24,20},{28,24},{1,29},{... | collective-permute-start | bytes 786440 | tf_op jit(solution)/shard_map/ppermute | solution.py:190
  37.8 12.6 %collective-permute-start.6 = (bf16[256,512]{1,0:T(8,128)(2,1)S(1)}, bf16[256,512]{1,0:T(8,128)(2,1)S(1)}, u32[]{:S(2)}, u32[]{:S(2)}) collective-permute-start(bf16[256,512]{1,0:T(8,128)(2,1)S(1)} %constant_dynamic-update-slice_fusion.2.refs_2_), channel_id=1, source_target_pairs={{0,4},{4,8},{8,12},{12,16},{16,20},{20,24},{24,28},{28,0},{1,5},{5... | collective-permute-start | bytes 786440 | tf_op jit(solution)/shard_map/ppermute | solution.py:190
  41.1 14.9 %copy-start.8 = (bf16[256,512]{1,0:T(8,128)(2,1)}, bf16[256,512]{1,0:T(8,128)(2,1)S(1)}, u32[]{:S(2)}) copy-start(bf16[256,512]{1,0:T(8,128)(2,1)S(1)} %collective-permute-done.9.refs_5_) | copy-start | bytes 786436
  41.1 11.2 %collective-permute-start.10 = (bf16[256,512]{1,0:T(8,128)(2,1)S(1)}, bf16[256,512]{1,0:T(8,128)(2,1)S(1)}, u32[]{:S(2)}, u32[]{:S(2)}) collective-permute-start(bf16[256,512]{1,0:T(8,128)(2,1)S(1)} %collective-permute-done.9.refs_5_), channel_id=1, source_target_pairs={{0,28},{4,0},{8,4},{12,8},{16,12},{20,16},{24,20},{28,24},{1,29},{... | collective-permute-start | bytes 786440 | tf_op jit(solution)/shard_map/ppermute | solution.py:190
  44.8 11.3 %copy-start.9 = (bf16[256,512]{1,0:T(8,128)(2,1)}, bf16[256,512]{1,0:T(8,128)(2,1)S(1)}, u32[]{:S(2)}) copy-start(bf16[256,512]{1,0:T(8,128)(2,1)S(1)} %collective-permute-done.1.refs_3_) | copy-start | bytes 786436
  44.8 11.2 %collective-permute-start.2 = (bf16[256,512]{1,0:T(8,128)(2,1)S(1)}, bf16[256,512]{1,0:T(8,128)(2,1)S(1)}, u32[]{:S(2)}, u32[]{:S(2)}) collective-permute-start(bf16[256,512]{1,0:T(8,128)(2,1)S(1)} %collective-permute-done.1.refs_3_), channel_id=1, source_target_pairs={{0,4},{4,8},{8,12},{12,16},{16,20},{20,24},{24,28},{28,0},{1,5},{5... | collective-permute-start | bytes 786440 | tf_op jit(solution)/shard_map/ppermute | solution.py:190
  46.7 14.9 %copy-start.10 = (bf16[256,512]{1,0:T(8,128)(2,1)}, bf16[256,512]{1,0:T(8,128)(2,1)S(1)}, u32[]{:S(2)}) copy-start(bf16[256,512]{1,0:T(8,128)(2,1)S(1)} %collective-permute-done.12.refs_6_) | copy-start | bytes 786436
  46.7 11.2 %collective-permute-start.13 = (bf16[256,512]{1,0:T(8,128)(2,1)S(1)}, bf16[256,512]{1,0:T(8,128)(2,1)S(1)}, u32[]{:S(2)}, u32[]{:S(2)}) collective-permute-start(bf16[256,512]{1,0:T(8,128)(2,1)S(1)} %collective-permute-done.12.refs_6_), channel_id=1, source_target_pairs={{0,28},{4,0},{8,4},{12,8},{16,12},{20,16},{24,20},{28,24},{1,29},{... | collective-permute-start | bytes 786440 | tf_op jit(solution)/shard_map/ppermute | solution.py:190
  50.5 15.9 %copy-start.11 = (bf16[256,512]{1,0:T(8,128)(2,1)}, bf16[256,512]{1,0:T(8,128)(2,1)S(1)}, u32[]{:S(2)}) copy-start(bf16[256,512]{1,0:T(8,128)(2,1)S(1)} %collective-permute-done.6.refs_4_) | copy-start | bytes 786436
  50.5 11.2 %collective-permute-start.7 = (bf16[256,512]{1,0:T(8,128)(2,1)S(1)}, bf16[256,512]{1,0:T(8,128)(2,1)S(1)}, u32[]{:S(2)}, u32[]{:S(2)}) collective-permute-start(bf16[256,512]{1,0:T(8,128)(2,1)S(1)} %collective-permute-done.6.refs_4_), channel_id=1, source_target_pairs={{0,4},{4,8},{8,12},{12,16},{16,20},{20,24},{24,28},{28,0},{1,5},{5... | collective-permute-start | bytes 786440 | tf_op jit(solution)/shard_map/ppermute | solution.py:190
  52.3 14.0 %copy-start.12 = (bf16[256,512]{1,0:T(8,128)(2,1)}, bf16[256,512]{1,0:T(8,128)(2,1)S(1)}, u32[]{:S(2)}) copy-start(bf16[256,512]{1,0:T(8,128)(2,1)S(1)} %collective-permute-done.10.refs_9_) | copy-start | bytes 786436
  52.4 10.6 %collective-permute-start.11 = (bf16[256,512]{1,0:T(8,128)(2,1)S(1)}, bf16[256,512]{1,0:T(8,128)(2,1)S(1)}, u32[]{:S(2)}, u32[]{:S(2)}) collective-permute-start(bf16[256,512]{1,0:T(8,128)(2,1)S(1)} %collective-permute-done.10.refs_9_), channel_id=1, source_target_pairs={{0,28},{4,0},{8,4},{12,8},{16,12},{20,16},{24,20},{28,24},{1,29},{... | collective-permute-start | bytes 786440 | tf_op jit(solution)/shard_map/ppermute | solution.py:190
  56.1 10.3 %copy-start.13 = (bf16[256,512]{1,0:T(8,128)(2,1)}, bf16[256,512]{1,0:T(8,128)(2,1)S(1)}, u32[]{:S(2)}) copy-start(bf16[256,512]{1,0:T(8,128)(2,1)S(1)} %collective-permute-done.2.refs_7_) | copy-start | bytes 786436
  56.1 10.3 %collective-permute-start.3 = (bf16[256,512]{1,0:T(8,128)(2,1)S(1)}, bf16[256,512]{1,0:T(8,128)(2,1)S(1)}, u32[]{:S(2)}, u32[]{:S(2)}) collective-permute-start(bf16[256,512]{1,0:T(8,128)(2,1)S(1)} %collective-permute-done.2.refs_7_), channel_id=1, source_target_pairs={{0,4},{4,8},{8,12},{12,16},{16,20},{20,24},{24,28},{28,0},{1,5},{5... | collective-permute-start | bytes 786440 | tf_op jit(solution)/shard_map/ppermute | solution.py:190
  58.0 8.4 %copy-start.14 = (bf16[256,512]{1,0:T(8,128)(2,1)}, bf16[256,512]{1,0:T(8,128)(2,1)S(1)}, u32[]{:S(2)}) copy-start(bf16[256,512]{1,0:T(8,128)(2,1)S(1)} %collective-permute-done.13.refs_10_) | copy-start | bytes 786436
  58.0 8.4 %collective-permute-start.14 = (bf16[256,512]{1,0:T(8,128)(2,1)S(1)}, bf16[256,512]{1,0:T(8,128)(2,1)S(1)}, u32[]{:S(2)}, u32[]{:S(2)}) collective-permute-start(bf16[256,512]{1,0:T(8,128)(2,1)S(1)} %collective-permute-done.13.refs_10_), channel_id=1, source_target_pairs={{0,28},{4,0},{8,4},{12,8},{16,12},{20,16},{24,20},{28,24},{1,29},{... | collective-permute-start | bytes 786440 | tf_op jit(solution)/shard_map/ppermute | solution.py:190
  61.7 4.7 %copy-start.15 = (bf16[256,512]{1,0:T(8,128)(2,1)}, bf16[256,512]{1,0:T(8,128)(2,1)S(1)}, u32[]{:S(2)}) copy-start(bf16[256,512]{1,0:T(8,128)(2,1)S(1)} %collective-permute-done.7.refs_8_) | copy-start | bytes 786436
  61.7 7.6 %collective-permute-start.8 = (bf16[256,512]{1,0:T(8,128)(2,1)S(1)}, bf16[256,512]{1,0:T(8,128)(2,1)S(1)}, u32[]{:S(2)}, u32[]{:S(2)}) collective-permute-start(bf16[256,512]{1,0:T(8,128)(2,1)S(1)} %collective-permute-done.7.refs_8_), channel_id=1, source_target_pairs={{0,4},{4,8},{8,12},{12,16},{16,20},{20,24},{24,28},{28,0},{1,5},{5... | collective-permute-start | bytes 786440 | tf_op jit(solution)/shard_map/ppermute | solution.py:190
  62.9 19.0 %copy-start.2 = (bf16[256,512]{1,0:T(8,128)(2,1)}, bf16[256,512]{1,0:T(8,128)(2,1)S(1)}, u32[]{:S(2)}) copy-start(bf16[256,512]{1,0:T(8,128)(2,1)S(1)} %collective-permute-done.11.refs_3_) | copy-start | bytes 786436
  66.3 15.6 %copy-start.3 = (bf16[256,512]{1,0:T(8,128)(2,1)}, bf16[256,512]{1,0:T(8,128)(2,1)S(1)}, u32[]{:S(2)}) copy-start(bf16[256,512]{1,0:T(8,128)(2,1)S(1)} %collective-permute-done.3.refs_1_) | copy-start | bytes 786436
  66.4 15.5 %copy-start.4 = (bf16[256,512]{1,0:T(8,128)(2,1)}, bf16[256,512]{1,0:T(8,128)(2,1)S(1)}, u32[]{:S(2)}) copy-start(bf16[256,512]{1,0:T(8,128)(2,1)S(1)} %collective-permute-done.14.refs_4_) | copy-start | bytes 786436
  69.3 12.6 %copy-start.5 = (bf16[256,512]{1,0:T(8,128)(2,1)}, bf16[256,512]{1,0:T(8,128)(2,1)S(1)}, u32[]{:S(2)}) copy-start(bf16[256,512]{1,0:T(8,128)(2,1)S(1)} %collective-permute-done.8.refs_2_) | copy-start | bytes 786436
  69.3 18.1 %collective-permute-start.15 = (bf16[256,512]{1,0:T(8,128)(2,1)S(1)}, bf16[256,512]{1,0:T(8,128)(2,1)S(1)}, u32[]{:S(2)}, u32[]{:S(2)}) collective-permute-start(bf16[256,512]{1,0:T(8,128)(2,1)S(1)} %collective-permute-done.3.refs_1_), channel_id=1, source_target_pairs={{0,4},{4,8},{8,12},{12,16},{16,20},{20,24},{24,28},{28,0},{1,5},{5... | collective-permute-start | bytes 786440 | tf_op jit(solution)/shard_map/ppermute | solution.py:190
  69.3 18.1 %collective-permute-start.16 = (bf16[256,512]{1,0:T(8,128)(2,1)S(1)}, bf16[256,512]{1,0:T(8,128)(2,1)S(1)}, u32[]{:S(2)}, u32[]{:S(2)}) collective-permute-start(bf16[256,512]{1,0:T(8,128)(2,1)S(1)} %collective-permute-done.14.refs_4_), channel_id=1, source_target_pairs={{0,28},{4,0},{8,4},{12,8},{16,12},{20,16},{24,20},{28,24},{1,29},{... | collective-permute-start | bytes 786440 | tf_op jit(solution)/shard_map/ppermute | solution.py:190
Sparse Core Ops, SparseCore 0:
  18.4 30.8 all-gather.2

commit v3 on v2

v3 whole, which is shorter than its diff:
```python
import functools

import jax
import jax.numpy as jnp
from jax import lax
from jax.experimental import pallas as pl
from jax.experimental.pallas import tpu as pltpu
from jax.sharding import Mesh
from jax.sharding import PartitionSpec as P

BLOCK = 128
SLOTS = 4
LEFT_SLOTS = 2
SHIFTS = (0, 3, 1, 2)
PLACES = (0, 2, 3, 1)
KERNEL_VMEM = 20 * 1024 * 1024
ROW, COL = ("y", "core"), ("z", "x")


def lanes(start, blocks=1):
    return pl.ds(pl.multiple_of(start * BLOCK, BLOCK), blocks * BLOCK)


def place_of(shift):
    place = jnp.int32(PLACES[3])
    for s in range(3):
        place = jnp.where(shift == s, PLACES[s], place)
    return place


def row_index():
    return lax.axis_index("y") * lax.axis_size("core") + lax.axis_index("core")


def col_index():
    return lax.axis_index("z") * lax.axis_size("x") + lax.axis_index("x")


def pack_right_kernel(pattern, right, out):
    row, col = row_index(), col_index()
    col_blocks = right.shape[1] // BLOCK
    out[...] = jnp.zeros_like(out)
    slot = jnp.int32(0)
    for j in range(col_blocks):
        present = pattern[col, row * col_blocks + j]

        @pl.when(present != 0)
        def _(j=j, slot=slot):
            out[:, lanes(slot)] = right[:, j * BLOCK : (j + 1) * BLOCK]

        slot = slot + present


def pack_left_kernel(pattern, left, out):
    row, col = row_index(), col_index()
    block_rows, inner_blocks = left.shape[0] // BLOCK, left.shape[1] // BLOCK
    out[...] = jnp.zeros_like(out)
    for i in range(block_rows):
        rows = slice(i * BLOCK, (i + 1) * BLOCK)
        slot = jnp.int32(0)
        for k in range(inner_blocks):
            present = pattern[row * inner_blocks + k, col * block_rows + i]

            @pl.when(present != 0)
            def _(k=k, slot=slot, rows=rows):
                out[rows, lanes(slot)] = left[rows, k * BLOCK : (k + 1) * BLOCK]

            slot = slot + present


def pack(kernel, name, pattern, values, slots):
    return pl.pallas_call(
        kernel,
        out_shape=jax.ShapeDtypeStruct((values.shape[0], slots * BLOCK), values.dtype),
        in_specs=[
            pl.BlockSpec(memory_space=pltpu.SMEM),
            pl.BlockSpec(memory_space=pltpu.VMEM),
        ],
        out_specs=pl.BlockSpec(memory_space=pltpu.VMEM),
        compiler_params=pltpu.CompilerParams(vmem_limit_bytes=4 * 1024 * 1024),
        name=name,
    )(pattern, values)


def product_kernel(shifts, first, last, right_pattern, left_pattern, *refs):
    refs = list(refs)
    mine, other = refs.pop(0), refs.pop(0)
    pieces = [refs.pop(0) for _ in range(2 * len(shifts))]
    total = None if first else refs.pop(0)
    out = refs.pop(0)
    sums = refs.pop(0) if last else None
    packed_left, packed_right, dense_left, dense_right, sem = refs
    row, col = row_index(), col_index()
    y, core = lax.axis_index("y"), lax.axis_index("core")
    z, x = lax.axis_index("z"), lax.axis_index("x")
    y_size, z_size, x_size = lax.axis_size("y"), lax.axis_size("z"), lax.axis_size("x")
    cores = lax.axis_size("core")
    block_rows = dense_left.shape[0] // BLOCK
    col_blocks = dense_right.shape[1] // BLOCK
    groups = [lax.rem(z + shift + z_size, z_size) for shift in shifts]
    half = pieces[0].shape[0]
    waits = []
    for n, group in enumerate(groups):
        there = place_of(lax.rem(lax.div(group, cores) - y + y_size, y_size))
        same = lax.rem(group, cores) == core
        for source, wanted in ((mine, same), (other, jnp.logical_not(same))):
            copy = pltpu.make_async_copy(
                source.at[there], packed_left.at[n, :, : LEFT_SLOTS * BLOCK], sem.at[3 * n]
            )
            pl.when(wanted)(copy.start)
        waits.append(copy)
        for h in range(2):
            copy = pltpu.make_async_copy(
                pieces[2 * n + h],
                packed_right.at[pl.ds((2 * n + h) * half, half), : SLOTS * BLOCK],
                sem.at[3 * n + 1 + h],
            )
            copy.start()
            waits.append(copy)
    packed_left[:, :, LEFT_SLOTS * BLOCK :] = jnp.zeros(
        (len(shifts), packed_left.shape[1], BLOCK), packed_left.dtype
    )
    packed_right[:, SLOTS * BLOCK :] = jnp.zeros(
        (packed_right.shape[0], BLOCK), packed_right.dtype
    )
    right_plan, left_plan = [], []
    for n, group in enumerate(groups):
        for inside in range(x_size):
            k = group * x_size + inside
            start = n * x_size * BLOCK
            to = slice(start + inside * BLOCK, start + (inside + 1) * BLOCK)
            place = place_of(lax.rem(inside - x + x_size, x_size))
            at = pl.ds(pl.multiple_of(start + place * BLOCK, BLOCK), BLOCK)
            slot = jnp.int32(0)
            for j in range(col_blocks):
                present = right_pattern[k, row * col_blocks + j]
                source = jnp.where(present != 0, jnp.minimum(slot, SLOTS), SLOTS)
                right_plan.append((at, to, j, source))
                slot = slot + present
        for i in range(block_rows):
            slot = jnp.int32(0)
            for inside in range(x_size):
                to = lanes(n * x_size + inside)
                present = left_pattern[group * x_size + inside, col * block_rows + i]
                source = jnp.where(present != 0, jnp.minimum(slot, LEFT_SLOTS), LEFT_SLOTS)
                left_plan.append((n, i, inside, source))
                slot = slot + present
    for copy in waits:
        copy.wait()
    for at, to, j, source in right_plan:
        dense_right[to, j * BLOCK : (j + 1) * BLOCK] = packed_right[at, lanes(source)]
    for n, i, inside, source in left_plan:
        rows = slice(i * BLOCK, (i + 1) * BLOCK)
        start = (n * x_size + inside) * BLOCK
        dense_left[rows, start : start + BLOCK] = packed_left[n, rows, lanes(source)]

    width = 256

    @pl.loop(0, out.shape[1] // width)
    def _(t):
        columns = pl.ds(pl.multiple_of(t * width, width), width)
        value = jnp.dot(
            dense_left[...], dense_right[:, columns], preferred_element_type=jnp.float32
        )
        if not first:
            value = value + total[:, columns]
        if last:
            value = value * value
            sums[:, columns] = jnp.sum(value, axis=0, keepdims=True)
        out[:, columns] = value


def product(shifts, right_pattern, left_pattern, left, pieces, total, last):
    rows, cols = left[0].shape[1], right_pattern.shape[1] // 8 * BLOCK
    inner = len(shifts) * 4 * BLOCK
    out_shape = [jax.ShapeDtypeStruct((rows, cols), jnp.float32)]
    if last:
        out_shape.append(jax.ShapeDtypeStruct((1, cols), jnp.float32))
    vmem = pl.BlockSpec(memory_space=pltpu.VMEM)
    left = [pltpu.with_memory_space_constraint(value, pltpu.HBM) for value in left]
    if not last:
        pieces = [pltpu.with_memory_space_constraint(piece, pltpu.HBM) for piece in pieces]
    operands = [right_pattern, left_pattern, *left, *pieces]
    in_specs = [pl.BlockSpec(memory_space=pltpu.SMEM)] * 2
    in_specs += [pl.BlockSpec(memory_space=pl.ANY)] * (len(operands) - 2)
    aliases = {}
    if total is not None:
        aliases = {len(operands): 0}
        operands.append(total)
        in_specs.append(vmem)
    return pl.pallas_call(
        functools.partial(product_kernel, shifts, total is None, last),
        out_shape=out_shape,
        in_specs=in_specs,
        out_specs=[vmem] * len(out_shape),
        scratch_shapes=[
            pltpu.VMEM((len(shifts), rows, (LEFT_SLOTS + 1) * BLOCK), jnp.bfloat16),
            pltpu.VMEM((inner, (SLOTS + 1) * BLOCK), jnp.bfloat16),
            pltpu.VMEM((rows, inner), jnp.bfloat16),
            pltpu.VMEM((inner, cols), jnp.bfloat16),
            pltpu.SemaphoreType.DMA((3 * len(shifts),)),
        ],
        input_output_aliases=aliases,
        compiler_params=pltpu.CompilerParams(vmem_limit_bytes=KERNEL_VMEM),
        cost_estimate=pl.CostEstimate(
            flops=2 * rows * inner * cols, bytes_accessed=4 * 1024 * 1024, transcendentals=0
        ),
        name="product_" + "_".join(str(s % 8) for s in shifts),
    )(*operands)


def moved(value, axis, step):
    size = lax.axis_size(axis)
    return lax.ppermute(value, axis, [(i, (i + step) % size) for i in range(size)])


def shards(left_values, left_pattern, right_values, right_pattern):
    left_pattern = left_pattern.T
    packed_right = pack(pack_right_kernel, "pack_right", right_pattern, right_values, SLOTS)
    near = [packed_right] + [moved(packed_right, "x", -shift) for shift in SHIFTS[1:]]
    packed_left = pack(pack_left_kernel, "pack_left", left_pattern, left_values, LEFT_SLOTS)
    packed_left, near = lax.optimization_barrier((packed_left, near))
    own = [jnp.concatenate(near[:2], 0), jnp.concatenate(near[2:], 0)]
    blocks = {0: own}
    up = [moved(piece, "z", 1) for piece in own]
    down = [moved(piece, "z", -1) for piece in own]
    columns = [packed_left] + [moved(packed_left, "y", -shift) for shift in SHIFTS[1:]]
    columns, up, down = lax.optimization_barrier((columns, up, down))
    mine = jnp.stack(columns)
    blocks[-1], blocks[1] = up, down
    up = [moved(piece, "z", 1) for piece in up]
    down = [moved(piece, "z", -1) for piece in down]
    other = moved(mine, "core", 1)
    left = (mine, other)
    blocks[-2], blocks[2] = up, down
    up = [moved(piece, "z", 1) for piece in up]
    down = [moved(piece, "z", -1) for piece in down]
    left, up, down = lax.optimization_barrier((left, up, down))
    blocks[-3], blocks[3] = up, down
    blocks[4] = [moved(up[0], "z", 1), moved(down[1], "z", -1)]

    def add(shifts, total, last=False):
        pieces = [piece for shift in shifts for piece in blocks[shift]]
        return product(shifts, right_pattern, left_pattern, left, pieces, total, last)

    (total,) = add((0, -1, 1, -2, 2, -3, 3), None)
    total, sums = add((4,), total, True)
    count = lax.axis_size("z") * lax.axis_size("x")
    spread = lax.all_to_all(
        jnp.broadcast_to(sums, (count, sums.shape[1])), COL, 0, 0, tiled=True
    )
    column_mean = jnp.sum(spread, axis=0) / (total.shape[0] * count)
    return total / column_mean[None, :]


def solution(mesh):
    finer = Mesh(mesh.devices.reshape(4, 2, 8, 4), (*ROW, *COL))
    return jax.shard_map(
        shards,
        mesh=finer,
        in_specs=(P(COL, ROW), P(), P(COL, ROW), P()),
        out_specs=P(COL, ROW),
        check_vma=False,
    )
```

time: 117 us -> 104 us (0.89); the launches traced: 115 us -> 103 us
  waiting for transfers between devices: 18.3 us -> 34.5 us
  Pallas kernels: 30.3 us -> 17 us
  between operations: 13.6 us -> 0.31 us
  starting transfers between devices: 34.9 us -> 29.2 us
  local copies, waits for them, and re-layouts: 1.14 us -> 3.61 us
  blocking collectives: 14.9 us -> 16.7 us
    ppermute x17 -> x21, waiting for transfers between devices: 18.3 us -> 34.5 us  [moved(): lax.ppermute(value, axis, [(i, (i + step) % size) for i in range(size)])]
    pallas_call x1 -> x2, Pallas kernels: 11.7 us -> 1.91 us  [pack(): pl.pallas_call(kernel, out_shape=jax.ShapeDtypeStruct((values.shape[0], s...]
    ppermute x17 -> x21, starting transfers between devices: 34.8 us -> 29.2 us  [moved(): lax.ppermute(value, axis, [(i, (i + step) % size) for i in range(size)])]
    pallas_call x3 -> x2, Pallas kernels: 18.6 us -> 15.1 us  [product(): pl.pallas_call(functools.partial(product_kernel, shifts, total is None, l...]
    unnamed x34 -> x46, local copies, waits for them, and re-layouts: 1.05 us -> 3.51 us
    all_to_all x1, blocking collectives: 14.9 us -> 16.7 us  [shards(): lax.all_to_all(jnp.broadcast_to(sums, (count, sums.shape[1])), COL, 0, 0,...]
  transfers between devices with their start and end apart: 18 -> 21, of which waited for: 8 -> 13; matrix products, arithmetic and copies ran while one was open for 1% -> 0% of each run, Pallas kernels for 13% -> 12%
where the time goes in v3:
time: 104 us; the launch traced here: 103 us
  waiting for transfers between devices  34.5 us (33%)
  starting transfers between devices  29.2 us (28%)
  Pallas kernels  17 us (16%)
  blocking collectives  16.7 us (16%)
  local copies, waits for them, and re-layouts  3.61 us (3%)
  other arithmetic  1.81 us (2%)
    ppermute x21, waiting for transfers between devices, moved(): lax.ppermute(value, axis, [(i, (i + step) % size) for i in range(size)])  34.5 us
    ppermute x21, starting transfers between devices, moved(): lax.ppermute(value, axis, [(i, (i + step) % size) for i in range(size)])  29.2 us
    all_to_all x1, blocking collectives, shards(): lax.all_to_all(jnp.broadcast_to(sums, (count, sums.shape[1])), COL, 0, 0,...  16.7 us
    pallas_call x2, Pallas kernels, product(): pl.pallas_call(functools.partial(product_kernel, shifts, total is None, l...  15.1 us
    unnamed x46, local copies, waits for them, and re-layouts  3.51 us
  transfers between devices with their start and end apart: 21, of which 13 were waited for; matrix products, arithmetic and copies ran while one was open for 0% of the time, Pallas kernels for 12%

profile of v3, /device:TPU:24, one launch (start us, length us, event | category | flops | bytes accessed | tf_op | source)
XLA Modules:
  0.0 103.1 jit_solution(16480968910814754151)
XLA Ops:
  0.0 0.9 copy-done.1
  1.0 0.7 copy-done.2
  1.7 0.9 pack_right.1
  2.6 3.1 %collective-permute-start.2 = (bf16[128,512]{1,0:T(8,128)(2,1)S(1)}, bf16[128,512]{1,0:T(8,128)(2,1)S(1)}, u32[]{:S(2)}, u32[]{:S(2)}) collective-permute-start(bf16[128,512]{1,0:T(8,128)(2,1)S(1)} %pack_right.1), channel_id=1, source_target_pairs={{0,2},{1,3},{2,0},{3,1},{4,6},{5,7},{6,4},{7,5},{8,10},{9,11},{10,... | collective-permute-start | bytes 393224 | tf_op jit(solution)/shard_map/ppermute | solution.py:214
  5.7 1.2 %collective-permute-start.1 = (bf16[128,512]{1,0:T(8,128)(2,1)S(1)}, bf16[128,512]{1,0:T(8,128)(2,1)S(1)}, u32[]{:S(2)}, u32[]{:S(2)}) collective-permute-start(bf16[128,512]{1,0:T(8,128)(2,1)S(1)} %pack_right.1), channel_id=1, source_target_pairs={{0,3},{1,0},{2,1},{3,2},{4,7},{5,4},{6,5},{7,6},{8,11},{9,8},{10,9... | collective-permute-start | bytes 393224 | tf_op jit(solution)/shard_map/ppermute | solution.py:214
  6.9 0.9 collective-permute-start
  7.7 1.0 %copy-done = bf16[512,512]{1,0:T(8,128)(2,1)S(1)} copy-done((bf16[512,512]{1,0:T(8,128)(2,1)S(1)}, bf16[512,512]{1,0:T(8,128)(2,1)}, u32[]{:S(2)}) %copy-start) | copy-done | bytes 524312
  8.8 0.7 copy-done.4
  9.5 1.0 pack_left.1
  10.5 0.0 collective-permute-done.2
  10.5 1.8 %collective-permute-done.1 = bf16[128,512]{1,0:T(8,128)(2,1)S(1)} collective-permute-done((bf16[128,512]{1,0:T(8,128)(2,1)S(1)}, bf16[128,512]{1,0:T(8,128)(2,1)S(1)}, u32[]{:S(2)}, u32[]{:S(2)}) %collective-permute-start.1) | collective-permute-done | bytes 131104 | tf_op jit(solution)/shard_map/ppermute | solution.py:214
  12.3 0.7 collective-permute-done
  13.1 0.0 copy-start.8
  13.1 5.9 %collective-permute-start.9 = (bf16[256,512]{1,0:T(8,128)(2,1)S(1)}, bf16[256,512]{1,0:T(8,128)(2,1)S(1)}, u32[]{:S(2)}, u32[]{:S(2)}) collective-permute-start(bf16[256,512]{1,0:T(8,128)(2,1)S(1)} %constant_dynamic-update-slice_fusion.2.refs_3_), channel_id=1, source_target_pairs={{0,28},{4,0},{8,4},{12,8},{16,12},{20,16},{24,20},{28,24},{1,29},{... | collective-permute-start | bytes 786440 | tf_op jit(solution)/shard_map/ppermute | solution.py:214
  19.0 0.0 collective-permute-start.7
  19.0 0.0 copy-start.9
  19.0 3.3 %collective-permute-start.8 = (bf16[256,512]{1,0:T(8,128)(2,1)S(1)}, bf16[256,512]{1,0:T(8,128)(2,1)S(1)}, u32[]{:S(2)}, u32[]{:S(2)}) collective-permute-start(bf16[256,512]{1,0:T(8,128)(2,1)S(1)} %constant_dynamic-update-slice_fusion.refs_2_), channel_id=1, source_target_pairs={{0,28},{4,0},{8,4},{12,8},{16,12},{20,16},{24,20},{28,24},{1,29},{... | collective-permute-start | bytes 786440 | tf_op jit(solution)/shard_map/ppermute | solution.py:214
  22.4 0.0 collective-permute-start.6
  22.4 1.2 %collective-permute-start.5 = (bf16[512,256]{1,0:T(8,128)(2,1)S(1)}, bf16[512,256]{1,0:T(8,128)(2,1)S(1)}, u32[]{:S(2)}, u32[]{:S(2)}) collective-permute-start(bf16[512,256]{1,0:T(8,128)(2,1)S(1)} %pack_left.1), channel_id=1, source_target_pairs={{0,128},{64,192},{128,0},{192,64},{1,129},{65,193},{129,1},{193,65... | collective-permute-start | bytes 786440 | tf_op jit(solution)/shard_map/ppermute | solution.py:214
  23.6 2.2 %collective-permute-done.9.refs_7_ = bf16[256,512]{1,0:T(8,128)(2,1)S(1)} collective-permute-done((bf16[256,512]{1,0:T(8,128)(2,1)S(1)}, bf16[256,512]{1,0:T(8,128)(2,1)S(1)}, u32[]{:S(2)}, u32[]{:S(2)}) %collective-permute-start.9) | collective-permute-done | bytes 262176 | tf_op jit(solution)/shard_map/ppermute | solution.py:214
  25.8 0.8 collective-permute-start.4
  26.5 2.8 %collective-permute-done.7.refs_5_ = bf16[256,512]{1,0:T(8,128)(2,1)S(1)} collective-permute-done((bf16[256,512]{1,0:T(8,128)(2,1)S(1)}, bf16[256,512]{1,0:T(8,128)(2,1)S(1)}, u32[]{:S(2)}, u32[]{:S(2)}) %collective-permute-start.7) | collective-permute-done | bytes 262176 | tf_op jit(solution)/shard_map/ppermute | solution.py:214
  29.3 0.2 collective-permute-start.3
  29.5 0.0 collective-permute-done.8.refs_6_
  29.5 2.6 %collective-permute-done.6.refs_4_ = bf16[256,512]{1,0:T(8,128)(2,1)S(1)} collective-permute-done((bf16[256,512]{1,0:T(8,128)(2,1)S(1)}, bf16[256,512]{1,0:T(8,128)(2,1)S(1)}, u32[]{:S(2)}, u32[]{:S(2)}) %collective-permute-start.6) | collective-permute-done | bytes 262176 | tf_op jit(solution)/shard_map/ppermute | solution.py:214
  32.1 0.4 collective-permute-done.5
  32.5 2.7 %collective-permute-done.4 = bf16[512,256]{1,0:T(8,128)(2,1)S(1)} collective-permute-done((bf16[512,256]{1,0:T(8,128)(2,1)S(1)}, bf16[512,256]{1,0:T(8,128)(2,1)S(1)}, u32[]{:S(2)}, u32[]{:S(2)}) %collective-permute-start.4) | collective-permute-done | bytes 262176 | tf_op jit(solution)/shard_map/ppermute | solution.py:214
  35.2 0.5 collective-permute-done.3
  35.7 0.1 pad_maximum_fusion.refs_0_
  35.8 0.0 copy-start.6
  35.8 0.1 collective-permute-start.10
  35.9 0.1 collective-permute-start.11
  36.0 0.1 collective-permute-start.13
  36.1 3.2 %collective-permute-start.15 = (bf16[256,512]{1,0:T(8,128)(2,1)S(1)}, bf16[256,512]{1,0:T(8,128)(2,1)S(1)}, u32[]{:S(2)}, u32[]{:S(2)}) collective-permute-start(bf16[256,512]{1,0:T(8,128)(2,1)S(1)} %collective-permute-done.8.refs_6_), channel_id=1, source_target_pairs={{0,28},{4,0},{8,4},{12,8},{16,12},{20,16},{24,20},{28,24},{1,29},{... | collective-permute-start | bytes 786440 | tf_op jit(solution)/shard_map/ppermute | solution.py:214
  39.3 1.9 %collective-permute-start.17 = (bf16[256,512]{1,0:T(8,128)(2,1)S(1)}, bf16[256,512]{1,0:T(8,128)(2,1)S(1)}, u32[]{:S(2)}, u32[]{:S(2)}) collective-permute-start(bf16[256,512]{1,0:T(8,128)(2,1)S(1)} %collective-permute-done.9.refs_7_), channel_id=1, source_target_pairs={{0,28},{4,0},{8,4},{12,8},{16,12},{20,16},{24,20},{28,24},{1,29},{... | collective-permute-start | bytes 786440 | tf_op jit(solution)/shard_map/ppermute | solution.py:214
  41.3 5.1 %collective-permute-done.11.refs_8_ = bf16[256,512]{1,0:T(8,128)(2,1)S(1)} collective-permute-done((bf16[256,512]{1,0:T(8,128)(2,1)S(1)}, bf16[256,512]{1,0:T(8,128)(2,1)S(1)}, u32[]{:S(2)}, u32[]{:S(2)}) %collective-permute-start.11) | collective-permute-done | bytes 262176 | tf_op jit(solution)/shard_map/ppermute | solution.py:214
  46.3 0.0 collective-permute-start.12
  46.3 5.6 %collective-permute-done.13.refs_9_ = bf16[256,512]{1,0:T(8,128)(2,1)S(1)} collective-permute-done((bf16[256,512]{1,0:T(8,128)(2,1)S(1)}, bf16[256,512]{1,0:T(8,128)(2,1)S(1)}, u32[]{:S(2)}, u32[]{:S(2)}) %collective-permute-start.13) | collective-permute-done | bytes 262176 | tf_op jit(solution)/shard_map/ppermute | solution.py:214
  52.0 0.0 collective-permute-start.14
  52.0 0.0 collective-permute-done.15.refs_10_
  52.0 0.0 copy-start.16
  52.0 3.2 %collective-permute-start.16 = (bf16[256,512]{1,0:T(8,128)(2,1)S(1)}, bf16[256,512]{1,0:T(8,128)(2,1)S(1)}, u32[]{:S(2)}, u32[]{:S(2)}) collective-permute-start(bf16[256,512]{1,0:T(8,128)(2,1)S(1)} %collective-permute-done.15.refs_10_), channel_id=1, source_target_pairs={{0,28},{4,0},{8,4},{12,8},{16,12},{20,16},{24,20},{28,24},{1,29},{... | collective-permute-start | bytes 786440 | tf_op jit(solution)/shard_map/ppermute | solution.py:214
  55.2 0.0 collective-permute-done.17.refs_11_
  55.2 0.1 collective-permute-start.18
  55.3 2.3 %collective-permute-done.12.refs_12_ = bf16[256,512]{1,0:T(8,128)(2,1)S(1)} collective-permute-done((bf16[256,512]{1,0:T(8,128)(2,1)S(1)}, bf16[256,512]{1,0:T(8,128)(2,1)S(1)}, u32[]{:S(2)}, u32[]{:S(2)}) %collective-permute-start.12) | collective-permute-done | bytes 262176 | tf_op jit(solution)/shard_map/ppermute | solution.py:214
  57.6 5.1 %collective-permute-done.14.refs_13_ = bf16[256,512]{1,0:T(8,128)(2,1)S(1)} collective-permute-done((bf16[256,512]{1,0:T(8,128)(2,1)S(1)}, bf16[256,512]{1,0:T(8,128)(2,1)S(1)}, u32[]{:S(2)}, u32[]{:S(2)}) %collective-permute-start.14) | collective-permute-done | bytes 262176 | tf_op jit(solution)/shard_map/ppermute | solution.py:214
  62.7 0.0 collective-permute-done.16.refs_14_
  62.7 2.7 %collective-permute-done.18.refs_15_ = bf16[256,512]{1,0:T(8,128)(2,1)S(1)} collective-permute-done((bf16[256,512]{1,0:T(8,128)(2,1)S(1)}, bf16[256,512]{1,0:T(8,128)(2,1)S(1)}, u32[]{:S(2)}, u32[]{:S(2)}) %collective-permute-start.18) | collective-permute-done | bytes 262176 | tf_op jit(solution)/shard_map/ppermute | solution.py:214
  65.5 0.0 collective-permute-done.10.refs_1_
  65.5 0.0 collective-permute-start.19
  65.5 3.8 %collective-permute-start.20 = (bf16[256,512]{1,0:T(8,128)(2,1)S(1)}, bf16[256,512]{1,0:T(8,128)(2,1)S(1)}, u32[]{:S(2)}, u32[]{:S(2)}) collective-permute-start(bf16[256,512]{1,0:T(8,128)(2,1)S(1)} %collective-permute-done.18.refs_15_), channel_id=1, source_target_pairs={{0,28},{4,0},{8,4},{12,8},{16,12},{20,16},{24,20},{28,24},{1,29},{... | collective-permute-start | bytes 786440 | tf_op jit(solution)/shard_map/ppermute | solution.py:214
  69.3 0.0 copy-done.8
  69.3 0.0 copy-done.9
  69.3 0.0 copy-done.10
  69.3 0.0 copy-done.11
  69.3 0.0 copy-done.12
  69.5 11.3 %product_0_7_1_6_2_5_3.1.refs_4_ = f32[512,1024]{1,0:T(8,128)S(1)} custom-call(s32[32,64]{1,0:T(8,128)S(1)} %copy-done.3, s32[32,128]{1,0:T(8,128)S(1)} %bitcast.8, bf16[4,512,256]{2,1,0:T(8,128)(2,1)} %copy-done.6, bf16[4,512,256]{2,1,0:T(8,128)(2,1)} %copy-done.7, bf16[256,512]{1,0:T(8,128)(2,1)} %copy-done.9, bf16[256,512]{1,0:T(8,128)(2,1)} %copy-done.8, ...), custom_call_target="tpu_custom_call" | custom-call | flops 3758096384 | bytes 4194304 | tf_op jit(solution)/shard_map/product_0_7_1_6_2_5_3/pallas_call | solution.py:191
  80.8 0.0 collective-permute-done.19.refs_2_
  80.8 0.0 collective-permute-done.20.refs_3_
  80.8 3.8 %product_4.1 = (f32[512,1024]{1,0:T(8,128)S(1)}, f32[1,1024]{1,0:T(1,128)S(1)}) custom-call(s32[32,64]{1,0:T(8,128)S(1)} %copy-done.3, s32[32,128]{1,0:T(8,128)S(1)} %bitcast.9, bf16[4,512,256]{2,1,0:T(8,128)(2,1)} %copy-done.6, bf16[4,512,256]{2,1,0:T(8,128)(2,1)} %copy-done.7, ...), custom_call_target="tpu_custom_call", output_to_operand_aliasing={{0}: (6, {})} | custom-call | flops 536870912 | bytes 4194304 | tf_op jit(solution)/shard_map/product_4/pallas_call | solution.py:191
  84.6 0.1 broadcast_in_dim.2
  84.7 16.7 %all_to_all.6 = f32[32,1,1024]{2,1,0:T(1,128)S(1)} all-to-all(f32[32,1,1024]{2,1,0:T(1,128)S(1)} %broadcast_in_dim.2), channel_id=1, replica_groups=mesh['y'=4,'core'=2,'z'=8,'x'=4] {'z','x'}, dimensions={0} | all-to-all | bytes 262144 | tf_op jit(solution)/shard_map/all_to_all | solution.py:249
  101.4 0.1 reduce_sum.9
  101.5 1.6 %broadcast_divide_fusion = f32[512,1024]{1,0:T(8,128)} fusion(f32[512,1024]{1,0:T(8,128)S(1)} %get-tuple-element.45, f32[1024]{0:T(1024)S(1)} %broadcast_multiply_fusion), kind=kLoop, calls=%fused_computation.1 | loop fusion | flops 524288 | bytes 4198400 | tf_op jit(solution)/shard_map/div | solution.py:253
  (36 shorter events, 0.1 us)
Async XLA Ops:
  0.0 0.9 copy-start.1
  1.0 0.7 copy-start.2
  1.7 67.8 %copy-start.3 = (s32[32,64]{1,0:T(8,128)S(1)}, s32[32,64]{1,0:T(8,128)}, u32[]{:S(2)}) copy-start(s32[32,64]{1,0:T(8,128)} %right_pattern.3) | copy-start | bytes 24580
  1.7 67.8 %copy-start.5 = (s32[128,32]{0,1:T(8,128)S(1)}, s32[128,32]{0,1:T(8,128)}, u32[]{:S(2)}) copy-start(s32[128,32]{0,1:T(8,128)} %param.5) | copy-start | bytes 49156
  2.6 7.9 %collective-permute-start.2 = (bf16[128,512]{1,0:T(8,128)(2,1)S(1)}, bf16[128,512]{1,0:T(8,128)(2,1)S(1)}, u32[]{:S(2)}, u32[]{:S(2)}) collective-permute-start(bf16[128,512]{1,0:T(8,128)(2,1)S(1)} %pack_right.1), channel_id=1, source_target_pairs={{0,2},{1,3},{2,0},{3,1},{4,6},{5,7},{6,4},{7,5},{8,10},{9,11},{10,... | collective-permute-start | bytes 393224 | tf_op jit(solution)/shard_map/ppermute | solution.py:214
  5.7 6.6 %collective-permute-start.1 = (bf16[128,512]{1,0:T(8,128)(2,1)S(1)}, bf16[128,512]{1,0:T(8,128)(2,1)S(1)}, u32[]{:S(2)}, u32[]{:S(2)}) collective-permute-start(bf16[128,512]{1,0:T(8,128)(2,1)S(1)} %pack_right.1), channel_id=1, source_target_pairs={{0,3},{1,0},{2,1},{3,2},{4,7},{5,4},{6,5},{7,6},{8,11},{9,8},{10,9... | collective-permute-start | bytes 393224 | tf_op jit(solution)/shard_map/ppermute | solution.py:214
  6.9 6.2 %collective-permute-start = (bf16[128,512]{1,0:T(8,128)(2,1)S(1)}, bf16[128,512]{1,0:T(8,128)(2,1)S(1)}, u32[]{:S(2)}, u32[]{:S(2)}) collective-permute-start(bf16[128,512]{1,0:T(8,128)(2,1)S(1)} %pack_right.1), channel_id=1, source_target_pairs={{0,1},{1,2},{2,3},{3,0},{4,5},{5,6},{6,7},{7,4},{8,9},{9,10},{10,1... | collective-permute-start | bytes 393224 | tf_op jit(solution)/shard_map/ppermute | solution.py:214
  7.7 1.0 %copy-start = (bf16[512,512]{1,0:T(8,128)(2,1)S(1)}, bf16[512,512]{1,0:T(8,128)(2,1)}, u32[]{:S(2)}) copy-start(bf16[512,512]{1,0:T(8,128)(2,1)} %left.1) | copy-start | bytes 1572868
  8.8 0.7 copy-start.4
  13.1 56.2 %copy-start.8 = (bf16[256,512]{1,0:T(8,128)(2,1)}, bf16[256,512]{1,0:T(8,128)(2,1)S(1)}, u32[]{:S(2)}) copy-start(bf16[256,512]{1,0:T(8,128)(2,1)S(1)} %constant_dynamic-update-slice_fusion.2.refs_3_) | copy-start | bytes 786436
  13.1 12.7 %collective-permute-start.9 = (bf16[256,512]{1,0:T(8,128)(2,1)S(1)}, bf16[256,512]{1,0:T(8,128)(2,1)S(1)}, u32[]{:S(2)}, u32[]{:S(2)}) collective-permute-start(bf16[256,512]{1,0:T(8,128)(2,1)S(1)} %constant_dynamic-update-slice_fusion.2.refs_3_), channel_id=1, source_target_pairs={{0,28},{4,0},{8,4},{12,8},{16,12},{20,16},{24,20},{28,24},{1,29},{... | collective-permute-start | bytes 786440 | tf_op jit(solution)/shard_map/ppermute | solution.py:214
  19.0 10.3 %collective-permute-start.7 = (bf16[256,512]{1,0:T(8,128)(2,1)S(1)}, bf16[256,512]{1,0:T(8,128)(2,1)S(1)}, u32[]{:S(2)}, u32[]{:S(2)}) collective-permute-start(bf16[256,512]{1,0:T(8,128)(2,1)S(1)} %constant_dynamic-update-slice_fusion.2.refs_3_), channel_id=1, source_target_pairs={{0,4},{4,8},{8,12},{12,16},{16,20},{20,24},{24,28},{28,0},{1,5},{5... | collective-permute-start | bytes 786440 | tf_op jit(solution)/shard_map/ppermute | solution.py:214
  19.0 50.3 %copy-start.9 = (bf16[256,512]{1,0:T(8,128)(2,1)}, bf16[256,512]{1,0:T(8,128)(2,1)S(1)}, u32[]{:S(2)}) copy-start(bf16[256,512]{1,0:T(8,128)(2,1)S(1)} %constant_dynamic-update-slice_fusion.refs_2_) | copy-start | bytes 786436
  19.0 10.5 %collective-permute-start.8 = (bf16[256,512]{1,0:T(8,128)(2,1)S(1)}, bf16[256,512]{1,0:T(8,128)(2,1)S(1)}, u32[]{:S(2)}, u32[]{:S(2)}) collective-permute-start(bf16[256,512]{1,0:T(8,128)(2,1)S(1)} %constant_dynamic-update-slice_fusion.refs_2_), channel_id=1, source_target_pairs={{0,28},{4,0},{8,4},{12,8},{16,12},{20,16},{24,20},{28,24},{1,29},{... | collective-permute-start | bytes 786440 | tf_op jit(solution)/shard_map/ppermute | solution.py:214
  22.4 9.8 %collective-permute-start.6 = (bf16[256,512]{1,0:T(8,128)(2,1)S(1)}, bf16[256,512]{1,0:T(8,128)(2,1)S(1)}, u32[]{:S(2)}, u32[]{:S(2)}) collective-permute-start(bf16[256,512]{1,0:T(8,128)(2,1)S(1)} %constant_dynamic-update-slice_fusion.refs_2_), channel_id=1, source_target_pairs={{0,4},{4,8},{8,12},{12,16},{16,20},{20,24},{24,28},{28,0},{1,5},{5... | collective-permute-start | bytes 786440 | tf_op jit(solution)/shard_map/ppermute | solution.py:214
  22.4 10.2 %collective-permute-start.5 = (bf16[512,256]{1,0:T(8,128)(2,1)S(1)}, bf16[512,256]{1,0:T(8,128)(2,1)S(1)}, u32[]{:S(2)}, u32[]{:S(2)}) collective-permute-start(bf16[512,256]{1,0:T(8,128)(2,1)S(1)} %pack_left.1), channel_id=1, source_target_pairs={{0,128},{64,192},{128,0},{192,64},{1,129},{65,193},{129,1},{193,65... | collective-permute-start | bytes 786440 | tf_op jit(solution)/shard_map/ppermute | solution.py:214
  25.8 43.6 %copy-start.10 = (bf16[256,512]{1,0:T(8,128)(2,1)}, bf16[256,512]{1,0:T(8,128)(2,1)S(1)}, u32[]{:S(2)}) copy-start(bf16[256,512]{1,0:T(8,128)(2,1)S(1)} %collective-permute-done.9.refs_7_) | copy-start | bytes 786436
  25.8 9.5 %collective-permute-start.4 = (bf16[512,256]{1,0:T(8,128)(2,1)S(1)}, bf16[512,256]{1,0:T(8,128)(2,1)S(1)}, u32[]{:S(2)}, u32[]{:S(2)}) collective-permute-start(bf16[512,256]{1,0:T(8,128)(2,1)S(1)} %pack_left.1), channel_id=1, source_target_pairs={{0,192},{64,0},{128,64},{192,128},{1,193},{65,1},{129,65},{193,129... | collective-permute-start | bytes 786440 | tf_op jit(solution)/shard_map/ppermute | solution.py:214
  29.3 40.0 %copy-start.11 = (bf16[256,512]{1,0:T(8,128)(2,1)}, bf16[256,512]{1,0:T(8,128)(2,1)S(1)}, u32[]{:S(2)}) copy-start(bf16[256,512]{1,0:T(8,128)(2,1)S(1)} %collective-permute-done.7.refs_5_) | copy-start | bytes 786436
  29.3 6.4 %collective-permute-start.3 = (bf16[512,256]{1,0:T(8,128)(2,1)S(1)}, bf16[512,256]{1,0:T(8,128)(2,1)S(1)}, u32[]{:S(2)}, u32[]{:S(2)}) collective-permute-start(bf16[512,256]{1,0:T(8,128)(2,1)S(1)} %pack_left.1), channel_id=1, source_target_pairs={{0,64},{64,128},{128,192},{192,0},{1,65},{65,129},{129,193},{193,1... | collective-permute-start | bytes 786440 | tf_op jit(solution)/shard_map/ppermute | solution.py:214
  29.5 39.8 %copy-start.12 = (bf16[256,512]{1,0:T(8,128)(2,1)}, bf16[256,512]{1,0:T(8,128)(2,1)S(1)}, u32[]{:S(2)}) copy-start(bf16[256,512]{1,0:T(8,128)(2,1)S(1)} %collective-permute-done.8.refs_6_) | copy-start | bytes 786436
  32.1 37.2 %copy-start.13 = (bf16[256,512]{1,0:T(8,128)(2,1)}, bf16[256,512]{1,0:T(8,128)(2,1)S(1)}, u32[]{:S(2)}) copy-start(bf16[256,512]{1,0:T(8,128)(2,1)S(1)} %collective-permute-done.6.refs_4_) | copy-start | bytes 786436
  35.8 33.5 %copy-start.6 = (bf16[4,512,256]{2,1,0:T(8,128)(2,1)}, bf16[4,512,256]{2,1,0:T(8,128)(2,1)S(1)}, u32[]{:S(2)}) copy-start(bf16[4,512,256]{2,1,0:T(8,128)(2,1)S(1)} %pad_maximum_fusion.refs_0_) | copy-start | bytes 3145732
  35.8 29.6 %collective-permute-start.10 = (bf16[4,512,256]{2,1,0:T(8,128)(2,1)S(1)}, bf16[4,512,256]{2,1,0:T(8,128)(2,1)S(1)}, u32[]{:S(2)}, u32[]{:S(2)}) collective-permute-start(bf16[4,512,256]{2,1,0:T(8,128)(2,1)S(1)} %pad_maximum_fusion.refs_0_), channel_id=1, source_target_pairs={{0,32},{32,0},{1,33},{33,1},{2,34},{34,2},{3,35},{35,3},{4,36},{36... | collective-permute-start | bytes 3145736 | tf_op jit(solution)/shard_map/ppermute | solution.py:214
  35.9 10.4 %collective-permute-start.11 = (bf16[256,512]{1,0:T(8,128)(2,1)S(1)}, bf16[256,512]{1,0:T(8,128)(2,1)S(1)}, u32[]{:S(2)}, u32[]{:S(2)}) collective-permute-start(bf16[256,512]{1,0:T(8,128)(2,1)S(1)} %collective-permute-done.6.refs_4_), channel_id=1, source_target_pairs={{0,4},{4,8},{8,12},{12,16},{16,20},{20,24},{24,28},{28,0},{1,5},{5... | collective-permute-start | bytes 786440 | tf_op jit(solution)/shard_map/ppermute | solution.py:214
  36.0 15.9 %collective-permute-start.13 = (bf16[256,512]{1,0:T(8,128)(2,1)S(1)}, bf16[256,512]{1,0:T(8,128)(2,1)S(1)}, u32[]{:S(2)}, u32[]{:S(2)}) collective-permute-start(bf16[256,512]{1,0:T(8,128)(2,1)S(1)} %collective-permute-done.7.refs_5_), channel_id=1, source_target_pairs={{0,4},{4,8},{8,12},{12,16},{16,20},{20,24},{24,28},{28,0},{1,5},{5... | collective-permute-start | bytes 786440 | tf_op jit(solution)/shard_map/ppermute | solution.py:214
  36.1 15.8 %collective-permute-start.15 = (bf16[256,512]{1,0:T(8,128)(2,1)S(1)}, bf16[256,512]{1,0:T(8,128)(2,1)S(1)}, u32[]{:S(2)}, u32[]{:S(2)}) collective-permute-start(bf16[256,512]{1,0:T(8,128)(2,1)S(1)} %collective-permute-done.8.refs_6_), channel_id=1, source_target_pairs={{0,28},{4,0},{8,4},{12,8},{16,12},{20,16},{24,20},{28,24},{1,29},{... | collective-permute-start | bytes 786440 | tf_op jit(solution)/shard_map/ppermute | solution.py:214
  39.3 15.9 %collective-permute-start.17 = (bf16[256,512]{1,0:T(8,128)(2,1)S(1)}, bf16[256,512]{1,0:T(8,128)(2,1)S(1)}, u32[]{:S(2)}, u32[]{:S(2)}) collective-permute-start(bf16[256,512]{1,0:T(8,128)(2,1)S(1)} %collective-permute-done.9.refs_7_), channel_id=1, source_target_pairs={{0,28},{4,0},{8,4},{12,8},{16,12},{20,16},{24,20},{28,24},{1,29},{... | collective-permute-start | bytes 786440 | tf_op jit(solution)/shard_map/ppermute | solution.py:214
  46.3 23.0 %copy-start.14 = (bf16[256,512]{1,0:T(8,128)(2,1)}, bf16[256,512]{1,0:T(8,128)(2,1)S(1)}, u32[]{:S(2)}) copy-start(bf16[256,512]{1,0:T(8,128)(2,1)S(1)} %collective-permute-done.11.refs_8_) | copy-start | bytes 786436
  46.3 11.2 %collective-permute-start.12 = (bf16[256,512]{1,0:T(8,128)(2,1)S(1)}, bf16[256,512]{1,0:T(8,128)(2,1)S(1)}, u32[]{:S(2)}, u32[]{:S(2)}) collective-permute-start(bf16[256,512]{1,0:T(8,128)(2,1)S(1)} %collective-permute-done.11.refs_8_), channel_id=1, source_target_pairs={{0,4},{4,8},{8,12},{12,16},{16,20},{20,24},{24,28},{28,0},{1,5},{5... | collective-permute-start | bytes 786440 | tf_op jit(solution)/shard_map/ppermute | solution.py:214
  52.0 17.4 %copy-start.15 = (bf16[256,512]{1,0:T(8,128)(2,1)}, bf16[256,512]{1,0:T(8,128)(2,1)S(1)}, u32[]{:S(2)}) copy-start(bf16[256,512]{1,0:T(8,128)(2,1)S(1)} %collective-permute-done.13.refs_9_) | copy-start | bytes 786436
  52.0 10.8 %collective-permute-start.14 = (bf16[256,512]{1,0:T(8,128)(2,1)S(1)}, bf16[256,512]{1,0:T(8,128)(2,1)S(1)}, u32[]{:S(2)}, u32[]{:S(2)}) collective-permute-start(bf16[256,512]{1,0:T(8,128)(2,1)S(1)} %collective-permute-done.13.refs_9_), channel_id=1, source_target_pairs={{0,4},{4,8},{8,12},{12,16},{16,20},{20,24},{24,28},{28,0},{1,5},{5... | collective-permute-start | bytes 786440 | tf_op jit(solution)/shard_map/ppermute | solution.py:214
  52.0 17.4 %copy-start.16 = (bf16[256,512]{1,0:T(8,128)(2,1)}, bf16[256,512]{1,0:T(8,128)(2,1)S(1)}, u32[]{:S(2)}) copy-start(bf16[256,512]{1,0:T(8,128)(2,1)S(1)} %collective-permute-done.15.refs_10_) | copy-start | bytes 786436
  52.0 10.8 %collective-permute-start.16 = (bf16[256,512]{1,0:T(8,128)(2,1)S(1)}, bf16[256,512]{1,0:T(8,128)(2,1)S(1)}, u32[]{:S(2)}, u32[]{:S(2)}) collective-permute-start(bf16[256,512]{1,0:T(8,128)(2,1)S(1)} %collective-permute-done.15.refs_10_), channel_id=1, source_target_pairs={{0,28},{4,0},{8,4},{12,8},{16,12},{20,16},{24,20},{28,24},{1,29},{... | collective-permute-start | bytes 786440 | tf_op jit(solution)/shard_map/ppermute | solution.py:214
  55.2 14.2 %copy-start.17 = (bf16[256,512]{1,0:T(8,128)(2,1)}, bf16[256,512]{1,0:T(8,128)(2,1)S(1)}, u32[]{:S(2)}) copy-start(bf16[256,512]{1,0:T(8,128)(2,1)S(1)} %collective-permute-done.17.refs_11_) | copy-start | bytes 786436
  55.2 10.2 %collective-permute-start.18 = (bf16[256,512]{1,0:T(8,128)(2,1)S(1)}, bf16[256,512]{1,0:T(8,128)(2,1)S(1)}, u32[]{:S(2)}, u32[]{:S(2)}) collective-permute-start(bf16[256,512]{1,0:T(8,128)(2,1)S(1)} %collective-permute-done.17.refs_11_), channel_id=1, source_target_pairs={{0,28},{4,0},{8,4},{12,8},{16,12},{20,16},{24,20},{28,24},{1,29},{... | collective-permute-start | bytes 786440 | tf_op jit(solution)/shard_map/ppermute | solution.py:214
  57.6 11.8 %copy-start.18 = (bf16[256,512]{1,0:T(8,128)(2,1)}, bf16[256,512]{1,0:T(8,128)(2,1)S(1)}, u32[]{:S(2)}) copy-start(bf16[256,512]{1,0:T(8,128)(2,1)S(1)} %collective-permute-done.12.refs_12_) | copy-start | bytes 786436
  62.7 6.7 %copy-start.19 = (bf16[256,512]{1,0:T(8,128)(2,1)}, bf16[256,512]{1,0:T(8,128)(2,1)S(1)}, u32[]{:S(2)}) copy-start(bf16[256,512]{1,0:T(8,128)(2,1)S(1)} %collective-permute-done.14.refs_13_) | copy-start | bytes 786436
  62.7 6.7 %copy-start.20 = (bf16[256,512]{1,0:T(8,128)(2,1)}, bf16[256,512]{1,0:T(8,128)(2,1)S(1)}, u32[]{:S(2)}) copy-start(bf16[256,512]{1,0:T(8,128)(2,1)S(1)} %collective-permute-done.16.refs_14_) | copy-start | bytes 786436
  65.4 4.0 %copy-start.21 = (bf16[256,512]{1,0:T(8,128)(2,1)}, bf16[256,512]{1,0:T(8,128)(2,1)S(1)}, u32[]{:S(2)}) copy-start(bf16[256,512]{1,0:T(8,128)(2,1)S(1)} %collective-permute-done.18.refs_15_) | copy-start | bytes 786436
  65.5 4.0 %copy-start.7 = (bf16[4,512,256]{2,1,0:T(8,128)(2,1)}, bf16[4,512,256]{2,1,0:T(8,128)(2,1)S(1)}, u32[]{:S(2)}) copy-start(bf16[4,512,256]{2,1,0:T(8,128)(2,1)S(1)} %collective-permute-done.10.refs_1_) | copy-start | bytes 3145732
  65.5 15.3 %collective-permute-start.19 = (bf16[256,512]{1,0:T(8,128)(2,1)S(1)}, bf16[256,512]{1,0:T(8,128)(2,1)S(1)}, u32[]{:S(2)}, u32[]{:S(2)}) collective-permute-start(bf16[256,512]{1,0:T(8,128)(2,1)S(1)} %collective-permute-done.12.refs_12_), channel_id=1, source_target_pairs={{0,4},{4,8},{8,12},{12,16},{16,20},{20,24},{24,28},{28,0},{1,5},{5... | collective-permute-start | bytes 786440 | tf_op jit(solution)/shard_map/ppermute | solution.py:214
  65.5 15.4 %collective-permute-start.20 = (bf16[256,512]{1,0:T(8,128)(2,1)S(1)}, bf16[256,512]{1,0:T(8,128)(2,1)S(1)}, u32[]{:S(2)}, u32[]{:S(2)}) collective-permute-start(bf16[256,512]{1,0:T(8,128)(2,1)S(1)} %collective-permute-done.18.refs_15_), channel_id=1, source_target_pairs={{0,28},{4,0},{8,4},{12,8},{16,12},{20,16},{24,20},{28,24},{1,29},{... | collective-permute-start | bytes 786440 | tf_op jit(solution)/shard_map/ppermute | solution.py:214

commit v4 on v3

v4 whole, which is shorter than its diff:
```python
import functools

import jax
import jax.numpy as jnp
from jax import lax
from jax.experimental import pallas as pl
from jax.experimental.pallas import tpu as pltpu
from jax.sharding import Mesh
from jax.sharding import PartitionSpec as P

BLOCK = 128
SLOTS = 4
LEFT_SLOTS = 2
SHIFTS = (0, 3, 1, 2)
PLACES = (0, 2, 3, 1)
FAR = (-3, 3, 4)
KERNEL_VMEM = 24 * 1024 * 1024
ROW, COL = ("y", "core"), ("z", "x")


def lanes(start, blocks=1):
    return pl.ds(pl.multiple_of(start * BLOCK, BLOCK), blocks * BLOCK)


def place_of(shift):
    place = jnp.int32(PLACES[3])
    for s in range(3):
        place = jnp.where(shift == s, PLACES[s], place)
    return place


def row_index():
    return lax.axis_index("y") * lax.axis_size("core") + lax.axis_index("core")


def col_index():
    return lax.axis_index("z") * lax.axis_size("x") + lax.axis_index("x")


def pack_right_kernel(pattern, right, out):
    row, col = row_index(), col_index()
    col_blocks = right.shape[1] // BLOCK
    out[...] = jnp.zeros_like(out)
    slot = jnp.int32(0)
    for j in range(col_blocks):
        present = pattern[col, row * col_blocks + j]

        @pl.when(present != 0)
        def _(j=j, slot=slot):
            out[:, lanes(slot)] = right[:, j * BLOCK : (j + 1) * BLOCK]

        slot = slot + present


def pack_left_kernel(pattern, left, out):
    row, col = row_index(), col_index()
    block_rows, inner_blocks = left.shape[0] // BLOCK, left.shape[1] // BLOCK
    out[...] = jnp.zeros_like(out)
    for i in range(block_rows):
        rows = slice(i * BLOCK, (i + 1) * BLOCK)
        slot = jnp.int32(0)
        for k in range(inner_blocks):
            present = pattern[row * inner_blocks + k, col * block_rows + i]

            @pl.when(present != 0)
            def _(k=k, slot=slot, rows=rows):
                out[rows, lanes(slot)] = left[rows, k * BLOCK : (k + 1) * BLOCK]

            slot = slot + present


def pack(kernel, name, pattern, values, slots):
    return pl.pallas_call(
        kernel,
        out_shape=jax.ShapeDtypeStruct((values.shape[0], slots * BLOCK), values.dtype),
        in_specs=[
            pl.BlockSpec(memory_space=pltpu.SMEM),
            pl.BlockSpec(memory_space=pltpu.VMEM),
        ],
        out_specs=pl.BlockSpec(memory_space=pltpu.VMEM),
        compiler_params=pltpu.CompilerParams(vmem_limit_bytes=4 * 1024 * 1024),
        name=name,
    )(pattern, values)


def product_kernel(blocks, copies, first, last, *refs):
    refs = list(refs)
    right_hbm, left_hbm, mine, other = [refs.pop(0) for _ in range(4)]
    pieces = [refs.pop(0) for _ in range(1 + max(copy[0] for copy in copies))]
    total = None if first else refs.pop(0)
    out = refs.pop(0)
    sums = refs.pop(0) if last else None
    right_pattern, left_pattern, plan, *refs = refs
    packed_left, packed_right, dense_left, dense_right, sem, pattern_sem = refs
    row, col = row_index(), col_index()
    y, core = lax.axis_index("y"), lax.axis_index("core")
    z, x = lax.axis_index("z"), lax.axis_index("x")
    y_size, z_size, x_size = lax.axis_size("y"), lax.axis_size("z"), lax.axis_size("x")
    cores = lax.axis_size("core")
    block_rows = dense_left.shape[0] // BLOCK
    col_blocks = dense_right.shape[1] // BLOCK
    z_shifts = sorted({block[0] for block in blocks})
    groups = [lax.rem(z + shift + z_size, z_size) for shift in z_shifts]
    patterns = [
        pltpu.make_async_copy(right_hbm, right_pattern, pattern_sem.at[0]),
        pltpu.make_async_copy(left_hbm, left_pattern, pattern_sem.at[1]),
    ]
    for copy in patterns:
        copy.start()
    waits = []
    for n, group in enumerate(groups):
        there = place_of(lax.rem(lax.div(group, cores) - y + y_size, y_size))
        same = lax.rem(group, cores) == core
        for source, wanted in ((mine, same), (other, jnp.logical_not(same))):
            copy = pltpu.make_async_copy(
                source.at[there], packed_left.at[n, :, : LEFT_SLOTS * BLOCK], sem.at[n]
            )
            pl.when(wanted)(copy.start)
        waits.append(copy)
    for c, (piece, start, rows, to) in enumerate(copies):
        copy = pltpu.make_async_copy(
            pieces[piece].at[pl.ds(start, rows)],
            packed_right.at[pl.ds(to, rows), : SLOTS * BLOCK],
            sem.at[len(groups) + c],
        )
        copy.start()
        waits.append(copy)
    packed_left[:, :, LEFT_SLOTS * BLOCK :] = jnp.zeros(
        (len(groups), packed_left.shape[1], BLOCK), packed_left.dtype
    )
    packed_right[:, SLOTS * BLOCK :] = jnp.zeros(
        (packed_right.shape[0], BLOCK), packed_right.dtype
    )
    for copy in patterns:
        copy.wait()
    for n, group in enumerate(groups):
        for i in range(block_rows):
            slot = jnp.int32(0)
            for inside in range(x_size):
                present = left_pattern[group * x_size + inside, col * block_rows + i]
                source = jnp.where(present != 0, jnp.minimum(slot, LEFT_SLOTS), LEFT_SLOTS)
                plan[(n * block_rows + i) * x_size + inside] = source
                slot = slot + present
    right_plan, left_plan = [], []
    for b, (z_shift, x_shift) in enumerate(blocks):
        n = z_shifts.index(z_shift)
        inside = lax.rem(x + x_shift, x_size)
        k = groups[n] * x_size + inside
        slot = jnp.int32(0)
        for j in range(col_blocks):
            present = right_pattern[k, row * col_blocks + j]
            right_plan.append((b, j, jnp.where(present != 0, jnp.minimum(slot, SLOTS), SLOTS)))
            slot = slot + present
        for i in range(block_rows):
            left_plan.append((n, b, i, plan[(n * block_rows + i) * x_size + inside]))
    for copy in waits:
        copy.wait()
    for b, j, source in right_plan:
        rows = slice(b * BLOCK, (b + 1) * BLOCK)
        dense_right[rows, j * BLOCK : (j + 1) * BLOCK] = packed_right[rows, lanes(source)]
    for n, b, i, source in left_plan:
        rows = slice(i * BLOCK, (i + 1) * BLOCK)
        dense_left[rows, b * BLOCK : (b + 1) * BLOCK] = packed_left[n, rows, lanes(source)]

    width = 256 if last else out.shape[1]

    @pl.loop(0, out.shape[1] // width)
    def _(t):
        columns = pl.ds(pl.multiple_of(t * width, width), width)
        value = jnp.dot(
            dense_left[...], dense_right[:, columns], preferred_element_type=jnp.float32
        )
        if not first:
            value = value + total[:, columns]
        if last:
            value = value * value
            sums[:, columns] = jnp.sum(value, axis=0, keepdims=True)
        out[:, columns] = value


def product(blocks, copies, right_pattern, left_pattern, left, pieces, total, last):
    rows, cols = left[0].shape[1], right_pattern.shape[1] // 8 * BLOCK
    inner = len(blocks) * BLOCK
    groups = len({block[0] for block in blocks})
    out_shape = [jax.ShapeDtypeStruct((rows, cols), jnp.float32)]
    if last:
        out_shape.append(jax.ShapeDtypeStruct((1, cols), jnp.float32))
    vmem = pl.BlockSpec(memory_space=pltpu.VMEM)
    left = [pltpu.with_memory_space_constraint(value, pltpu.HBM) for value in left]
    if not last:
        pieces = [pltpu.with_memory_space_constraint(piece, pltpu.HBM) for piece in pieces]
    operands = [right_pattern, left_pattern, *left, *pieces]
    in_specs = [pl.BlockSpec(memory_space=pl.ANY)] * len(operands)
    aliases = {}
    if total is not None:
        aliases = {len(operands): 0}
        operands.append(total)
        in_specs.append(vmem)
    return pl.pallas_call(
        functools.partial(product_kernel, blocks, copies, total is None, last),
        out_shape=out_shape,
        in_specs=in_specs,
        out_specs=[vmem] * len(out_shape),
        scratch_shapes=[
            pltpu.SMEM(right_pattern.shape, jnp.int32),
            pltpu.SMEM(left_pattern.shape, jnp.int32),
            pltpu.SMEM((groups * rows // BLOCK * 4,), jnp.int32),
            pltpu.VMEM((groups, rows, (LEFT_SLOTS + 1) * BLOCK), jnp.bfloat16),
            pltpu.VMEM((inner, (SLOTS + 1) * BLOCK), jnp.bfloat16),
            pltpu.VMEM((rows, inner), jnp.bfloat16),
            pltpu.VMEM((inner, cols), jnp.bfloat16),
            pltpu.SemaphoreType.DMA((groups + len(copies),)),
            pltpu.SemaphoreType.DMA((2,)),
        ],
        input_output_aliases=aliases,
        compiler_params=pltpu.CompilerParams(vmem_limit_bytes=KERNEL_VMEM),
        cost_estimate=pl.CostEstimate(
            flops=2 * rows * inner * cols, bytes_accessed=4 * 1024 * 1024, transcendentals=0
        ),
        name="product_last" if last else "product_first",
    )(*operands)


def moved(value, axis, step):
    size = lax.axis_size(axis)
    return lax.ppermute(value, axis, [(i, (i + step) % size) for i in range(size)])


def shards(left_values, left_pattern, right_values, right_pattern):
    left_pattern = left_pattern.T
    packed_right = pack(pack_right_kernel, "pack_right", right_pattern, right_values, SLOTS)
    near = [packed_right] + [moved(packed_right, "x", -shift) for shift in SHIFTS[1:]]
    far = [moved(packed_right, "z", -shift) for shift in FAR]
    packed_left = pack(pack_left_kernel, "pack_left", left_pattern, left_values, LEFT_SLOTS)
    own = jnp.concatenate(near, 0)
    packed_left, own = lax.optimization_barrier((packed_left, own))
    up, down = moved(own, "z", 1), moved(own, "z", -1)
    columns = [packed_left] + [moved(packed_left, "y", -shift) for shift in SHIFTS[1:]]
    columns, far, up, down = lax.optimization_barrier((columns, far, up, down))
    far = jnp.concatenate(far, 0)
    far_3, far_1 = moved(far, "x", 1), moved(far, "x", -1)
    mine = jnp.stack(columns)
    left = (mine, moved(mine, "core", 1))
    further_up, further_down = moved(up, "z", 1), moved(down, "z", -1)
    left, far_3, far_1 = lax.optimization_barrier((left, far_3, far_1))
    half = far.shape[0] // 2
    far_2 = (moved(far_3[:half], "x", 1), moved(far_1[half:], "x", -1))
    whole = own.shape[0]
    blocks, copies = [], []
    for piece, z_shift in enumerate((0, -1, 1)):
        blocks += [(z_shift, x_shift) for x_shift in SHIFTS]
        copies.append((piece, 0, whole, piece * whole))
    for n, x_shift in enumerate((0, 3, 1)):
        copies.append((3 + n, 0, 2 * half, len(blocks) * BLOCK))
        blocks += [(z_shift, x_shift) for z_shift in FAR]
    pieces = [own, up, down, far, far_3, far_1]
    (total,) = product(blocks, copies, right_pattern, left_pattern, left, pieces, None, False)
    blocks = [(z_shift, x_shift) for z_shift in (-2, 2) for x_shift in SHIFTS]
    blocks += [(z_shift, 2) for z_shift in FAR]
    copies = [(0, 0, whole, 0), (1, 0, whole, whole), (2, 0, half, 2 * whole), (3, 0, half, 2 * whole + half)]
    pieces = [further_up, further_down, *far_2]
    total, sums = product(blocks, copies, right_pattern, left_pattern, left, pieces, total, True)
    count = lax.axis_size("z") * lax.axis_size("x")
    spread = lax.all_to_all(
        jnp.broadcast_to(sums, (count, sums.shape[1])), COL, 0, 0, tiled=True
    )
    column_mean = jnp.sum(spread, axis=0) / (total.shape[0] * count)
    return total / column_mean[None, :]


def solution(mesh):
    finer = Mesh(mesh.devices.reshape(4, 2, 8, 4), (*ROW, *COL))
    return jax.shard_map(
        shards,
        mesh=finer,
        in_specs=(P(COL, ROW), P(), P(COL, ROW), P()),
        out_specs=P(COL, ROW),
        check_vma=False,
    )
```

time: 104 us -> 106 us (1.019)
  Pallas kernels: 17 us -> 13.3 us
  starting transfers between devices: 29.2 us -> 32.9 us
  blocking collectives: 16.7 us -> 18.4 us
    ppermute x21 -> x18, starting transfers between devices: 29.2 us -> 32.9 us  [moved(): lax.ppermute(value, axis, [(i, (i + step) % size) for i in range(size)])]
    pallas_call x2, Pallas kernels: 15.1 us -> 11.4 us  [product(): pl.pallas_call(functools.partial(product_kernel, blocks, copies, total is...]
    all_to_all x1, blocking collectives: 16.7 us -> 18.4 us  [shards(): lax.all_to_all(jnp.broadcast_to(sums, (count, sums.shape[1])), COL, 0, 0,...]
    ppermute x21 -> x18, waiting for transfers between devices: 34.5 us -> 34.9 us  [moved(): lax.ppermute(value, axis, [(i, (i + step) % size) for i in range(size)])]
    unnamed x46 -> x30, local copies, waits for them, and re-layouts: 3.51 us -> 3.49 us
  transfers between devices with their start and end apart: 21 -> 18, of which waited for: 13 -> 6; matrix products, arithmetic and copies ran while one was open for 0% -> 0% of each run, Pallas kernels for 12% -> 7%
where the time goes in v4:
time: 106 us; the launch traced here: 105 us
  waiting for transfers between devices  34.9 us (33%)
  starting transfers between devices  32.9 us (31%)
  blocking collectives  18.4 us (17%)
  Pallas kernels  13.3 us (13%)
  local copies, waits for them, and re-layouts  3.6 us (3%)
  other arithmetic  1.85 us (2%)
    ppermute x18, waiting for transfers between devices, moved(): lax.ppermute(value, axis, [(i, (i + step) % size) for i in range(size)])  34.9 us
    ppermute x18, starting transfers between devices, moved(): lax.ppermute(value, axis, [(i, (i + step) % size) for i in range(size)])  32.9 us
    all_to_all x1, blocking collectives, shards(): lax.all_to_all(jnp.broadcast_to(sums, (count, sums.shape[1])), COL, 0, 0,...  18.4 us
    pallas_call x2, Pallas kernels, product(): pl.pallas_call(functools.partial(product_kernel, blocks, copies, total is...  11.4 us
    unnamed x30, local copies, waits for them, and re-layouts  3.49 us
  transfers between devices with their start and end apart: 18, of which 6 were waited for; matrix products, arithmetic and copies ran while one was open for 0% of the time, Pallas kernels for 7%

profile of v4, /device:TPU:24, one launch (start us, length us, event | category | flops | bytes accessed | tf_op | source)
XLA Modules:
  0.0 105.3 jit_solution(14096465408403789411)
XLA Ops:
  0.0 0.9 copy-done.1
  1.0 0.7 copy-done.2
  1.7 0.9 pack_right.1
  2.6 1.6 %collective-permute-start = (bf16[128,512]{1,0:T(8,128)(2,1)S(1)}, bf16[128,512]{1,0:T(8,128)(2,1)S(1)}, u32[]{:S(2)}, u32[]{:S(2)}) collective-permute-start(bf16[128,512]{1,0:T(8,128)(2,1)S(1)} %pack_right.1), channel_id=1, source_target_pairs={{0,1},{1,2},{2,3},{3,0},{4,5},{5,6},{6,7},{7,4},{8,9},{9,10},{10,1... | collective-permute-start | bytes 393224 | tf_op jit(solution)/shard_map/ppermute | solution.py:226
  4.2 1.7 %collective-permute-start.1 = (bf16[128,512]{1,0:T(8,128)(2,1)S(1)}, bf16[128,512]{1,0:T(8,128)(2,1)S(1)}, u32[]{:S(2)}, u32[]{:S(2)}) collective-permute-start(bf16[128,512]{1,0:T(8,128)(2,1)S(1)} %pack_right.1), channel_id=1, source_target_pairs={{0,3},{1,0},{2,1},{3,2},{4,7},{5,4},{6,5},{7,6},{8,11},{9,8},{10,9... | collective-permute-start | bytes 393224 | tf_op jit(solution)/shard_map/ppermute | solution.py:226
  5.9 1.8 %collective-permute-start.2 = (bf16[128,512]{1,0:T(8,128)(2,1)S(1)}, bf16[128,512]{1,0:T(8,128)(2,1)S(1)}, u32[]{:S(2)}, u32[]{:S(2)}) collective-permute-start(bf16[128,512]{1,0:T(8,128)(2,1)S(1)} %pack_right.1), channel_id=1, source_target_pairs={{0,2},{1,3},{2,0},{3,1},{4,6},{5,7},{6,4},{7,5},{8,10},{9,11},{10,... | collective-permute-start | bytes 393224 | tf_op jit(solution)/shard_map/ppermute | solution.py:226
  7.7 1.0 copy-done
  8.8 0.7 copy-done.4
  9.5 1.0 pack_left.1
  10.5 0.0 collective-permute-done
  10.5 0.7 collective-permute-done.1
  11.2 1.7 %collective-permute-done.2 = bf16[128,512]{1,0:T(8,128)(2,1)S(1)} collective-permute-done((bf16[128,512]{1,0:T(8,128)(2,1)S(1)}, bf16[128,512]{1,0:T(8,128)(2,1)S(1)}, u32[]{:S(2)}, u32[]{:S(2)}) %collective-permute-start.2) | collective-permute-done | bytes 131104 | tf_op jit(solution)/shard_map/ppermute | solution.py:226
  12.9 0.0 copy-start.8
  13.0 0.0 copy-start.3
  13.0 0.0 copy-start.5
  13.0 5.9 %collective-permute-start.10 = (bf16[512,512]{1,0:T(8,128)(2,1)S(1)}, bf16[512,512]{1,0:T(8,128)(2,1)S(1)}, u32[]{:S(2)}, u32[]{:S(2)}) collective-permute-start(bf16[512,512]{1,0:T(8,128)(2,1)S(1)} %pad_maximum_fusion.1.refs_4_), channel_id=1, source_target_pairs={{0,28},{4,0},{8,4},{12,8},{16,12},{20,16},{24,20},{28,24},{1,29},{... | collective-permute-start | bytes 1572872 | tf_op jit(solution)/shard_map/ppermute | solution.py:226
  18.9 0.0 collective-permute-start.9
  18.9 2.0 %collective-permute-start.6 = (bf16[128,512]{1,0:T(8,128)(2,1)S(1)}, bf16[128,512]{1,0:T(8,128)(2,1)S(1)}, u32[]{:S(2)}, u32[]{:S(2)}) collective-permute-start(bf16[128,512]{1,0:T(8,128)(2,1)S(1)} %pack_right.1), channel_id=1, source_target_pairs={{0,12},{4,16},{8,20},{12,24},{16,28},{20,0},{24,4},{28,8},{1,13},{... | collective-permute-start | bytes 393224 | tf_op jit(solution)/shard_map/ppermute | solution.py:226
  20.9 3.0 %collective-permute-start.7 = (bf16[128,512]{1,0:T(8,128)(2,1)S(1)}, bf16[128,512]{1,0:T(8,128)(2,1)S(1)}, u32[]{:S(2)}, u32[]{:S(2)}) collective-permute-start(bf16[128,512]{1,0:T(8,128)(2,1)S(1)} %pack_right.1), channel_id=1, source_target_pairs={{0,20},{4,24},{8,28},{12,0},{16,4},{20,8},{24,12},{28,16},{1,21},{... | collective-permute-start | bytes 393224 | tf_op jit(solution)/shard_map/ppermute | solution.py:226
  24.0 3.4 %collective-permute-start.8 = (bf16[128,512]{1,0:T(8,128)(2,1)S(1)}, bf16[128,512]{1,0:T(8,128)(2,1)S(1)}, u32[]{:S(2)}, u32[]{:S(2)}) collective-permute-start(bf16[128,512]{1,0:T(8,128)(2,1)S(1)} %pack_right.1), channel_id=1, source_target_pairs={{0,16},{4,20},{8,24},{12,28},{16,0},{20,4},{24,8},{28,12},{1,17},{... | collective-permute-start | bytes 393224 | tf_op jit(solution)/shard_map/ppermute | solution.py:226
  27.3 16.3 %collective-permute-done.6 = bf16[128,512]{1,0:T(8,128)(2,1)S(1)} collective-permute-done((bf16[128,512]{1,0:T(8,128)(2,1)S(1)}, bf16[128,512]{1,0:T(8,128)(2,1)S(1)}, u32[]{:S(2)}, u32[]{:S(2)}) %collective-permute-start.6) | collective-permute-done | bytes 131104 | tf_op jit(solution)/shard_map/ppermute | solution.py:226
  43.6 0.2 collective-permute-start.3
  43.8 0.0 collective-permute-done.7
  43.8 1.8 %collective-permute-start.4 = (bf16[512,256]{1,0:T(8,128)(2,1)S(1)}, bf16[512,256]{1,0:T(8,128)(2,1)S(1)}, u32[]{:S(2)}, u32[]{:S(2)}) collective-permute-start(bf16[512,256]{1,0:T(8,128)(2,1)S(1)} %pack_left.1), channel_id=1, source_target_pairs={{0,192},{64,0},{128,64},{192,128},{1,193},{65,1},{129,65},{193,129... | collective-permute-start | bytes 786440 | tf_op jit(solution)/shard_map/ppermute | solution.py:226
  45.6 0.0 collective-permute-done.8
  45.6 1.2 %collective-permute-start.5 = (bf16[512,256]{1,0:T(8,128)(2,1)S(1)}, bf16[512,256]{1,0:T(8,128)(2,1)S(1)}, u32[]{:S(2)}, u32[]{:S(2)}) collective-permute-start(bf16[512,256]{1,0:T(8,128)(2,1)S(1)} %pack_left.1), channel_id=1, source_target_pairs={{0,128},{64,192},{128,0},{192,64},{1,129},{65,193},{129,1},{193,65... | collective-permute-start | bytes 786440 | tf_op jit(solution)/shard_map/ppermute | solution.py:226
  46.8 4.9 %collective-permute-done.3 = bf16[512,256]{1,0:T(8,128)(2,1)S(1)} collective-permute-done((bf16[512,256]{1,0:T(8,128)(2,1)S(1)}, bf16[512,256]{1,0:T(8,128)(2,1)S(1)}, u32[]{:S(2)}, u32[]{:S(2)}) %collective-permute-start.3) | collective-permute-done | bytes 262176 | tf_op jit(solution)/shard_map/ppermute | solution.py:226
  51.8 5.0 %collective-permute-done.4 = bf16[512,256]{1,0:T(8,128)(2,1)S(1)} collective-permute-done((bf16[512,256]{1,0:T(8,128)(2,1)S(1)}, bf16[512,256]{1,0:T(8,128)(2,1)S(1)}, u32[]{:S(2)}, u32[]{:S(2)}) %collective-permute-start.4) | collective-permute-done | bytes 262176 | tf_op jit(solution)/shard_map/ppermute | solution.py:226
  56.8 0.0 collective-permute-done.5
  56.8 0.0 collective-permute-done.10.refs_6_
  56.8 0.0 collective-permute-done.9.refs_5_
  56.8 0.0 copy-start.13
  56.8 0.1 pad_maximum_fusion.refs_2_
  56.9 0.0 copy-start.6
  57.0 0.1 collective-permute-start.11
  57.1 0.0 copy-start.11
  57.1 0.1 collective-permute-start.12
  57.2 3.2 %collective-permute-start.13 = (bf16[384,512]{1,0:T(8,128)(2,1)S(1)}, bf16[384,512]{1,0:T(8,128)(2,1)S(1)}, u32[]{:S(2)}, u32[]{:S(2)}) collective-permute-start(bf16[384,512]{1,0:T(8,128)(2,1)S(1)} %constant_dynamic-update-slice_fusion.refs_7_), channel_id=1, source_target_pairs={{0,3},{1,0},{2,1},{3,2},{4,7},{5,4},{6,5},{7,6},{8,11},{9,8},{10,9... | collective-permute-start | bytes 1179656 | tf_op jit(solution)/shard_map/ppermute | solution.py:226
  60.4 1.1 %collective-permute-start.14 = (bf16[512,512]{1,0:T(8,128)(2,1)S(1)}, bf16[512,512]{1,0:T(8,128)(2,1)S(1)}, u32[]{:S(2)}, u32[]{:S(2)}) collective-permute-start(bf16[512,512]{1,0:T(8,128)(2,1)S(1)} %collective-permute-done.9.refs_5_), channel_id=1, source_target_pairs={{0,4},{4,8},{8,12},{12,16},{16,20},{20,24},{24,28},{28,0},{1,5},{5... | collective-permute-start | bytes 1572872 | tf_op jit(solution)/shard_map/ppermute | solution.py:226
  61.5 2.1 %collective-permute-start.15 = (bf16[512,512]{1,0:T(8,128)(2,1)S(1)}, bf16[512,512]{1,0:T(8,128)(2,1)S(1)}, u32[]{:S(2)}, u32[]{:S(2)}) collective-permute-start(bf16[512,512]{1,0:T(8,128)(2,1)S(1)} %collective-permute-done.10.refs_6_), channel_id=1, source_target_pairs={{0,28},{4,0},{8,4},{12,8},{16,12},{20,16},{24,20},{28,24},{1,29},{... | collective-permute-start | bytes 1572872 | tf_op jit(solution)/shard_map/ppermute | solution.py:226
  63.7 6.2 %collective-permute-done.12.refs_8_ = bf16[384,512]{1,0:T(8,128)(2,1)S(1)} collective-permute-done((bf16[384,512]{1,0:T(8,128)(2,1)S(1)}, bf16[384,512]{1,0:T(8,128)(2,1)S(1)}, u32[]{:S(2)}, u32[]{:S(2)}) %collective-permute-start.12) | collective-permute-done | bytes 393248 | tf_op jit(solution)/shard_map/ppermute | solution.py:226
  69.9 0.0 collective-permute-done.13.refs_9_
  69.9 0.0 collective-permute-done.11.refs_3_
  69.9 0.0 copy-start.7
  70.0 0.3 collective-permute-start.16
  70.3 3.3 %collective-permute-start.17 = (bf16[192,512]{1,0:T(8,128)(2,1)S(1)}, bf16[192,512]{1,0:T(8,128)(2,1)S(1)}, u32[]{:S(2)}, u32[]{:S(2)}) collective-permute-start(bf16[192,512]{1,0:T(8,128)(2,1)S(1)} %slice.7), channel_id=1, source_target_pairs={{0,3},{1,0},{2,1},{3,2},{4,7},{5,4},{6,5},{7,6},{8,11},{9,8},{10,9... | collective-permute-start | bytes 589832 | tf_op jit(solution)/shard_map/ppermute | solution.py:226
  73.6 0.0 copy-done.8
  73.6 0.0 copy-done.12
  73.6 0.0 copy-done.13
  73.6 0.0 copy-done.6
  73.6 0.0 copy-done.11
  73.6 0.0 copy-done.9
  73.6 0.0 copy-done.10
  73.6 0.0 copy-done.7
  73.6 6.1 %product_first.1.refs_8_ = f32[512,1024]{1,0:T(8,128)S(1)} custom-call(s32[32,64]{1,0:T(8,128)S(1)} %copy-done.3, s32[32,128]{1,0:T(8,128)S(1)} %bitcast.8, bf16[4,512,256]{2,1,0:T(8,128)(2,1)} %copy-done.6, bf16[4,512,256]{2,1,0:T(8,128)(2,1)} %copy-done.7, bf16[512,512]{1,0:T(8,128)(2,1)} %copy-done.8, bf16[512,512]{1,0:T(8,128)(2,1)} %copy-done.13, ...), custom_call_target="tpu_custom_call" | custom-call | flops 2818572288 | bytes 4194304 | tf_op jit(solution)/shard_map/product_first/pallas_call | solution.py:199
  79.8 0.0 collective-permute-done.14.refs_4_
  79.8 0.0 collective-permute-done.15.refs_5_
  79.8 0.0 collective-permute-done.16.refs_6_
  79.8 0.0 collective-permute-done.17.refs_7_
  79.8 5.3 %product_last.1 = (f32[512,1024]{1,0:T(8,128)S(1)}, f32[1,1024]{1,0:T(1,128)S(1)}) custom-call(s32[32,64]{1,0:T(8,128)S(1)} %copy-done.3, s32[32,128]{1,0:T(8,128)S(1)} %bitcast.9, bf16[4,512,256]{2,1,0:T(8,128)(2,1)} %copy-done.6, bf16[4,512,256]{2,1,0:T(8,128)(2,1)} %copy-done.7, ...), custom_call_target="tpu_custom_call", output_to_operand_aliasing={{0}: (8, {})} | custom-call | flops 1476395008 | bytes 4194304 | tf_op jit(solution)/shard_map/product_last/pallas_call | solution.py:199
  85.1 0.1 broadcast_in_dim.2
  85.1 18.4 %all_to_all.6 = f32[32,1,1024]{2,1,0:T(1,128)S(1)} all-to-all(f32[32,1,1024]{2,1,0:T(1,128)S(1)} %broadcast_in_dim.2), channel_id=1, replica_groups=mesh['y'=4,'core'=2,'z'=8,'x'=4] {'z','x'}, dimensions={0} | all-to-all | bytes 262144 | tf_op jit(solution)/shard_map/all_to_all | solution.py:264
  103.6 0.1 reduce_sum.9
  103.7 1.6 %broadcast_divide_fusion = f32[512,1024]{1,0:T(8,128)} fusion(f32[512,1024]{1,0:T(8,128)S(1)} %get-tuple-element.37, f32[1024]{0:T(1024)S(1)} %broadcast_multiply_fusion), kind=kLoop, calls=%fused_computation.1 | loop fusion | flops 524288 | bytes 4198400 | tf_op jit(solution)/shard_map/div | solution.py:268
  (16 shorter events, 0.1 us)
Async XLA Ops:
  0.0 0.9 copy-start.1
  1.0 0.7 copy-start.2
  2.6 7.9 %collective-permute-start = (bf16[128,512]{1,0:T(8,128)(2,1)S(1)}, bf16[128,512]{1,0:T(8,128)(2,1)S(1)}, u32[]{:S(2)}, u32[]{:S(2)}) collective-permute-start(bf16[128,512]{1,0:T(8,128)(2,1)S(1)} %pack_right.1), channel_id=1, source_target_pairs={{0,1},{1,2},{2,3},{3,0},{4,5},{5,6},{6,7},{7,4},{8,9},{9,10},{10,1... | collective-permute-start | bytes 393224 | tf_op jit(solution)/shard_map/ppermute | solution.py:226
  4.2 7.1 %collective-permute-start.1 = (bf16[128,512]{1,0:T(8,128)(2,1)S(1)}, bf16[128,512]{1,0:T(8,128)(2,1)S(1)}, u32[]{:S(2)}, u32[]{:S(2)}) collective-permute-start(bf16[128,512]{1,0:T(8,128)(2,1)S(1)} %pack_right.1), channel_id=1, source_target_pairs={{0,3},{1,0},{2,1},{3,2},{4,7},{5,4},{6,5},{7,6},{8,11},{9,8},{10,9... | collective-permute-start | bytes 393224 | tf_op jit(solution)/shard_map/ppermute | solution.py:226
  5.9 7.0 %collective-permute-start.2 = (bf16[128,512]{1,0:T(8,128)(2,1)S(1)}, bf16[128,512]{1,0:T(8,128)(2,1)S(1)}, u32[]{:S(2)}, u32[]{:S(2)}) collective-permute-start(bf16[128,512]{1,0:T(8,128)(2,1)S(1)} %pack_right.1), channel_id=1, source_target_pairs={{0,2},{1,3},{2,0},{3,1},{4,6},{5,7},{6,4},{7,5},{8,10},{9,11},{10,... | collective-permute-start | bytes 393224 | tf_op jit(solution)/shard_map/ppermute | solution.py:226
  7.7 1.0 copy-start
  8.8 0.7 copy-start.4
  12.9 60.6 %copy-start.8 = (bf16[512,512]{1,0:T(8,128)(2,1)}, bf16[512,512]{1,0:T(8,128)(2,1)S(1)}, u32[]{:S(2)}) copy-start(bf16[512,512]{1,0:T(8,128)(2,1)S(1)} %pad_maximum_fusion.1.refs_4_) | copy-start | bytes 1572868
  13.0 60.7 %copy-start.3 = (s32[32,64]{1,0:T(8,128)S(1)}, s32[32,64]{1,0:T(8,128)}, u32[]{:S(2)}) copy-start(s32[32,64]{1,0:T(8,128)} %refs_0_.3) | copy-start | bytes 24580
  13.0 60.7 %copy-start.5 = (s32[128,32]{0,1:T(8,128)S(1)}, s32[128,32]{0,1:T(8,128)}, u32[]{:S(2)}) copy-start(s32[128,32]{0,1:T(8,128)} %param.5) | copy-start | bytes 49156
  13.0 43.8 %collective-permute-start.10 = (bf16[512,512]{1,0:T(8,128)(2,1)S(1)}, bf16[512,512]{1,0:T(8,128)(2,1)S(1)}, u32[]{:S(2)}, u32[]{:S(2)}) collective-permute-start(bf16[512,512]{1,0:T(8,128)(2,1)S(1)} %pad_maximum_fusion.1.refs_4_), channel_id=1, source_target_pairs={{0,28},{4,0},{8,4},{12,8},{16,12},{20,16},{24,20},{28,24},{1,29},{... | collective-permute-start | bytes 1572872 | tf_op jit(solution)/shard_map/ppermute | solution.py:226
  18.9 37.9 %collective-permute-start.9 = (bf16[512,512]{1,0:T(8,128)(2,1)S(1)}, bf16[512,512]{1,0:T(8,128)(2,1)S(1)}, u32[]{:S(2)}, u32[]{:S(2)}) collective-permute-start(bf16[512,512]{1,0:T(8,128)(2,1)S(1)} %pad_maximum_fusion.1.refs_4_), channel_id=1, source_target_pairs={{0,4},{4,8},{8,12},{12,16},{16,20},{20,24},{24,28},{28,0},{1,5},{5... | collective-permute-start | bytes 1572872 | tf_op jit(solution)/shard_map/ppermute | solution.py:226
  18.9 24.7 %collective-permute-start.6 = (bf16[128,512]{1,0:T(8,128)(2,1)S(1)}, bf16[128,512]{1,0:T(8,128)(2,1)S(1)}, u32[]{:S(2)}, u32[]{:S(2)}) collective-permute-start(bf16[128,512]{1,0:T(8,128)(2,1)S(1)} %pack_right.1), channel_id=1, source_target_pairs={{0,12},{4,16},{8,20},{12,24},{16,28},{20,0},{24,4},{28,8},{1,13},{... | collective-permute-start | bytes 393224 | tf_op jit(solution)/shard_map/ppermute | solution.py:226
  20.9 22.9 %collective-permute-start.7 = (bf16[128,512]{1,0:T(8,128)(2,1)S(1)}, bf16[128,512]{1,0:T(8,128)(2,1)S(1)}, u32[]{:S(2)}, u32[]{:S(2)}) collective-permute-start(bf16[128,512]{1,0:T(8,128)(2,1)S(1)} %pack_right.1), channel_id=1, source_target_pairs={{0,20},{4,24},{8,28},{12,0},{16,4},{20,8},{24,12},{28,16},{1,21},{... | collective-permute-start | bytes 393224 | tf_op jit(solution)/shard_map/ppermute | solution.py:226
  24.0 21.7 %collective-permute-start.8 = (bf16[128,512]{1,0:T(8,128)(2,1)S(1)}, bf16[128,512]{1,0:T(8,128)(2,1)S(1)}, u32[]{:S(2)}, u32[]{:S(2)}) collective-permute-start(bf16[128,512]{1,0:T(8,128)(2,1)S(1)} %pack_right.1), channel_id=1, source_target_pairs={{0,16},{4,20},{8,24},{12,28},{16,0},{20,4},{24,8},{28,12},{1,17},{... | collective-permute-start | bytes 393224 | tf_op jit(solution)/shard_map/ppermute | solution.py:226
  43.6 8.2 %collective-permute-start.3 = (bf16[512,256]{1,0:T(8,128)(2,1)S(1)}, bf16[512,256]{1,0:T(8,128)(2,1)S(1)}, u32[]{:S(2)}, u32[]{:S(2)}) collective-permute-start(bf16[512,256]{1,0:T(8,128)(2,1)S(1)} %pack_left.1), channel_id=1, source_target_pairs={{0,64},{64,128},{128,192},{192,0},{1,65},{65,129},{129,193},{193,1... | collective-permute-start | bytes 786440 | tf_op jit(solution)/shard_map/ppermute | solution.py:226
  43.8 12.9 %collective-permute-start.4 = (bf16[512,256]{1,0:T(8,128)(2,1)S(1)}, bf16[512,256]{1,0:T(8,128)(2,1)S(1)}, u32[]{:S(2)}, u32[]{:S(2)}) collective-permute-start(bf16[512,256]{1,0:T(8,128)(2,1)S(1)} %pack_left.1), channel_id=1, source_target_pairs={{0,192},{64,0},{128,64},{192,128},{1,193},{65,1},{129,65},{193,129... | collective-permute-start | bytes 786440 | tf_op jit(solution)/shard_map/ppermute | solution.py:226
  45.6 11.2 %collective-permute-start.5 = (bf16[512,256]{1,0:T(8,128)(2,1)S(1)}, bf16[512,256]{1,0:T(8,128)(2,1)S(1)}, u32[]{:S(2)}, u32[]{:S(2)}) collective-permute-start(bf16[512,256]{1,0:T(8,128)(2,1)S(1)} %pack_left.1), channel_id=1, source_target_pairs={{0,128},{64,192},{128,0},{192,64},{1,129},{65,193},{129,1},{193,65... | collective-permute-start | bytes 786440 | tf_op jit(solution)/shard_map/ppermute | solution.py:226
  56.8 16.8 %copy-start.12 = (bf16[512,512]{1,0:T(8,128)(2,1)}, bf16[512,512]{1,0:T(8,128)(2,1)S(1)}, u32[]{:S(2)}) copy-start(bf16[512,512]{1,0:T(8,128)(2,1)S(1)} %collective-permute-done.10.refs_6_) | copy-start | bytes 1572868
  56.8 16.8 %copy-start.13 = (bf16[512,512]{1,0:T(8,128)(2,1)}, bf16[512,512]{1,0:T(8,128)(2,1)S(1)}, u32[]{:S(2)}) copy-start(bf16[512,512]{1,0:T(8,128)(2,1)S(1)} %collective-permute-done.9.refs_5_) | copy-start | bytes 1572868
  56.9 16.6 %copy-start.6 = (bf16[4,512,256]{2,1,0:T(8,128)(2,1)}, bf16[4,512,256]{2,1,0:T(8,128)(2,1)S(1)}, u32[]{:S(2)}) copy-start(bf16[4,512,256]{2,1,0:T(8,128)(2,1)S(1)} %pad_maximum_fusion.refs_2_) | copy-start | bytes 3145732
  57.0 13.0 %collective-permute-start.11 = (bf16[4,512,256]{2,1,0:T(8,128)(2,1)S(1)}, bf16[4,512,256]{2,1,0:T(8,128)(2,1)S(1)}, u32[]{:S(2)}, u32[]{:S(2)}) collective-permute-start(bf16[4,512,256]{2,1,0:T(8,128)(2,1)S(1)} %pad_maximum_fusion.refs_2_), channel_id=1, source_target_pairs={{0,32},{32,0},{1,33},{33,1},{2,34},{34,2},{3,35},{35,3},{4,36},{36... | collective-permute-start | bytes 3145736 | tf_op jit(solution)/shard_map/ppermute | solution.py:226
  57.1 16.5 %copy-start.11 = (bf16[384,512]{1,0:T(8,128)(2,1)}, bf16[384,512]{1,0:T(8,128)(2,1)S(1)}, u32[]{:S(2)}) copy-start(bf16[384,512]{1,0:T(8,128)(2,1)S(1)} %constant_dynamic-update-slice_fusion.refs_7_) | copy-start | bytes 1179652
  57.1 12.8 %collective-permute-start.12 = (bf16[384,512]{1,0:T(8,128)(2,1)S(1)}, bf16[384,512]{1,0:T(8,128)(2,1)S(1)}, u32[]{:S(2)}, u32[]{:S(2)}) collective-permute-start(bf16[384,512]{1,0:T(8,128)(2,1)S(1)} %constant_dynamic-update-slice_fusion.refs_7_), channel_id=1, source_target_pairs={{0,1},{1,2},{2,3},{3,0},{4,5},{5,6},{6,7},{7,4},{8,9},{9,10},{10,1... | collective-permute-start | bytes 1179656 | tf_op jit(solution)/shard_map/ppermute | solution.py:226
  57.2 12.7 %collective-permute-start.13 = (bf16[384,512]{1,0:T(8,128)(2,1)S(1)}, bf16[384,512]{1,0:T(8,128)(2,1)S(1)}, u32[]{:S(2)}, u32[]{:S(2)}) collective-permute-start(bf16[384,512]{1,0:T(8,128)(2,1)S(1)} %constant_dynamic-update-slice_fusion.refs_7_), channel_id=1, source_target_pairs={{0,3},{1,0},{2,1},{3,2},{4,7},{5,4},{6,5},{7,6},{8,11},{9,8},{10,9... | collective-permute-start | bytes 1179656 | tf_op jit(solution)/shard_map/ppermute | solution.py:226
  60.4 19.3 %collective-permute-start.14 = (bf16[512,512]{1,0:T(8,128)(2,1)S(1)}, bf16[512,512]{1,0:T(8,128)(2,1)S(1)}, u32[]{:S(2)}, u32[]{:S(2)}) collective-permute-start(bf16[512,512]{1,0:T(8,128)(2,1)S(1)} %collective-permute-done.9.refs_5_), channel_id=1, source_target_pairs={{0,4},{4,8},{8,12},{12,16},{16,20},{20,24},{24,28},{28,0},{1,5},{5... | collective-permute-start | bytes 1572872 | tf_op jit(solution)/shard_map/ppermute | solution.py:226
  61.5 18.2 %collective-permute-start.15 = (bf16[512,512]{1,0:T(8,128)(2,1)S(1)}, bf16[512,512]{1,0:T(8,128)(2,1)S(1)}, u32[]{:S(2)}, u32[]{:S(2)}) collective-permute-start(bf16[512,512]{1,0:T(8,128)(2,1)S(1)} %collective-permute-done.10.refs_6_), channel_id=1, source_target_pairs={{0,28},{4,0},{8,4},{12,8},{16,12},{20,16},{24,20},{28,24},{1,29},{... | collective-permute-start | bytes 1572872 | tf_op jit(solution)/shard_map/ppermute | solution.py:226
  69.9 3.7 %copy-start.9 = (bf16[384,512]{1,0:T(8,128)(2,1)}, bf16[384,512]{1,0:T(8,128)(2,1)S(1)}, u32[]{:S(2)}) copy-start(bf16[384,512]{1,0:T(8,128)(2,1)S(1)} %collective-permute-done.12.refs_8_) | copy-start | bytes 1179652
  69.9 3.7 %copy-start.10 = (bf16[384,512]{1,0:T(8,128)(2,1)}, bf16[384,512]{1,0:T(8,128)(2,1)S(1)}, u32[]{:S(2)}) copy-start(bf16[384,512]{1,0:T(8,128)(2,1)S(1)} %collective-permute-done.13.refs_9_) | copy-start | bytes 1179652
  69.9 3.7 %copy-start.7 = (bf16[4,512,256]{2,1,0:T(8,128)(2,1)}, bf16[4,512,256]{2,1,0:T(8,128)(2,1)S(1)}, u32[]{:S(2)}) copy-start(bf16[4,512,256]{2,1,0:T(8,128)(2,1)S(1)} %collective-permute-done.11.refs_3_) | copy-start | bytes 3145732
  70.0 9.8 %collective-permute-start.16 = (bf16[192,512]{1,0:T(8,128)(2,1)S(1)}, bf16[192,512]{1,0:T(8,128)(2,1)S(1)}, u32[]{:S(2)}, u32[]{:S(2)}) collective-permute-start(bf16[192,512]{1,0:T(8,128)(2,1)S(1)} %slice.6), channel_id=1, source_target_pairs={{0,1},{1,2},{2,3},{3,0},{4,5},{5,6},{6,7},{7,4},{8,9},{9,10},{10,1... | collective-permute-start | bytes 589832 | tf_op jit(solution)/shard_map/ppermute | solution.py:226
  70.3 9.5 %collective-permute-start.17 = (bf16[192,512]{1,0:T(8,128)(2,1)S(1)}, bf16[192,512]{1,0:T(8,128)(2,1)S(1)}, u32[]{:S(2)}, u32[]{:S(2)}) collective-permute-start(bf16[192,512]{1,0:T(8,128)(2,1)S(1)} %slice.7), channel_id=1, source_target_pairs={{0,3},{1,0},{2,1},{3,2},{4,7},{5,4},{6,5},{7,6},{8,11},{9,8},{10,9... | collective-permute-start | bytes 589832 | tf_op jit(solution)/shard_map/ppermute | solution.py:226

commit v5 on v4

--- a/solution.py
+++ b/solution.py
@@ -229,20 +229,19 @@
 def shards(left_values, left_pattern, right_values, right_pattern):
     left_pattern = left_pattern.T
     packed_right = pack(pack_right_kernel, "pack_right", right_pattern, right_values, SLOTS)
+    far = [moved(packed_right, "z", -shift) for shift in FAR[:2]]
     near = [packed_right] + [moved(packed_right, "x", -shift) for shift in SHIFTS[1:]]
-    far = [moved(packed_right, "z", -shift) for shift in FAR]
     packed_left = pack(pack_left_kernel, "pack_left", left_pattern, left_values, LEFT_SLOTS)
-    own = jnp.concatenate(near, 0)
-    packed_left, own = lax.optimization_barrier((packed_left, own))
+    near, packed_left = lax.optimization_barrier((near, packed_left))
+    far.append(moved(near[0], "z", -FAR[2]))
+    columns = [packed_left] + [moved(packed_left, "y", -shift) for shift in SHIFTS[1:]]
+    near, far, columns = lax.optimization_barrier((near, far, columns))
+    own, far, mine = jnp.concatenate(near, 0), jnp.concatenate(far, 0), jnp.stack(columns)
     up, down = moved(own, "z", 1), moved(own, "z", -1)
-    columns = [packed_left] + [moved(packed_left, "y", -shift) for shift in SHIFTS[1:]]
-    columns, far, up, down = lax.optimization_barrier((columns, far, up, down))
-    far = jnp.concatenate(far, 0)
     far_3, far_1 = moved(far, "x", 1), moved(far, "x", -1)
-    mine = jnp.stack(columns)
     left = (mine, moved(mine, "core", 1))
+    left, up, down, far_3, far_1 = lax.optimization_barrier((left, up, down, far_3, far_1))
     further_up, further_down = moved(up, "z", 1), moved(down, "z", -1)
-    left, far_3, far_1 = lax.optimization_barrier((left, far_3, far_1))
     half = far.shape[0] // 2
     far_2 = (moved(far_3[:half], "x", 1), moved(far_1[half:], "x", -1))
     whole = own.shape[0]

time: 106 us -> 94.5 us (0.89)
  waiting for transfers between devices: 34.9 us -> 24.1 us
    ppermute x18, waiting for transfers between devices: 34.9 us -> 24.1 us  [moved(): lax.ppermute(value, axis, [(i, (i + step) % size) for i in range(size)])]
    all_to_all x1, blocking collectives: 18.4 us -> 17.4 us  [shards(): lax.all_to_all(jnp.broadcast_to(sums, (count, sums.shape[1])), COL, 0, 0,...]
    unnamed x30 -> x33, local copies, waits for them, and re-layouts: 3.49 us -> 3.52 us
  transfers between devices with their start and end apart: 18 -> 18, of which waited for: 6 -> 7; matrix products, arithmetic and copies ran while one was open for 0% -> 0% of each run, Pallas kernels for 7% -> 8%
where the time goes in v5:
time: 94.5 us; the launch traced here: 94.1 us
  starting transfers between devices  33.7 us (36%)
  waiting for transfers between devices  24.1 us (26%)
  blocking collectives  17.4 us (18%)
  Pallas kernels  13.2 us (14%)
  local copies, waits for them, and re-layouts  3.64 us (4%)
  other arithmetic  1.81 us (2%)
    ppermute x18, starting transfers between devices, moved(): lax.ppermute(value, axis, [(i, (i + step) % size) for i in range(size)])  33.7 us
    ppermute x18, waiting for transfers between devices, moved(): lax.ppermute(value, axis, [(i, (i + step) % size) for i in range(size)])  24.1 us
    all_to_all x1, blocking collectives, shards(): lax.all_to_all(jnp.broadcast_to(sums, (count, sums.shape[1])), COL, 0, 0,...  17.4 us
    pallas_call x2, Pallas kernels, product(): pl.pallas_call(functools.partial(product_kernel, blocks, copies, total is...  11.3 us
    unnamed x33, local copies, waits for them, and re-layouts  3.52 us
    pallas_call x2, Pallas kernels, pack(): pl.pallas_call(kernel, out_shape=jax.ShapeDtypeStruct((values.shape[0], s...  1.91 us
  transfers between devices with their start and end apart: 18, of which 7 were waited for; matrix products, arithmetic and copies ran while one was open for 0% of the time, Pallas kernels for 8%

profile of v5, /device:TPU:24, one launch (start us, length us, event | category | flops | bytes accessed | tf_op | source)
XLA Modules:
  0.0 94.1 jit_solution(12561008225555324260)
XLA Ops:
  0.0 0.9 %copy-done.1 = bf16[128,1024]{1,0:T(8,128)(2,1)S(1)} copy-done((bf16[128,1024]{1,0:T(8,128)(2,1)S(1)}, bf16[128,1024]{1,0:T(8,128)(2,1)}, u32[]{:S(2)}) %copy-start.1) | copy-done | bytes 262168
  1.0 0.7 copy-done.2
  1.7 0.9 pack_right.1
  2.6 3.1 %collective-permute-start.2 = (bf16[128,512]{1,0:T(8,128)(2,1)S(1)}, bf16[128,512]{1,0:T(8,128)(2,1)S(1)}, u32[]{:S(2)}, u32[]{:S(2)}) collective-permute-start(bf16[128,512]{1,0:T(8,128)(2,1)S(1)} %pack_right.1), channel_id=1, source_target_pairs={{0,2},{1,3},{2,0},{3,1},{4,6},{5,7},{6,4},{7,5},{8,10},{9,11},{10,... | collective-permute-start | bytes 393224 | tf_op jit(solution)/shard_map/ppermute | solution.py:226
  5.7 1.1 %collective-permute-start.1 = (bf16[128,512]{1,0:T(8,128)(2,1)S(1)}, bf16[128,512]{1,0:T(8,128)(2,1)S(1)}, u32[]{:S(2)}, u32[]{:S(2)}) collective-permute-start(bf16[128,512]{1,0:T(8,128)(2,1)S(1)} %pack_right.1), channel_id=1, source_target_pairs={{0,3},{1,0},{2,1},{3,2},{4,7},{5,4},{6,5},{7,6},{8,11},{9,8},{10,9... | collective-permute-start | bytes 393224 | tf_op jit(solution)/shard_map/ppermute | solution.py:226
  6.9 0.9 collective-permute-start
  7.7 6.7 %collective-permute-start.4 = (bf16[128,512]{1,0:T(8,128)(2,1)S(1)}, bf16[128,512]{1,0:T(8,128)(2,1)S(1)}, u32[]{:S(2)}, u32[]{:S(2)}) collective-permute-start(bf16[128,512]{1,0:T(8,128)(2,1)S(1)} %pack_right.1), channel_id=1, source_target_pairs={{0,20},{4,24},{8,28},{12,0},{16,4},{20,8},{24,12},{28,16},{1,21},{... | collective-permute-start | bytes 393224 | tf_op jit(solution)/shard_map/ppermute | solution.py:226
  14.5 1.0 %copy-done = bf16[512,512]{1,0:T(8,128)(2,1)S(1)} copy-done((bf16[512,512]{1,0:T(8,128)(2,1)S(1)}, bf16[512,512]{1,0:T(8,128)(2,1)}, u32[]{:S(2)}) %copy-start) | copy-done | bytes 524312
  15.5 0.7 copy-done.4
  16.2 1.0 %pack_left.1 = bf16[512,256]{1,0:T(8,128)(2,1)S(1)} custom-call(s32[32,128]{1,0:T(8,128)S(1)} %bitcast.7, bf16[512,512]{1,0:T(8,128)(2,1)S(1)} %copy-done), custom_call_target="tpu_custom_call" | custom-call | tf_op jit(solution)/shard_map/pack_left/pallas_call | solution.py:73
  17.2 0.0 collective-permute-done.2
  17.3 0.0 collective-permute-done.1
  17.3 0.0 collective-permute-done
  17.3 1.3 %collective-permute-start.8 = (bf16[512,256]{1,0:T(8,128)(2,1)S(1)}, bf16[512,256]{1,0:T(8,128)(2,1)S(1)}, u32[]{:S(2)}, u32[]{:S(2)}) collective-permute-start(bf16[512,256]{1,0:T(8,128)(2,1)S(1)} %pack_left.1), channel_id=1, source_target_pairs={{0,128},{64,192},{128,0},{192,64},{1,129},{65,193},{129,1},{193,65... | collective-permute-start | bytes 786440 | tf_op jit(solution)/shard_map/ppermute | solution.py:226
  18.6 0.0 collective-permute-start.7
  18.6 3.2 %collective-permute-start.6 = (bf16[512,256]{1,0:T(8,128)(2,1)S(1)}, bf16[512,256]{1,0:T(8,128)(2,1)S(1)}, u32[]{:S(2)}, u32[]{:S(2)}) collective-permute-start(bf16[512,256]{1,0:T(8,128)(2,1)S(1)} %pack_left.1), channel_id=1, source_target_pairs={{0,64},{64,128},{128,192},{192,0},{1,65},{65,129},{129,193},{193,1... | collective-permute-start | bytes 786440 | tf_op jit(solution)/shard_map/ppermute | solution.py:226
  21.8 0.3 collective-permute-start.3
  22.1 0.0 collective-permute-done.4
  22.1 4.5 %collective-permute-start.5 = (bf16[128,512]{1,0:T(8,128)(2,1)S(1)}, bf16[128,512]{1,0:T(8,128)(2,1)S(1)}, u32[]{:S(2)}, u32[]{:S(2)}) collective-permute-start(bf16[128,512]{1,0:T(8,128)(2,1)S(1)} %pack_right.1), channel_id=1, source_target_pairs={{0,16},{4,20},{8,24},{12,28},{16,0},{20,4},{24,8},{28,12},{1,17},{... | collective-permute-start | bytes 393224 | tf_op jit(solution)/shard_map/ppermute | solution.py:226
  26.6 9.3 %collective-permute-done.3 = bf16[128,512]{1,0:T(8,128)(2,1)S(1)} collective-permute-done((bf16[128,512]{1,0:T(8,128)(2,1)S(1)}, bf16[128,512]{1,0:T(8,128)(2,1)S(1)}, u32[]{:S(2)}, u32[]{:S(2)}) %collective-permute-start.3) | collective-permute-done | bytes 131104 | tf_op jit(solution)/shard_map/ppermute | solution.py:226
  35.9 0.0 collective-permute-done.5
  35.9 0.0 collective-permute-done.8
  35.9 0.0 collective-permute-done.7
  35.9 0.0 collective-permute-done.6
  35.9 0.0 copy-start.3
  35.9 0.0 copy-start.5
  36.0 0.1 pad_maximum_fusion.refs_2_
  36.1 0.0 copy-start.6
  36.1 0.1 collective-permute-start.9
  36.3 0.0 copy-start.11
  36.3 0.8 collective-permute-start.11
  37.0 2.1 %collective-permute-start.10 = (bf16[512,512]{1,0:T(8,128)(2,1)S(1)}, bf16[512,512]{1,0:T(8,128)(2,1)S(1)}, u32[]{:S(2)}, u32[]{:S(2)}) collective-permute-start(bf16[512,512]{1,0:T(8,128)(2,1)S(1)} %constant_dynamic-update-slice_fusion.refs_4_), channel_id=1, source_target_pairs={{0,4},{4,8},{8,12},{12,16},{16,20},{20,24},{24,28},{28,0},{1,5},{5... | collective-permute-start | bytes 1572872 | tf_op jit(solution)/shard_map/ppermute | solution.py:226
  39.1 0.0 copy-start.10
  39.2 2.5 %collective-permute-start.13 = (bf16[384,512]{1,0:T(8,128)(2,1)S(1)}, bf16[384,512]{1,0:T(8,128)(2,1)S(1)}, u32[]{:S(2)}, u32[]{:S(2)}) collective-permute-start(bf16[384,512]{1,0:T(8,128)(2,1)S(1)} %constant_dynamic-update-slice_fusion.4.refs_7_), channel_id=1, source_target_pairs={{0,3},{1,0},{2,1},{3,2},{4,7},{5,4},{6,5},{7,6},{8,11},{9,8},{10,9... | collective-permute-start | bytes 1179656 | tf_op jit(solution)/shard_map/ppermute | solution.py:226
  41.7 0.0 collective-permute-start.12
  41.7 8.8 %collective-permute-done.13.refs_9_ = bf16[384,512]{1,0:T(8,128)(2,1)S(1)} collective-permute-done((bf16[384,512]{1,0:T(8,128)(2,1)S(1)}, bf16[384,512]{1,0:T(8,128)(2,1)S(1)}, u32[]{:S(2)}, u32[]{:S(2)}) %collective-permute-start.13) | collective-permute-done | bytes 393248 | tf_op jit(solution)/shard_map/ppermute | solution.py:226
  50.5 3.4 %collective-permute-done.12.refs_8_ = bf16[384,512]{1,0:T(8,128)(2,1)S(1)} collective-permute-done((bf16[384,512]{1,0:T(8,128)(2,1)S(1)}, bf16[384,512]{1,0:T(8,128)(2,1)S(1)}, u32[]{:S(2)}, u32[]{:S(2)}) %collective-permute-start.12) | collective-permute-done | bytes 393248 | tf_op jit(solution)/shard_map/ppermute | solution.py:226
  53.9 0.0 collective-permute-done.11.refs_6_
  53.9 0.4 collective-permute-done.10.refs_5_
  54.3 0.0 collective-permute-done.9.refs_3_
  54.3 2.9 %collective-permute-start.14 = (bf16[512,512]{1,0:T(8,128)(2,1)S(1)}, bf16[512,512]{1,0:T(8,128)(2,1)S(1)}, u32[]{:S(2)}, u32[]{:S(2)}) collective-permute-start(bf16[512,512]{1,0:T(8,128)(2,1)S(1)} %collective-permute-done.10.refs_5_), channel_id=1, source_target_pairs={{0,4},{4,8},{8,12},{12,16},{16,20},{20,24},{24,28},{28,0},{1,5},{5... | collective-permute-start | bytes 1572872 | tf_op jit(solution)/shard_map/ppermute | solution.py:226
  57.2 0.8 collective-permute-start.15
  58.0 3.4 %collective-permute-start.17 = (bf16[192,512]{1,0:T(8,128)(2,1)S(1)}, bf16[192,512]{1,0:T(8,128)(2,1)S(1)}, u32[]{:S(2)}, u32[]{:S(2)}) collective-permute-start(bf16[192,512]{1,0:T(8,128)(2,1)S(1)} %slice.7), channel_id=1, source_target_pairs={{0,3},{1,0},{2,1},{3,2},{4,7},{5,4},{6,5},{7,6},{8,11},{9,8},{10,9... | collective-permute-start | bytes 589832 | tf_op jit(solution)/shard_map/ppermute | solution.py:226
  61.3 0.0 collective-permute-start.16
  61.3 0.0 copy-done.6
  61.3 0.0 copy-done.11
  61.4 0.0 copy-done.10
  61.4 0.0 copy-done.8
  61.4 0.0 copy-done.9
  61.4 0.0 copy-done.12
  61.4 0.0 copy-done.13
  61.4 0.0 copy-done.7
  61.4 0.0 copy-done.3
  61.4 0.0 copy-done.5
  61.4 6.1 %product_first.1.refs_8_ = f32[512,1024]{1,0:T(8,128)S(1)} custom-call(s32[32,64]{1,0:T(8,128)S(1)} %copy-done.3, s32[32,128]{1,0:T(8,128)S(1)} %bitcast.8, bf16[4,512,256]{2,1,0:T(8,128)(2,1)} %copy-done.6, bf16[4,512,256]{2,1,0:T(8,128)(2,1)} %copy-done.7, bf16[512,512]{1,0:T(8,128)(2,1)} %copy-done.11, bf16[512,512]{1,0:T(8,128)(2,1)} %copy-done.13, ...), custom_call_target="tpu_custom_call" | custom-call | flops 2818572288 | bytes 4194304 | tf_op jit(solution)/shard_map/product_first/pallas_call | solution.py:199
  67.5 0.0 collective-permute-done.17.refs_7_
  67.6 0.7 collective-permute-done.16.refs_6_
  68.2 0.9 collective-permute-done.14.refs_4_
  69.1 0.7 collective-permute-done.15.refs_5_
  69.8 5.2 %product_last.1 = (f32[512,1024]{1,0:T(8,128)S(1)}, f32[1,1024]{1,0:T(1,128)S(1)}) custom-call(s32[32,64]{1,0:T(8,128)S(1)} %copy-done.3, s32[32,128]{1,0:T(8,128)S(1)} %bitcast.9, bf16[4,512,256]{2,1,0:T(8,128)(2,1)} %copy-done.6, bf16[4,512,256]{2,1,0:T(8,128)(2,1)} %copy-done.7, ...), custom_call_target="tpu_custom_call", output_to_operand_aliasing={{0}: (8, {})} | custom-call | flops 1476395008 | bytes 4194304 | tf_op jit(solution)/shard_map/product_last/pallas_call | solution.py:199
  75.0 0.1 broadcast_in_dim.2
  75.1 17.4 %all_to_all.6 = f32[32,1,1024]{2,1,0:T(1,128)S(1)} all-to-all(f32[32,1,1024]{2,1,0:T(1,128)S(1)} %broadcast_in_dim.2), channel_id=1, replica_groups=mesh['y'=4,'core'=2,'z'=8,'x'=4] {'z','x'}, dimensions={0} | all-to-all | bytes 262144 | tf_op jit(solution)/shard_map/all_to_all | solution.py:263
  92.5 0.1 reduce_sum.9
  92.6 1.6 %broadcast_divide_fusion = f32[512,1024]{1,0:T(8,128)} fusion(f32[512,1024]{1,0:T(8,128)S(1)} %get-tuple-element.51, f32[1024]{0:T(1024)S(1)} %broadcast_multiply_fusion), kind=kLoop, calls=%fused_computation.1 | loop fusion | flops 524288 | bytes 4198400 | tf_op jit(solution)/shard_map/div | solution.py:267
  (19 shorter events, 0.1 us)
Async XLA Ops:
  0.0 0.9 %copy-start.1 = (bf16[128,1024]{1,0:T(8,128)(2,1)S(1)}, bf16[128,1024]{1,0:T(8,128)(2,1)}, u32[]{:S(2)}) copy-start(bf16[128,1024]{1,0:T(8,128)(2,1)} %right.1) | copy-start | bytes 786436
  1.0 0.7 copy-start.2
  2.6 14.7 %collective-permute-start.2 = (bf16[128,512]{1,0:T(8,128)(2,1)S(1)}, bf16[128,512]{1,0:T(8,128)(2,1)S(1)}, u32[]{:S(2)}, u32[]{:S(2)}) collective-permute-start(bf16[128,512]{1,0:T(8,128)(2,1)S(1)} %pack_right.1), channel_id=1, source_target_pairs={{0,2},{1,3},{2,0},{3,1},{4,6},{5,7},{6,4},{7,5},{8,10},{9,11},{10,... | collective-permute-start | bytes 393224 | tf_op jit(solution)/shard_map/ppermute | solution.py:226
  5.7 11.6 %collective-permute-start.1 = (bf16[128,512]{1,0:T(8,128)(2,1)S(1)}, bf16[128,512]{1,0:T(8,128)(2,1)S(1)}, u32[]{:S(2)}, u32[]{:S(2)}) collective-permute-start(bf16[128,512]{1,0:T(8,128)(2,1)S(1)} %pack_right.1), channel_id=1, source_target_pairs={{0,3},{1,0},{2,1},{3,2},{4,7},{5,4},{6,5},{7,6},{8,11},{9,8},{10,9... | collective-permute-start | bytes 393224 | tf_op jit(solution)/shard_map/ppermute | solution.py:226
  6.9 10.4 %collective-permute-start = (bf16[128,512]{1,0:T(8,128)(2,1)S(1)}, bf16[128,512]{1,0:T(8,128)(2,1)S(1)}, u32[]{:S(2)}, u32[]{:S(2)}) collective-permute-start(bf16[128,512]{1,0:T(8,128)(2,1)S(1)} %pack_right.1), channel_id=1, source_target_pairs={{0,1},{1,2},{2,3},{3,0},{4,5},{5,6},{6,7},{7,4},{8,9},{9,10},{10,1... | collective-permute-start | bytes 393224 | tf_op jit(solution)/shard_map/ppermute | solution.py:226
  7.7 14.4 %collective-permute-start.4 = (bf16[128,512]{1,0:T(8,128)(2,1)S(1)}, bf16[128,512]{1,0:T(8,128)(2,1)S(1)}, u32[]{:S(2)}, u32[]{:S(2)}) collective-permute-start(bf16[128,512]{1,0:T(8,128)(2,1)S(1)} %pack_right.1), channel_id=1, source_target_pairs={{0,20},{4,24},{8,28},{12,0},{16,4},{20,8},{24,12},{28,16},{1,21},{... | collective-permute-start | bytes 393224 | tf_op jit(solution)/shard_map/ppermute | solution.py:226
  14.5 1.0 %copy-start = (bf16[512,512]{1,0:T(8,128)(2,1)S(1)}, bf16[512,512]{1,0:T(8,128)(2,1)}, u32[]{:S(2)}) copy-start(bf16[512,512]{1,0:T(8,128)(2,1)} %left.1) | copy-start | bytes 1572868
  15.5 0.7 copy-start.4
  17.3 18.6 %collective-permute-start.8 = (bf16[512,256]{1,0:T(8,128)(2,1)S(1)}, bf16[512,256]{1,0:T(8,128)(2,1)S(1)}, u32[]{:S(2)}, u32[]{:S(2)}) collective-permute-start(bf16[512,256]{1,0:T(8,128)(2,1)S(1)} %pack_left.1), channel_id=1, source_target_pairs={{0,128},{64,192},{128,0},{192,64},{1,129},{65,193},{129,1},{193,65... | collective-permute-start | bytes 786440 | tf_op jit(solution)/shard_map/ppermute | solution.py:226
  18.6 17.3 %collective-permute-start.7 = (bf16[512,256]{1,0:T(8,128)(2,1)S(1)}, bf16[512,256]{1,0:T(8,128)(2,1)S(1)}, u32[]{:S(2)}, u32[]{:S(2)}) collective-permute-start(bf16[512,256]{1,0:T(8,128)(2,1)S(1)} %pack_left.1), channel_id=1, source_target_pairs={{0,192},{64,0},{128,64},{192,128},{1,193},{65,1},{129,65},{193,129... | collective-permute-start | bytes 786440 | tf_op jit(solution)/shard_map/ppermute | solution.py:226
  18.6 17.3 %collective-permute-start.6 = (bf16[512,256]{1,0:T(8,128)(2,1)S(1)}, bf16[512,256]{1,0:T(8,128)(2,1)S(1)}, u32[]{:S(2)}, u32[]{:S(2)}) collective-permute-start(bf16[512,256]{1,0:T(8,128)(2,1)S(1)} %pack_left.1), channel_id=1, source_target_pairs={{0,64},{64,128},{128,192},{192,0},{1,65},{65,129},{129,193},{193,1... | collective-permute-start | bytes 786440 | tf_op jit(solution)/shard_map/ppermute | solution.py:226
  21.8 14.1 %collective-permute-start.3 = (bf16[128,512]{1,0:T(8,128)(2,1)S(1)}, bf16[128,512]{1,0:T(8,128)(2,1)S(1)}, u32[]{:S(2)}, u32[]{:S(2)}) collective-permute-start(bf16[128,512]{1,0:T(8,128)(2,1)S(1)} %pack_right.1), channel_id=1, source_target_pairs={{0,12},{4,16},{8,20},{12,24},{16,28},{20,0},{24,4},{28,8},{1,13},{... | collective-permute-start | bytes 393224 | tf_op jit(solution)/shard_map/ppermute | solution.py:226
  22.1 13.8 %collective-permute-start.5 = (bf16[128,512]{1,0:T(8,128)(2,1)S(1)}, bf16[128,512]{1,0:T(8,128)(2,1)S(1)}, u32[]{:S(2)}, u32[]{:S(2)}) collective-permute-start(bf16[128,512]{1,0:T(8,128)(2,1)S(1)} %pack_right.1), channel_id=1, source_target_pairs={{0,16},{4,20},{8,24},{12,28},{16,0},{20,4},{24,8},{28,12},{1,17},{... | collective-permute-start | bytes 393224 | tf_op jit(solution)/shard_map/ppermute | solution.py:226
  35.9 25.5 %copy-start.3 = (s32[32,64]{1,0:T(8,128)S(1)}, s32[32,64]{1,0:T(8,128)}, u32[]{:S(2)}) copy-start(s32[32,64]{1,0:T(8,128)} %refs_0_.3) | copy-start | bytes 24580
  35.9 25.5 %copy-start.5 = (s32[128,32]{0,1:T(8,128)S(1)}, s32[128,32]{0,1:T(8,128)}, u32[]{:S(2)}) copy-start(s32[128,32]{0,1:T(8,128)} %param.5) | copy-start | bytes 49156
  36.1 25.2 %copy-start.6 = (bf16[4,512,256]{2,1,0:T(8,128)(2,1)}, bf16[4,512,256]{2,1,0:T(8,128)(2,1)S(1)}, u32[]{:S(2)}) copy-start(bf16[4,512,256]{2,1,0:T(8,128)(2,1)S(1)} %pad_maximum_fusion.refs_2_) | copy-start | bytes 3145732
  36.1 18.2 %collective-permute-start.9 = (bf16[4,512,256]{2,1,0:T(8,128)(2,1)S(1)}, bf16[4,512,256]{2,1,0:T(8,128)(2,1)S(1)}, u32[]{:S(2)}, u32[]{:S(2)}) collective-permute-start(bf16[4,512,256]{2,1,0:T(8,128)(2,1)S(1)} %pad_maximum_fusion.refs_2_), channel_id=1, source_target_pairs={{0,32},{32,0},{1,33},{33,1},{2,34},{34,2},{3,35},{35,3},{4,36},{36... | collective-permute-start | bytes 3145736 | tf_op jit(solution)/shard_map/ppermute | solution.py:226
  36.3 25.1 %copy-start.11 = (bf16[512,512]{1,0:T(8,128)(2,1)}, bf16[512,512]{1,0:T(8,128)(2,1)S(1)}, u32[]{:S(2)}) copy-start(bf16[512,512]{1,0:T(8,128)(2,1)S(1)} %constant_dynamic-update-slice_fusion.refs_4_) | copy-start | bytes 1572868
  36.3 17.6 %collective-permute-start.11 = (bf16[512,512]{1,0:T(8,128)(2,1)S(1)}, bf16[512,512]{1,0:T(8,128)(2,1)S(1)}, u32[]{:S(2)}, u32[]{:S(2)}) collective-permute-start(bf16[512,512]{1,0:T(8,128)(2,1)S(1)} %constant_dynamic-update-slice_fusion.refs_4_), channel_id=1, source_target_pairs={{0,28},{4,0},{8,4},{12,8},{16,12},{20,16},{24,20},{28,24},{1,29},{... | collective-permute-start | bytes 1572872 | tf_op jit(solution)/shard_map/ppermute | solution.py:226
  37.0 17.2 %collective-permute-start.10 = (bf16[512,512]{1,0:T(8,128)(2,1)S(1)}, bf16[512,512]{1,0:T(8,128)(2,1)S(1)}, u32[]{:S(2)}, u32[]{:S(2)}) collective-permute-start(bf16[512,512]{1,0:T(8,128)(2,1)S(1)} %constant_dynamic-update-slice_fusion.refs_4_), channel_id=1, source_target_pairs={{0,4},{4,8},{8,12},{12,16},{16,20},{20,24},{24,28},{28,0},{1,5},{5... | collective-permute-start | bytes 1572872 | tf_op jit(solution)/shard_map/ppermute | solution.py:226
  39.1 22.2 %copy-start.10 = (bf16[384,512]{1,0:T(8,128)(2,1)}, bf16[384,512]{1,0:T(8,128)(2,1)S(1)}, u32[]{:S(2)}) copy-start(bf16[384,512]{1,0:T(8,128)(2,1)S(1)} %constant_dynamic-update-slice_fusion.4.refs_7_) | copy-start | bytes 1179652
  39.2 11.3 %collective-permute-start.13 = (bf16[384,512]{1,0:T(8,128)(2,1)S(1)}, bf16[384,512]{1,0:T(8,128)(2,1)S(1)}, u32[]{:S(2)}, u32[]{:S(2)}) collective-permute-start(bf16[384,512]{1,0:T(8,128)(2,1)S(1)} %constant_dynamic-update-slice_fusion.4.refs_7_), channel_id=1, source_target_pairs={{0,3},{1,0},{2,1},{3,2},{4,7},{5,4},{6,5},{7,6},{8,11},{9,8},{10,9... | collective-permute-start | bytes 1179656 | tf_op jit(solution)/shard_map/ppermute | solution.py:226
  41.7 12.2 %collective-permute-start.12 = (bf16[384,512]{1,0:T(8,128)(2,1)S(1)}, bf16[384,512]{1,0:T(8,128)(2,1)S(1)}, u32[]{:S(2)}, u32[]{:S(2)}) collective-permute-start(bf16[384,512]{1,0:T(8,128)(2,1)S(1)} %constant_dynamic-update-slice_fusion.4.refs_7_), channel_id=1, source_target_pairs={{0,1},{1,2},{2,3},{3,0},{4,5},{5,6},{6,7},{7,4},{8,9},{9,10},{10,1... | collective-permute-start | bytes 1179656 | tf_op jit(solution)/shard_map/ppermute | solution.py:226
  50.5 10.9 %copy-start.8 = (bf16[384,512]{1,0:T(8,128)(2,1)}, bf16[384,512]{1,0:T(8,128)(2,1)S(1)}, u32[]{:S(2)}) copy-start(bf16[384,512]{1,0:T(8,128)(2,1)S(1)} %collective-permute-done.13.refs_9_) | copy-start | bytes 1179652
  53.9 7.5 %copy-start.9 = (bf16[384,512]{1,0:T(8,128)(2,1)}, bf16[384,512]{1,0:T(8,128)(2,1)S(1)}, u32[]{:S(2)}) copy-start(bf16[384,512]{1,0:T(8,128)(2,1)S(1)} %collective-permute-done.12.refs_8_) | copy-start | bytes 1179652
  53.9 7.5 %copy-start.12 = (bf16[512,512]{1,0:T(8,128)(2,1)}, bf16[512,512]{1,0:T(8,128)(2,1)S(1)}, u32[]{:S(2)}) copy-start(bf16[512,512]{1,0:T(8,128)(2,1)S(1)} %collective-permute-done.11.refs_6_) | copy-start | bytes 1572868
  54.3 7.1 %copy-start.13 = (bf16[512,512]{1,0:T(8,128)(2,1)}, bf16[512,512]{1,0:T(8,128)(2,1)S(1)}, u32[]{:S(2)}) copy-start(bf16[512,512]{1,0:T(8,128)(2,1)S(1)} %collective-permute-done.10.refs_5_) | copy-start | bytes 1572868
  54.3 7.1 %copy-start.7 = (bf16[4,512,256]{2,1,0:T(8,128)(2,1)}, bf16[4,512,256]{2,1,0:T(8,128)(2,1)S(1)}, u32[]{:S(2)}) copy-start(bf16[4,512,256]{2,1,0:T(8,128)(2,1)S(1)} %collective-permute-done.9.refs_3_) | copy-start | bytes 3145732
  54.3 14.8 %collective-permute-start.14 = (bf16[512,512]{1,0:T(8,128)(2,1)S(1)}, bf16[512,512]{1,0:T(8,128)(2,1)S(1)}, u32[]{:S(2)}, u32[]{:S(2)}) collective-permute-start(bf16[512,512]{1,0:T(8,128)(2,1)S(1)} %collective-permute-done.10.refs_5_), channel_id=1, source_target_pairs={{0,4},{4,8},{8,12},{12,16},{16,20},{20,24},{24,28},{28,0},{1,5},{5... | collective-permute-start | bytes 1572872 | tf_op jit(solution)/shard_map/ppermute | solution.py:226
  57.2 12.6 %collective-permute-start.15 = (bf16[512,512]{1,0:T(8,128)(2,1)S(1)}, bf16[512,512]{1,0:T(8,128)(2,1)S(1)}, u32[]{:S(2)}, u32[]{:S(2)}) collective-permute-start(bf16[512,512]{1,0:T(8,128)(2,1)S(1)} %collective-permute-done.11.refs_6_), channel_id=1, source_target_pairs={{0,28},{4,0},{8,4},{12,8},{16,12},{20,16},{24,20},{28,24},{1,29},{... | collective-permute-start | bytes 1572872 | tf_op jit(solution)/shard_map/ppermute | solution.py:226
  58.0 9.6 %collective-permute-start.17 = (bf16[192,512]{1,0:T(8,128)(2,1)S(1)}, bf16[192,512]{1,0:T(8,128)(2,1)S(1)}, u32[]{:S(2)}, u32[]{:S(2)}) collective-permute-start(bf16[192,512]{1,0:T(8,128)(2,1)S(1)} %slice.7), channel_id=1, source_target_pairs={{0,3},{1,0},{2,1},{3,2},{4,7},{5,4},{6,5},{7,6},{8,11},{9,8},{10,9... | collective-permute-start | bytes 589832 | tf_op jit(solution)/shard_map/ppermute | solution.py:226
  61.3 6.9 %collective-permute-start.16 = (bf16[192,512]{1,0:T(8,128)(2,1)S(1)}, bf16[192,512]{1,0:T(8,128)(2,1)S(1)}, u32[]{:S(2)}, u32[]{:S(2)}) collective-permute-start(bf16[192,512]{1,0:T(8,128)(2,1)S(1)} %slice.6), channel_id=1, source_target_pairs={{0,1},{1,2},{2,3},{3,0},{4,5},{5,6},{6,7},{7,4},{8,9},{9,10},{10,1... | collective-permute-start | bytes 589832 | tf_op jit(solution)/shard_map/ppermute | solution.py:226

commit v6 on v5

--- a/solution.py
+++ b/solution.py
@@ -12,21 +12,12 @@
 SLOTS = 4
 LEFT_SLOTS = 2
 SHIFTS = (0, 3, 1, 2)
-PLACES = (0, 2, 3, 1)
-FAR = (-3, 3, 4)
 KERNEL_VMEM = 24 * 1024 * 1024
 ROW, COL = ("y", "core"), ("z", "x")
 
 
 def lanes(start, blocks=1):
     return pl.ds(pl.multiple_of(start * BLOCK, BLOCK), blocks * BLOCK)
-
-
-def place_of(shift):
-    place = jnp.int32(PLACES[3])
-    for s in range(3):
-        place = jnp.where(shift == s, PLACES[s], place)
-    return place
 
 
 def row_index():
@@ -85,7 +76,9 @@
 
 def product_kernel(blocks, copies, first, last, *refs):
     refs = list(refs)
-    right_hbm, left_hbm, mine, other = [refs.pop(0) for _ in range(4)]
+    right_hbm, left_hbm, near_left, sent_left, swapped_left, far_left = [
+        refs.pop(0) for _ in range(6)
+    ]
     pieces = [refs.pop(0) for _ in range(1 + max(copy[0] for copy in copies))]
     total = None if first else refs.pop(0)
     out = refs.pop(0)
@@ -109,11 +102,18 @@
         copy.start()
     waits = []
     for n, group in enumerate(groups):
-        there = place_of(lax.rem(lax.div(group, cores) - y + y_size, y_size))
-        same = lax.rem(group, cores) == core
-        for source, wanted in ((mine, same), (other, jnp.logical_not(same))):
+        away = lax.rem(lax.div(group, cores) - y + y_size, y_size)
+        part = jnp.where(lax.rem(group, cores) == core, 0, 1)
+        came = away == jnp.where(core == 0, y_size - 1, 1)
+        beside = away == jnp.where(core == 0, 1, y_size - 1)
+        for source, index, wanted in (
+            (near_left, part, away == 0),
+            (sent_left, part, came),
+            (swapped_left, 1 - part, beside),
+            (far_left, part, away == 2),
+        ):
             copy = pltpu.make_async_copy(
-                source.at[there], packed_left.at[n, :, : LEFT_SLOTS * BLOCK], sem.at[n]
+                source.at[index], packed_left.at[n, :, : LEFT_SLOTS * BLOCK], sem.at[n]
             )
             pl.when(wanted)(copy.start)
         waits.append(copy)
@@ -217,7 +217,7 @@
         cost_estimate=pl.CostEstimate(
             flops=2 * rows * inner * cols, bytes_accessed=4 * 1024 * 1024, transcendentals=0
         ),
-        name="product_last" if last else "product_first",
+        name="product_last" if last else "product_first" if total is None else "product_next",
     )(*operands)
 
 
@@ -226,45 +226,57 @@
     return lax.ppermute(value, axis, [(i, (i + step) % size) for i in range(size)])
 
 
+def around(value):
+    size, cores = lax.axis_size("y"), lax.axis_size("core")
+    pairs = []
+    for y in range(size):
+        for core in range(cores):
+            to = (y + 1) % size if core == 0 else (y - 1) % size
+            pairs.append((y * cores + core, to * cores + core))
+    return lax.ppermute(value, ("y", "core"), pairs)
+
+
 def shards(left_values, left_pattern, right_values, right_pattern):
     left_pattern = left_pattern.T
     packed_right = pack(pack_right_kernel, "pack_right", right_pattern, right_values, SLOTS)
-    far = [moved(packed_right, "z", -shift) for shift in FAR[:2]]
     near = [packed_right] + [moved(packed_right, "x", -shift) for shift in SHIFTS[1:]]
+    left_values, _ = lax.optimization_barrier((left_values, packed_right))
     packed_left = pack(pack_left_kernel, "pack_left", left_pattern, left_values, LEFT_SLOTS)
-    near, packed_left = lax.optimization_barrier((near, packed_left))
-    far.append(moved(near[0], "z", -FAR[2]))
-    columns = [packed_left] + [moved(packed_left, "y", -shift) for shift in SHIFTS[1:]]
-    near, far, columns = lax.optimization_barrier((near, far, columns))
-    own, far, mine = jnp.concatenate(near, 0), jnp.concatenate(far, 0), jnp.stack(columns)
-    up, down = moved(own, "z", 1), moved(own, "z", -1)
-    far_3, far_1 = moved(far, "x", 1), moved(far, "x", -1)
-    left = (mine, moved(mine, "core", 1))
-    left, up, down, far_3, far_1 = lax.optimization_barrier((left, up, down, far_3, far_1))
-    further_up, further_down = moved(up, "z", 1), moved(down, "z", -1)
-    half = far.shape[0] // 2
-    far_2 = (moved(far_3[:half], "x", 1), moved(far_1[half:], "x", -1))
-    whole = own.shape[0]
-    blocks, copies = [], []
-    for piece, z_shift in enumerate((0, -1, 1)):
-        blocks += [(z_shift, x_shift) for x_shift in SHIFTS]
-        copies.append((piece, 0, whole, piece * whole))
-    for n, x_shift in enumerate((0, 3, 1)):
-        copies.append((3 + n, 0, 2 * half, len(blocks) * BLOCK))
-        blocks += [(z_shift, x_shift) for z_shift in FAR]
-    pieces = [own, up, down, far, far_3, far_1]
-    (total,) = product(blocks, copies, right_pattern, left_pattern, left, pieces, None, False)
-    blocks = [(z_shift, x_shift) for z_shift in (-2, 2) for x_shift in SHIFTS]
-    blocks += [(z_shift, 2) for z_shift in FAR]
-    copies = [(0, 0, whole, 0), (1, 0, whole, whole), (2, 0, half, 2 * whole), (3, 0, half, 2 * whole + half)]
-    pieces = [further_up, further_down, *far_2]
-    total, sums = product(blocks, copies, right_pattern, left_pattern, left, pieces, total, True)
+    other_left = moved(packed_left, "core", 1)
+    near, packed_left, other_left = lax.optimization_barrier((near, packed_left, other_left))
+    own = [jnp.concatenate(near[:2], 0), jnp.concatenate(near[2:], 0)]
+    half = own[0].shape[0]
+    came = {0: own}
+
+    def ring(step):
+        came[-step] = [moved(piece, "z", 1) for piece in came[1 - step]]
+        came[step] = [moved(piece, "z", -1) for piece in came[step - 1]]
+
+    def tied(values, step):
+        values, came[-step][0] = lax.optimization_barrier((values, came[-step][0]))
+        return values
+
+    def add(shifts, total, last=False):
+        blocks = [(shift, x_shift) for shift in shifts for x_shift in SHIFTS]
+        pieces = [piece for shift in shifts for piece in came[shift]]
+        copies = [(n, 0, half, n * half) for n in range(len(pieces))]
+        return product(blocks, copies, right_pattern, left_pattern, left, pieces, total, last)
+
+    ring(1)
+    near_left = jnp.stack([packed_left, other_left])
+    sent_left = tied(around(near_left), 1)
+    ring(2)
+    left = tied([near_left, sent_left, moved(sent_left, "core", 1), around(sent_left)], 2)
+    ring(3)
+    total = tied(add((0, -1, 1), None)[0], 3)
+    came[4] = [moved(came[-3][0], "z", 1), moved(came[3][1], "z", -1)]
+    (total,) = add((-2, 2, -3, 3), total)
+    total, sums = add((4,), total, True)
     count = lax.axis_size("z") * lax.axis_size("x")
     spread = lax.all_to_all(
         jnp.broadcast_to(sums, (count, sums.shape[1])), COL, 0, 0, tiled=True
     )
-    column_mean = jnp.sum(spread, axis=0) / (total.shape[0] * count)
-    return total / column_mean[None, :]
+    return total * ((total.shape[0] * count) / jnp.sum(spread, axis=0))[None, :]
 
 
 def solution(mesh):

time: 94.5 us -> 98 us (1.037)
  waiting for transfers between devices: 24.1 us -> 30.4 us
  starting transfers between devices: 33.7 us -> 30.5 us
  blocking collectives: 17.4 us -> 15.9 us
  local copies, waits for them, and re-layouts: 3.64 us -> 4.96 us
    ppermute x18 -> x19, waiting for transfers between devices: 24.1 us -> 30.4 us  [moved(): lax.ppermute(value, axis, [(i, (i + step) % size) for i in range(size)])]
    ppermute x18 -> x19, starting transfers between devices: 33.7 us -> 27.4 us  [moved(): lax.ppermute(value, axis, [(i, (i + step) % size) for i in range(size)])]
    ppermute x0 -> x2, starting transfers between devices: none -> 3.04 us  [around(): return lax.ppermute(value, ('y', 'core'), pairs)]
    div x2 -> x1, other arithmetic: 1.58 us -> 0.01 us  [shards(): return total * (total.shape[0] * count / jnp.sum(spread, axis=0))[None, :]]
    mul x0 -> x1, other arithmetic: none -> 1.55 us  [shards(): return total * (total.shape[0] * count / jnp.sum(spread, axis=0))[None, :]]
    all_to_all x1, blocking collectives: 17.4 us -> 15.9 us  [shards(): lax.all_to_all(jnp.broadcast_to(sums, (count, sums.shape[1])), COL, 0, 0,...]
    unnamed x33 -> x50, local copies, waits for them, and re-layouts: 3.52 us -> 4.87 us
    pallas_call x2 -> x3, Pallas kernels: 11.3 us -> 11.8 us  [product(): pl.pallas_call(functools.partial(product_kernel, blocks, copies, total is...]
  transfers between devices with their start and end apart: 18 -> 21, of which waited for: 7 -> 9; matrix products, arithmetic and copies ran while one was open for 0% -> 0% of each run, Pallas kernels for 8% -> 9%
where the time goes in v6:
time: 98 us; the launch traced here: 97.5 us
  starting transfers between devices  30.5 us (31%)
  waiting for transfers between devices  30.4 us (31%)
  blocking collectives  15.9 us (16%)
  Pallas kernels  13.7 us (14%)
  local copies, waits for them, and re-layouts  4.96 us (5%)
  other arithmetic  1.7 us (2%)
    ppermute x19, waiting for transfers between devices, moved(): lax.ppermute(value, axis, [(i, (i + step) % size) for i in range(size)])  30.4 us
    ppermute x19, starting transfers between devices, moved(): lax.ppermute(value, axis, [(i, (i + step) % size) for i in range(size)])  27.4 us
    all_to_all x1, blocking collectives, shards(): lax.all_to_all(jnp.broadcast_to(sums, (count, sums.shape[1])), COL, 0, 0,...  15.9 us
    pallas_call x3, Pallas kernels, product(): pl.pallas_call(functools.partial(product_kernel, blocks, copies, total is...  11.8 us
    unnamed x50, local copies, waits for them, and re-layouts  4.87 us
    ppermute x2, starting transfers between devices, around(): return lax.ppermute(value, ('y', 'core'), pairs)  3.04 us
  transfers between devices with their start and end apart: 21, of which 9 were waited for; matrix products, arithmetic and copies ran while one was open for 0% of the time, Pallas kernels for 9%

profile of v6, /device:TPU:24, one launch (start us, length us, event | category | flops | bytes accessed | tf_op | source)
XLA Modules:
  0.0 97.5 jit_solution(101421262720242390)
XLA Ops:
  0.0 0.9 copy-done.1
  1.0 0.7 copy-done.2
  1.7 0.9 pack_right.1
  2.6 0.0 copy-start
  2.6 1.0 %copy-done = bf16[512,512]{1,0:T(8,128)(2,1)S(1)} copy-done((bf16[512,512]{1,0:T(8,128)(2,1)S(1)}, bf16[512,512]{1,0:T(8,128)(2,1)}, u32[]{:S(2)}) %copy-start) | copy-done | bytes 524312
  3.6 0.7 copy-done.4
  4.4 1.0 %pack_left.1 = bf16[512,256]{1,0:T(8,128)(2,1)S(1)} custom-call(s32[32,128]{1,0:T(8,128)S(1)} %bitcast.5, bf16[512,512]{1,0:T(8,128)(2,1)S(1)} %copy-done), custom_call_target="tpu_custom_call" | custom-call | tf_op jit(solution)/shard_map/pack_left/pallas_call | solution.py:64
  5.4 0.1 collective-permute-start.3
  5.5 1.6 %collective-permute-start = (bf16[128,512]{1,0:T(8,128)(2,1)S(1)}, bf16[128,512]{1,0:T(8,128)(2,1)S(1)}, u32[]{:S(2)}, u32[]{:S(2)}) collective-permute-start(bf16[128,512]{1,0:T(8,128)(2,1)S(1)} %pack_right.1), channel_id=1, source_target_pairs={{0,1},{1,2},{2,3},{3,0},{4,5},{5,6},{6,7},{7,4},{8,9},{9,10},{10,1... | collective-permute-start | bytes 393224 | tf_op jit(solution)/shard_map/ppermute | solution.py:226
  7.0 1.7 %collective-permute-start.1 = (bf16[128,512]{1,0:T(8,128)(2,1)S(1)}, bf16[128,512]{1,0:T(8,128)(2,1)S(1)}, u32[]{:S(2)}, u32[]{:S(2)}) collective-permute-start(bf16[128,512]{1,0:T(8,128)(2,1)S(1)} %pack_right.1), channel_id=1, source_target_pairs={{0,3},{1,0},{2,1},{3,2},{4,7},{5,4},{6,5},{7,6},{8,11},{9,8},{10,9... | collective-permute-start | bytes 393224 | tf_op jit(solution)/shard_map/ppermute | solution.py:226
  8.8 1.8 %collective-permute-start.2 = (bf16[128,512]{1,0:T(8,128)(2,1)S(1)}, bf16[128,512]{1,0:T(8,128)(2,1)S(1)}, u32[]{:S(2)}, u32[]{:S(2)}) collective-permute-start(bf16[128,512]{1,0:T(8,128)(2,1)S(1)} %pack_right.1), channel_id=1, source_target_pairs={{0,2},{1,3},{2,0},{3,1},{4,6},{5,7},{6,4},{7,5},{8,10},{9,11},{10,... | collective-permute-start | bytes 393224 | tf_op jit(solution)/shard_map/ppermute | solution.py:226
  10.6 2.0 %collective-permute-done = bf16[128,512]{1,0:T(8,128)(2,1)S(1)} collective-permute-done((bf16[128,512]{1,0:T(8,128)(2,1)S(1)}, bf16[128,512]{1,0:T(8,128)(2,1)S(1)}, u32[]{:S(2)}, u32[]{:S(2)}) %collective-permute-start) | collective-permute-done | bytes 131104 | tf_op jit(solution)/shard_map/ppermute | solution.py:226
  12.6 2.1 %collective-permute-done.1 = bf16[128,512]{1,0:T(8,128)(2,1)S(1)} collective-permute-done((bf16[128,512]{1,0:T(8,128)(2,1)S(1)}, bf16[128,512]{1,0:T(8,128)(2,1)S(1)}, u32[]{:S(2)}, u32[]{:S(2)}) %collective-permute-start.1) | collective-permute-done | bytes 131104 | tf_op jit(solution)/shard_map/ppermute | solution.py:226
  14.7 1.7 %collective-permute-done.2 = bf16[128,512]{1,0:T(8,128)(2,1)S(1)} collective-permute-done((bf16[128,512]{1,0:T(8,128)(2,1)S(1)}, bf16[128,512]{1,0:T(8,128)(2,1)S(1)}, u32[]{:S(2)}, u32[]{:S(2)}) %collective-permute-start.2) | collective-permute-done | bytes 131104 | tf_op jit(solution)/shard_map/ppermute | solution.py:226
  16.4 0.0 collective-permute-done.3
  16.4 0.1 pad_maximum_fusion.refs_2_
  16.4 0.0 copy-start.6
  16.5 1.2 %collective-permute-start.4 = (bf16[2,512,256]{2,1,0:T(8,128)(2,1)S(1)}, bf16[2,512,256]{2,1,0:T(8,128)(2,1)S(1)}, u32[]{:S(2)}, u32[]{:S(2)}) collective-permute-start(bf16[2,512,256]{2,1,0:T(8,128)(2,1)S(1)} %pad_maximum_fusion.refs_2_), channel_id=1, source_target_pairs={{0,64},{32,224},{64,128},{96,32},{128,192},{160,96},{192,0},{224,1... | collective-permute-start | bytes 1572872 | tf_op jit(solution)/shard_map/ppermute | solution.py:236
  17.7 1.1 %collective-permute-start.5 = (bf16[256,512]{1,0:T(8,128)(2,1)S(1)}, bf16[256,512]{1,0:T(8,128)(2,1)S(1)}, u32[]{:S(2)}, u32[]{:S(2)}) collective-permute-start(bf16[256,512]{1,0:T(8,128)(2,1)S(1)} %constant_dynamic-update-slice_fusion.refs_6_), channel_id=1, source_target_pairs={{0,4},{4,8},{8,12},{12,16},{16,20},{20,24},{24,28},{28,0},{1,5},{5... | collective-permute-start | bytes 786440 | tf_op jit(solution)/shard_map/ppermute | solution.py:226
  18.8 4.0 %collective-permute-start.11 = (bf16[256,512]{1,0:T(8,128)(2,1)S(1)}, bf16[256,512]{1,0:T(8,128)(2,1)S(1)}, u32[]{:S(2)}, u32[]{:S(2)}) collective-permute-start(bf16[256,512]{1,0:T(8,128)(2,1)S(1)} %constant_dynamic-update-slice_fusion.2.refs_7_), channel_id=1, source_target_pairs={{0,28},{4,0},{8,4},{12,8},{16,12},{20,16},{24,20},{28,24},{1,29},{... | collective-permute-start | bytes 786440 | tf_op jit(solution)/shard_map/ppermute | solution.py:226
  22.9 0.0 collective-permute-start.9
  22.9 7.0 %collective-permute-done.5.refs_8_ = bf16[256,512]{1,0:T(8,128)(2,1)S(1)} collective-permute-done((bf16[256,512]{1,0:T(8,128)(2,1)S(1)}, bf16[256,512]{1,0:T(8,128)(2,1)S(1)}, u32[]{:S(2)}, u32[]{:S(2)}) %collective-permute-start.5) | collective-permute-done | bytes 262176 | tf_op jit(solution)/shard_map/ppermute | solution.py:226
  29.9 0.0 collective-permute-done.4.refs_3_
  29.9 0.1 collective-permute-start.6
  30.0 1.8 %collective-permute-start.7 = (bf16[2,512,256]{2,1,0:T(8,128)(2,1)S(1)}, bf16[2,512,256]{2,1,0:T(8,128)(2,1)S(1)}, u32[]{:S(2)}, u32[]{:S(2)}) collective-permute-start(bf16[2,512,256]{2,1,0:T(8,128)(2,1)S(1)} %collective-permute-done.4.refs_3_), channel_id=1, source_target_pairs={{0,64},{32,224},{64,128},{96,32},{128,192},{160,96},{192,0},{224,1... | collective-permute-start | bytes 1572872 | tf_op jit(solution)/shard_map/ppermute | solution.py:236
  31.8 1.9 %collective-permute-start.10 = (bf16[256,512]{1,0:T(8,128)(2,1)S(1)}, bf16[256,512]{1,0:T(8,128)(2,1)S(1)}, u32[]{:S(2)}, u32[]{:S(2)}) collective-permute-start(bf16[256,512]{1,0:T(8,128)(2,1)S(1)} %constant_dynamic-update-slice_fusion.refs_6_), channel_id=1, source_target_pairs={{0,28},{4,0},{8,4},{12,8},{16,12},{20,16},{24,20},{28,24},{1,29},{... | collective-permute-start | bytes 786440 | tf_op jit(solution)/shard_map/ppermute | solution.py:226
  33.7 0.0 collective-permute-done.11.refs_11_
  33.7 1.0 %collective-permute-start.14 = (bf16[256,512]{1,0:T(8,128)(2,1)S(1)}, bf16[256,512]{1,0:T(8,128)(2,1)S(1)}, u32[]{:S(2)}, u32[]{:S(2)}) collective-permute-start(bf16[256,512]{1,0:T(8,128)(2,1)S(1)} %collective-permute-done.11.refs_11_), channel_id=1, source_target_pairs={{0,28},{4,0},{8,4},{12,8},{16,12},{20,16},{24,20},{28,24},{1,29},{... | collective-permute-start | bytes 786440 | tf_op jit(solution)/shard_map/ppermute | solution.py:226
  34.7 0.0 collective-permute-done.9.refs_9_
  34.7 1.0 %collective-permute-start.8 = (bf16[256,512]{1,0:T(8,128)(2,1)S(1)}, bf16[256,512]{1,0:T(8,128)(2,1)S(1)}, u32[]{:S(2)}, u32[]{:S(2)}) collective-permute-start(bf16[256,512]{1,0:T(8,128)(2,1)S(1)} %collective-permute-done.5.refs_8_), channel_id=1, source_target_pairs={{0,4},{4,8},{8,12},{12,16},{16,20},{20,24},{24,28},{28,0},{1,5},{5... | collective-permute-start | bytes 786440 | tf_op jit(solution)/shard_map/ppermute | solution.py:226
  35.7 5.2 %collective-permute-done.10.refs_10_ = bf16[256,512]{1,0:T(8,128)(2,1)S(1)} collective-permute-done((bf16[256,512]{1,0:T(8,128)(2,1)S(1)}, bf16[256,512]{1,0:T(8,128)(2,1)S(1)}, u32[]{:S(2)}, u32[]{:S(2)}) %collective-permute-start.10) | collective-permute-done | bytes 262176 | tf_op jit(solution)/shard_map/ppermute | solution.py:226
  40.9 0.0 collective-permute-start.17
  40.9 5.0 %collective-permute-done.14.refs_9_ = bf16[256,512]{1,0:T(8,128)(2,1)S(1)} collective-permute-done((bf16[256,512]{1,0:T(8,128)(2,1)S(1)}, bf16[256,512]{1,0:T(8,128)(2,1)S(1)}, u32[]{:S(2)}, u32[]{:S(2)}) %collective-permute-start.14) | collective-permute-done | bytes 262176 | tf_op jit(solution)/shard_map/ppermute | solution.py:226
  45.9 3.2 %collective-permute-start.18 = (bf16[256,512]{1,0:T(8,128)(2,1)S(1)}, bf16[256,512]{1,0:T(8,128)(2,1)S(1)}, u32[]{:S(2)}, u32[]{:S(2)}) collective-permute-start(bf16[256,512]{1,0:T(8,128)(2,1)S(1)} %collective-permute-done.10.refs_10_), channel_id=1, source_target_pairs={{0,28},{4,0},{8,4},{12,8},{16,12},{20,16},{24,20},{28,24},{1,29},{... | collective-permute-start | bytes 786440 | tf_op jit(solution)/shard_map/ppermute | solution.py:226
  49.2 0.0 collective-permute-done.8.refs_6_
  49.2 0.1 collective-permute-start.15
  49.2 0.0 collective-permute-done.6.refs_4_
  49.3 0.0 collective-permute-done.7.refs_5_
  49.3 2.2 %collective-permute-start.12 = (bf16[256,512]{1,0:T(8,128)(2,1)S(1)}, bf16[256,512]{1,0:T(8,128)(2,1)S(1)}, u32[]{:S(2)}, u32[]{:S(2)}) collective-permute-start(bf16[256,512]{1,0:T(8,128)(2,1)S(1)} %collective-permute-done.8.refs_6_), channel_id=1, source_target_pairs={{0,4},{4,8},{8,12},{12,16},{16,20},{20,24},{24,28},{28,0},{1,5},{5... | collective-permute-start | bytes 786440 | tf_op jit(solution)/shard_map/ppermute | solution.py:226
  51.5 0.0 collective-permute-done.17.refs_7_
  51.5 0.1 collective-permute-start.19
  51.6 4.3 %collective-permute-done.18.refs_8_ = bf16[256,512]{1,0:T(8,128)(2,1)S(1)} collective-permute-done((bf16[256,512]{1,0:T(8,128)(2,1)S(1)}, bf16[256,512]{1,0:T(8,128)(2,1)S(1)}, u32[]{:S(2)}, u32[]{:S(2)}) %collective-permute-start.18) | collective-permute-done | bytes 262176 | tf_op jit(solution)/shard_map/ppermute | solution.py:226
  55.9 3.7 %collective-permute-start.20 = (bf16[256,512]{1,0:T(8,128)(2,1)S(1)}, bf16[256,512]{1,0:T(8,128)(2,1)S(1)}, u32[]{:S(2)}, u32[]{:S(2)}) collective-permute-start(bf16[256,512]{1,0:T(8,128)(2,1)S(1)} %collective-permute-done.18.refs_8_), channel_id=1, source_target_pairs={{0,28},{4,0},{8,4},{12,8},{16,12},{20,16},{24,20},{28,24},{1,29},{... | collective-permute-start | bytes 786440 | tf_op jit(solution)/shard_map/ppermute | solution.py:226
  59.6 1.9 %collective-permute-done.15.refs_13_ = bf16[256,512]{1,0:T(8,128)(2,1)S(1)} collective-permute-done((bf16[256,512]{1,0:T(8,128)(2,1)S(1)}, bf16[256,512]{1,0:T(8,128)(2,1)S(1)}, u32[]{:S(2)}, u32[]{:S(2)}) %collective-permute-start.15) | collective-permute-done | bytes 262176 | tf_op jit(solution)/shard_map/ppermute | solution.py:226
  61.5 3.7 %collective-permute-start.16 = (bf16[256,512]{1,0:T(8,128)(2,1)S(1)}, bf16[256,512]{1,0:T(8,128)(2,1)S(1)}, u32[]{:S(2)}, u32[]{:S(2)}) collective-permute-start(bf16[256,512]{1,0:T(8,128)(2,1)S(1)} %collective-permute-done.15.refs_13_), channel_id=1, source_target_pairs={{0,28},{4,0},{8,4},{12,8},{16,12},{20,16},{24,20},{28,24},{1,29},{... | collective-permute-start | bytes 786440 | tf_op jit(solution)/shard_map/ppermute | solution.py:226
  65.2 0.0 copy-done.6
  65.2 0.0 copy-done.7
  65.2 0.0 copy-done.21
  65.3 3.8 %product_first.1.refs_14_ = f32[512,1024]{1,0:T(8,128)S(1)} custom-call(s32[32,64]{1,0:T(8,128)S(1)} %copy-done.3, s32[32,128]{1,0:T(8,128)S(1)} %bitcast.6, bf16[2,512,256]{2,1,0:T(8,128)(2,1)} %copy-done.6, bf16[2,512,256]{2,1,0:T(8,128)(2,1)} %copy-done.7, bf16[2,512,256]{2,1,0:T(8,128)(2,1)} %copy-done.8, bf16[2,512,256]{2,1,0:T(8,128)(2,1)} %copy-done.9, ...), custom_call_target="tpu_custom_call" | custom-call | flops 1610612736 | bytes 4194304 | tf_op jit(solution)/shard_map/product_first/pallas_call | solution.py:199
  69.2 0.0 collective-permute-done.12.refs_10_
  69.2 0.1 collective-permute-start.13
  69.3 0.0 collective-permute-done.19.refs_11_
  69.3 0.0 collective-permute-done.20.refs_12_
  69.3 0.6 copy-done.15
  69.9 0.1 copy-done.16
  70.0 0.7 copy-done.17
  70.7 5.0 %product_next.1.refs_8_ = f32[512,1024]{1,0:T(8,128)S(1)} custom-call(s32[32,64]{1,0:T(8,128)S(1)} %copy-done.3, s32[32,128]{1,0:T(8,128)S(1)} %bitcast.7, bf16[2,512,256]{2,1,0:T(8,128)(2,1)} %copy-done.6, bf16[2,512,256]{2,1,0:T(8,128)(2,1)} %copy-done.7, bf16[2,512,256]{2,1,0:T(8,128)(2,1)} %copy-done.8, ...), custom_call_target="tpu_custom_call", output_to_operand_aliasing={{}: (14, {})} | custom-call | flops 2147483648 | bytes 4194304 | tf_op jit(solution)/shard_map/product_next/pallas_call | solution.py:199
  75.7 0.0 collective-permute-done.16.refs_7_
  75.7 1.1 %collective-permute-done.13.refs_6_ = bf16[256,512]{1,0:T(8,128)(2,1)S(1)} collective-permute-done((bf16[256,512]{1,0:T(8,128)(2,1)S(1)}, bf16[256,512]{1,0:T(8,128)(2,1)S(1)}, u32[]{:S(2)}, u32[]{:S(2)}) %collective-permute-start.13) | collective-permute-done | bytes 262176 | tf_op jit(solution)/shard_map/ppermute | solution.py:226
  76.9 3.0 %product_last.1 = (f32[512,1024]{1,0:T(8,128)S(1)}, f32[1,1024]{1,0:T(1,128)S(1)}) custom-call(s32[32,64]{1,0:T(8,128)S(1)} %copy-done.3, s32[32,128]{1,0:T(8,128)S(1)} %bitcast.8, bf16[2,512,256]{2,1,0:T(8,128)(2,1)} %copy-done.6, bf16[2,512,256]{2,1,0:T(8,128)(2,1)} %copy-done.7, bf16[2,512,256]{2,1,0:T(8,128)(2,1)} %copy-done.8, ...), custom_call_target="tpu_custom_call", output_to_operand_aliasing={{0}: (8, {})} | custom-call | flops 536870912 | bytes 4194304 | tf_op jit(solution)/shard_map/product_last/pallas_call | solution.py:199
  79.8 0.1 broadcast_in_dim.2
  79.9 15.9 %all_to_all.6 = f32[32,1,1024]{2,1,0:T(1,128)S(1)} all-to-all(f32[32,1,1024]{2,1,0:T(1,128)S(1)} %broadcast_in_dim.2), channel_id=1, replica_groups=mesh['y'=4,'core'=2,'z'=8,'x'=4] {'z','x'}, dimensions={0} | all-to-all | bytes 262144 | tf_op jit(solution)/shard_map/all_to_all | solution.py:276
  95.8 0.1 reduce_sum.9
  95.9 1.5 %broadcast_multiply_fusion = f32[512,1024]{1,0:T(8,128)} fusion(f32[512,1024]{1,0:T(8,128)S(1)} %get-tuple-element.39, f32[1024]{0:T(1024)S(1)} %broadcast_divide_fusion), kind=kLoop, calls=%fused_computation | loop fusion | flops 524288 | bytes 4198400 | tf_op jit(solution)/shard_map/mul | solution.py:279
  (41 shorter events, 0.1 us)
Async XLA Ops:
  0.0 0.9 copy-start.1
  1.0 0.7 copy-start.2
  1.7 63.6 %copy-start.3 = (s32[32,64]{1,0:T(8,128)S(1)}, s32[32,64]{1,0:T(8,128)}, u32[]{:S(2)}) copy-start(s32[32,64]{1,0:T(8,128)} %refs_0_.5) | copy-start | bytes 24580
  1.7 63.6 %copy-start.5 = (s32[128,32]{0,1:T(8,128)S(1)}, s32[128,32]{0,1:T(8,128)}, u32[]{:S(2)}) copy-start(s32[128,32]{0,1:T(8,128)} %param.5) | copy-start | bytes 49156
  2.6 1.0 %copy-start = (bf16[512,512]{1,0:T(8,128)(2,1)S(1)}, bf16[512,512]{1,0:T(8,128)(2,1)}, u32[]{:S(2)}) copy-start(bf16[512,512]{1,0:T(8,128)(2,1)} %left) | copy-start | bytes 1572868
  3.6 0.7 copy-start.4
  5.4 11.0 %collective-permute-start.3 = (bf16[512,256]{1,0:T(8,128)(2,1)S(1)}, bf16[512,256]{1,0:T(8,128)(2,1)S(1)}, u32[]{:S(2)}, u32[]{:S(2)}) collective-permute-start(bf16[512,256]{1,0:T(8,128)(2,1)S(1)} %pack_left.1), channel_id=1, source_target_pairs={{0,32},{32,0},{1,33},{33,1},{2,34},{34,2},{3,35},{35,3},{4,36},{36... | collective-permute-start | bytes 786440 | tf_op jit(solution)/shard_map/ppermute | solution.py:226
  5.5 7.1 %collective-permute-start = (bf16[128,512]{1,0:T(8,128)(2,1)S(1)}, bf16[128,512]{1,0:T(8,128)(2,1)S(1)}, u32[]{:S(2)}, u32[]{:S(2)}) collective-permute-start(bf16[128,512]{1,0:T(8,128)(2,1)S(1)} %pack_right.1), channel_id=1, source_target_pairs={{0,1},{1,2},{2,3},{3,0},{4,5},{5,6},{6,7},{7,4},{8,9},{9,10},{10,1... | collective-permute-start | bytes 393224 | tf_op jit(solution)/shard_map/ppermute | solution.py:226
  7.0 7.7 %collective-permute-start.1 = (bf16[128,512]{1,0:T(8,128)(2,1)S(1)}, bf16[128,512]{1,0:T(8,128)(2,1)S(1)}, u32[]{:S(2)}, u32[]{:S(2)}) collective-permute-start(bf16[128,512]{1,0:T(8,128)(2,1)S(1)} %pack_right.1), channel_id=1, source_target_pairs={{0,3},{1,0},{2,1},{3,2},{4,7},{5,4},{6,5},{7,6},{8,11},{9,8},{10,9... | collective-permute-start | bytes 393224 | tf_op jit(solution)/shard_map/ppermute | solution.py:226
  8.8 7.6 %collective-permute-start.2 = (bf16[128,512]{1,0:T(8,128)(2,1)S(1)}, bf16[128,512]{1,0:T(8,128)(2,1)S(1)}, u32[]{:S(2)}, u32[]{:S(2)}) collective-permute-start(bf16[128,512]{1,0:T(8,128)(2,1)S(1)} %pack_right.1), channel_id=1, source_target_pairs={{0,2},{1,3},{2,0},{3,1},{4,6},{5,7},{6,4},{7,5},{8,10},{9,11},{10,... | collective-permute-start | bytes 393224 | tf_op jit(solution)/shard_map/ppermute | solution.py:226
  16.4 48.8 %copy-start.6 = (bf16[2,512,256]{2,1,0:T(8,128)(2,1)}, bf16[2,512,256]{2,1,0:T(8,128)(2,1)S(1)}, u32[]{:S(2)}) copy-start(bf16[2,512,256]{2,1,0:T(8,128)(2,1)S(1)} %pad_maximum_fusion.refs_2_) | copy-start | bytes 1572868
  16.5 13.4 %collective-permute-start.4 = (bf16[2,512,256]{2,1,0:T(8,128)(2,1)S(1)}, bf16[2,512,256]{2,1,0:T(8,128)(2,1)S(1)}, u32[]{:S(2)}, u32[]{:S(2)}) collective-permute-start(bf16[2,512,256]{2,1,0:T(8,128)(2,1)S(1)} %pad_maximum_fusion.refs_2_), channel_id=1, source_target_pairs={{0,64},{32,224},{64,128},{96,32},{128,192},{160,96},{192,0},{224,1... | collective-permute-start | bytes 1572872 | tf_op jit(solution)/shard_map/ppermute | solution.py:236
  17.7 47.5 %copy-start.18 = (bf16[256,512]{1,0:T(8,128)(2,1)}, bf16[256,512]{1,0:T(8,128)(2,1)S(1)}, u32[]{:S(2)}) copy-start(bf16[256,512]{1,0:T(8,128)(2,1)S(1)} %constant_dynamic-update-slice_fusion.refs_6_) | copy-start | bytes 786436
  17.7 12.2 %collective-permute-start.5 = (bf16[256,512]{1,0:T(8,128)(2,1)S(1)}, bf16[256,512]{1,0:T(8,128)(2,1)S(1)}, u32[]{:S(2)}, u32[]{:S(2)}) collective-permute-start(bf16[256,512]{1,0:T(8,128)(2,1)S(1)} %constant_dynamic-update-slice_fusion.refs_6_), channel_id=1, source_target_pairs={{0,4},{4,8},{8,12},{12,16},{16,20},{20,24},{24,28},{28,0},{1,5},{5... | collective-permute-start | bytes 786440 | tf_op jit(solution)/shard_map/ppermute | solution.py:226
  18.8 46.4 %copy-start.19 = (bf16[256,512]{1,0:T(8,128)(2,1)}, bf16[256,512]{1,0:T(8,128)(2,1)S(1)}, u32[]{:S(2)}) copy-start(bf16[256,512]{1,0:T(8,128)(2,1)S(1)} %constant_dynamic-update-slice_fusion.2.refs_7_) | copy-start | bytes 786436
  18.8 14.8 %collective-permute-start.11 = (bf16[256,512]{1,0:T(8,128)(2,1)S(1)}, bf16[256,512]{1,0:T(8,128)(2,1)S(1)}, u32[]{:S(2)}, u32[]{:S(2)}) collective-permute-start(bf16[256,512]{1,0:T(8,128)(2,1)S(1)} %constant_dynamic-update-slice_fusion.2.refs_7_), channel_id=1, source_target_pairs={{0,28},{4,0},{8,4},{12,8},{16,12},{20,16},{24,20},{28,24},{1,29},{... | collective-permute-start | bytes 786440 | tf_op jit(solution)/shard_map/ppermute | solution.py:226
  22.9 11.8 %collective-permute-start.9 = (bf16[256,512]{1,0:T(8,128)(2,1)S(1)}, bf16[256,512]{1,0:T(8,128)(2,1)S(1)}, u32[]{:S(2)}, u32[]{:S(2)}) collective-permute-start(bf16[256,512]{1,0:T(8,128)(2,1)S(1)} %constant_dynamic-update-slice_fusion.2.refs_7_), channel_id=1, source_target_pairs={{0,4},{4,8},{8,12},{12,16},{16,20},{20,24},{24,28},{28,0},{1,5},{5... | collective-permute-start | bytes 786440 | tf_op jit(solution)/shard_map/ppermute | solution.py:226
  29.9 35.4 %copy-start.20 = (bf16[256,512]{1,0:T(8,128)(2,1)}, bf16[256,512]{1,0:T(8,128)(2,1)S(1)}, u32[]{:S(2)}) copy-start(bf16[256,512]{1,0:T(8,128)(2,1)S(1)} %collective-permute-done.5.refs_8_) | copy-start | bytes 786436
  29.9 35.4 %copy-start.7 = (bf16[2,512,256]{2,1,0:T(8,128)(2,1)}, bf16[2,512,256]{2,1,0:T(8,128)(2,1)S(1)}, u32[]{:S(2)}) copy-start(bf16[2,512,256]{2,1,0:T(8,128)(2,1)S(1)} %collective-permute-done.4.refs_3_) | copy-start | bytes 1572868
  29.9 19.4 %collective-permute-start.6 = (bf16[2,512,256]{2,1,0:T(8,128)(2,1)S(1)}, bf16[2,512,256]{2,1,0:T(8,128)(2,1)S(1)}, u32[]{:S(2)}, u32[]{:S(2)}) collective-permute-start(bf16[2,512,256]{2,1,0:T(8,128)(2,1)S(1)} %collective-permute-done.4.refs_3_), channel_id=1, source_target_pairs={{0,32},{32,0},{1,33},{33,1},{2,34},{34,2},{3,35},{35,3},{4,36},{36... | collective-permute-start | bytes 1572872 | tf_op jit(solution)/shard_map/ppermute | solution.py:226
  30.0 19.3 %collective-permute-start.7 = (bf16[2,512,256]{2,1,0:T(8,128)(2,1)S(1)}, bf16[2,512,256]{2,1,0:T(8,128)(2,1)S(1)}, u32[]{:S(2)}, u32[]{:S(2)}) collective-permute-start(bf16[2,512,256]{2,1,0:T(8,128)(2,1)S(1)} %collective-permute-done.4.refs_3_), channel_id=1, source_target_pairs={{0,64},{32,224},{64,128},{96,32},{128,192},{160,96},{192,0},{224,1... | collective-permute-start | bytes 1572872 | tf_op jit(solution)/shard_map/ppermute | solution.py:236
  31.8 9.1 %collective-permute-start.10 = (bf16[256,512]{1,0:T(8,128)(2,1)S(1)}, bf16[256,512]{1,0:T(8,128)(2,1)S(1)}, u32[]{:S(2)}, u32[]{:S(2)}) collective-permute-start(bf16[256,512]{1,0:T(8,128)(2,1)S(1)} %constant_dynamic-update-slice_fusion.refs_6_), channel_id=1, source_target_pairs={{0,28},{4,0},{8,4},{12,8},{16,12},{20,16},{24,20},{28,24},{1,29},{... | collective-permute-start | bytes 786440 | tf_op jit(solution)/shard_map/ppermute | solution.py:226
  33.7 31.6 %copy-start.21 = (bf16[256,512]{1,0:T(8,128)(2,1)}, bf16[256,512]{1,0:T(8,128)(2,1)S(1)}, u32[]{:S(2)}) copy-start(bf16[256,512]{1,0:T(8,128)(2,1)S(1)} %collective-permute-done.11.refs_11_) | copy-start | bytes 786436
  33.7 12.2 %collective-permute-start.14 = (bf16[256,512]{1,0:T(8,128)(2,1)S(1)}, bf16[256,512]{1,0:T(8,128)(2,1)S(1)}, u32[]{:S(2)}, u32[]{:S(2)}) collective-permute-start(bf16[256,512]{1,0:T(8,128)(2,1)S(1)} %collective-permute-done.11.refs_11_), channel_id=1, source_target_pairs={{0,28},{4,0},{8,4},{12,8},{16,12},{20,16},{24,20},{28,24},{1,29},{... | collective-permute-start | bytes 786440 | tf_op jit(solution)/shard_map/ppermute | solution.py:226
  34.7 30.5 %copy-start.22 = (bf16[256,512]{1,0:T(8,128)(2,1)}, bf16[256,512]{1,0:T(8,128)(2,1)S(1)}, u32[]{:S(2)}) copy-start(bf16[256,512]{1,0:T(8,128)(2,1)S(1)} %collective-permute-done.9.refs_9_) | copy-start | bytes 786436
  34.7 14.5 %collective-permute-start.8 = (bf16[256,512]{1,0:T(8,128)(2,1)S(1)}, bf16[256,512]{1,0:T(8,128)(2,1)S(1)}, u32[]{:S(2)}, u32[]{:S(2)}) collective-permute-start(bf16[256,512]{1,0:T(8,128)(2,1)S(1)} %collective-permute-done.5.refs_8_), channel_id=1, source_target_pairs={{0,4},{4,8},{8,12},{12,16},{16,20},{20,24},{24,28},{28,0},{1,5},{5... | collective-permute-start | bytes 786440 | tf_op jit(solution)/shard_map/ppermute | solution.py:226
  40.9 24.3 %copy-start.23 = (bf16[256,512]{1,0:T(8,128)(2,1)}, bf16[256,512]{1,0:T(8,128)(2,1)S(1)}, u32[]{:S(2)}) copy-start(bf16[256,512]{1,0:T(8,128)(2,1)S(1)} %collective-permute-done.10.refs_10_) | copy-start | bytes 786436
  40.9 10.6 %collective-permute-start.17 = (bf16[256,512]{1,0:T(8,128)(2,1)S(1)}, bf16[256,512]{1,0:T(8,128)(2,1)S(1)}, u32[]{:S(2)}, u32[]{:S(2)}) collective-permute-start(bf16[256,512]{1,0:T(8,128)(2,1)S(1)} %collective-permute-done.9.refs_9_), channel_id=1, source_target_pairs={{0,4},{4,8},{8,12},{12,16},{16,20},{20,24},{24,28},{28,0},{1,5},{5... | collective-permute-start | bytes 786440 | tf_op jit(solution)/shard_map/ppermute | solution.py:226
  45.9 23.4 %copy-start.10 = (bf16[256,512]{1,0:T(8,128)(2,1)}, bf16[256,512]{1,0:T(8,128)(2,1)S(1)}, u32[]{:S(2)}) copy-start(bf16[256,512]{1,0:T(8,128)(2,1)S(1)} %collective-permute-done.14.refs_9_) | copy-start | bytes 786436
  45.9 10.0 %collective-permute-start.18 = (bf16[256,512]{1,0:T(8,128)(2,1)S(1)}, bf16[256,512]{1,0:T(8,128)(2,1)S(1)}, u32[]{:S(2)}, u32[]{:S(2)}) collective-permute-start(bf16[256,512]{1,0:T(8,128)(2,1)S(1)} %collective-permute-done.10.refs_10_), channel_id=1, source_target_pairs={{0,28},{4,0},{8,4},{12,8},{16,12},{20,16},{24,20},{28,24},{1,29},{... | collective-permute-start | bytes 786440 | tf_op jit(solution)/shard_map/ppermute | solution.py:226
  49.2 20.2 %copy-start.11 = (bf16[256,512]{1,0:T(8,128)(2,1)}, bf16[256,512]{1,0:T(8,128)(2,1)S(1)}, u32[]{:S(2)}) copy-start(bf16[256,512]{1,0:T(8,128)(2,1)S(1)} %collective-permute-done.8.refs_6_) | copy-start | bytes 786436
  49.2 12.4 %collective-permute-start.15 = (bf16[256,512]{1,0:T(8,128)(2,1)S(1)}, bf16[256,512]{1,0:T(8,128)(2,1)S(1)}, u32[]{:S(2)}, u32[]{:S(2)}) collective-permute-start(bf16[256,512]{1,0:T(8,128)(2,1)S(1)} %collective-permute-done.14.refs_9_), channel_id=1, source_target_pairs={{0,28},{4,0},{8,4},{12,8},{16,12},{20,16},{24,20},{28,24},{1,29},{... | collective-permute-start | bytes 786440 | tf_op jit(solution)/shard_map/ppermute | solution.py:226
  49.3 16.0 %copy-start.8 = (bf16[2,512,256]{2,1,0:T(8,128)(2,1)}, bf16[2,512,256]{2,1,0:T(8,128)(2,1)S(1)}, u32[]{:S(2)}) copy-start(bf16[2,512,256]{2,1,0:T(8,128)(2,1)S(1)} %collective-permute-done.6.refs_4_) | copy-start | bytes 1572868
  49.3 16.0 %copy-start.9 = (bf16[2,512,256]{2,1,0:T(8,128)(2,1)}, bf16[2,512,256]{2,1,0:T(8,128)(2,1)S(1)}, u32[]{:S(2)}) copy-start(bf16[2,512,256]{2,1,0:T(8,128)(2,1)S(1)} %collective-permute-done.7.refs_5_) | copy-start | bytes 1572868
  49.3 19.9 %collective-permute-start.12 = (bf16[256,512]{1,0:T(8,128)(2,1)S(1)}, bf16[256,512]{1,0:T(8,128)(2,1)S(1)}, u32[]{:S(2)}, u32[]{:S(2)}) collective-permute-start(bf16[256,512]{1,0:T(8,128)(2,1)S(1)} %collective-permute-done.8.refs_6_), channel_id=1, source_target_pairs={{0,4},{4,8},{8,12},{12,16},{16,20},{20,24},{24,28},{28,0},{1,5},{5... | collective-permute-start | bytes 786440 | tf_op jit(solution)/shard_map/ppermute | solution.py:226
  51.5 17.7 %copy-start.12 = (bf16[256,512]{1,0:T(8,128)(2,1)}, bf16[256,512]{1,0:T(8,128)(2,1)S(1)}, u32[]{:S(2)}) copy-start(bf16[256,512]{1,0:T(8,128)(2,1)S(1)} %collective-permute-done.17.refs_7_) | copy-start | bytes 786436
  51.5 17.8 %collective-permute-start.19 = (bf16[256,512]{1,0:T(8,128)(2,1)S(1)}, bf16[256,512]{1,0:T(8,128)(2,1)S(1)}, u32[]{:S(2)}, u32[]{:S(2)}) collective-permute-start(bf16[256,512]{1,0:T(8,128)(2,1)S(1)} %collective-permute-done.17.refs_7_), channel_id=1, source_target_pairs={{0,4},{4,8},{8,12},{12,16},{16,20},{20,24},{24,28},{28,0},{1,5},{5... | collective-permute-start | bytes 786440 | tf_op jit(solution)/shard_map/ppermute | solution.py:226
  55.9 13.3 %copy-start.13 = (bf16[256,512]{1,0:T(8,128)(2,1)}, bf16[256,512]{1,0:T(8,128)(2,1)S(1)}, u32[]{:S(2)}) copy-start(bf16[256,512]{1,0:T(8,128)(2,1)S(1)} %collective-permute-done.18.refs_8_) | copy-start | bytes 786436
  55.9 13.4 %collective-permute-start.20 = (bf16[256,512]{1,0:T(8,128)(2,1)S(1)}, bf16[256,512]{1,0:T(8,128)(2,1)S(1)}, u32[]{:S(2)}, u32[]{:S(2)}) collective-permute-start(bf16[256,512]{1,0:T(8,128)(2,1)S(1)} %collective-permute-done.18.refs_8_), channel_id=1, source_target_pairs={{0,28},{4,0},{8,4},{12,8},{16,12},{20,16},{24,20},{28,24},{1,29},{... | collective-permute-start | bytes 786440 | tf_op jit(solution)/shard_map/ppermute | solution.py:226
  61.5 7.7 %copy-start.14 = (bf16[256,512]{1,0:T(8,128)(2,1)}, bf16[256,512]{1,0:T(8,128)(2,1)S(1)}, u32[]{:S(2)}) copy-start(bf16[256,512]{1,0:T(8,128)(2,1)S(1)} %collective-permute-done.15.refs_13_) | copy-start | bytes 786436
  61.5 14.2 %collective-permute-start.16 = (bf16[256,512]{1,0:T(8,128)(2,1)S(1)}, bf16[256,512]{1,0:T(8,128)(2,1)S(1)}, u32[]{:S(2)}, u32[]{:S(2)}) collective-permute-start(bf16[256,512]{1,0:T(8,128)(2,1)S(1)} %collective-permute-done.15.refs_13_), channel_id=1, source_target_pairs={{0,28},{4,0},{8,4},{12,8},{16,12},{20,16},{24,20},{28,24},{1,29},{... | collective-permute-start | bytes 786440 | tf_op jit(solution)/shard_map/ppermute | solution.py:226
  69.2 0.7 copy-start.15
  69.2 7.7 %collective-permute-start.13 = (bf16[256,512]{1,0:T(8,128)(2,1)S(1)}, bf16[256,512]{1,0:T(8,128)(2,1)S(1)}, u32[]{:S(2)}, u32[]{:S(2)}) collective-permute-start(bf16[256,512]{1,0:T(8,128)(2,1)S(1)} %collective-permute-done.12.refs_10_), channel_id=1, source_target_pairs={{0,4},{4,8},{8,12},{12,16},{16,20},{20,24},{24,28},{28,0},{1,5},{5... | collective-permute-start | bytes 786440 | tf_op jit(solution)/shard_map/ppermute | solution.py:226
  69.3 0.7 copy-start.16
  70.0 0.7 copy-start.17

commit v7 on v6

--- a/solution.py
+++ b/solution.py
@@ -12,6 +12,7 @@
 SLOTS = 4
 LEFT_SLOTS = 2
 SHIFTS = (0, 3, 1, 2)
+FAR = (-3, 3, 4)
 KERNEL_VMEM = 24 * 1024 * 1024
 ROW, COL = ("y", "core"), ("z", "x")
 
@@ -240,38 +241,42 @@
     left_pattern = left_pattern.T
     packed_right = pack(pack_right_kernel, "pack_right", right_pattern, right_values, SLOTS)
     near = [packed_right] + [moved(packed_right, "x", -shift) for shift in SHIFTS[1:]]
+    far = [moved(packed_right, "z", -shift) for shift in FAR[:2]]
     left_values, _ = lax.optimization_barrier((left_values, packed_right))
     packed_left = pack(pack_left_kernel, "pack_left", left_pattern, left_values, LEFT_SLOTS)
     other_left = moved(packed_left, "core", 1)
     near, packed_left, other_left = lax.optimization_barrier((near, packed_left, other_left))
-    own = [jnp.concatenate(near[:2], 0), jnp.concatenate(near[2:], 0)]
-    half = own[0].shape[0]
-    came = {0: own}
-
-    def ring(step):
-        came[-step] = [moved(piece, "z", 1) for piece in came[1 - step]]
-        came[step] = [moved(piece, "z", -1) for piece in came[step - 1]]
-
-    def tied(values, step):
-        values, came[-step][0] = lax.optimization_barrier((values, came[-step][0]))
-        return values
-
-    def add(shifts, total, last=False):
-        blocks = [(shift, x_shift) for shift in shifts for x_shift in SHIFTS]
-        pieces = [piece for shift in shifts for piece in came[shift]]
-        copies = [(n, 0, half, n * half) for n in range(len(pieces))]
+    own = jnp.concatenate(near, 0)
+    up, down = moved(own, "z", 1), moved(own, "z", -1)
+    near_left = jnp.stack([packed_left, other_left])
+    sent_left = around(near_left)
+    far, sent_left = lax.optimization_barrier((far, sent_left))
+    far.append(moved(far[0], "z", 1))
+    left = [near_left, sent_left, moved(sent_left, "core", 1), around(sent_left)]
+    up, down, far, left = lax.optimization_barrier((up, down, far, left))
+    far = jnp.concatenate(far, 0)
+    further_up, further_down = moved(up, "z", 1), moved(down, "z", -1)
+    far_3, far_1 = moved(far, "x", 1), moved(far, "x", -1)
+    whole, half = own.shape[0], far.shape[0] // 2
+
+    def add(blocks, copies, pieces, total, last=False):
         return product(blocks, copies, right_pattern, left_pattern, left, pieces, total, last)
 
-    ring(1)
-    near_left = jnp.stack([packed_left, other_left])
-    sent_left = tied(around(near_left), 1)
-    ring(2)
-    left = tied([near_left, sent_left, moved(sent_left, "core", 1), around(sent_left)], 2)
-    ring(3)
-    total = tied(add((0, -1, 1), None)[0], 3)
-    came[4] = [moved(came[-3][0], "z", 1), moved(came[3][1], "z", -1)]
-    (total,) = add((-2, 2, -3, 3), total)
-    total, sums = add((4,), total, True)
+    blocks = [(z_shift, x_shift) for z_shift in (0, -1, 1) for x_shift in SHIFTS]
+    blocks += [(z_shift, 0) for z_shift in FAR]
+    copies = [(0, 0, whole, 0), (1, 0, whole, whole), (2, 0, whole, 2 * whole)]
+    copies += [(3, 0, 2 * half, 3 * whole)]
+    (total,) = add(blocks, copies, [own, up, down, far], None)
+    total, far_3, far_1 = lax.optimization_barrier((total, far_3, far_1))
+    far_2 = (moved(far_3[:half], "x", 1), moved(far_1[half:], "x", -1))
+    blocks = [(z_shift, x_shift) for x_shift in (3, 1) for z_shift in FAR]
+    copies = [(0, 0, 2 * half, 0), (1, 0, 2 * half, 2 * half)]
+    (total,) = add(blocks, copies, [far_3, far_1], total)
+    blocks = [(z_shift, x_shift) for z_shift in (-2, 2) for x_shift in SHIFTS]
+    blocks += [(z_shift, 2) for z_shift in FAR]
+    copies = [(0, 0, whole, 0), (1, 0, whole, whole)]
+    copies += [(2, 0, half, 2 * whole), (3, 0, half, 2 * whole + half)]
+    total, sums = add(blocks, copies, [further_up, further_down, *far_2], total, True)
     count = lax.axis_size("z") * lax.axis_size("x")
     spread = lax.all_to_all(
         jnp.broadcast_to(sums, (count, sums.shape[1])), COL, 0, 0, tiled=True

time: 98 us -> 96.1 us (0.981); the launches traced: 97.5 us -> 94.6 us
  starting transfers between devices: 30.5 us -> 28.8 us
  waiting for transfers between devices: 30.4 us -> 28.7 us
  local copies, waits for them, and re-layouts: 4.96 us -> 3.64 us
  Pallas kernels: 13.7 us -> 14.9 us
    ppermute x19 -> x16, starting transfers between devices: 27.4 us -> 24.7 us  [moved(): lax.ppermute(value, axis, [(i, (i + step) % size) for i in range(size)])]
    ppermute x19 -> x16, waiting for transfers between devices: 30.4 us -> 28.7 us  [moved(): lax.ppermute(value, axis, [(i, (i + step) % size) for i in range(size)])]
    unnamed x50 -> x37, local copies, waits for them, and re-layouts: 4.87 us -> 3.52 us
    pallas_call x3, Pallas kernels: 11.8 us -> 13 us  [product(): pl.pallas_call(functools.partial(product_kernel, blocks, copies, total is...]
    ppermute x2, starting transfers between devices: 3.04 us -> 4.16 us  [around(): return lax.ppermute(value, ('y', 'core'), pairs)]
  transfers between devices with their start and end apart: 21 -> 18, of which waited for: 9 -> 10; matrix products, arithmetic and copies ran while one was open for 0% -> 0% of each run, Pallas kernels for 9% -> 8%
where the time goes in v7:
time: 96.1 us; the launch traced here: 94.6 us
  starting transfers between devices  28.8 us (30%)
  waiting for transfers between devices  28.7 us (30%)
  blocking collectives  16.5 us (17%)
  Pallas kernels  14.9 us (16%)
  local copies, waits for them, and re-layouts  3.64 us (4%)
  other arithmetic  1.7 us (2%)
    ppermute x16, waiting for transfers between devices, moved(): lax.ppermute(value, axis, [(i, (i + step) % size) for i in range(size)])  28.7 us
    ppermute x16, starting transfers between devices, moved(): lax.ppermute(value, axis, [(i, (i + step) % size) for i in range(size)])  24.7 us
    all_to_all x1, blocking collectives, shards(): lax.all_to_all(jnp.broadcast_to(sums, (count, sums.shape[1])), COL, 0, 0,...  16.5 us
    pallas_call x3, Pallas kernels, product(): pl.pallas_call(functools.partial(product_kernel, blocks, copies, total is...  13 us
    ppermute x2, starting transfers between devices, around(): return lax.ppermute(value, ('y', 'core'), pairs)  4.16 us
    unnamed x37, local copies, waits for them, and re-layouts  3.52 us
  transfers between devices with their start and end apart: 18, of which 10 were waited for; matrix products, arithmetic and copies ran while one was open for 0% of the time, Pallas kernels for 8%

profile of v7, /device:TPU:24, one launch (start us, length us, event | category | flops | bytes accessed | tf_op | source)
XLA Modules:
  0.0 94.6 jit_solution(2794752313664475298)
XLA Ops:
  0.0 0.9 %copy-done.1 = bf16[128,1024]{1,0:T(8,128)(2,1)S(1)} copy-done((bf16[128,1024]{1,0:T(8,128)(2,1)S(1)}, bf16[128,1024]{1,0:T(8,128)(2,1)}, u32[]{:S(2)}) %copy-start.1) | copy-done | bytes 262168
  1.0 0.7 copy-done.2
  1.7 0.9 pack_right.1
  2.6 0.0 copy-start
  2.6 1.0 %copy-done = bf16[512,512]{1,0:T(8,128)(2,1)S(1)} copy-done((bf16[512,512]{1,0:T(8,128)(2,1)S(1)}, bf16[512,512]{1,0:T(8,128)(2,1)}, u32[]{:S(2)}) %copy-start) | copy-done | bytes 524312
  3.7 0.7 copy-done.4
  4.4 1.0 %pack_left.1 = bf16[512,256]{1,0:T(8,128)(2,1)S(1)} custom-call(s32[32,128]{1,0:T(8,128)S(1)} %bitcast.5, bf16[512,512]{1,0:T(8,128)(2,1)S(1)} %copy-done), custom_call_target="tpu_custom_call" | custom-call | tf_op jit(solution)/shard_map/pack_left/pallas_call | solution.py:65
  5.4 0.1 collective-permute-start.3
  5.5 3.1 %collective-permute-start.2 = (bf16[128,512]{1,0:T(8,128)(2,1)S(1)}, bf16[128,512]{1,0:T(8,128)(2,1)S(1)}, u32[]{:S(2)}, u32[]{:S(2)}) collective-permute-start(bf16[128,512]{1,0:T(8,128)(2,1)S(1)} %pack_right.1), channel_id=1, source_target_pairs={{0,2},{1,3},{2,0},{3,1},{4,6},{5,7},{6,4},{7,5},{8,10},{9,11},{10,... | collective-permute-start | bytes 393224 | tf_op jit(solution)/shard_map/ppermute | solution.py:227
  8.6 1.1 %collective-permute-start.1 = (bf16[128,512]{1,0:T(8,128)(2,1)S(1)}, bf16[128,512]{1,0:T(8,128)(2,1)S(1)}, u32[]{:S(2)}, u32[]{:S(2)}) collective-permute-start(bf16[128,512]{1,0:T(8,128)(2,1)S(1)} %pack_right.1), channel_id=1, source_target_pairs={{0,3},{1,0},{2,1},{3,2},{4,7},{5,4},{6,5},{7,6},{8,11},{9,8},{10,9... | collective-permute-start | bytes 393224 | tf_op jit(solution)/shard_map/ppermute | solution.py:227
  9.7 0.9 collective-permute-start
  10.6 2.8 %collective-permute-done.2 = bf16[128,512]{1,0:T(8,128)(2,1)S(1)} collective-permute-done((bf16[128,512]{1,0:T(8,128)(2,1)S(1)}, bf16[128,512]{1,0:T(8,128)(2,1)S(1)}, u32[]{:S(2)}, u32[]{:S(2)}) %collective-permute-start.2) | collective-permute-done | bytes 131104 | tf_op jit(solution)/shard_map/ppermute | solution.py:227
  13.4 2.4 %collective-permute-done.1 = bf16[128,512]{1,0:T(8,128)(2,1)S(1)} collective-permute-done((bf16[128,512]{1,0:T(8,128)(2,1)S(1)}, bf16[128,512]{1,0:T(8,128)(2,1)S(1)}, u32[]{:S(2)}, u32[]{:S(2)}) %collective-permute-start.1) | collective-permute-done | bytes 131104 | tf_op jit(solution)/shard_map/ppermute | solution.py:227
  15.8 0.4 collective-permute-done
  16.2 0.0 collective-permute-done.3
  16.2 0.1 pad_maximum_fusion.refs_2_
  16.3 0.0 copy-start.6
  16.3 1.5 %collective-permute-start.8 = (bf16[2,512,256]{2,1,0:T(8,128)(2,1)S(1)}, bf16[2,512,256]{2,1,0:T(8,128)(2,1)S(1)}, u32[]{:S(2)}, u32[]{:S(2)}) collective-permute-start(bf16[2,512,256]{2,1,0:T(8,128)(2,1)S(1)} %pad_maximum_fusion.refs_2_), channel_id=1, source_target_pairs={{0,64},{32,224},{64,128},{96,32},{128,192},{160,96},{192,0},{224,1... | collective-permute-start | bytes 1572872 | tf_op jit(solution)/shard_map/ppermute | solution.py:237
  17.8 5.5 %collective-permute-start.7 = (bf16[128,512]{1,0:T(8,128)(2,1)S(1)}, bf16[128,512]{1,0:T(8,128)(2,1)S(1)}, u32[]{:S(2)}, u32[]{:S(2)}) collective-permute-start(bf16[128,512]{1,0:T(8,128)(2,1)S(1)} %pack_right.1), channel_id=1, source_target_pairs={{0,20},{4,24},{8,28},{12,0},{16,4},{20,8},{24,12},{28,16},{1,21},{... | collective-permute-start | bytes 393224 | tf_op jit(solution)/shard_map/ppermute | solution.py:227
  23.3 0.0 collective-permute-start.6
  23.4 0.0 copy-start.13
  23.4 4.2 %collective-permute-start.5 = (bf16[512,512]{1,0:T(8,128)(2,1)S(1)}, bf16[512,512]{1,0:T(8,128)(2,1)S(1)}, u32[]{:S(2)}, u32[]{:S(2)}) collective-permute-start(bf16[512,512]{1,0:T(8,128)(2,1)S(1)} %constant_dynamic-update-slice_fusion.refs_6_), channel_id=1, source_target_pairs={{0,28},{4,0},{8,4},{12,8},{16,12},{20,16},{24,20},{28,24},{1,29},{... | collective-permute-start | bytes 1572872 | tf_op jit(solution)/shard_map/ppermute | solution.py:227
  27.6 0.0 collective-permute-start.4
  27.6 4.2 %collective-permute-done.7 = bf16[128,512]{1,0:T(8,128)(2,1)S(1)} collective-permute-done((bf16[128,512]{1,0:T(8,128)(2,1)S(1)}, bf16[128,512]{1,0:T(8,128)(2,1)S(1)}, u32[]{:S(2)}, u32[]{:S(2)}) %collective-permute-start.7) | collective-permute-done | bytes 131104 | tf_op jit(solution)/shard_map/ppermute | solution.py:227
  31.8 4.5 %collective-permute-done.6 = bf16[128,512]{1,0:T(8,128)(2,1)S(1)} collective-permute-done((bf16[128,512]{1,0:T(8,128)(2,1)S(1)}, bf16[128,512]{1,0:T(8,128)(2,1)S(1)}, u32[]{:S(2)}, u32[]{:S(2)}) %collective-permute-start.6) | collective-permute-done | bytes 131104 | tf_op jit(solution)/shard_map/ppermute | solution.py:227
  36.3 0.0 collective-permute-done.8.refs_3_
  36.3 2.6 %collective-permute-start.11 = (bf16[2,512,256]{2,1,0:T(8,128)(2,1)S(1)}, bf16[2,512,256]{2,1,0:T(8,128)(2,1)S(1)}, u32[]{:S(2)}, u32[]{:S(2)}) collective-permute-start(bf16[2,512,256]{2,1,0:T(8,128)(2,1)S(1)} %collective-permute-done.8.refs_3_), channel_id=1, source_target_pairs={{0,64},{32,224},{64,128},{96,32},{128,192},{160,96},{192,0},{224,1... | collective-permute-start | bytes 1572872 | tf_op jit(solution)/shard_map/ppermute | solution.py:237
  38.9 0.0 collective-permute-start.10
  38.9 0.0 collective-permute-start.9
  38.9 3.6 %collective-permute-done.5.refs_8_ = bf16[512,512]{1,0:T(8,128)(2,1)S(1)} collective-permute-done((bf16[512,512]{1,0:T(8,128)(2,1)S(1)}, bf16[512,512]{1,0:T(8,128)(2,1)S(1)}, u32[]{:S(2)}, u32[]{:S(2)}) %collective-permute-start.5) | collective-permute-done | bytes 524320 | tf_op jit(solution)/shard_map/ppermute | solution.py:227
  42.5 5.4 %collective-permute-done.4.refs_7_ = bf16[512,512]{1,0:T(8,128)(2,1)S(1)} collective-permute-done((bf16[512,512]{1,0:T(8,128)(2,1)S(1)}, bf16[512,512]{1,0:T(8,128)(2,1)S(1)}, u32[]{:S(2)}, u32[]{:S(2)}) %collective-permute-start.4) | collective-permute-done | bytes 524320 | tf_op jit(solution)/shard_map/ppermute | solution.py:227
  48.0 1.7 %collective-permute-done.9 = bf16[128,512]{1,0:T(8,128)(2,1)S(1)} collective-permute-done((bf16[128,512]{1,0:T(8,128)(2,1)S(1)}, bf16[128,512]{1,0:T(8,128)(2,1)S(1)}, u32[]{:S(2)}, u32[]{:S(2)}) %collective-permute-start.9) | collective-permute-done | bytes 131104 | tf_op jit(solution)/shard_map/ppermute | solution.py:227
  49.7 0.0 collective-permute-done.11.refs_5_
  49.7 0.0 collective-permute-done.10.refs_4_
  49.7 0.0 copy-start.9
  49.8 0.0 copy-start.12
  49.8 3.2 %collective-permute-start.15 = (bf16[384,512]{1,0:T(8,128)(2,1)S(1)}, bf16[384,512]{1,0:T(8,128)(2,1)S(1)}, u32[]{:S(2)}, u32[]{:S(2)}) collective-permute-start(bf16[384,512]{1,0:T(8,128)(2,1)S(1)} %constant_dynamic-update-slice_fusion.4.refs_9_), channel_id=1, source_target_pairs={{0,3},{1,0},{2,1},{3,2},{4,7},{5,4},{6,5},{7,6},{8,11},{9,8},{10,9... | collective-permute-start | bytes 1179656 | tf_op jit(solution)/shard_map/ppermute | solution.py:227
  52.9 0.0 collective-permute-start.14
  52.9 0.0 collective-permute-start.12
  52.9 3.2 %collective-permute-start.13 = (bf16[512,512]{1,0:T(8,128)(2,1)S(1)}, bf16[512,512]{1,0:T(8,128)(2,1)S(1)}, u32[]{:S(2)}, u32[]{:S(2)}) collective-permute-start(bf16[512,512]{1,0:T(8,128)(2,1)S(1)} %collective-permute-done.5.refs_8_), channel_id=1, source_target_pairs={{0,28},{4,0},{8,4},{12,8},{16,12},{20,16},{24,20},{28,24},{1,29},{... | collective-permute-start | bytes 1572872 | tf_op jit(solution)/shard_map/ppermute | solution.py:227
  56.2 0.0 copy-done.6
  56.2 0.0 copy-done.13
  56.2 0.0 copy-done.7
  56.2 0.0 copy-done.14
  56.2 0.0 copy-done.15
  56.2 0.0 copy-done.8
  56.2 0.0 copy-done.9
  56.2 0.0 copy-done.12
  56.2 0.0 copy-done.3
  56.2 4.9 %product_first.1.refs_8_ = f32[512,1024]{1,0:T(8,128)S(1)} custom-call(s32[32,64]{1,0:T(8,128)S(1)} %copy-done.3, s32[32,128]{1,0:T(8,128)S(1)} %bitcast.6, bf16[2,512,256]{2,1,0:T(8,128)(2,1)} %copy-done.6, bf16[2,512,256]{2,1,0:T(8,128)(2,1)} %copy-done.7, bf16[2,512,256]{2,1,0:T(8,128)(2,1)} %copy-done.9, bf16[2,512,256]{2,1,0:T(8,128)(2,1)} %copy-done.8, ...), custom_call_target="tpu_custom_call" | custom-call | flops 2013265920 | bytes 4194304 | tf_op jit(solution)/shard_map/product_first/pallas_call | solution.py:200
  61.1 0.0 collective-permute-done.15.refs_7_
  61.1 3.0 %collective-permute-done.14.refs_6_ = bf16[384,512]{1,0:T(8,128)(2,1)S(1)} collective-permute-done((bf16[384,512]{1,0:T(8,128)(2,1)S(1)}, bf16[384,512]{1,0:T(8,128)(2,1)S(1)}, u32[]{:S(2)}, u32[]{:S(2)}) %collective-permute-start.14) | collective-permute-done | bytes 393248 | tf_op jit(solution)/shard_map/ppermute | solution.py:227
  64.2 0.1 collective-permute-start.16
  64.3 3.2 %collective-permute-start.17 = (bf16[192,512]{1,0:T(8,128)(2,1)S(1)}, bf16[192,512]{1,0:T(8,128)(2,1)S(1)}, u32[]{:S(2)}, u32[]{:S(2)}) collective-permute-start(bf16[192,512]{1,0:T(8,128)(2,1)S(1)} %slice.7), channel_id=1, source_target_pairs={{0,3},{1,0},{2,1},{3,2},{4,7},{5,4},{6,5},{7,6},{8,11},{9,8},{10,9... | collective-permute-start | bytes 589832 | tf_op jit(solution)/shard_map/ppermute | solution.py:227
  67.5 2.9 %product_next.1.refs_10_ = f32[512,1024]{1,0:T(8,128)S(1)} custom-call(s32[32,64]{1,0:T(8,128)S(1)} %copy-done.3, s32[32,128]{1,0:T(8,128)S(1)} %bitcast.7, bf16[2,512,256]{2,1,0:T(8,128)(2,1)} %copy-done.6, bf16[2,512,256]{2,1,0:T(8,128)(2,1)} %copy-done.7, bf16[2,512,256]{2,1,0:T(8,128)(2,1)} %copy-done.9, ...), custom_call_target="tpu_custom_call", output_to_operand_aliasing={{}: (8, {})} | custom-call | flops 805306368 | bytes 4194304 | tf_op jit(solution)/shard_map/product_next/pallas_call | solution.py:200
  70.4 0.0 collective-permute-done.12.refs_6_
  70.4 0.0 collective-permute-done.13.refs_7_
  70.4 0.7 collective-permute-done.16.refs_8_
  71.2 0.0 collective-permute-done.17.refs_9_
  71.2 5.2 %product_last.1 = (f32[512,1024]{1,0:T(8,128)S(1)}, f32[1,1024]{1,0:T(1,128)S(1)}) custom-call(s32[32,64]{1,0:T(8,128)S(1)} %copy-done.3, s32[32,128]{1,0:T(8,128)S(1)} %bitcast.8, bf16[2,512,256]{2,1,0:T(8,128)(2,1)} %copy-done.6, bf16[2,512,256]{2,1,0:T(8,128)(2,1)} %copy-done.7, bf16[2,512,256]{2,1,0:T(8,128)(2,1)} %copy-done.9, ...), custom_call_target="tpu_custom_call", output_to_operand_aliasing={{0}: (10, {})} | custom-call | flops 1476395008 | bytes 4194304 | tf_op jit(solution)/shard_map/product_last/pallas_call | solution.py:200
  76.4 0.1 broadcast_in_dim.2
  76.5 16.5 %all_to_all.6 = f32[32,1,1024]{2,1,0:T(1,128)S(1)} all-to-all(f32[32,1,1024]{2,1,0:T(1,128)S(1)} %broadcast_in_dim.2), channel_id=1, replica_groups=mesh['y'=4,'core'=2,'z'=8,'x'=4] {'z','x'}, dimensions={0} | all-to-all | bytes 262144 | tf_op jit(solution)/shard_map/all_to_all | solution.py:281
  92.9 0.1 reduce_sum.9
  93.0 1.5 %broadcast_multiply_fusion = f32[512,1024]{1,0:T(8,128)} fusion(f32[512,1024]{1,0:T(8,128)S(1)} %get-tuple-element.51, f32[1024]{0:T(1024)S(1)} %broadcast_divide_fusion), kind=kLoop, calls=%fused_computation | loop fusion | flops 524288 | bytes 4198400 | tf_op jit(solution)/shard_map/mul | solution.py:284
  (24 shorter events, 0.1 us)
Async XLA Ops:
  0.0 0.9 %copy-start.1 = (bf16[128,1024]{1,0:T(8,128)(2,1)S(1)}, bf16[128,1024]{1,0:T(8,128)(2,1)}, u32[]{:S(2)}) copy-start(bf16[128,1024]{1,0:T(8,128)(2,1)} %right.1) | copy-start | bytes 786436
  1.0 0.7 copy-start.2
  1.7 54.5 %copy-start.3 = (s32[32,64]{1,0:T(8,128)S(1)}, s32[32,64]{1,0:T(8,128)}, u32[]{:S(2)}) copy-start(s32[32,64]{1,0:T(8,128)} %refs_0_.5) | copy-start | bytes 24580
  1.7 54.5 %copy-start.5 = (s32[128,32]{0,1:T(8,128)S(1)}, s32[128,32]{0,1:T(8,128)}, u32[]{:S(2)}) copy-start(s32[128,32]{0,1:T(8,128)} %param.5) | copy-start | bytes 49156
  2.6 1.0 %copy-start = (bf16[512,512]{1,0:T(8,128)(2,1)S(1)}, bf16[512,512]{1,0:T(8,128)(2,1)}, u32[]{:S(2)}) copy-start(bf16[512,512]{1,0:T(8,128)(2,1)} %left) | copy-start | bytes 1572868
  3.6 0.7 copy-start.4
  5.4 10.8 %collective-permute-start.3 = (bf16[512,256]{1,0:T(8,128)(2,1)S(1)}, bf16[512,256]{1,0:T(8,128)(2,1)S(1)}, u32[]{:S(2)}, u32[]{:S(2)}) collective-permute-start(bf16[512,256]{1,0:T(8,128)(2,1)S(1)} %pack_left.1), channel_id=1, source_target_pairs={{0,32},{32,0},{1,33},{33,1},{2,34},{34,2},{3,35},{35,3},{4,36},{36... | collective-permute-start | bytes 786440 | tf_op jit(solution)/shard_map/ppermute | solution.py:227
  5.5 7.9 %collective-permute-start.2 = (bf16[128,512]{1,0:T(8,128)(2,1)S(1)}, bf16[128,512]{1,0:T(8,128)(2,1)S(1)}, u32[]{:S(2)}, u32[]{:S(2)}) collective-permute-start(bf16[128,512]{1,0:T(8,128)(2,1)S(1)} %pack_right.1), channel_id=1, source_target_pairs={{0,2},{1,3},{2,0},{3,1},{4,6},{5,7},{6,4},{7,5},{8,10},{9,11},{10,... | collective-permute-start | bytes 393224 | tf_op jit(solution)/shard_map/ppermute | solution.py:227
  8.6 7.2 %collective-permute-start.1 = (bf16[128,512]{1,0:T(8,128)(2,1)S(1)}, bf16[128,512]{1,0:T(8,128)(2,1)S(1)}, u32[]{:S(2)}, u32[]{:S(2)}) collective-permute-start(bf16[128,512]{1,0:T(8,128)(2,1)S(1)} %pack_right.1), channel_id=1, source_target_pairs={{0,3},{1,0},{2,1},{3,2},{4,7},{5,4},{6,5},{7,6},{8,11},{9,8},{10,9... | collective-permute-start | bytes 393224 | tf_op jit(solution)/shard_map/ppermute | solution.py:227
  9.7 6.5 %collective-permute-start = (bf16[128,512]{1,0:T(8,128)(2,1)S(1)}, bf16[128,512]{1,0:T(8,128)(2,1)S(1)}, u32[]{:S(2)}, u32[]{:S(2)}) collective-permute-start(bf16[128,512]{1,0:T(8,128)(2,1)S(1)} %pack_right.1), channel_id=1, source_target_pairs={{0,1},{1,2},{2,3},{3,0},{4,5},{5,6},{6,7},{7,4},{8,9},{9,10},{10,1... | collective-permute-start | bytes 393224 | tf_op jit(solution)/shard_map/ppermute | solution.py:227
  16.3 39.9 %copy-start.6 = (bf16[2,512,256]{2,1,0:T(8,128)(2,1)}, bf16[2,512,256]{2,1,0:T(8,128)(2,1)S(1)}, u32[]{:S(2)}) copy-start(bf16[2,512,256]{2,1,0:T(8,128)(2,1)S(1)} %pad_maximum_fusion.refs_2_) | copy-start | bytes 1572868
  16.3 20.0 %collective-permute-start.8 = (bf16[2,512,256]{2,1,0:T(8,128)(2,1)S(1)}, bf16[2,512,256]{2,1,0:T(8,128)(2,1)S(1)}, u32[]{:S(2)}, u32[]{:S(2)}) collective-permute-start(bf16[2,512,256]{2,1,0:T(8,128)(2,1)S(1)} %pad_maximum_fusion.refs_2_), channel_id=1, source_target_pairs={{0,64},{32,224},{64,128},{96,32},{128,192},{160,96},{192,0},{224,1... | collective-permute-start | bytes 1572872 | tf_op jit(solution)/shard_map/ppermute | solution.py:237
  17.8 14.0 %collective-permute-start.7 = (bf16[128,512]{1,0:T(8,128)(2,1)S(1)}, bf16[128,512]{1,0:T(8,128)(2,1)S(1)}, u32[]{:S(2)}, u32[]{:S(2)}) collective-permute-start(bf16[128,512]{1,0:T(8,128)(2,1)S(1)} %pack_right.1), channel_id=1, source_target_pairs={{0,20},{4,24},{8,28},{12,0},{16,4},{20,8},{24,12},{28,16},{1,21},{... | collective-permute-start | bytes 393224 | tf_op jit(solution)/shard_map/ppermute | solution.py:227
  23.3 13.0 %collective-permute-start.6 = (bf16[128,512]{1,0:T(8,128)(2,1)S(1)}, bf16[128,512]{1,0:T(8,128)(2,1)S(1)}, u32[]{:S(2)}, u32[]{:S(2)}) collective-permute-start(bf16[128,512]{1,0:T(8,128)(2,1)S(1)} %pack_right.1), channel_id=1, source_target_pairs={{0,12},{4,16},{8,20},{12,24},{16,28},{20,0},{24,4},{28,8},{1,13},{... | collective-permute-start | bytes 393224 | tf_op jit(solution)/shard_map/ppermute | solution.py:227
  23.4 32.8 %copy-start.13 = (bf16[512,512]{1,0:T(8,128)(2,1)}, bf16[512,512]{1,0:T(8,128)(2,1)S(1)}, u32[]{:S(2)}) copy-start(bf16[512,512]{1,0:T(8,128)(2,1)S(1)} %constant_dynamic-update-slice_fusion.refs_6_) | copy-start | bytes 1572868
  23.4 19.2 %collective-permute-start.5 = (bf16[512,512]{1,0:T(8,128)(2,1)S(1)}, bf16[512,512]{1,0:T(8,128)(2,1)S(1)}, u32[]{:S(2)}, u32[]{:S(2)}) collective-permute-start(bf16[512,512]{1,0:T(8,128)(2,1)S(1)} %constant_dynamic-update-slice_fusion.refs_6_), channel_id=1, source_target_pairs={{0,28},{4,0},{8,4},{12,8},{16,12},{20,16},{24,20},{28,24},{1,29},{... | collective-permute-start | bytes 1572872 | tf_op jit(solution)/shard_map/ppermute | solution.py:227
  27.6 20.4 %collective-permute-start.4 = (bf16[512,512]{1,0:T(8,128)(2,1)S(1)}, bf16[512,512]{1,0:T(8,128)(2,1)S(1)}, u32[]{:S(2)}, u32[]{:S(2)}) collective-permute-start(bf16[512,512]{1,0:T(8,128)(2,1)S(1)} %constant_dynamic-update-slice_fusion.refs_6_), channel_id=1, source_target_pairs={{0,4},{4,8},{8,12},{12,16},{16,20},{20,24},{24,28},{28,0},{1,5},{5... | collective-permute-start | bytes 1572872 | tf_op jit(solution)/shard_map/ppermute | solution.py:227
  36.3 19.9 %copy-start.7 = (bf16[2,512,256]{2,1,0:T(8,128)(2,1)}, bf16[2,512,256]{2,1,0:T(8,128)(2,1)S(1)}, u32[]{:S(2)}) copy-start(bf16[2,512,256]{2,1,0:T(8,128)(2,1)S(1)} %collective-permute-done.8.refs_3_) | copy-start | bytes 1572868
  36.3 13.4 %collective-permute-start.11 = (bf16[2,512,256]{2,1,0:T(8,128)(2,1)S(1)}, bf16[2,512,256]{2,1,0:T(8,128)(2,1)S(1)}, u32[]{:S(2)}, u32[]{:S(2)}) collective-permute-start(bf16[2,512,256]{2,1,0:T(8,128)(2,1)S(1)} %collective-permute-done.8.refs_3_), channel_id=1, source_target_pairs={{0,64},{32,224},{64,128},{96,32},{128,192},{160,96},{192,0},{224,1... | collective-permute-start | bytes 1572872 | tf_op jit(solution)/shard_map/ppermute | solution.py:237
  38.9 10.8 %collective-permute-start.10 = (bf16[2,512,256]{2,1,0:T(8,128)(2,1)S(1)}, bf16[2,512,256]{2,1,0:T(8,128)(2,1)S(1)}, u32[]{:S(2)}, u32[]{:S(2)}) collective-permute-start(bf16[2,512,256]{2,1,0:T(8,128)(2,1)S(1)} %collective-permute-done.8.refs_3_), channel_id=1, source_target_pairs={{0,32},{32,0},{1,33},{33,1},{2,34},{34,2},{3,35},{35,3},{4,36},{36... | collective-permute-start | bytes 1572872 | tf_op jit(solution)/shard_map/ppermute | solution.py:227
  38.9 10.7 %collective-permute-start.9 = (bf16[128,512]{1,0:T(8,128)(2,1)S(1)}, bf16[128,512]{1,0:T(8,128)(2,1)S(1)}, u32[]{:S(2)}, u32[]{:S(2)}) collective-permute-start(bf16[128,512]{1,0:T(8,128)(2,1)S(1)} %collective-permute-done.6), channel_id=1, source_target_pairs={{0,4},{4,8},{8,12},{12,16},{16,20},{20,24},{24,28},{28,0},{1,5},{5... | collective-permute-start | bytes 393224 | tf_op jit(solution)/shard_map/ppermute | solution.py:227
  42.5 13.6 %copy-start.14 = (bf16[512,512]{1,0:T(8,128)(2,1)}, bf16[512,512]{1,0:T(8,128)(2,1)S(1)}, u32[]{:S(2)}) copy-start(bf16[512,512]{1,0:T(8,128)(2,1)S(1)} %collective-permute-done.5.refs_8_) | copy-start | bytes 1572868
  48.0 8.2 %copy-start.15 = (bf16[512,512]{1,0:T(8,128)(2,1)}, bf16[512,512]{1,0:T(8,128)(2,1)S(1)}, u32[]{:S(2)}) copy-start(bf16[512,512]{1,0:T(8,128)(2,1)S(1)} %collective-permute-done.4.refs_7_) | copy-start | bytes 1572868
  49.7 6.5 %copy-start.8 = (bf16[2,512,256]{2,1,0:T(8,128)(2,1)}, bf16[2,512,256]{2,1,0:T(8,128)(2,1)S(1)}, u32[]{:S(2)}) copy-start(bf16[2,512,256]{2,1,0:T(8,128)(2,1)S(1)} %collective-permute-done.11.refs_5_) | copy-start | bytes 1572868
  49.7 6.5 %copy-start.9 = (bf16[2,512,256]{2,1,0:T(8,128)(2,1)}, bf16[2,512,256]{2,1,0:T(8,128)(2,1)S(1)}, u32[]{:S(2)}) copy-start(bf16[2,512,256]{2,1,0:T(8,128)(2,1)S(1)} %collective-permute-done.10.refs_4_) | copy-start | bytes 1572868
  49.8 6.4 %copy-start.12 = (bf16[384,512]{1,0:T(8,128)(2,1)}, bf16[384,512]{1,0:T(8,128)(2,1)S(1)}, u32[]{:S(2)}) copy-start(bf16[384,512]{1,0:T(8,128)(2,1)S(1)} %constant_dynamic-update-slice_fusion.4.refs_9_) | copy-start | bytes 1179652
  49.8 11.4 %collective-permute-start.15 = (bf16[384,512]{1,0:T(8,128)(2,1)S(1)}, bf16[384,512]{1,0:T(8,128)(2,1)S(1)}, u32[]{:S(2)}, u32[]{:S(2)}) collective-permute-start(bf16[384,512]{1,0:T(8,128)(2,1)S(1)} %constant_dynamic-update-slice_fusion.4.refs_9_), channel_id=1, source_target_pairs={{0,3},{1,0},{2,1},{3,2},{4,7},{5,4},{6,5},{7,6},{8,11},{9,8},{10,9... | collective-permute-start | bytes 1179656 | tf_op jit(solution)/shard_map/ppermute | solution.py:227
  52.9 11.2 %collective-permute-start.14 = (bf16[384,512]{1,0:T(8,128)(2,1)S(1)}, bf16[384,512]{1,0:T(8,128)(2,1)S(1)}, u32[]{:S(2)}, u32[]{:S(2)}) collective-permute-start(bf16[384,512]{1,0:T(8,128)(2,1)S(1)} %constant_dynamic-update-slice_fusion.4.refs_9_), channel_id=1, source_target_pairs={{0,1},{1,2},{2,3},{3,0},{4,5},{5,6},{6,7},{7,4},{8,9},{9,10},{10,1... | collective-permute-start | bytes 1179656 | tf_op jit(solution)/shard_map/ppermute | solution.py:227
  52.9 17.5 %collective-permute-start.12 = (bf16[512,512]{1,0:T(8,128)(2,1)S(1)}, bf16[512,512]{1,0:T(8,128)(2,1)S(1)}, u32[]{:S(2)}, u32[]{:S(2)}) collective-permute-start(bf16[512,512]{1,0:T(8,128)(2,1)S(1)} %collective-permute-done.4.refs_7_), channel_id=1, source_target_pairs={{0,4},{4,8},{8,12},{12,16},{16,20},{20,24},{24,28},{28,0},{1,5},{5... | collective-permute-start | bytes 1572872 | tf_op jit(solution)/shard_map/ppermute | solution.py:227
  52.9 17.5 %collective-permute-start.13 = (bf16[512,512]{1,0:T(8,128)(2,1)S(1)}, bf16[512,512]{1,0:T(8,128)(2,1)S(1)}, u32[]{:S(2)}, u32[]{:S(2)}) collective-permute-start(bf16[512,512]{1,0:T(8,128)(2,1)S(1)} %collective-permute-done.5.refs_8_), channel_id=1, source_target_pairs={{0,28},{4,0},{8,4},{12,8},{16,12},{20,16},{24,20},{28,24},{1,29},{... | collective-permute-start | bytes 1572872 | tf_op jit(solution)/shard_map/ppermute | solution.py:227
  61.1 6.4 %copy-start.10 = (bf16[384,512]{1,0:T(8,128)(2,1)}, bf16[384,512]{1,0:T(8,128)(2,1)S(1)}, u32[]{:S(2)}) copy-start(bf16[384,512]{1,0:T(8,128)(2,1)S(1)} %collective-permute-done.15.refs_7_) | copy-start | bytes 1179652
  64.2 3.4 %copy-start.11 = (bf16[384,512]{1,0:T(8,128)(2,1)}, bf16[384,512]{1,0:T(8,128)(2,1)S(1)}, u32[]{:S(2)}) copy-start(bf16[384,512]{1,0:T(8,128)(2,1)S(1)} %collective-permute-done.14.refs_6_) | copy-start | bytes 1179652
  64.2 7.0 %collective-permute-start.16 = (bf16[192,512]{1,0:T(8,128)(2,1)S(1)}, bf16[192,512]{1,0:T(8,128)(2,1)S(1)}, u32[]{:S(2)}, u32[]{:S(2)}) collective-permute-start(bf16[192,512]{1,0:T(8,128)(2,1)S(1)} %slice.6), channel_id=1, source_target_pairs={{0,1},{1,2},{2,3},{3,0},{4,5},{5,6},{6,7},{7,4},{8,9},{9,10},{10,1... | collective-permute-start | bytes 589832 | tf_op jit(solution)/shard_map/ppermute | solution.py:227
  64.3 6.9 %collective-permute-start.17 = (bf16[192,512]{1,0:T(8,128)(2,1)S(1)}, bf16[192,512]{1,0:T(8,128)(2,1)S(1)}, u32[]{:S(2)}, u32[]{:S(2)}) collective-permute-start(bf16[192,512]{1,0:T(8,128)(2,1)S(1)} %slice.7), channel_id=1, source_target_pairs={{0,3},{1,0},{2,1},{3,2},{4,7},{5,4},{6,5},{7,6},{8,11},{9,8},{10,9... | collective-permute-start | bytes 589832 | tf_op jit(solution)/shard_map/ppermute | solution.py:227

commit v8 on v6

--- a/solution.py
+++ b/solution.py
@@ -242,36 +242,36 @@
     near = [packed_right] + [moved(packed_right, "x", -shift) for shift in SHIFTS[1:]]
     left_values, _ = lax.optimization_barrier((left_values, packed_right))
     packed_left = pack(pack_left_kernel, "pack_left", left_pattern, left_values, LEFT_SLOTS)
+    near, packed_left = lax.optimization_barrier((near, packed_left))
     other_left = moved(packed_left, "core", 1)
-    near, packed_left, other_left = lax.optimization_barrier((near, packed_left, other_left))
-    own = [jnp.concatenate(near[:2], 0), jnp.concatenate(near[2:], 0)]
-    half = own[0].shape[0]
-    came = {0: own}
+    came = {0: jnp.concatenate(near, 0)}
+    whole = came[0].shape[0]
+    half = whole // 2
 
     def ring(step):
-        came[-step] = [moved(piece, "z", 1) for piece in came[1 - step]]
-        came[step] = [moved(piece, "z", -1) for piece in came[step - 1]]
-
-    def tied(values, step):
-        values, came[-step][0] = lax.optimization_barrier((values, came[-step][0]))
-        return values
-
-    def add(shifts, total, last=False):
+        came[-step] = moved(came[1 - step], "z", 1)
+        came[step] = moved(came[step - 1], "z", -1)
+
+    def add(shifts, total, pieces, last=False):
         blocks = [(shift, x_shift) for shift in shifts for x_shift in SHIFTS]
-        pieces = [piece for shift in shifts for piece in came[shift]]
-        copies = [(n, 0, half, n * half) for n in range(len(pieces))]
+        rows = pieces[0].shape[0]
+        copies = [(n, 0, rows, n * rows) for n in range(len(pieces))]
         return product(blocks, copies, right_pattern, left_pattern, left, pieces, total, last)
 
     ring(1)
     near_left = jnp.stack([packed_left, other_left])
-    sent_left = tied(around(near_left), 1)
+    sent_left = around(near_left)
+    sent_left, came[-1], came[1] = lax.optimization_barrier((sent_left, came[-1], came[1]))
     ring(2)
-    left = tied([near_left, sent_left, moved(sent_left, "core", 1), around(sent_left)], 2)
+    left = [near_left, sent_left, moved(sent_left, "core", 1), around(sent_left)]
+    left, came[-2], came[2] = lax.optimization_barrier((left, came[-2], came[2]))
     ring(3)
-    total = tied(add((0, -1, 1), None)[0], 3)
-    came[4] = [moved(came[-3][0], "z", 1), moved(came[3][1], "z", -1)]
-    (total,) = add((-2, 2, -3, 3), total)
-    total, sums = add((4,), total, True)
+    shifts = (0, -1, 1, -2, 2)
+    (total,) = add(shifts, None, [came[shift] for shift in shifts])
+    total, came[-3], came[3] = lax.optimization_barrier((total, came[-3], came[3]))
+    far = [moved(came[-3][:half], "z", 1), moved(came[3][half:], "z", -1)]
+    (total,) = add((-3, 3), total, [came[-3], came[3]])
+    total, sums = add((4,), total, far, True)
     count = lax.axis_size("z") * lax.axis_size("x")
     spread = lax.all_to_all(
         jnp.broadcast_to(sums, (count, sums.shape[1])), COL, 0, 0, tiled=True

time: 98 us -> 92.1 us (0.940)
  starting transfers between devices: 30.5 us -> 21.5 us
  waiting for transfers between devices: 30.4 us -> 34.1 us
  local copies, waits for them, and re-layouts: 4.96 us -> 3.63 us
  blocking collectives: 15.9 us -> 16.9 us
    ppermute x19 -> x13, starting transfers between devices: 27.4 us -> 21 us  [moved(): lax.ppermute(value, axis, [(i, (i + step) % size) for i in range(size)])]
    ppermute x19 -> x13, waiting for transfers between devices: 30.4 us -> 34.1 us  [moved(): lax.ppermute(value, axis, [(i, (i + step) % size) for i in range(size)])]
    ppermute x2, starting transfers between devices: 3.04 us -> 0.49 us  [around(): return lax.ppermute(value, ('y', 'core'), pairs)]
    unnamed x50 -> x37, local copies, waits for them, and re-layouts: 4.87 us -> 3.51 us
  transfers between devices with their start and end apart: 21 -> 15, of which waited for: 9 -> 7; matrix products, arithmetic and copies ran while one was open for 0% -> 0% of each run, Pallas kernels for 9% -> 11%
where the time goes in v8:
time: 92.1 us; the launch traced here: 91.8 us
  waiting for transfers between devices  34.1 us (37%)
  starting transfers between devices  21.5 us (23%)
  blocking collectives  16.9 us (18%)
  Pallas kernels  13.7 us (15%)
  local copies, waits for them, and re-layouts  3.63 us (4%)
  other arithmetic  1.7 us (2%)
    ppermute x13, waiting for transfers between devices, moved(): lax.ppermute(value, axis, [(i, (i + step) % size) for i in range(size)])  34.1 us
    ppermute x13, starting transfers between devices, moved(): lax.ppermute(value, axis, [(i, (i + step) % size) for i in range(size)])  21 us
    all_to_all x1, blocking collectives, shards(): lax.all_to_all(jnp.broadcast_to(sums, (count, sums.shape[1])), COL, 0, 0,...  16.9 us
    pallas_call x3, Pallas kernels, product(): pl.pallas_call(functools.partial(product_kernel, blocks, copies, total is...  11.8 us
    unnamed x37, local copies, waits for them, and re-layouts  3.51 us
    pallas_call x2, Pallas kernels, pack(): pl.pallas_call(kernel, out_shape=jax.ShapeDtypeStruct((values.shape[0], s...  1.91 us
  transfers between devices with their start and end apart: 15, of which 7 were waited for; matrix products, arithmetic and copies ran while one was open for 0% of the time, Pallas kernels for 11%

profile of v8, /device:TPU:24, one launch (start us, length us, event | category | flops | bytes accessed | tf_op | source)
XLA Modules:
  0.0 91.8 jit_solution(5095219386712337345)
XLA Ops:
  0.0 0.0 copy-start.1
  0.0 0.9 %copy-done.1 = bf16[128,1024]{1,0:T(8,128)(2,1)S(1)} copy-done((bf16[128,1024]{1,0:T(8,128)(2,1)S(1)}, bf16[128,1024]{1,0:T(8,128)(2,1)}, u32[]{:S(2)}) %copy-start.1) | copy-done | bytes 262168
  1.0 0.0 copy-start.2
  1.0 0.7 copy-done.2
  1.7 0.0 copy-start.3
  1.7 0.9 pack_right.1
  2.6 3.1 %collective-permute-start.2 = (bf16[128,512]{1,0:T(8,128)(2,1)S(1)}, bf16[128,512]{1,0:T(8,128)(2,1)S(1)}, u32[]{:S(2)}, u32[]{:S(2)}) collective-permute-start(bf16[128,512]{1,0:T(8,128)(2,1)S(1)} %pack_right.1), channel_id=1, source_target_pairs={{0,2},{1,3},{2,0},{3,1},{4,6},{5,7},{6,4},{7,5},{8,10},{9,11},{10,... | collective-permute-start | bytes 393224 | tf_op jit(solution)/shard_map/ppermute | solution.py:226
  5.7 1.1 %collective-permute-start.1 = (bf16[128,512]{1,0:T(8,128)(2,1)S(1)}, bf16[128,512]{1,0:T(8,128)(2,1)S(1)}, u32[]{:S(2)}, u32[]{:S(2)}) collective-permute-start(bf16[128,512]{1,0:T(8,128)(2,1)S(1)} %pack_right.1), channel_id=1, source_target_pairs={{0,3},{1,0},{2,1},{3,2},{4,7},{5,4},{6,5},{7,6},{8,11},{9,8},{10,9... | collective-permute-start | bytes 393224 | tf_op jit(solution)/shard_map/ppermute | solution.py:226
  6.9 0.9 collective-permute-start
  7.7 1.0 %copy-done = bf16[512,512]{1,0:T(8,128)(2,1)S(1)} copy-done((bf16[512,512]{1,0:T(8,128)(2,1)S(1)}, bf16[512,512]{1,0:T(8,128)(2,1)}, u32[]{:S(2)}) %copy-start) | copy-done | bytes 524312
  8.8 0.7 copy-done.4
  9.5 1.0 %pack_left.1 = bf16[512,256]{1,0:T(8,128)(2,1)S(1)} custom-call(s32[32,128]{1,0:T(8,128)S(1)} %bitcast.5, bf16[512,512]{1,0:T(8,128)(2,1)S(1)} %copy-done), custom_call_target="tpu_custom_call" | custom-call | tf_op jit(solution)/shard_map/pack_left/pallas_call | solution.py:64
  10.5 0.0 collective-permute-done.2
  10.5 1.8 %collective-permute-done.1 = bf16[128,512]{1,0:T(8,128)(2,1)S(1)} collective-permute-done((bf16[128,512]{1,0:T(8,128)(2,1)S(1)}, bf16[128,512]{1,0:T(8,128)(2,1)S(1)}, u32[]{:S(2)}, u32[]{:S(2)}) %collective-permute-start.1) | collective-permute-done | bytes 131104 | tf_op jit(solution)/shard_map/ppermute | solution.py:226
  12.3 0.7 collective-permute-done
  13.0 0.0 collective-permute-start.3
  13.1 0.0 copy-start.12
  13.1 5.9 %collective-permute-start.6 = (bf16[512,512]{1,0:T(8,128)(2,1)S(1)}, bf16[512,512]{1,0:T(8,128)(2,1)S(1)}, u32[]{:S(2)}, u32[]{:S(2)}) collective-permute-start(bf16[512,512]{1,0:T(8,128)(2,1)S(1)} %constant_dynamic-update-slice_fusion.refs_6_), channel_id=1, source_target_pairs={{0,28},{4,0},{8,4},{12,8},{16,12},{20,16},{24,20},{28,24},{1,29},{... | collective-permute-start | bytes 1572872 | tf_op jit(solution)/shard_map/ppermute | solution.py:226
  19.1 0.0 collective-permute-start.5
  19.1 0.0 collective-permute-done.3
  19.1 0.1 pad_maximum_fusion.refs_2_
  19.1 0.0 copy-start.6
  19.1 0.3 collective-permute-start.4
  19.4 11.5 %collective-permute-done.6.refs_8_ = bf16[512,512]{1,0:T(8,128)(2,1)S(1)} collective-permute-done((bf16[512,512]{1,0:T(8,128)(2,1)S(1)}, bf16[512,512]{1,0:T(8,128)(2,1)S(1)}, u32[]{:S(2)}, u32[]{:S(2)}) %collective-permute-start.6) | collective-permute-done | bytes 524320 | tf_op jit(solution)/shard_map/ppermute | solution.py:226
  30.9 3.4 %collective-permute-done.5.refs_7_ = bf16[512,512]{1,0:T(8,128)(2,1)S(1)} collective-permute-done((bf16[512,512]{1,0:T(8,128)(2,1)S(1)}, bf16[512,512]{1,0:T(8,128)(2,1)S(1)}, u32[]{:S(2)}, u32[]{:S(2)}) %collective-permute-start.5) | collective-permute-done | bytes 524320 | tf_op jit(solution)/shard_map/ppermute | solution.py:226
  34.3 0.0 collective-permute-done.4.refs_3_
  34.3 0.1 collective-permute-start.9
  34.4 3.2 %collective-permute-start.10 = (bf16[512,512]{1,0:T(8,128)(2,1)S(1)}, bf16[512,512]{1,0:T(8,128)(2,1)S(1)}, u32[]{:S(2)}, u32[]{:S(2)}) collective-permute-start(bf16[512,512]{1,0:T(8,128)(2,1)S(1)} %collective-permute-done.6.refs_8_), channel_id=1, source_target_pairs={{0,28},{4,0},{8,4},{12,8},{16,12},{20,16},{24,20},{28,24},{1,29},{... | collective-permute-start | bytes 1572872 | tf_op jit(solution)/shard_map/ppermute | solution.py:226
  37.6 0.2 collective-permute-start.8
  37.8 0.0 collective-permute-start.7
  37.8 11.0 %collective-permute-done.9.refs_9_ = bf16[512,512]{1,0:T(8,128)(2,1)S(1)} collective-permute-done((bf16[512,512]{1,0:T(8,128)(2,1)S(1)}, bf16[512,512]{1,0:T(8,128)(2,1)S(1)}, u32[]{:S(2)}, u32[]{:S(2)}) %collective-permute-start.9) | collective-permute-done | bytes 524320 | tf_op jit(solution)/shard_map/ppermute | solution.py:226
  48.8 0.0 collective-permute-done.10.refs_10_
  48.9 0.0 collective-permute-done.8.refs_5_
  48.9 0.0 copy-start.8
  48.9 0.0 collective-permute-done.7.refs_4_
  48.9 0.0 copy-start.9
  48.9 0.1 collective-permute-start.11
  49.0 3.2 %collective-permute-start.12 = (bf16[512,512]{1,0:T(8,128)(2,1)S(1)}, bf16[512,512]{1,0:T(8,128)(2,1)S(1)}, u32[]{:S(2)}, u32[]{:S(2)}) collective-permute-start(bf16[512,512]{1,0:T(8,128)(2,1)S(1)} %collective-permute-done.10.refs_10_), channel_id=1, source_target_pairs={{0,28},{4,0},{8,4},{12,8},{16,12},{20,16},{24,20},{28,24},{1,29},{... | collective-permute-start | bytes 1572872 | tf_op jit(solution)/shard_map/ppermute | solution.py:226
  52.2 0.0 copy-done.12
  52.2 0.0 copy-done.6
  52.2 0.0 copy-done.13
  52.2 0.0 copy-done.14
  52.2 0.0 copy-done.7
  52.2 0.0 copy-done.15
  52.2 0.0 copy-done.16
  52.2 0.0 copy-done.8
  52.3 0.0 copy-done.9
  52.3 0.0 copy-done.3
  52.3 0.0 copy-done.5
  52.3 5.6 %product_first.1.refs_8_ = f32[512,1024]{1,0:T(8,128)S(1)} custom-call(s32[32,64]{1,0:T(8,128)S(1)} %copy-done.3, s32[32,128]{1,0:T(8,128)S(1)} %bitcast.6, bf16[2,512,256]{2,1,0:T(8,128)(2,1)} %copy-done.6, bf16[2,512,256]{2,1,0:T(8,128)(2,1)} %copy-done.7, bf16[2,512,256]{2,1,0:T(8,128)(2,1)} %copy-done.9, bf16[2,512,256]{2,1,0:T(8,128)(2,1)} %copy-done.8, ...), custom_call_target="tpu_custom_call" | custom-call | flops 2684354560 | bytes 4194304 | tf_op jit(solution)/shard_map/product_first/pallas_call | solution.py:199
  57.9 4.6 %collective-permute-done.11.refs_6_ = bf16[512,512]{1,0:T(8,128)(2,1)S(1)} collective-permute-done((bf16[512,512]{1,0:T(8,128)(2,1)S(1)}, bf16[512,512]{1,0:T(8,128)(2,1)S(1)}, u32[]{:S(2)}, u32[]{:S(2)}) %collective-permute-start.11) | collective-permute-done | bytes 524320 | tf_op jit(solution)/shard_map/ppermute | solution.py:226
  62.5 0.0 collective-permute-done.12.refs_7_
  62.5 0.2 collective-permute-start.13
  62.8 3.1 %collective-permute-start.14 = (bf16[256,512]{1,0:T(8,128)(2,1)S(1)}, bf16[256,512]{1,0:T(8,128)(2,1)S(1)}, u32[]{:S(2)}, u32[]{:S(2)}) collective-permute-start(bf16[256,512]{1,0:T(8,128)(2,1)S(1)} %slice.7), channel_id=1, source_target_pairs={{0,28},{4,0},{8,4},{12,8},{16,12},{20,16},{24,20},{28,24},{1,29},{... | collective-permute-start | bytes 786440 | tf_op jit(solution)/shard_map/ppermute | solution.py:226
  65.9 0.0 copy-done.10
  65.9 0.0 copy-done.11
  65.9 3.2 %product_next.1.refs_8_ = f32[512,1024]{1,0:T(8,128)S(1)} custom-call(s32[32,64]{1,0:T(8,128)S(1)} %copy-done.3, s32[32,128]{1,0:T(8,128)S(1)} %bitcast.7, bf16[2,512,256]{2,1,0:T(8,128)(2,1)} %copy-done.6, bf16[2,512,256]{2,1,0:T(8,128)(2,1)} %copy-done.7, bf16[2,512,256]{2,1,0:T(8,128)(2,1)} %copy-done.9, ...), custom_call_target="tpu_custom_call", output_to_operand_aliasing={{}: (8, {})} | custom-call | flops 1073741824 | bytes 4194304 | tf_op jit(solution)/shard_map/product_next/pallas_call | solution.py:199
  69.1 1.1 %collective-permute-done.13.refs_6_ = bf16[256,512]{1,0:T(8,128)(2,1)S(1)} collective-permute-done((bf16[256,512]{1,0:T(8,128)(2,1)S(1)}, bf16[256,512]{1,0:T(8,128)(2,1)S(1)}, u32[]{:S(2)}, u32[]{:S(2)}) %collective-permute-start.13) | collective-permute-done | bytes 262176 | tf_op jit(solution)/shard_map/ppermute | solution.py:226
  70.2 0.0 collective-permute-done.14.refs_7_
  70.2 3.0 %product_last.1 = (f32[512,1024]{1,0:T(8,128)S(1)}, f32[1,1024]{1,0:T(1,128)S(1)}) custom-call(s32[32,64]{1,0:T(8,128)S(1)} %copy-done.3, s32[32,128]{1,0:T(8,128)S(1)} %bitcast.8, bf16[2,512,256]{2,1,0:T(8,128)(2,1)} %copy-done.6, bf16[2,512,256]{2,1,0:T(8,128)(2,1)} %copy-done.7, bf16[2,512,256]{2,1,0:T(8,128)(2,1)} %copy-done.9, ...), custom_call_target="tpu_custom_call", output_to_operand_aliasing={{0}: (8, {})} | custom-call | flops 536870912 | bytes 4194304 | tf_op jit(solution)/shard_map/product_last/pallas_call | solution.py:199
  73.2 0.1 broadcast_in_dim.2
  73.3 16.9 %all_to_all.6 = f32[32,1,1024]{2,1,0:T(1,128)S(1)} all-to-all(f32[32,1,1024]{2,1,0:T(1,128)S(1)} %broadcast_in_dim.2), channel_id=1, replica_groups=mesh['y'=4,'core'=2,'z'=8,'x'=4] {'z','x'}, dimensions={0} | all-to-all | bytes 262144 | tf_op jit(solution)/shard_map/all_to_all | solution.py:276
  90.1 0.1 reduce_sum.9
  90.2 1.5 %broadcast_multiply_fusion = f32[512,1024]{1,0:T(8,128)} fusion(f32[512,1024]{1,0:T(8,128)S(1)} %get-tuple-element.43, f32[1024]{0:T(1024)S(1)} %broadcast_divide_fusion), kind=kLoop, calls=%fused_computation | loop fusion | flops 524288 | bytes 4198400 | tf_op jit(solution)/shard_map/mul | solution.py:279
  (17 shorter events, 0.1 us)
Async XLA Ops:
  0.0 0.9 %copy-start.1 = (bf16[128,1024]{1,0:T(8,128)(2,1)S(1)}, bf16[128,1024]{1,0:T(8,128)(2,1)}, u32[]{:S(2)}) copy-start(bf16[128,1024]{1,0:T(8,128)(2,1)} %right.1) | copy-start | bytes 786436
  1.0 0.7 copy-start.2
  1.7 50.6 %copy-start.3 = (s32[32,64]{1,0:T(8,128)S(1)}, s32[32,64]{1,0:T(8,128)}, u32[]{:S(2)}) copy-start(s32[32,64]{1,0:T(8,128)} %refs_0_.5) | copy-start | bytes 24580
  1.7 50.6 %copy-start.5 = (s32[128,32]{0,1:T(8,128)S(1)}, s32[128,32]{0,1:T(8,128)}, u32[]{:S(2)}) copy-start(s32[128,32]{0,1:T(8,128)} %param.5) | copy-start | bytes 49156
  2.6 7.9 %collective-permute-start.2 = (bf16[128,512]{1,0:T(8,128)(2,1)S(1)}, bf16[128,512]{1,0:T(8,128)(2,1)S(1)}, u32[]{:S(2)}, u32[]{:S(2)}) collective-permute-start(bf16[128,512]{1,0:T(8,128)(2,1)S(1)} %pack_right.1), channel_id=1, source_target_pairs={{0,2},{1,3},{2,0},{3,1},{4,6},{5,7},{6,4},{7,5},{8,10},{9,11},{10,... | collective-permute-start | bytes 393224 | tf_op jit(solution)/shard_map/ppermute | solution.py:226
  5.7 6.6 %collective-permute-start.1 = (bf16[128,512]{1,0:T(8,128)(2,1)S(1)}, bf16[128,512]{1,0:T(8,128)(2,1)S(1)}, u32[]{:S(2)}, u32[]{:S(2)}) collective-permute-start(bf16[128,512]{1,0:T(8,128)(2,1)S(1)} %pack_right.1), channel_id=1, source_target_pairs={{0,3},{1,0},{2,1},{3,2},{4,7},{5,4},{6,5},{7,6},{8,11},{9,8},{10,9... | collective-permute-start | bytes 393224 | tf_op jit(solution)/shard_map/ppermute | solution.py:226
  6.9 6.2 %collective-permute-start = (bf16[128,512]{1,0:T(8,128)(2,1)S(1)}, bf16[128,512]{1,0:T(8,128)(2,1)S(1)}, u32[]{:S(2)}, u32[]{:S(2)}) collective-permute-start(bf16[128,512]{1,0:T(8,128)(2,1)S(1)} %pack_right.1), channel_id=1, source_target_pairs={{0,1},{1,2},{2,3},{3,0},{4,5},{5,6},{6,7},{7,4},{8,9},{9,10},{10,1... | collective-permute-start | bytes 393224 | tf_op jit(solution)/shard_map/ppermute | solution.py:226
  7.7 1.0 %copy-start = (bf16[512,512]{1,0:T(8,128)(2,1)S(1)}, bf16[512,512]{1,0:T(8,128)(2,1)}, u32[]{:S(2)}) copy-start(bf16[512,512]{1,0:T(8,128)(2,1)} %left) | copy-start | bytes 1572868
  8.8 0.7 copy-start.4
  13.0 6.0 %collective-permute-start.3 = (bf16[512,256]{1,0:T(8,128)(2,1)S(1)}, bf16[512,256]{1,0:T(8,128)(2,1)S(1)}, u32[]{:S(2)}, u32[]{:S(2)}) collective-permute-start(bf16[512,256]{1,0:T(8,128)(2,1)S(1)} %pack_left.1), channel_id=1, source_target_pairs={{0,32},{32,0},{1,33},{33,1},{2,34},{34,2},{3,35},{35,3},{4,36},{36... | collective-permute-start | bytes 786440 | tf_op jit(solution)/shard_map/ppermute | solution.py:226
  13.1 39.1 %copy-start.12 = (bf16[512,512]{1,0:T(8,128)(2,1)}, bf16[512,512]{1,0:T(8,128)(2,1)S(1)}, u32[]{:S(2)}) copy-start(bf16[512,512]{1,0:T(8,128)(2,1)S(1)} %constant_dynamic-update-slice_fusion.refs_6_) | copy-start | bytes 1572868
  13.1 17.8 %collective-permute-start.6 = (bf16[512,512]{1,0:T(8,128)(2,1)S(1)}, bf16[512,512]{1,0:T(8,128)(2,1)S(1)}, u32[]{:S(2)}, u32[]{:S(2)}) collective-permute-start(bf16[512,512]{1,0:T(8,128)(2,1)S(1)} %constant_dynamic-update-slice_fusion.refs_6_), channel_id=1, source_target_pairs={{0,28},{4,0},{8,4},{12,8},{16,12},{20,16},{24,20},{28,24},{1,29},{... | collective-permute-start | bytes 1572872 | tf_op jit(solution)/shard_map/ppermute | solution.py:226
  19.1 15.3 %collective-permute-start.5 = (bf16[512,512]{1,0:T(8,128)(2,1)S(1)}, bf16[512,512]{1,0:T(8,128)(2,1)S(1)}, u32[]{:S(2)}, u32[]{:S(2)}) collective-permute-start(bf16[512,512]{1,0:T(8,128)(2,1)S(1)} %constant_dynamic-update-slice_fusion.refs_6_), channel_id=1, source_target_pairs={{0,4},{4,8},{8,12},{12,16},{16,20},{20,24},{24,28},{28,0},{1,5},{5... | collective-permute-start | bytes 1572872 | tf_op jit(solution)/shard_map/ppermute | solution.py:226
  19.1 33.1 %copy-start.6 = (bf16[2,512,256]{2,1,0:T(8,128)(2,1)}, bf16[2,512,256]{2,1,0:T(8,128)(2,1)S(1)}, u32[]{:S(2)}) copy-start(bf16[2,512,256]{2,1,0:T(8,128)(2,1)S(1)} %pad_maximum_fusion.refs_2_) | copy-start | bytes 1572868
  19.1 15.2 %collective-permute-start.4 = (bf16[2,512,256]{2,1,0:T(8,128)(2,1)S(1)}, bf16[2,512,256]{2,1,0:T(8,128)(2,1)S(1)}, u32[]{:S(2)}, u32[]{:S(2)}) collective-permute-start(bf16[2,512,256]{2,1,0:T(8,128)(2,1)S(1)} %pad_maximum_fusion.refs_2_), channel_id=1, source_target_pairs={{0,64},{32,224},{64,128},{96,32},{128,192},{160,96},{192,0},{224,1... | collective-permute-start | bytes 1572872 | tf_op jit(solution)/shard_map/ppermute | solution.py:236
  30.9 21.3 %copy-start.13 = (bf16[512,512]{1,0:T(8,128)(2,1)}, bf16[512,512]{1,0:T(8,128)(2,1)S(1)}, u32[]{:S(2)}) copy-start(bf16[512,512]{1,0:T(8,128)(2,1)S(1)} %collective-permute-done.6.refs_8_) | copy-start | bytes 1572868
  34.3 17.9 %copy-start.14 = (bf16[512,512]{1,0:T(8,128)(2,1)}, bf16[512,512]{1,0:T(8,128)(2,1)S(1)}, u32[]{:S(2)}) copy-start(bf16[512,512]{1,0:T(8,128)(2,1)S(1)} %collective-permute-done.5.refs_7_) | copy-start | bytes 1572868
  34.3 17.9 %copy-start.7 = (bf16[2,512,256]{2,1,0:T(8,128)(2,1)}, bf16[2,512,256]{2,1,0:T(8,128)(2,1)S(1)}, u32[]{:S(2)}) copy-start(bf16[2,512,256]{2,1,0:T(8,128)(2,1)S(1)} %collective-permute-done.4.refs_3_) | copy-start | bytes 1572868
  34.3 14.5 %collective-permute-start.9 = (bf16[512,512]{1,0:T(8,128)(2,1)S(1)}, bf16[512,512]{1,0:T(8,128)(2,1)S(1)}, u32[]{:S(2)}, u32[]{:S(2)}) collective-permute-start(bf16[512,512]{1,0:T(8,128)(2,1)S(1)} %collective-permute-done.5.refs_7_), channel_id=1, source_target_pairs={{0,4},{4,8},{8,12},{12,16},{16,20},{20,24},{24,28},{28,0},{1,5},{5... | collective-permute-start | bytes 1572872 | tf_op jit(solution)/shard_map/ppermute | solution.py:226
  34.4 14.4 %collective-permute-start.10 = (bf16[512,512]{1,0:T(8,128)(2,1)S(1)}, bf16[512,512]{1,0:T(8,128)(2,1)S(1)}, u32[]{:S(2)}, u32[]{:S(2)}) collective-permute-start(bf16[512,512]{1,0:T(8,128)(2,1)S(1)} %collective-permute-done.6.refs_8_), channel_id=1, source_target_pairs={{0,28},{4,0},{8,4},{12,8},{16,12},{20,16},{24,20},{28,24},{1,29},{... | collective-permute-start | bytes 1572872 | tf_op jit(solution)/shard_map/ppermute | solution.py:226
  37.6 11.2 %collective-permute-start.8 = (bf16[2,512,256]{2,1,0:T(8,128)(2,1)S(1)}, bf16[2,512,256]{2,1,0:T(8,128)(2,1)S(1)}, u32[]{:S(2)}, u32[]{:S(2)}) collective-permute-start(bf16[2,512,256]{2,1,0:T(8,128)(2,1)S(1)} %collective-permute-done.4.refs_3_), channel_id=1, source_target_pairs={{0,64},{32,224},{64,128},{96,32},{128,192},{160,96},{192,0},{224,1... | collective-permute-start | bytes 1572872 | tf_op jit(solution)/shard_map/ppermute | solution.py:236
  37.8 11.0 %collective-permute-start.7 = (bf16[2,512,256]{2,1,0:T(8,128)(2,1)S(1)}, bf16[2,512,256]{2,1,0:T(8,128)(2,1)S(1)}, u32[]{:S(2)}, u32[]{:S(2)}) collective-permute-start(bf16[2,512,256]{2,1,0:T(8,128)(2,1)S(1)} %collective-permute-done.4.refs_3_), channel_id=1, source_target_pairs={{0,32},{32,0},{1,33},{33,1},{2,34},{34,2},{3,35},{35,3},{4,36},{36... | collective-permute-start | bytes 1572872 | tf_op jit(solution)/shard_map/ppermute | solution.py:226
  48.8 3.4 %copy-start.15 = (bf16[512,512]{1,0:T(8,128)(2,1)}, bf16[512,512]{1,0:T(8,128)(2,1)S(1)}, u32[]{:S(2)}) copy-start(bf16[512,512]{1,0:T(8,128)(2,1)S(1)} %collective-permute-done.9.refs_9_) | copy-start | bytes 1572868
  48.8 3.4 %copy-start.16 = (bf16[512,512]{1,0:T(8,128)(2,1)}, bf16[512,512]{1,0:T(8,128)(2,1)S(1)}, u32[]{:S(2)}) copy-start(bf16[512,512]{1,0:T(8,128)(2,1)S(1)} %collective-permute-done.10.refs_10_) | copy-start | bytes 1572868
  48.9 3.4 %copy-start.8 = (bf16[2,512,256]{2,1,0:T(8,128)(2,1)}, bf16[2,512,256]{2,1,0:T(8,128)(2,1)S(1)}, u32[]{:S(2)}) copy-start(bf16[2,512,256]{2,1,0:T(8,128)(2,1)S(1)} %collective-permute-done.8.refs_5_) | copy-start | bytes 1572868
  48.9 3.4 %copy-start.9 = (bf16[2,512,256]{2,1,0:T(8,128)(2,1)}, bf16[2,512,256]{2,1,0:T(8,128)(2,1)S(1)}, u32[]{:S(2)}) copy-start(bf16[2,512,256]{2,1,0:T(8,128)(2,1)S(1)} %collective-permute-done.7.refs_4_) | copy-start | bytes 1572868
  48.9 13.6 %collective-permute-start.11 = (bf16[512,512]{1,0:T(8,128)(2,1)S(1)}, bf16[512,512]{1,0:T(8,128)(2,1)S(1)}, u32[]{:S(2)}, u32[]{:S(2)}) collective-permute-start(bf16[512,512]{1,0:T(8,128)(2,1)S(1)} %collective-permute-done.9.refs_9_), channel_id=1, source_target_pairs={{0,4},{4,8},{8,12},{12,16},{16,20},{20,24},{24,28},{28,0},{1,5},{5... | collective-permute-start | bytes 1572872 | tf_op jit(solution)/shard_map/ppermute | solution.py:226
  49.0 13.5 %collective-permute-start.12 = (bf16[512,512]{1,0:T(8,128)(2,1)S(1)}, bf16[512,512]{1,0:T(8,128)(2,1)S(1)}, u32[]{:S(2)}, u32[]{:S(2)}) collective-permute-start(bf16[512,512]{1,0:T(8,128)(2,1)S(1)} %collective-permute-done.10.refs_10_), channel_id=1, source_target_pairs={{0,28},{4,0},{8,4},{12,8},{16,12},{20,16},{24,20},{28,24},{1,29},{... | collective-permute-start | bytes 1572872 | tf_op jit(solution)/shard_map/ppermute | solution.py:226
  62.5 3.4 %copy-start.10 = (bf16[512,512]{1,0:T(8,128)(2,1)}, bf16[512,512]{1,0:T(8,128)(2,1)S(1)}, u32[]{:S(2)}) copy-start(bf16[512,512]{1,0:T(8,128)(2,1)S(1)} %collective-permute-done.11.refs_6_) | copy-start | bytes 1572868
  62.5 3.4 %copy-start.11 = (bf16[512,512]{1,0:T(8,128)(2,1)}, bf16[512,512]{1,0:T(8,128)(2,1)S(1)}, u32[]{:S(2)}) copy-start(bf16[512,512]{1,0:T(8,128)(2,1)S(1)} %collective-permute-done.12.refs_7_) | copy-start | bytes 1572868
  62.5 7.7 %collective-permute-start.13 = (bf16[256,512]{1,0:T(8,128)(2,1)S(1)}, bf16[256,512]{1,0:T(8,128)(2,1)S(1)}, u32[]{:S(2)}, u32[]{:S(2)}) collective-permute-start(bf16[256,512]{1,0:T(8,128)(2,1)S(1)} %slice.6), channel_id=1, source_target_pairs={{0,4},{4,8},{8,12},{12,16},{16,20},{20,24},{24,28},{28,0},{1,5},{5... | collective-permute-start | bytes 786440 | tf_op jit(solution)/shard_map/ppermute | solution.py:226
  62.8 7.4 %collective-permute-start.14 = (bf16[256,512]{1,0:T(8,128)(2,1)S(1)}, bf16[256,512]{1,0:T(8,128)(2,1)S(1)}, u32[]{:S(2)}, u32[]{:S(2)}) collective-permute-start(bf16[256,512]{1,0:T(8,128)(2,1)S(1)} %slice.7), channel_id=1, source_target_pairs={{0,28},{4,0},{8,4},{12,8},{16,12},{20,16},{24,20},{28,24},{1,29},{... | collective-permute-start | bytes 786440 | tf_op jit(solution)/shard_map/ppermute | solution.py:226

commit v9 on v8

--- a/solution.py
+++ b/solution.py
@@ -28,10 +28,18 @@
     return lax.axis_index("z") * lax.axis_size("x") + lax.axis_index("x")
 
 
-def pack_right_kernel(pattern, right, out):
+def pack_right_kernel(pattern_hbm, right_hbm, out, pattern, right, sem):
+    copies = [
+        pltpu.make_async_copy(pattern_hbm, pattern, sem.at[0]),
+        pltpu.make_async_copy(right_hbm, right, sem.at[1]),
+    ]
+    for copy in copies:
+        copy.start()
     row, col = row_index(), col_index()
     col_blocks = right.shape[1] // BLOCK
     out[...] = jnp.zeros_like(out)
+    for copy in copies:
+        copy.wait()
     slot = jnp.int32(0)
     for j in range(col_blocks):
         present = pattern[col, row * col_blocks + j]
@@ -41,6 +49,25 @@
             out[:, lanes(slot)] = right[:, j * BLOCK : (j + 1) * BLOCK]
 
         slot = slot + present
+
+
+def pack_right(pattern, values):
+    pattern, values = [
+        pltpu.with_memory_space_constraint(value, pltpu.HBM) for value in (pattern, values)
+    ]
+    return pl.pallas_call(
+        pack_right_kernel,
+        out_shape=jax.ShapeDtypeStruct((values.shape[0], SLOTS * BLOCK), values.dtype),
+        in_specs=[pl.BlockSpec(memory_space=pl.ANY)] * 2,
+        out_specs=pl.BlockSpec(memory_space=pltpu.VMEM),
+        scratch_shapes=[
+            pltpu.SMEM(pattern.shape, pattern.dtype),
+            pltpu.VMEM(values.shape, values.dtype),
+            pltpu.SemaphoreType.DMA((2,)),
+        ],
+        compiler_params=pltpu.CompilerParams(vmem_limit_bytes=4 * 1024 * 1024),
+        name="pack_right",
+    )(pattern, values)
 
 
 def pack_left_kernel(pattern, left, out):
@@ -238,7 +265,7 @@
 
 def shards(left_values, left_pattern, right_values, right_pattern):
     left_pattern = left_pattern.T
-    packed_right = pack(pack_right_kernel, "pack_right", right_pattern, right_values, SLOTS)
+    packed_right = pack_right(right_pattern, right_values)
     near = [packed_right] + [moved(packed_right, "x", -shift) for shift in SHIFTS[1:]]
     left_values, _ = lax.optimization_barrier((left_values, packed_right))
     packed_left = pack(pack_left_kernel, "pack_left", left_pattern, left_values, LEFT_SLOTS)

time: 92.1 us -> 90.6 us (0.984)
  local copies, waits for them, and re-layouts: 3.63 us -> 1.96 us
    unnamed x37 -> x33, local copies, waits for them, and re-layouts: 3.51 us -> 1.84 us
    pallas_call x0 -> x1, Pallas kernels: none -> 1.18 us  [pack_right(): pl.pallas_call(pack_right_kernel, out_shape=jax.ShapeDtypeStruct((values....]
    pallas_call x2 -> x1, Pallas kernels: 1.91 us -> 1 us  [pack(): pl.pallas_call(kernel, out_shape=jax.ShapeDtypeStruct((values.shape[0], s...]
where the time goes in v9:
time: 90.6 us; the launch traced here: 90.4 us
  waiting for transfers between devices  34.1 us (38%)
  starting transfers between devices  21.5 us (24%)
  blocking collectives  16.9 us (19%)
  Pallas kernels  14 us (15%)
  local copies, waits for them, and re-layouts  1.96 us (2%)
  other arithmetic  1.7 us (2%)
    ppermute x13, waiting for transfers between devices, moved(): lax.ppermute(value, axis, [(i, (i + step) % size) for i in range(size)])  34.1 us
    ppermute x13, starting transfers between devices, moved(): lax.ppermute(value, axis, [(i, (i + step) % size) for i in range(size)])  21 us
    all_to_all x1, blocking collectives, shards(): lax.all_to_all(jnp.broadcast_to(sums, (count, sums.shape[1])), COL, 0, 0,...  16.9 us
    pallas_call x3, Pallas kernels, product(): pl.pallas_call(functools.partial(product_kernel, blocks, copies, total is...  11.8 us
    unnamed x33, local copies, waits for them, and re-layouts  1.84 us
  transfers between devices with their start and end apart: 15, of which 7 were waited for; matrix products, arithmetic and copies ran while one was open for 0% of the time, Pallas kernels for 11%

profile of v9, /device:TPU:24, one launch (start us, length us, event | category | flops | bytes accessed | tf_op | source)
XLA Modules:
  0.0 90.4 jit_solution(7759165267720350089)
XLA Ops:
  0.0 0.0 copy-start.1
  0.0 0.0 copy-start.3
  0.0 1.2 %pack_right.1 = bf16[128,512]{1,0:T(8,128)(2,1)S(1)} custom-call(s32[32,64]{1,0:T(8,128)} %refs_0_.5, bf16[128,1024]{1,0:T(8,128)(2,1)} %right_hbm.1), custom_call_target="tpu_custom_call" | custom-call | tf_op jit(solution)/shard_map/pack_right/pallas_call | solution.py:58
  1.2 3.1 %collective-permute-start.2 = (bf16[128,512]{1,0:T(8,128)(2,1)S(1)}, bf16[128,512]{1,0:T(8,128)(2,1)S(1)}, u32[]{:S(2)}, u32[]{:S(2)}) collective-permute-start(bf16[128,512]{1,0:T(8,128)(2,1)S(1)} %pack_right.1), channel_id=1, source_target_pairs={{0,2},{1,3},{2,0},{3,1},{4,6},{5,7},{6,4},{7,5},{8,10},{9,11},{10,... | collective-permute-start | bytes 393224 | tf_op jit(solution)/shard_map/ppermute | solution.py:253
  4.3 1.1 %collective-permute-start.1 = (bf16[128,512]{1,0:T(8,128)(2,1)S(1)}, bf16[128,512]{1,0:T(8,128)(2,1)S(1)}, u32[]{:S(2)}, u32[]{:S(2)}) collective-permute-start(bf16[128,512]{1,0:T(8,128)(2,1)S(1)} %pack_right.1), channel_id=1, source_target_pairs={{0,3},{1,0},{2,1},{3,2},{4,7},{5,4},{6,5},{7,6},{8,11},{9,8},{10,9... | collective-permute-start | bytes 393224 | tf_op jit(solution)/shard_map/ppermute | solution.py:253
  5.4 0.9 collective-permute-start
  6.3 1.0 %copy-done = bf16[512,512]{1,0:T(8,128)(2,1)S(1)} copy-done((bf16[512,512]{1,0:T(8,128)(2,1)S(1)}, bf16[512,512]{1,0:T(8,128)(2,1)}, u32[]{:S(2)}) %copy-start) | copy-done | bytes 524312
  7.4 0.0 copy-start.2
  7.4 0.7 copy-done.2
  8.1 1.0 %pack_left.1 = bf16[512,256]{1,0:T(8,128)(2,1)S(1)} custom-call(s32[32,128]{1,0:T(8,128)S(1)} %bitcast.5, bf16[512,512]{1,0:T(8,128)(2,1)S(1)} %copy-done), custom_call_target="tpu_custom_call" | custom-call | tf_op jit(solution)/shard_map/pack_left/pallas_call | solution.py:91
  9.1 0.0 collective-permute-done.2
  9.1 1.8 %collective-permute-done.1 = bf16[128,512]{1,0:T(8,128)(2,1)S(1)} collective-permute-done((bf16[128,512]{1,0:T(8,128)(2,1)S(1)}, bf16[128,512]{1,0:T(8,128)(2,1)S(1)}, u32[]{:S(2)}, u32[]{:S(2)}) %collective-permute-start.1) | collective-permute-done | bytes 131104 | tf_op jit(solution)/shard_map/ppermute | solution.py:253
  10.9 0.7 collective-permute-done
  11.6 0.0 collective-permute-start.3
  11.7 0.0 copy-start.10
  11.7 5.9 %collective-permute-start.6 = (bf16[512,512]{1,0:T(8,128)(2,1)S(1)}, bf16[512,512]{1,0:T(8,128)(2,1)S(1)}, u32[]{:S(2)}, u32[]{:S(2)}) collective-permute-start(bf16[512,512]{1,0:T(8,128)(2,1)S(1)} %constant_dynamic-update-slice_fusion.refs_6_), channel_id=1, source_target_pairs={{0,28},{4,0},{8,4},{12,8},{16,12},{20,16},{24,20},{28,24},{1,29},{... | collective-permute-start | bytes 1572872 | tf_op jit(solution)/shard_map/ppermute | solution.py:253
  17.6 0.0 collective-permute-start.5
  17.6 0.0 collective-permute-done.3
  17.6 0.1 pad_maximum_fusion.refs_2_
  17.7 0.0 copy-start.4
  17.7 0.3 collective-permute-start.4
  18.0 11.5 %collective-permute-done.6.refs_8_ = bf16[512,512]{1,0:T(8,128)(2,1)S(1)} collective-permute-done((bf16[512,512]{1,0:T(8,128)(2,1)S(1)}, bf16[512,512]{1,0:T(8,128)(2,1)S(1)}, u32[]{:S(2)}, u32[]{:S(2)}) %collective-permute-start.6) | collective-permute-done | bytes 524320 | tf_op jit(solution)/shard_map/ppermute | solution.py:253
  29.5 0.0 copy-start.11
  29.5 3.4 %collective-permute-done.5.refs_7_ = bf16[512,512]{1,0:T(8,128)(2,1)S(1)} collective-permute-done((bf16[512,512]{1,0:T(8,128)(2,1)S(1)}, bf16[512,512]{1,0:T(8,128)(2,1)S(1)}, u32[]{:S(2)}, u32[]{:S(2)}) %collective-permute-start.5) | collective-permute-done | bytes 524320 | tf_op jit(solution)/shard_map/ppermute | solution.py:253
  32.9 0.0 copy-start.12
  32.9 0.0 collective-permute-done.4.refs_3_
  32.9 0.1 collective-permute-start.9
  33.0 3.2 %collective-permute-start.10 = (bf16[512,512]{1,0:T(8,128)(2,1)S(1)}, bf16[512,512]{1,0:T(8,128)(2,1)S(1)}, u32[]{:S(2)}, u32[]{:S(2)}) collective-permute-start(bf16[512,512]{1,0:T(8,128)(2,1)S(1)} %collective-permute-done.6.refs_8_), channel_id=1, source_target_pairs={{0,28},{4,0},{8,4},{12,8},{16,12},{20,16},{24,20},{28,24},{1,29},{... | collective-permute-start | bytes 1572872 | tf_op jit(solution)/shard_map/ppermute | solution.py:253
  36.2 0.2 collective-permute-start.8
  36.4 0.0 collective-permute-start.7
  36.4 11.0 %collective-permute-done.9.refs_9_ = bf16[512,512]{1,0:T(8,128)(2,1)S(1)} collective-permute-done((bf16[512,512]{1,0:T(8,128)(2,1)S(1)}, bf16[512,512]{1,0:T(8,128)(2,1)S(1)}, u32[]{:S(2)}, u32[]{:S(2)}) %collective-permute-start.9) | collective-permute-done | bytes 524320 | tf_op jit(solution)/shard_map/ppermute | solution.py:253
  47.4 0.0 collective-permute-done.10.refs_10_
  47.4 0.0 collective-permute-done.8.refs_5_
  47.4 0.0 copy-start.6
  47.4 0.0 collective-permute-done.7.refs_4_
  47.5 0.0 copy-start.7
  47.5 0.1 collective-permute-start.11
  47.6 3.2 %collective-permute-start.12 = (bf16[512,512]{1,0:T(8,128)(2,1)S(1)}, bf16[512,512]{1,0:T(8,128)(2,1)S(1)}, u32[]{:S(2)}, u32[]{:S(2)}) collective-permute-start(bf16[512,512]{1,0:T(8,128)(2,1)S(1)} %collective-permute-done.10.refs_10_), channel_id=1, source_target_pairs={{0,28},{4,0},{8,4},{12,8},{16,12},{20,16},{24,20},{28,24},{1,29},{... | collective-permute-start | bytes 1572872 | tf_op jit(solution)/shard_map/ppermute | solution.py:253
  50.8 0.0 copy-done.10
  50.8 0.0 copy-done.4
  50.8 0.0 copy-done.11
  50.8 0.0 copy-done.12
  50.8 0.0 copy-done.5
  50.8 0.0 copy-done.13
  50.8 0.0 copy-done.14
  50.8 0.0 copy-done.6
  50.8 0.0 copy-done.7
  50.8 0.0 copy-done.1
  50.9 0.0 copy-done.3
  50.9 5.6 %product_first.1.refs_8_ = f32[512,1024]{1,0:T(8,128)S(1)} custom-call(s32[32,64]{1,0:T(8,128)S(1)} %copy-done.1, s32[32,128]{1,0:T(8,128)S(1)} %bitcast.6, bf16[2,512,256]{2,1,0:T(8,128)(2,1)} %copy-done.4, bf16[2,512,256]{2,1,0:T(8,128)(2,1)} %copy-done.5, bf16[2,512,256]{2,1,0:T(8,128)(2,1)} %copy-done.7, bf16[2,512,256]{2,1,0:T(8,128)(2,1)} %copy-done.6, ...), custom_call_target="tpu_custom_call" | custom-call | flops 2684354560 | bytes 4194304 | tf_op jit(solution)/shard_map/product_first/pallas_call | solution.py:226
  56.5 4.6 %collective-permute-done.11.refs_6_ = bf16[512,512]{1,0:T(8,128)(2,1)S(1)} collective-permute-done((bf16[512,512]{1,0:T(8,128)(2,1)S(1)}, bf16[512,512]{1,0:T(8,128)(2,1)S(1)}, u32[]{:S(2)}, u32[]{:S(2)}) %collective-permute-start.11) | collective-permute-done | bytes 524320 | tf_op jit(solution)/shard_map/ppermute | solution.py:253
  61.1 0.0 collective-permute-done.12.refs_7_
  61.1 0.2 collective-permute-start.13
  61.4 3.1 %collective-permute-start.14 = (bf16[256,512]{1,0:T(8,128)(2,1)S(1)}, bf16[256,512]{1,0:T(8,128)(2,1)S(1)}, u32[]{:S(2)}, u32[]{:S(2)}) collective-permute-start(bf16[256,512]{1,0:T(8,128)(2,1)S(1)} %slice.7), channel_id=1, source_target_pairs={{0,28},{4,0},{8,4},{12,8},{16,12},{20,16},{24,20},{28,24},{1,29},{... | collective-permute-start | bytes 786440 | tf_op jit(solution)/shard_map/ppermute | solution.py:253
  64.4 0.0 copy-done.8
  64.4 0.0 copy-done.9
  64.4 3.2 %product_next.1.refs_8_ = f32[512,1024]{1,0:T(8,128)S(1)} custom-call(s32[32,64]{1,0:T(8,128)S(1)} %copy-done.1, s32[32,128]{1,0:T(8,128)S(1)} %bitcast.7, bf16[2,512,256]{2,1,0:T(8,128)(2,1)} %copy-done.4, bf16[2,512,256]{2,1,0:T(8,128)(2,1)} %copy-done.5, bf16[2,512,256]{2,1,0:T(8,128)(2,1)} %copy-done.7, ...), custom_call_target="tpu_custom_call", output_to_operand_aliasing={{}: (8, {})} | custom-call | flops 1073741824 | bytes 4194304 | tf_op jit(solution)/shard_map/product_next/pallas_call | solution.py:226
  67.7 1.1 %collective-permute-done.13.refs_6_ = bf16[256,512]{1,0:T(8,128)(2,1)S(1)} collective-permute-done((bf16[256,512]{1,0:T(8,128)(2,1)S(1)}, bf16[256,512]{1,0:T(8,128)(2,1)S(1)}, u32[]{:S(2)}, u32[]{:S(2)}) %collective-permute-start.13) | collective-permute-done | bytes 262176 | tf_op jit(solution)/shard_map/ppermute | solution.py:253
  68.8 0.0 collective-permute-done.14.refs_7_
  68.8 3.0 %product_last.1 = (f32[512,1024]{1,0:T(8,128)S(1)}, f32[1,1024]{1,0:T(1,128)S(1)}) custom-call(s32[32,64]{1,0:T(8,128)S(1)} %copy-done.1, s32[32,128]{1,0:T(8,128)S(1)} %bitcast.8, bf16[2,512,256]{2,1,0:T(8,128)(2,1)} %copy-done.4, bf16[2,512,256]{2,1,0:T(8,128)(2,1)} %copy-done.5, bf16[2,512,256]{2,1,0:T(8,128)(2,1)} %copy-done.7, ...), custom_call_target="tpu_custom_call", output_to_operand_aliasing={{0}: (8, {})} | custom-call | flops 536870912 | bytes 4194304 | tf_op jit(solution)/shard_map/product_last/pallas_call | solution.py:226
  71.8 0.1 broadcast_in_dim.2
  71.8 16.9 %all_to_all.6 = f32[32,1,1024]{2,1,0:T(1,128)S(1)} all-to-all(f32[32,1,1024]{2,1,0:T(1,128)S(1)} %broadcast_in_dim.2), channel_id=1, replica_groups=mesh['y'=4,'core'=2,'z'=8,'x'=4] {'z','x'}, dimensions={0} | all-to-all | bytes 262144 | tf_op jit(solution)/shard_map/all_to_all | solution.py:303
  88.7 0.1 reduce_sum.9
  88.8 1.5 %broadcast_multiply_fusion = f32[512,1024]{1,0:T(8,128)} fusion(f32[512,1024]{1,0:T(8,128)S(1)} %get-tuple-element.43, f32[1024]{0:T(1024)S(1)} %broadcast_divide_fusion), kind=kLoop, calls=%fused_computation | loop fusion | flops 524288 | bytes 4198400 | tf_op jit(solution)/shard_map/mul | solution.py:306
  (13 shorter events, 0.1 us)
Async XLA Ops:
  0.0 50.8 %copy-start.1 = (s32[32,64]{1,0:T(8,128)S(1)}, s32[32,64]{1,0:T(8,128)}, u32[]{:S(2)}) copy-start(s32[32,64]{1,0:T(8,128)} %refs_0_.5) | copy-start | bytes 24580
  0.0 50.9 %copy-start.3 = (s32[128,32]{0,1:T(8,128)S(1)}, s32[128,32]{0,1:T(8,128)}, u32[]{:S(2)}) copy-start(s32[128,32]{0,1:T(8,128)} %param.5) | copy-start | bytes 49156
  1.2 7.9 %collective-permute-start.2 = (bf16[128,512]{1,0:T(8,128)(2,1)S(1)}, bf16[128,512]{1,0:T(8,128)(2,1)S(1)}, u32[]{:S(2)}, u32[]{:S(2)}) collective-permute-start(bf16[128,512]{1,0:T(8,128)(2,1)S(1)} %pack_right.1), channel_id=1, source_target_pairs={{0,2},{1,3},{2,0},{3,1},{4,6},{5,7},{6,4},{7,5},{8,10},{9,11},{10,... | collective-permute-start | bytes 393224 | tf_op jit(solution)/shard_map/ppermute | solution.py:253
  4.3 6.6 %collective-permute-start.1 = (bf16[128,512]{1,0:T(8,128)(2,1)S(1)}, bf16[128,512]{1,0:T(8,128)(2,1)S(1)}, u32[]{:S(2)}, u32[]{:S(2)}) collective-permute-start(bf16[128,512]{1,0:T(8,128)(2,1)S(1)} %pack_right.1), channel_id=1, source_target_pairs={{0,3},{1,0},{2,1},{3,2},{4,7},{5,4},{6,5},{7,6},{8,11},{9,8},{10,9... | collective-permute-start | bytes 393224 | tf_op jit(solution)/shard_map/ppermute | solution.py:253
  5.4 6.2 %collective-permute-start = (bf16[128,512]{1,0:T(8,128)(2,1)S(1)}, bf16[128,512]{1,0:T(8,128)(2,1)S(1)}, u32[]{:S(2)}, u32[]{:S(2)}) collective-permute-start(bf16[128,512]{1,0:T(8,128)(2,1)S(1)} %pack_right.1), channel_id=1, source_target_pairs={{0,1},{1,2},{2,3},{3,0},{4,5},{5,6},{6,7},{7,4},{8,9},{9,10},{10,1... | collective-permute-start | bytes 393224 | tf_op jit(solution)/shard_map/ppermute | solution.py:253
  6.3 1.0 %copy-start = (bf16[512,512]{1,0:T(8,128)(2,1)S(1)}, bf16[512,512]{1,0:T(8,128)(2,1)}, u32[]{:S(2)}) copy-start(bf16[512,512]{1,0:T(8,128)(2,1)} %left) | copy-start | bytes 1572868
  7.4 0.7 copy-start.2
  11.6 6.0 %collective-permute-start.3 = (bf16[512,256]{1,0:T(8,128)(2,1)S(1)}, bf16[512,256]{1,0:T(8,128)(2,1)S(1)}, u32[]{:S(2)}, u32[]{:S(2)}) collective-permute-start(bf16[512,256]{1,0:T(8,128)(2,1)S(1)} %pack_left.1), channel_id=1, source_target_pairs={{0,32},{32,0},{1,33},{33,1},{2,34},{34,2},{3,35},{35,3},{4,36},{36... | collective-permute-start | bytes 786440 | tf_op jit(solution)/shard_map/ppermute | solution.py:253
  11.7 39.1 %copy-start.10 = (bf16[512,512]{1,0:T(8,128)(2,1)}, bf16[512,512]{1,0:T(8,128)(2,1)S(1)}, u32[]{:S(2)}) copy-start(bf16[512,512]{1,0:T(8,128)(2,1)S(1)} %constant_dynamic-update-slice_fusion.refs_6_) | copy-start | bytes 1572868
  11.7 17.8 %collective-permute-start.6 = (bf16[512,512]{1,0:T(8,128)(2,1)S(1)}, bf16[512,512]{1,0:T(8,128)(2,1)S(1)}, u32[]{:S(2)}, u32[]{:S(2)}) collective-permute-start(bf16[512,512]{1,0:T(8,128)(2,1)S(1)} %constant_dynamic-update-slice_fusion.refs_6_), channel_id=1, source_target_pairs={{0,28},{4,0},{8,4},{12,8},{16,12},{20,16},{24,20},{28,24},{1,29},{... | collective-permute-start | bytes 1572872 | tf_op jit(solution)/shard_map/ppermute | solution.py:253
  17.6 15.3 %collective-permute-start.5 = (bf16[512,512]{1,0:T(8,128)(2,1)S(1)}, bf16[512,512]{1,0:T(8,128)(2,1)S(1)}, u32[]{:S(2)}, u32[]{:S(2)}) collective-permute-start(bf16[512,512]{1,0:T(8,128)(2,1)S(1)} %constant_dynamic-update-slice_fusion.refs_6_), channel_id=1, source_target_pairs={{0,4},{4,8},{8,12},{12,16},{16,20},{20,24},{24,28},{28,0},{1,5},{5... | collective-permute-start | bytes 1572872 | tf_op jit(solution)/shard_map/ppermute | solution.py:253
  17.7 33.1 %copy-start.4 = (bf16[2,512,256]{2,1,0:T(8,128)(2,1)}, bf16[2,512,256]{2,1,0:T(8,128)(2,1)S(1)}, u32[]{:S(2)}) copy-start(bf16[2,512,256]{2,1,0:T(8,128)(2,1)S(1)} %pad_maximum_fusion.refs_2_) | copy-start | bytes 1572868
  17.7 15.2 %collective-permute-start.4 = (bf16[2,512,256]{2,1,0:T(8,128)(2,1)S(1)}, bf16[2,512,256]{2,1,0:T(8,128)(2,1)S(1)}, u32[]{:S(2)}, u32[]{:S(2)}) collective-permute-start(bf16[2,512,256]{2,1,0:T(8,128)(2,1)S(1)} %pad_maximum_fusion.refs_2_), channel_id=1, source_target_pairs={{0,64},{32,224},{64,128},{96,32},{128,192},{160,96},{192,0},{224,1... | collective-permute-start | bytes 1572872 | tf_op jit(solution)/shard_map/ppermute | solution.py:263
  29.5 21.3 %copy-start.11 = (bf16[512,512]{1,0:T(8,128)(2,1)}, bf16[512,512]{1,0:T(8,128)(2,1)S(1)}, u32[]{:S(2)}) copy-start(bf16[512,512]{1,0:T(8,128)(2,1)S(1)} %collective-permute-done.6.refs_8_) | copy-start | bytes 1572868
  32.9 17.9 %copy-start.12 = (bf16[512,512]{1,0:T(8,128)(2,1)}, bf16[512,512]{1,0:T(8,128)(2,1)S(1)}, u32[]{:S(2)}) copy-start(bf16[512,512]{1,0:T(8,128)(2,1)S(1)} %collective-permute-done.5.refs_7_) | copy-start | bytes 1572868
  32.9 17.9 %copy-start.5 = (bf16[2,512,256]{2,1,0:T(8,128)(2,1)}, bf16[2,512,256]{2,1,0:T(8,128)(2,1)S(1)}, u32[]{:S(2)}) copy-start(bf16[2,512,256]{2,1,0:T(8,128)(2,1)S(1)} %collective-permute-done.4.refs_3_) | copy-start | bytes 1572868
  32.9 14.5 %collective-permute-start.9 = (bf16[512,512]{1,0:T(8,128)(2,1)S(1)}, bf16[512,512]{1,0:T(8,128)(2,1)S(1)}, u32[]{:S(2)}, u32[]{:S(2)}) collective-permute-start(bf16[512,512]{1,0:T(8,128)(2,1)S(1)} %collective-permute-done.5.refs_7_), channel_id=1, source_target_pairs={{0,4},{4,8},{8,12},{12,16},{16,20},{20,24},{24,28},{28,0},{1,5},{5... | collective-permute-start | bytes 1572872 | tf_op jit(solution)/shard_map/ppermute | solution.py:253
  33.0 14.4 %collective-permute-start.10 = (bf16[512,512]{1,0:T(8,128)(2,1)S(1)}, bf16[512,512]{1,0:T(8,128)(2,1)S(1)}, u32[]{:S(2)}, u32[]{:S(2)}) collective-permute-start(bf16[512,512]{1,0:T(8,128)(2,1)S(1)} %collective-permute-done.6.refs_8_), channel_id=1, source_target_pairs={{0,28},{4,0},{8,4},{12,8},{16,12},{20,16},{24,20},{28,24},{1,29},{... | collective-permute-start | bytes 1572872 | tf_op jit(solution)/shard_map/ppermute | solution.py:253
  36.2 11.2 %collective-permute-start.8 = (bf16[2,512,256]{2,1,0:T(8,128)(2,1)S(1)}, bf16[2,512,256]{2,1,0:T(8,128)(2,1)S(1)}, u32[]{:S(2)}, u32[]{:S(2)}) collective-permute-start(bf16[2,512,256]{2,1,0:T(8,128)(2,1)S(1)} %collective-permute-done.4.refs_3_), channel_id=1, source_target_pairs={{0,64},{32,224},{64,128},{96,32},{128,192},{160,96},{192,0},{224,1... | collective-permute-start | bytes 1572872 | tf_op jit(solution)/shard_map/ppermute | solution.py:263
  36.4 11.0 %collective-permute-start.7 = (bf16[2,512,256]{2,1,0:T(8,128)(2,1)S(1)}, bf16[2,512,256]{2,1,0:T(8,128)(2,1)S(1)}, u32[]{:S(2)}, u32[]{:S(2)}) collective-permute-start(bf16[2,512,256]{2,1,0:T(8,128)(2,1)S(1)} %collective-permute-done.4.refs_3_), channel_id=1, source_target_pairs={{0,32},{32,0},{1,33},{33,1},{2,34},{34,2},{3,35},{35,3},{4,36},{36... | collective-permute-start | bytes 1572872 | tf_op jit(solution)/shard_map/ppermute | solution.py:253
  47.4 3.4 %copy-start.13 = (bf16[512,512]{1,0:T(8,128)(2,1)}, bf16[512,512]{1,0:T(8,128)(2,1)S(1)}, u32[]{:S(2)}) copy-start(bf16[512,512]{1,0:T(8,128)(2,1)S(1)} %collective-permute-done.9.refs_9_) | copy-start | bytes 1572868
  47.4 3.4 %copy-start.14 = (bf16[512,512]{1,0:T(8,128)(2,1)}, bf16[512,512]{1,0:T(8,128)(2,1)S(1)}, u32[]{:S(2)}) copy-start(bf16[512,512]{1,0:T(8,128)(2,1)S(1)} %collective-permute-done.10.refs_10_) | copy-start | bytes 1572868
  47.4 3.4 %copy-start.6 = (bf16[2,512,256]{2,1,0:T(8,128)(2,1)}, bf16[2,512,256]{2,1,0:T(8,128)(2,1)S(1)}, u32[]{:S(2)}) copy-start(bf16[2,512,256]{2,1,0:T(8,128)(2,1)S(1)} %collective-permute-done.8.refs_5_) | copy-start | bytes 1572868
  47.5 3.4 %copy-start.7 = (bf16[2,512,256]{2,1,0:T(8,128)(2,1)}, bf16[2,512,256]{2,1,0:T(8,128)(2,1)S(1)}, u32[]{:S(2)}) copy-start(bf16[2,512,256]{2,1,0:T(8,128)(2,1)S(1)} %collective-permute-done.7.refs_4_) | copy-start | bytes 1572868
  47.5 13.6 %collective-permute-start.11 = (bf16[512,512]{1,0:T(8,128)(2,1)S(1)}, bf16[512,512]{1,0:T(8,128)(2,1)S(1)}, u32[]{:S(2)}, u32[]{:S(2)}) collective-permute-start(bf16[512,512]{1,0:T(8,128)(2,1)S(1)} %collective-permute-done.9.refs_9_), channel_id=1, source_target_pairs={{0,4},{4,8},{8,12},{12,16},{16,20},{20,24},{24,28},{28,0},{1,5},{5... | collective-permute-start | bytes 1572872 | tf_op jit(solution)/shard_map/ppermute | solution.py:253
  47.6 13.5 %collective-permute-start.12 = (bf16[512,512]{1,0:T(8,128)(2,1)S(1)}, bf16[512,512]{1,0:T(8,128)(2,1)S(1)}, u32[]{:S(2)}, u32[]{:S(2)}) collective-permute-start(bf16[512,512]{1,0:T(8,128)(2,1)S(1)} %collective-permute-done.10.refs_10_), channel_id=1, source_target_pairs={{0,28},{4,0},{8,4},{12,8},{16,12},{20,16},{24,20},{28,24},{1,29},{... | collective-permute-start | bytes 1572872 | tf_op jit(solution)/shard_map/ppermute | solution.py:253
  61.1 3.4 %copy-start.8 = (bf16[512,512]{1,0:T(8,128)(2,1)}, bf16[512,512]{1,0:T(8,128)(2,1)S(1)}, u32[]{:S(2)}) copy-start(bf16[512,512]{1,0:T(8,128)(2,1)S(1)} %collective-permute-done.11.refs_6_) | copy-start | bytes 1572868
  61.1 3.4 %copy-start.9 = (bf16[512,512]{1,0:T(8,128)(2,1)}, bf16[512,512]{1,0:T(8,128)(2,1)S(1)}, u32[]{:S(2)}) copy-start(bf16[512,512]{1,0:T(8,128)(2,1)S(1)} %collective-permute-done.12.refs_7_) | copy-start | bytes 1572868
  61.1 7.7 %collective-permute-start.13 = (bf16[256,512]{1,0:T(8,128)(2,1)S(1)}, bf16[256,512]{1,0:T(8,128)(2,1)S(1)}, u32[]{:S(2)}, u32[]{:S(2)}) collective-permute-start(bf16[256,512]{1,0:T(8,128)(2,1)S(1)} %slice.6), channel_id=1, source_target_pairs={{0,4},{4,8},{8,12},{12,16},{16,20},{20,24},{24,28},{28,0},{1,5},{5... | collective-permute-start | bytes 786440 | tf_op jit(solution)/shard_map/ppermute | solution.py:253
  61.4 7.4 %collective-permute-start.14 = (bf16[256,512]{1,0:T(8,128)(2,1)S(1)}, bf16[256,512]{1,0:T(8,128)(2,1)S(1)}, u32[]{:S(2)}, u32[]{:S(2)}) collective-permute-start(bf16[256,512]{1,0:T(8,128)(2,1)S(1)} %slice.7), channel_id=1, source_target_pairs={{0,28},{4,0},{8,4},{12,8},{16,12},{20,16},{24,20},{28,24},{1,29},{... | collective-permute-start | bytes 786440 | tf_op jit(solution)/shard_map/ppermute | solution.py:253

commit v10 on v9

--- a/solution.py
+++ b/solution.py
@@ -269,9 +269,9 @@
     near = [packed_right] + [moved(packed_right, "x", -shift) for shift in SHIFTS[1:]]
     left_values, _ = lax.optimization_barrier((left_values, packed_right))
     packed_left = pack(pack_left_kernel, "pack_left", left_pattern, left_values, LEFT_SLOTS)
-    near, packed_left = lax.optimization_barrier((near, packed_left))
+    own, packed_left = lax.optimization_barrier((jnp.concatenate(near, 0), packed_left))
     other_left = moved(packed_left, "core", 1)
-    came = {0: jnp.concatenate(near, 0)}
+    came = {0: own}
     whole = came[0].shape[0]
     half = whole // 2
 

time: 90.6 us -> 90.5 us (level)
    unnamed x33 -> x30, local copies, waits for them, and re-layouts: 1.84 us -> 1.81 us
where the time goes in v10:
time: 90.5 us; the launch traced here: 90.2 us
  waiting for transfers between devices  33.9 us (37%)
  starting transfers between devices  21.6 us (24%)
  blocking collectives  16.9 us (19%)
  Pallas kernels  14 us (15%)
  local copies, waits for them, and re-layouts  1.92 us (2%)
  other arithmetic  1.73 us (2%)
    ppermute x13, waiting for transfers between devices, moved(): lax.ppermute(value, axis, [(i, (i + step) % size) for i in range(size)])  33.9 us
    ppermute x13, starting transfers between devices, moved(): lax.ppermute(value, axis, [(i, (i + step) % size) for i in range(size)])  21.1 us
    all_to_all x1, blocking collectives, shards(): lax.all_to_all(jnp.broadcast_to(sums, (count, sums.shape[1])), COL, 0, 0,...  16.9 us
    pallas_call x3, Pallas kernels, product(): pl.pallas_call(functools.partial(product_kernel, blocks, copies, total is...  11.8 us
    unnamed x30, local copies, waits for them, and re-layouts  1.81 us
  transfers between devices with their start and end apart: 15, of which 7 were waited for; matrix products, arithmetic and copies ran while one was open for 0% of the time, Pallas kernels for 11%

profile of v10, /device:TPU:24, one launch (start us, length us, event | category | flops | bytes accessed | tf_op | source)
XLA Modules:
  0.0 90.2 jit_solution(14176793981252536849)
XLA Ops:
  0.0 0.0 copy-start.1
  0.0 0.0 copy-start.3
  0.0 1.2 %pack_right.1 = bf16[128,512]{1,0:T(8,128)(2,1)S(1)} custom-call(s32[32,64]{1,0:T(8,128)} %refs_0_.5, bf16[128,1024]{1,0:T(8,128)(2,1)} %right_hbm.1), custom_call_target="tpu_custom_call" | custom-call | tf_op jit(solution)/shard_map/pack_right/pallas_call | solution.py:58
  1.2 3.1 %collective-permute-start.2 = (bf16[128,512]{1,0:T(8,128)(2,1)S(1)}, bf16[128,512]{1,0:T(8,128)(2,1)S(1)}, u32[]{:S(2)}, u32[]{:S(2)}) collective-permute-start(bf16[128,512]{1,0:T(8,128)(2,1)S(1)} %pack_right.1), channel_id=1, source_target_pairs={{0,2},{1,3},{2,0},{3,1},{4,6},{5,7},{6,4},{7,5},{8,10},{9,11},{10,... | collective-permute-start | bytes 393224 | tf_op jit(solution)/shard_map/ppermute | solution.py:253
  4.3 1.1 %collective-permute-start.1 = (bf16[128,512]{1,0:T(8,128)(2,1)S(1)}, bf16[128,512]{1,0:T(8,128)(2,1)S(1)}, u32[]{:S(2)}, u32[]{:S(2)}) collective-permute-start(bf16[128,512]{1,0:T(8,128)(2,1)S(1)} %pack_right.1), channel_id=1, source_target_pairs={{0,3},{1,0},{2,1},{3,2},{4,7},{5,4},{6,5},{7,6},{8,11},{9,8},{10,9... | collective-permute-start | bytes 393224 | tf_op jit(solution)/shard_map/ppermute | solution.py:253
  5.4 0.9 collective-permute-start
  6.3 1.0 %copy-done = bf16[512,512]{1,0:T(8,128)(2,1)S(1)} copy-done((bf16[512,512]{1,0:T(8,128)(2,1)S(1)}, bf16[512,512]{1,0:T(8,128)(2,1)}, u32[]{:S(2)}) %copy-start) | copy-done | bytes 524312
  7.4 0.0 copy-start.2
  7.4 0.7 copy-done.2
  8.1 1.0 %pack_left.1 = bf16[512,256]{1,0:T(8,128)(2,1)S(1)} custom-call(s32[32,128]{1,0:T(8,128)S(1)} %bitcast.5, bf16[512,512]{1,0:T(8,128)(2,1)S(1)} %copy-done), custom_call_target="tpu_custom_call" | custom-call | tf_op jit(solution)/shard_map/pack_left/pallas_call | solution.py:91
  9.1 0.0 collective-permute-done.2
  9.1 1.8 %collective-permute-done.1 = bf16[128,512]{1,0:T(8,128)(2,1)S(1)} collective-permute-done((bf16[128,512]{1,0:T(8,128)(2,1)S(1)}, bf16[128,512]{1,0:T(8,128)(2,1)S(1)}, u32[]{:S(2)}, u32[]{:S(2)}) %collective-permute-start.1) | collective-permute-done | bytes 131104 | tf_op jit(solution)/shard_map/ppermute | solution.py:253
  10.9 0.7 collective-permute-done
  11.7 0.0 copy-start.10
  11.7 0.1 collective-permute-start.3
  11.8 5.9 %collective-permute-start.6 = (bf16[512,512]{1,0:T(8,128)(2,1)S(1)}, bf16[512,512]{1,0:T(8,128)(2,1)S(1)}, u32[]{:S(2)}, u32[]{:S(2)}) collective-permute-start(bf16[512,512]{1,0:T(8,128)(2,1)S(1)} %pad_maximum_fusion.refs_6_), channel_id=1, source_target_pairs={{0,28},{4,0},{8,4},{12,8},{16,12},{20,16},{24,20},{28,24},{1,29},{... | collective-permute-start | bytes 1572872 | tf_op jit(solution)/shard_map/ppermute | solution.py:253
  17.7 0.0 collective-permute-start.5
  17.7 0.0 collective-permute-done.3
  17.7 0.1 pad_maximum_fusion.1.refs_2_
  17.8 0.0 copy-start.4
  17.8 0.3 collective-permute-start.4
  18.1 11.4 %collective-permute-done.6.refs_8_ = bf16[512,512]{1,0:T(8,128)(2,1)S(1)} collective-permute-done((bf16[512,512]{1,0:T(8,128)(2,1)S(1)}, bf16[512,512]{1,0:T(8,128)(2,1)S(1)}, u32[]{:S(2)}, u32[]{:S(2)}) %collective-permute-start.6) | collective-permute-done | bytes 524320 | tf_op jit(solution)/shard_map/ppermute | solution.py:253
  29.5 0.0 copy-start.11
  29.5 3.4 %collective-permute-done.5.refs_7_ = bf16[512,512]{1,0:T(8,128)(2,1)S(1)} collective-permute-done((bf16[512,512]{1,0:T(8,128)(2,1)S(1)}, bf16[512,512]{1,0:T(8,128)(2,1)S(1)}, u32[]{:S(2)}, u32[]{:S(2)}) %collective-permute-start.5) | collective-permute-done | bytes 524320 | tf_op jit(solution)/shard_map/ppermute | solution.py:253
  32.9 0.0 copy-start.12
  32.9 0.0 collective-permute-done.4.refs_3_
  32.9 0.1 collective-permute-start.9
  33.0 3.2 %collective-permute-start.10 = (bf16[512,512]{1,0:T(8,128)(2,1)S(1)}, bf16[512,512]{1,0:T(8,128)(2,1)S(1)}, u32[]{:S(2)}, u32[]{:S(2)}) collective-permute-start(bf16[512,512]{1,0:T(8,128)(2,1)S(1)} %collective-permute-done.6.refs_8_), channel_id=1, source_target_pairs={{0,28},{4,0},{8,4},{12,8},{16,12},{20,16},{24,20},{28,24},{1,29},{... | collective-permute-start | bytes 1572872 | tf_op jit(solution)/shard_map/ppermute | solution.py:253
  36.2 0.2 collective-permute-start.8
  36.4 0.0 collective-permute-start.7
  36.4 10.9 %collective-permute-done.9.refs_9_ = bf16[512,512]{1,0:T(8,128)(2,1)S(1)} collective-permute-done((bf16[512,512]{1,0:T(8,128)(2,1)S(1)}, bf16[512,512]{1,0:T(8,128)(2,1)S(1)}, u32[]{:S(2)}, u32[]{:S(2)}) %collective-permute-start.9) | collective-permute-done | bytes 524320 | tf_op jit(solution)/shard_map/ppermute | solution.py:253
  47.3 0.0 collective-permute-done.10.refs_10_
  47.3 0.0 collective-permute-done.8.refs_5_
  47.4 0.0 copy-start.6
  47.4 0.0 collective-permute-done.7.refs_4_
  47.4 0.0 copy-start.7
  47.4 0.1 collective-permute-start.11
  47.5 3.2 %collective-permute-start.12 = (bf16[512,512]{1,0:T(8,128)(2,1)S(1)}, bf16[512,512]{1,0:T(8,128)(2,1)S(1)}, u32[]{:S(2)}, u32[]{:S(2)}) collective-permute-start(bf16[512,512]{1,0:T(8,128)(2,1)S(1)} %collective-permute-done.10.refs_10_), channel_id=1, source_target_pairs={{0,28},{4,0},{8,4},{12,8},{16,12},{20,16},{24,20},{28,24},{1,29},{... | collective-permute-start | bytes 1572872 | tf_op jit(solution)/shard_map/ppermute | solution.py:253
  50.7 0.0 copy-done.10
  50.7 0.0 copy-done.4
  50.7 0.0 copy-done.11
  50.7 0.0 copy-done.12
  50.7 0.0 copy-done.5
  50.7 0.0 copy-done.13
  50.7 0.0 copy-done.14
  50.7 0.0 copy-done.6
  50.8 0.0 copy-done.7
  50.8 0.0 copy-done.1
  50.8 0.0 copy-done.3
  50.8 5.6 %product_first.1.refs_8_ = f32[512,1024]{1,0:T(8,128)S(1)} custom-call(s32[32,64]{1,0:T(8,128)S(1)} %copy-done.1, s32[32,128]{1,0:T(8,128)S(1)} %bitcast.6, bf16[2,512,256]{2,1,0:T(8,128)(2,1)} %copy-done.4, bf16[2,512,256]{2,1,0:T(8,128)(2,1)} %copy-done.5, bf16[2,512,256]{2,1,0:T(8,128)(2,1)} %copy-done.7, bf16[2,512,256]{2,1,0:T(8,128)(2,1)} %copy-done.6, ...), custom_call_target="tpu_custom_call" | custom-call | flops 2684354560 | bytes 4194304 | tf_op jit(solution)/shard_map/product_first/pallas_call | solution.py:226
  56.4 4.5 %collective-permute-done.11.refs_6_ = bf16[512,512]{1,0:T(8,128)(2,1)S(1)} collective-permute-done((bf16[512,512]{1,0:T(8,128)(2,1)S(1)}, bf16[512,512]{1,0:T(8,128)(2,1)S(1)}, u32[]{:S(2)}, u32[]{:S(2)}) %collective-permute-start.11) | collective-permute-done | bytes 524320 | tf_op jit(solution)/shard_map/ppermute | solution.py:253
  60.9 0.0 collective-permute-done.12.refs_7_
  61.0 0.1 collective-permute-start.13
  61.1 3.2 %collective-permute-start.14 = (bf16[256,512]{1,0:T(8,128)(2,1)S(1)}, bf16[256,512]{1,0:T(8,128)(2,1)S(1)}, u32[]{:S(2)}, u32[]{:S(2)}) collective-permute-start(bf16[256,512]{1,0:T(8,128)(2,1)S(1)} %slice.7), channel_id=1, source_target_pairs={{0,28},{4,0},{8,4},{12,8},{16,12},{20,16},{24,20},{28,24},{1,29},{... | collective-permute-start | bytes 786440 | tf_op jit(solution)/shard_map/ppermute | solution.py:253
  64.3 0.0 copy-done.8
  64.3 0.0 copy-done.9
  64.3 3.2 %product_next.1.refs_8_ = f32[512,1024]{1,0:T(8,128)S(1)} custom-call(s32[32,64]{1,0:T(8,128)S(1)} %copy-done.1, s32[32,128]{1,0:T(8,128)S(1)} %bitcast.7, bf16[2,512,256]{2,1,0:T(8,128)(2,1)} %copy-done.4, bf16[2,512,256]{2,1,0:T(8,128)(2,1)} %copy-done.5, bf16[2,512,256]{2,1,0:T(8,128)(2,1)} %copy-done.7, ...), custom_call_target="tpu_custom_call", output_to_operand_aliasing={{}: (8, {})} | custom-call | flops 1073741824 | bytes 4194304 | tf_op jit(solution)/shard_map/product_next/pallas_call | solution.py:226
  67.5 1.1 %collective-permute-done.13.refs_6_ = bf16[256,512]{1,0:T(8,128)(2,1)S(1)} collective-permute-done((bf16[256,512]{1,0:T(8,128)(2,1)S(1)}, bf16[256,512]{1,0:T(8,128)(2,1)S(1)}, u32[]{:S(2)}, u32[]{:S(2)}) %collective-permute-start.13) | collective-permute-done | bytes 262176 | tf_op jit(solution)/shard_map/ppermute | solution.py:253
  68.6 0.0 collective-permute-done.14.refs_7_
  68.6 3.0 %product_last.1 = (f32[512,1024]{1,0:T(8,128)S(1)}, f32[1,1024]{1,0:T(1,128)S(1)}) custom-call(s32[32,64]{1,0:T(8,128)S(1)} %copy-done.1, s32[32,128]{1,0:T(8,128)S(1)} %bitcast.8, bf16[2,512,256]{2,1,0:T(8,128)(2,1)} %copy-done.4, bf16[2,512,256]{2,1,0:T(8,128)(2,1)} %copy-done.5, bf16[2,512,256]{2,1,0:T(8,128)(2,1)} %copy-done.7, ...), custom_call_target="tpu_custom_call", output_to_operand_aliasing={{0}: (8, {})} | custom-call | flops 536870912 | bytes 4194304 | tf_op jit(solution)/shard_map/product_last/pallas_call | solution.py:226
  71.6 0.1 broadcast_in_dim.2
  71.7 16.9 %all_to_all.6 = f32[32,1,1024]{2,1,0:T(1,128)S(1)} all-to-all(f32[32,1,1024]{2,1,0:T(1,128)S(1)} %broadcast_in_dim.2), channel_id=1, replica_groups=mesh['y'=4,'core'=2,'z'=8,'x'=4] {'z','x'}, dimensions={0} | all-to-all | bytes 262144 | tf_op jit(solution)/shard_map/all_to_all | solution.py:303
  88.5 0.1 reduce_sum.9
  88.7 1.5 %broadcast_multiply_fusion = f32[512,1024]{1,0:T(8,128)} fusion(f32[512,1024]{1,0:T(8,128)S(1)} %get-tuple-element.37, f32[1024]{0:T(1024)S(1)} %broadcast_divide_fusion), kind=kLoop, calls=%fused_computation | loop fusion | flops 524288 | bytes 4198400 | tf_op jit(solution)/shard_map/mul | solution.py:306
  (10 shorter events, 0.1 us)
Async XLA Ops:
  0.0 50.8 %copy-start.1 = (s32[32,64]{1,0:T(8,128)S(1)}, s32[32,64]{1,0:T(8,128)}, u32[]{:S(2)}) copy-start(s32[32,64]{1,0:T(8,128)} %refs_0_.5) | copy-start | bytes 24580
  0.0 50.8 %copy-start.3 = (s32[128,32]{0,1:T(8,128)S(1)}, s32[128,32]{0,1:T(8,128)}, u32[]{:S(2)}) copy-start(s32[128,32]{0,1:T(8,128)} %param.5) | copy-start | bytes 49156
  1.2 7.9 %collective-permute-start.2 = (bf16[128,512]{1,0:T(8,128)(2,1)S(1)}, bf16[128,512]{1,0:T(8,128)(2,1)S(1)}, u32[]{:S(2)}, u32[]{:S(2)}) collective-permute-start(bf16[128,512]{1,0:T(8,128)(2,1)S(1)} %pack_right.1), channel_id=1, source_target_pairs={{0,2},{1,3},{2,0},{3,1},{4,6},{5,7},{6,4},{7,5},{8,10},{9,11},{10,... | collective-permute-start | bytes 393224 | tf_op jit(solution)/shard_map/ppermute | solution.py:253
  4.3 6.6 %collective-permute-start.1 = (bf16[128,512]{1,0:T(8,128)(2,1)S(1)}, bf16[128,512]{1,0:T(8,128)(2,1)S(1)}, u32[]{:S(2)}, u32[]{:S(2)}) collective-permute-start(bf16[128,512]{1,0:T(8,128)(2,1)S(1)} %pack_right.1), channel_id=1, source_target_pairs={{0,3},{1,0},{2,1},{3,2},{4,7},{5,4},{6,5},{7,6},{8,11},{9,8},{10,9... | collective-permute-start | bytes 393224 | tf_op jit(solution)/shard_map/ppermute | solution.py:253
  5.4 6.2 %collective-permute-start = (bf16[128,512]{1,0:T(8,128)(2,1)S(1)}, bf16[128,512]{1,0:T(8,128)(2,1)S(1)}, u32[]{:S(2)}, u32[]{:S(2)}) collective-permute-start(bf16[128,512]{1,0:T(8,128)(2,1)S(1)} %pack_right.1), channel_id=1, source_target_pairs={{0,1},{1,2},{2,3},{3,0},{4,5},{5,6},{6,7},{7,4},{8,9},{9,10},{10,1... | collective-permute-start | bytes 393224 | tf_op jit(solution)/shard_map/ppermute | solution.py:253
  6.3 1.0 %copy-start = (bf16[512,512]{1,0:T(8,128)(2,1)S(1)}, bf16[512,512]{1,0:T(8,128)(2,1)}, u32[]{:S(2)}) copy-start(bf16[512,512]{1,0:T(8,128)(2,1)} %left) | copy-start | bytes 1572868
  7.4 0.7 copy-start.2
  11.7 39.0 %copy-start.10 = (bf16[512,512]{1,0:T(8,128)(2,1)}, bf16[512,512]{1,0:T(8,128)(2,1)S(1)}, u32[]{:S(2)}) copy-start(bf16[512,512]{1,0:T(8,128)(2,1)S(1)} %pad_maximum_fusion.refs_6_) | copy-start | bytes 1572868
  11.7 6.0 %collective-permute-start.3 = (bf16[512,256]{1,0:T(8,128)(2,1)S(1)}, bf16[512,256]{1,0:T(8,128)(2,1)S(1)}, u32[]{:S(2)}, u32[]{:S(2)}) collective-permute-start(bf16[512,256]{1,0:T(8,128)(2,1)S(1)} %pack_left.1), channel_id=1, source_target_pairs={{0,32},{32,0},{1,33},{33,1},{2,34},{34,2},{3,35},{35,3},{4,36},{36... | collective-permute-start | bytes 786440 | tf_op jit(solution)/shard_map/ppermute | solution.py:253
  11.8 17.7 %collective-permute-start.6 = (bf16[512,512]{1,0:T(8,128)(2,1)S(1)}, bf16[512,512]{1,0:T(8,128)(2,1)S(1)}, u32[]{:S(2)}, u32[]{:S(2)}) collective-permute-start(bf16[512,512]{1,0:T(8,128)(2,1)S(1)} %pad_maximum_fusion.refs_6_), channel_id=1, source_target_pairs={{0,28},{4,0},{8,4},{12,8},{16,12},{20,16},{24,20},{28,24},{1,29},{... | collective-permute-start | bytes 1572872 | tf_op jit(solution)/shard_map/ppermute | solution.py:253
  17.7 15.2 %collective-permute-start.5 = (bf16[512,512]{1,0:T(8,128)(2,1)S(1)}, bf16[512,512]{1,0:T(8,128)(2,1)S(1)}, u32[]{:S(2)}, u32[]{:S(2)}) collective-permute-start(bf16[512,512]{1,0:T(8,128)(2,1)S(1)} %pad_maximum_fusion.refs_6_), channel_id=1, source_target_pairs={{0,4},{4,8},{8,12},{12,16},{16,20},{20,24},{24,28},{28,0},{1,5},{5... | collective-permute-start | bytes 1572872 | tf_op jit(solution)/shard_map/ppermute | solution.py:253
  17.8 32.9 %copy-start.4 = (bf16[2,512,256]{2,1,0:T(8,128)(2,1)}, bf16[2,512,256]{2,1,0:T(8,128)(2,1)S(1)}, u32[]{:S(2)}) copy-start(bf16[2,512,256]{2,1,0:T(8,128)(2,1)S(1)} %pad_maximum_fusion.1.refs_2_) | copy-start | bytes 1572868
  17.8 15.1 %collective-permute-start.4 = (bf16[2,512,256]{2,1,0:T(8,128)(2,1)S(1)}, bf16[2,512,256]{2,1,0:T(8,128)(2,1)S(1)}, u32[]{:S(2)}, u32[]{:S(2)}) collective-permute-start(bf16[2,512,256]{2,1,0:T(8,128)(2,1)S(1)} %pad_maximum_fusion.1.refs_2_), channel_id=1, source_target_pairs={{0,64},{32,224},{64,128},{96,32},{128,192},{160,96},{192,0},{224,1... | collective-permute-start | bytes 1572872 | tf_op jit(solution)/shard_map/ppermute | solution.py:263
  29.5 21.2 %copy-start.11 = (bf16[512,512]{1,0:T(8,128)(2,1)}, bf16[512,512]{1,0:T(8,128)(2,1)S(1)}, u32[]{:S(2)}) copy-start(bf16[512,512]{1,0:T(8,128)(2,1)S(1)} %collective-permute-done.6.refs_8_) | copy-start | bytes 1572868
  32.9 17.8 %copy-start.12 = (bf16[512,512]{1,0:T(8,128)(2,1)}, bf16[512,512]{1,0:T(8,128)(2,1)S(1)}, u32[]{:S(2)}) copy-start(bf16[512,512]{1,0:T(8,128)(2,1)S(1)} %collective-permute-done.5.refs_7_) | copy-start | bytes 1572868
  32.9 17.8 %copy-start.5 = (bf16[2,512,256]{2,1,0:T(8,128)(2,1)}, bf16[2,512,256]{2,1,0:T(8,128)(2,1)S(1)}, u32[]{:S(2)}) copy-start(bf16[2,512,256]{2,1,0:T(8,128)(2,1)S(1)} %collective-permute-done.4.refs_3_) | copy-start | bytes 1572868
  32.9 14.4 %collective-permute-start.9 = (bf16[512,512]{1,0:T(8,128)(2,1)S(1)}, bf16[512,512]{1,0:T(8,128)(2,1)S(1)}, u32[]{:S(2)}, u32[]{:S(2)}) collective-permute-start(bf16[512,512]{1,0:T(8,128)(2,1)S(1)} %collective-permute-done.5.refs_7_), channel_id=1, source_target_pairs={{0,4},{4,8},{8,12},{12,16},{16,20},{20,24},{24,28},{28,0},{1,5},{5... | collective-permute-start | bytes 1572872 | tf_op jit(solution)/shard_map/ppermute | solution.py:253
  33.0 14.4 %collective-permute-start.10 = (bf16[512,512]{1,0:T(8,128)(2,1)S(1)}, bf16[512,512]{1,0:T(8,128)(2,1)S(1)}, u32[]{:S(2)}, u32[]{:S(2)}) collective-permute-start(bf16[512,512]{1,0:T(8,128)(2,1)S(1)} %collective-permute-done.6.refs_8_), channel_id=1, source_target_pairs={{0,28},{4,0},{8,4},{12,8},{16,12},{20,16},{24,20},{28,24},{1,29},{... | collective-permute-start | bytes 1572872 | tf_op jit(solution)/shard_map/ppermute | solution.py:253
  36.2 11.1 %collective-permute-start.8 = (bf16[2,512,256]{2,1,0:T(8,128)(2,1)S(1)}, bf16[2,512,256]{2,1,0:T(8,128)(2,1)S(1)}, u32[]{:S(2)}, u32[]{:S(2)}) collective-permute-start(bf16[2,512,256]{2,1,0:T(8,128)(2,1)S(1)} %collective-permute-done.4.refs_3_), channel_id=1, source_target_pairs={{0,64},{32,224},{64,128},{96,32},{128,192},{160,96},{192,0},{224,1... | collective-permute-start | bytes 1572872 | tf_op jit(solution)/shard_map/ppermute | solution.py:263
  36.4 10.9 %collective-permute-start.7 = (bf16[2,512,256]{2,1,0:T(8,128)(2,1)S(1)}, bf16[2,512,256]{2,1,0:T(8,128)(2,1)S(1)}, u32[]{:S(2)}, u32[]{:S(2)}) collective-permute-start(bf16[2,512,256]{2,1,0:T(8,128)(2,1)S(1)} %collective-permute-done.4.refs_3_), channel_id=1, source_target_pairs={{0,32},{32,0},{1,33},{33,1},{2,34},{34,2},{3,35},{35,3},{4,36},{36... | collective-permute-start | bytes 1572872 | tf_op jit(solution)/shard_map/ppermute | solution.py:253
  47.3 3.4 %copy-start.13 = (bf16[512,512]{1,0:T(8,128)(2,1)}, bf16[512,512]{1,0:T(8,128)(2,1)S(1)}, u32[]{:S(2)}) copy-start(bf16[512,512]{1,0:T(8,128)(2,1)S(1)} %collective-permute-done.9.refs_9_) | copy-start | bytes 1572868
  47.3 3.4 %copy-start.14 = (bf16[512,512]{1,0:T(8,128)(2,1)}, bf16[512,512]{1,0:T(8,128)(2,1)S(1)}, u32[]{:S(2)}) copy-start(bf16[512,512]{1,0:T(8,128)(2,1)S(1)} %collective-permute-done.10.refs_10_) | copy-start | bytes 1572868
  47.4 3.4 %copy-start.6 = (bf16[2,512,256]{2,1,0:T(8,128)(2,1)}, bf16[2,512,256]{2,1,0:T(8,128)(2,1)S(1)}, u32[]{:S(2)}) copy-start(bf16[2,512,256]{2,1,0:T(8,128)(2,1)S(1)} %collective-permute-done.8.refs_5_) | copy-start | bytes 1572868
  47.4 3.4 %copy-start.7 = (bf16[2,512,256]{2,1,0:T(8,128)(2,1)}, bf16[2,512,256]{2,1,0:T(8,128)(2,1)S(1)}, u32[]{:S(2)}) copy-start(bf16[2,512,256]{2,1,0:T(8,128)(2,1)S(1)} %collective-permute-done.7.refs_4_) | copy-start | bytes 1572868
  47.4 13.5 %collective-permute-start.11 = (bf16[512,512]{1,0:T(8,128)(2,1)S(1)}, bf16[512,512]{1,0:T(8,128)(2,1)S(1)}, u32[]{:S(2)}, u32[]{:S(2)}) collective-permute-start(bf16[512,512]{1,0:T(8,128)(2,1)S(1)} %collective-permute-done.9.refs_9_), channel_id=1, source_target_pairs={{0,4},{4,8},{8,12},{12,16},{16,20},{20,24},{24,28},{28,0},{1,5},{5... | collective-permute-start | bytes 1572872 | tf_op jit(solution)/shard_map/ppermute | solution.py:253
  47.5 13.4 %collective-permute-start.12 = (bf16[512,512]{1,0:T(8,128)(2,1)S(1)}, bf16[512,512]{1,0:T(8,128)(2,1)S(1)}, u32[]{:S(2)}, u32[]{:S(2)}) collective-permute-start(bf16[512,512]{1,0:T(8,128)(2,1)S(1)} %collective-permute-done.10.refs_10_), channel_id=1, source_target_pairs={{0,28},{4,0},{8,4},{12,8},{16,12},{20,16},{24,20},{28,24},{1,29},{... | collective-permute-start | bytes 1572872 | tf_op jit(solution)/shard_map/ppermute | solution.py:253
  60.9 3.4 %copy-start.8 = (bf16[512,512]{1,0:T(8,128)(2,1)}, bf16[512,512]{1,0:T(8,128)(2,1)S(1)}, u32[]{:S(2)}) copy-start(bf16[512,512]{1,0:T(8,128)(2,1)S(1)} %collective-permute-done.11.refs_6_) | copy-start | bytes 1572868
  60.9 3.4 %copy-start.9 = (bf16[512,512]{1,0:T(8,128)(2,1)}, bf16[512,512]{1,0:T(8,128)(2,1)S(1)}, u32[]{:S(2)}) copy-start(bf16[512,512]{1,0:T(8,128)(2,1)S(1)} %collective-permute-done.12.refs_7_) | copy-start | bytes 1572868
  61.0 7.7 %collective-permute-start.13 = (bf16[256,512]{1,0:T(8,128)(2,1)S(1)}, bf16[256,512]{1,0:T(8,128)(2,1)S(1)}, u32[]{:S(2)}, u32[]{:S(2)}) collective-permute-start(bf16[256,512]{1,0:T(8,128)(2,1)S(1)} %slice.6), channel_id=1, source_target_pairs={{0,4},{4,8},{8,12},{12,16},{16,20},{20,24},{24,28},{28,0},{1,5},{5... | collective-permute-start | bytes 786440 | tf_op jit(solution)/shard_map/ppermute | solution.py:253
  61.1 7.6 %collective-permute-start.14 = (bf16[256,512]{1,0:T(8,128)(2,1)S(1)}, bf16[256,512]{1,0:T(8,128)(2,1)S(1)}, u32[]{:S(2)}, u32[]{:S(2)}) collective-permute-start(bf16[256,512]{1,0:T(8,128)(2,1)S(1)} %slice.7), channel_id=1, source_target_pairs={{0,28},{4,0},{8,4},{12,8},{16,12},{20,16},{24,20},{28,24},{1,29},{... | collective-permute-start | bytes 786440 | tf_op jit(solution)/shard_map/ppermute | solution.py:253
